TPU v7x, 256 devices: a whole 4x4x8 slice. The times are simulated.
256 devices in a mesh: row: 16 (over y, z_hi, core), col: 16 (over x, z_lo).
Axes of the slice: x: 4, y: 4, z: 8 (z_hi: 2, z_lo: 4; z = z_hi * 4 + z_lo), core: 2. Of those that a mesh axis runs over, the one named last changes fastest.
Arguments:
- values: bfloat16 [65536, 128], P('row'), may hold values from -30 to 30
- points0: bfloat16 [2, 65536], P(None, 'row'), may hold values from 0 to 1
- points1: bfloat16 [2, 16384], P(None, 'row'), may hold values from 0 to 1
- points2: bfloat16 [2, 2048], P(None, 'row'), may hold values from 0 to 1
- tiles_a0: int32 [16, 16, 2, 384], P('row', 'col'), may hold values from 0 to 31, as said below
- tiles_e1: int32 [16, 16, 2, 160], P('row', 'col'), may hold values from 0 to 31, as said below
- tiles_a1: int32 [16, 16, 2, 32], P('row', 'col'), may hold values from 0 to 7, as said below
- factor: bfloat16 [2048, 2048], P('row', 'col'), as said below
Outputs:
- fine_coef: float32 [65536, 128], P(('row', 'col'))
- mid_coef: float32 [16384, 128], P('col')
- coarse_coef: float32 [2048, 128], P('row')
- norms: float32 [1], replicated
Inputs may be any that keep to these rules, and one draw needn't show every extreme that they name: `tiles_a0`: within each block the 384 listed tile pairs are distinct; tile rows are below 32 and tile columns below 32. `tiles_e1`: within each block the 160 listed tile pairs are distinct; tile rows are below 32 and tile columns below 8. `tiles_a1`: within each block the 32 listed tile pairs are distinct; tile rows are below 8 and tile columns below 8. `factor`: upper triangular; diagonal entries from 1 to 2.
All inputs are finite; a program needn't handle non-finite values.
Results may differ from a plain program's by a relative error of at most 0.0042.
Values may be sent and summed in bfloat16 or wider, within the bound.
No kernel may reach another device: no remote copies, remote signals or barrier semaphores. Data moves between devices by JAX's collectives and lax.ppermute only.
A program may use at most 64 MiB of HBM per device.

v0:
```python
import math

import jax
import jax.numpy as jnp
from jax import lax
from jax.sharding import PartitionSpec as P

TILE = 128


support_fine = 0.35
support_mid = 0.55
support_coarse = 0.8


def picked(x, axis, root):
    return lax.dynamic_index_in_dim(lax.all_gather(x, axis), root, 0, keepdims=False)


def in_blocks(x, dim, peers):
    dims = x.shape
    blocks = x.reshape(*dims[:dim], peers, dims[dim] // peers, *dims[dim + 1 :])
    return jnp.moveaxis(blocks, dim, 0)


def summed_on_arrival(x, axis, dim):
    blocks = in_blocks(x, dim, lax.axis_size(axis))
    arrived = lax.all_to_all(blocks, axis, split_axis=0, concat_axis=0, tiled=True)
    return arrived.sum(axis=0)


def rows_for(lines, peers):
    spare = -len(lines) % peers
    return jnp.pad(lines, [(0, spare)] + [(0, 0)] * (lines.ndim - 1))


def from_everyone(x, axis):
    copies = jnp.broadcast_to(x, (lax.axis_size(axis), *x.shape))
    return lax.all_to_all(copies, axis, split_axis=0, concat_axis=0, tiled=True)


def in_order(blocks, dim):
    blocks = jnp.moveaxis(blocks, 0, dim)
    dims = blocks.shape
    return blocks.reshape(*dims[:dim], dims[dim] * dims[dim + 1], *dims[dim + 2 :])


def gather_directly(x, axis, dim):
    blocks = from_everyone(x, axis)
    return in_order(blocks, dim)


def total_of(x, axes):
    lines = x.reshape(-1, x.shape[-1])
    own = summed_on_arrival(rows_for(lines, lax.axis_size(axes)), axes, 0)
    whole = gather_directly(own, axes, 0)
    return whole[: len(lines)].reshape(x.shape)


def total_of_2(x, axes):
    own = summed_on_arrival(rows_for(x, lax.axis_size(axes)), axes, 0)
    whole = gather_directly(own, axes, 0)
    return whole[: len(x)].reshape(x.shape)


def in_one(arrays, axis):
    ends = [0]
    for a in arrays:
        ends.append(ends[-1] + a.size)
    total = total_of_2(jnp.concatenate([a.ravel() for a in arrays]), axis)
    return tuple((total[b:e].reshape(a.shape) for a, b, e in zip(arrays, ends, ends[1:])))


def of_everyone(x, axis):
    return from_everyone(x, axis).sum(axis=0)


def wendland(left_pts, right_pts, support):
    left = left_pts.astype(jnp.float32)
    right = right_pts.astype(jnp.float32)
    across = left[0][..., :, None] - right[0][..., None, :]
    upward = left[1][..., :, None] - right[1][..., None, :]
    ratio_t = jnp.sqrt(across * across + upward * upward) / support
    margin = jnp.maximum(1.0 - ratio_t, 0.0)
    squared = margin * margin
    return (squared * squared * (4.0 * ratio_t + 1.0)).astype(jnp.bfloat16)


def listed_terms(row_pts, col_pts, listing, vector, support, flipped):
    row_tiles = row_pts.reshape(2, -1, TILE)
    col_tiles = col_pts.reshape(2, -1, TILE)
    listed = listing.shape[-1]
    group = math.gcd(listed, 32)
    order = listing.reshape(2, listed // group, group)
    fields = vector.shape[-1]
    inputs = vector.reshape(-1, TILE, fields)
    target = col_tiles.shape[1] if flipped else row_tiles.shape[1]
    total = jnp.zeros((target, TILE, fields), jnp.float32)

    def add_group(total, pair):
        tile_rows, tile_cols = pair
        kernel = wendland(row_tiles[:, tile_rows], col_tiles[:, tile_cols], support)
        if flipped:
            contrib = jnp.einsum(
                "gij,gir->gjr", kernel, inputs[tile_rows], preferred_element_type=jnp.float32
            )
            return (total.at[tile_cols].add(contrib), None)
        contrib = jnp.einsum(
            "gij,gjr->gir", kernel, inputs[tile_cols], preferred_element_type=jnp.float32
        )
        return (total.at[tile_rows].add(contrib), None)

    total, unused = lax.scan(add_group, total, (order[0], order[1]))
    return total.reshape(-1, fields)


def per_device(values, points0, points1, points2, tiles_a0, tiles_e1, tiles_a1, factor):
    row_count = lax.axis_size("row")
    col_count = lax.axis_size("col")
    col_id = lax.axis_index("col")
    col_per_row = col_count // row_count
    rows_fine, fields = values.shape
    rows_mid = points1.shape[1]
    share = rows_fine // col_count
    source = col_id // col_per_row
    value_cols, fine_cols, mid_cols = (
        picked(values, "row", source),
        picked(points0, "row", source),
        picked(points1, "row", source),
    )
    scale_a0 = (rows_fine / (col_count * tiles_a0.shape[-1] * TILE * TILE)) ** 0.5
    scale_e1 = (rows_fine / (col_count * tiles_e1.shape[-1] * TILE * TILE)) ** 0.5
    scale_a1 = (rows_mid / (col_count * tiles_a1.shape[-1] * TILE * TILE)) ** 0.5
    scale_e2 = (1.0 / (rows_mid * row_count)) ** 0.5
    fine_data = values.astype(jnp.float32)
    own_data = lax.dynamic_slice_in_dim(values, col_id * share, share, 0).astype(jnp.float32)
    product_part = listed_terms(points0, fine_cols, tiles_a0[0, 0], value_cols, support_fine, False)
    product_whole = total_of(product_part, "col")
    fine_residual = fine_data - 0.5 * (scale_a0 * product_whole)
    fine_square = jnp.sum(fine_residual * fine_residual)
    restrict_part = listed_terms(
        points0, mid_cols, tiles_e1[0, 0], fine_residual.astype(jnp.bfloat16), support_mid, True
    )
    restrict_sum, fine_total = in_one((restrict_part, fine_square), "row")
    mid_data = scale_e1 * restrict_sum
    mid_part = listed_terms(
        points1, mid_cols, tiles_a1[0, 0], mid_data.astype(jnp.bfloat16), support_mid, False
    )
    mid_whole = (scale_a1 * total_of(mid_part, "col")).astype(jnp.bfloat16)
    mid_turned = picked(mid_whole, "row", source)
    mid_residual = mid_data - 0.5 * mid_turned.astype(jnp.float32)
    coarse_kernel = wendland(points2, mid_cols, support_coarse)
    coarse_part = jnp.dot(
        coarse_kernel, mid_residual.astype(jnp.bfloat16), preferred_element_type=jnp.float32
    )
    coarse_sum = of_everyone(coarse_part, "col")
    coarse_data = (scale_e2 * coarse_sum).astype(jnp.bfloat16)
    halfway_part = lax.dot_general(
        factor, coarse_data, (((0,), (0,)), ((), ())), preferred_element_type=jnp.float32
    )
    halfway = of_everyone(halfway_part, "row").astype(jnp.bfloat16)
    coarse_part_two = jnp.dot(factor, halfway, preferred_element_type=jnp.float32)
    coarse_coef = of_everyone(coarse_part_two, "col")
    prolong_part = lax.dot_general(
        coarse_kernel,
        coarse_coef.astype(jnp.bfloat16),
        (((0,), (0,)), ((), ())),
        preferred_element_type=jnp.float32,
    )
    mid_coef = 0.5 * mid_data + scale_e2 * total_of(prolong_part, "row")
    fine_part = listed_terms(
        points0, mid_cols, tiles_e1[0, 0], mid_coef.astype(jnp.bfloat16), support_mid, False
    )
    fine_coef = 0.5 * own_data + scale_e1 * summed_on_arrival(fine_part, "col", 0)
    fine_norm = fine_total / (rows_fine * row_count * fields)
    return (fine_coef, mid_coef, coarse_coef, jnp.stack([fine_norm]))


def solution(mesh):
    return jax.shard_map(
        per_device,
        mesh=mesh,
        in_specs=(
            P("row", None),
            P(None, "row"),
            P(None, "row"),
            P(None, "row"),
            P("row", "col", None, None),
            P("row", "col", None, None),
            P("row", "col", None, None),
            P("row", "col"),
        ),
        out_specs=(P(("row", "col"), None), P("col", None), P("row", None), P()),
        check_vma=False,
    )
```

profile of v0, /device:TPU:1, one launch (start us, length us, event | category | flops | bytes accessed | tf_op | source)
XLA Modules:
  0.0 947.4 jit_solution(3241295076004023425)
XLA Ops:
  8.9 40.1 %all-gather.4 = bf16[16,2,4096]{2,1,0:T(2,128)(2,1)S(1)} all-gather(bf16[1,2,4096]{2,1,0:T(2,128)(2,1)} %bitcast.184), channel_id=3, replica_groups=mesh['row'=16,'col'=16] {'row'}, dimensions={0}, use_global_device_ids=true | all-gather | bytes 278528 | tf_op jit(solution)/shard_map/all_gather | solution.py:17
  48.9 142.2 %all-gather.10.cloned.1.call-done = bf16[65536,128]{1,0:T(8,128)(2,1)} async-done(((bf16[4096,128]{1,0:T(8,128)(2,1)}), bf16[65536,128]{1,0:T(8,128)(2,1)}) %all-gather.10.cloned.1.call-update) | async-done | bytes 16777232 | tf_op jit(solution)/shard_map/all_gather | solution.py:17
  192.7 139.1 %while.40 = (s32[]{:T(128)}, f32[32,128,128]{2,1,0:T(8,128)S(1)}, s32[12,32]{1,0:T(8,128)S(1)}, bf16[2,32,128]{2,0,1:T(2,128)(2,1)S(1)}, s32[12,32]{1,0:T(8,128)...) while((s32[]{:T(128)}, f32[32,128,128]{2,1,0:T(8,128)S(1)}, ...), condition=%wide.region_2.3_spmd, body=%wide.region_0.2_spmd.sunk | while | flops 142100672 | bytes 11904345 | solution.py:113
  222.8 4.7 scatter_fusion
  234.3 4.7 scatter_fusion
  269.1 4.7 scatter_fusion
  280.7 4.7 scatter_fusion
  292.3 4.7 scatter_fusion
  303.9 4.7 scatter_fusion
  331.7 53.5 %all_to_all.66 = f32[16,256,128]{2,1,0:T(8,128)} all-to-all(f32[16,256,128]{2,1,0:T(8,128)S(1)} %bitcast.179), channel_id=1, replica_groups=mesh['row'=16,'col'=16] {'col'}, dimensions={0} | all-to-all | bytes 4194304 | tf_op jit(solution)/shard_map/all_to_all | solution.py:28
  392.9 57.2 %all-gather.3 = bf16[16,2,1024]{2,1,0:T(2,128)(2,1)S(1)} all-gather(bf16[1,2,1024]{2,1,0:T(2,128)(2,1)S(1)} %bitcast.201), channel_id=2, replica_groups=mesh['row'=16,'col'=16] {'row'}, dimensions={0}, use_global_device_ids=true | all-gather | bytes 69632 | tf_op jit(solution)/shard_map/all_gather | solution.py:17
  453.5 52.8 %while.41 = (s32[]{:T(128)}, f32[8,128,128]{2,1,0:T(8,128)S(1)}, s32[5,32]{1,0:T(8,128)S(1)}, s32[5,32]{1,0:T(8,128)S(1)}, bf16[2,32,128]{2,0,1:T(2,128)(2,1)S(1...) while((s32[]{:T(128)}, f32[8,128,128]{2,1,0:T(8,128)S(1)}, ...), condition=%wide.region_6.7_spmd, body=%wide.region_4.6_spmd.sunk | while | flops 142100672 | bytes 11904345 | solution.py:113
  512.6 16.6 %all-to-all-done.2 = f32[16,1,8193]{2,1,0:T(1,128)S(1)} async-done(((f32[16,1,8193]{2,1,0:T(1,128)}), f32[16,1,8193]{2,1,0:T(1,128)S(1)}, u32[]{:S(2)}, u32[]{:S(2)}) %all-to-all-start.2) | async-done | bytes 524384 | tf_op jit(solution)/shard_map/all_to_all | solution.py:28
  530.6 5.4 all-to-all-start.3
  537.0 14.9 %all-to-all-done.3 = f32[16,1,8193]{2,1,0:T(1,128)S(1)} async-done(((f32[16,1,8193]{2,1,0:T(1,128)}), f32[16,1,8193]{2,1,0:T(1,128)S(1)}, u32[]{:S(2)}, u32[]{:S(2)}) %all-to-all-start.3) | async-done | bytes 524384 | tf_op jit(solution)/shard_map/all_to_all | solution.py:39
  562.3 21.0 %all_to_all.67 = f32[16,64,128]{2,1,0:T(8,128)S(1)} all-to-all(f32[16,64,128]{2,1,0:T(8,128)S(1)} %bitcast.181), channel_id=1, replica_groups=mesh['row'=16,'col'=16] {'col'}, dimensions={0} | all-to-all | bytes 1048576 | tf_op jit(solution)/shard_map/all_to_all | solution.py:28
  583.5 18.9 %all_to_all.65 = f32[16,64,128]{2,1,0:T(8,128)S(1)} all-to-all(f32[16,64,128]{2,1,0:T(8,128)S(1)} %broadcast_in_dim.30), channel_id=1, replica_groups=mesh['row'=16,'col'=16] {'col'}, dimensions={0} | all-to-all | bytes 1048576 | tf_op jit(solution)/shard_map/all_to_all | solution.py:39
  603.2 75.5 %all-gather.8.cloned.1.call-done = bf16[16,1024,128]{2,1,0:T(8,128)(2,1)} async-done(((bf16[1,1024,128]{2,1,0:T(8,128)(2,1)}), bf16[16,1024,128]{2,1,0:T(8,128)(2,1)}) %all-gather.8.cloned.1.call-update) | async-done | bytes 4194320 | tf_op jit(solution)/shard_map/all_gather | solution.py:17
  680.3 30.9 %all_to_all.68 = f32[16,128,128]{2,1,0:T(8,128)S(1)} all-to-all(f32[16,128,128]{2,1,0:T(8,128)S(1)} %broadcast_in_dim.31), channel_id=1, replica_groups=mesh['row'=16,'col'=16] {'col'}, dimensions={0} | all-to-all | bytes 2097152 | tf_op jit(solution)/shard_map/all_to_all | solution.py:39
  711.7 34.6 %all_to_all.69 = f32[16,128,128]{2,1,0:T(8,128)S(1)} all-to-all(f32[16,128,128]{2,1,0:T(8,128)S(1)} %broadcast_in_dim.32), channel_id=1, replica_groups=mesh['row'=16,'col'=16] {'row'}, dimensions={0} | all-to-all | bytes 2097152 | tf_op jit(solution)/shard_map/all_to_all | solution.py:39
  746.8 31.3 %all_to_all.70 = f32[16,128,128]{2,1,0:T(8,128)S(1)} all-to-all(f32[16,128,128]{2,1,0:T(8,128)S(1)} %broadcast_in_dim.33), channel_id=1, replica_groups=mesh['row'=16,'col'=16] {'col'}, dimensions={0} | all-to-all | bytes 2097152 | tf_op jit(solution)/shard_map/all_to_all | solution.py:39
  778.8 22.1 %all_to_all.71 = f32[16,64,128]{2,1,0:T(8,128)S(1)} all-to-all(f32[16,64,128]{2,1,0:T(8,128)S(1)} %bitcast.188), channel_id=1, replica_groups=mesh['row'=16,'col'=16] {'row'}, dimensions={0} | all-to-all | bytes 1048576 | tf_op jit(solution)/shard_map/all_to_all | solution.py:28
  801.8 6.0 all-to-all-start.10
  807.8 15.1 %all-to-all-done.10 = f32[16,64,128]{2,1,0:T(8,128)S(1)} async-done(((f32[16,64,128]{2,1,0:T(8,128)}), f32[16,64,128]{2,1,0:T(8,128)S(1)}, u32[]{:S(2)}, u32[]{:S(2)}) %all-to-all-start.10) | async-done | bytes 524320 | tf_op jit(solution)/shard_map/all_to_all | solution.py:39
  824.6 56.3 %while.42 = (s32[]{:T(128)}, f32[32,128,128]{2,1,0:T(8,128)}, s32[5,32]{1,0:T(8,128)S(1)}, bf16[2,32,128]{2,0,1:T(2,128)(2,1)S(1)}, s32[5,32]{1,0:T(8,128)S(1)},...) while((s32[]{:T(128)}, f32[32,128,128]{2,1,0:T(8,128)}, ...), condition=%wide.region_17.18_spmd, body=%wide.region_15.17_spmd.sunk | while | flops 142100672 | bytes 11904345 | solution.py:113
  829.7 6.1 scatter_fusion.2
  840.9 6.2 scatter_fusion.2
  852.2 6.2 scatter_fusion.2
  863.5 6.2 scatter_fusion.2
  874.7 6.2 scatter_fusion.2
  880.9 7.0 all-to-all-start.11
  890.0 47.8 %all-to-all-done.11 = f32[16,256,128]{2,1,0:T(8,128)S(1)} async-done(((f32[16,256,128]{2,1,0:T(8,128)}), f32[16,256,128]{2,1,0:T(8,128)S(1)}, u32[]{:S(2)}, u32[]{:S(2)}) %all-to-all-start.11) | async-done | bytes 2097184 | tf_op jit(solution)/shard_map/all_to_all | solution.py:28
  (348 shorter events, 230.5 us)
Async XLA Ops:
  7.2 704.1 %copy-start = (bf16[128,128]{1,0:T(8,128)(2,1)S(1)}, bf16[128,128]{1,0:T(8,128)(2,1)}, u32[]{:S(2)}) copy-start(bf16[128,128]{1,0:T(8,128)(2,1)} %param.21) | copy-start | bytes 98308
  7.2 183.9 %all-gather.10.cloned.1.call-start = ((), (), s32[]{:S(2)}) async-start(), calls=%async_computation.13 | async-start | bytes 17825792 | tf_op jit(solution)/shard_map/all_gather | solution.py:17
  191.1 1.5 copy-start.6
  388.5 4.3 copy-start.10
  388.5 4.4 copy-start.8
  388.5 61.7 %all-to-all-start.1 = ((f32[16,256,128]{2,1,0:T(8,128)}), f32[16,256,128]{2,1,0:T(8,128)S(1)}, u32[]{:S(2)}, u32[]{:S(2)}) async-start(f32[16,256,128]{2,1,0:T(8,128)} %broadcast_in_dim.28), calls=%async_computation.1 | async-start | bytes 4194304 | tf_op jit(solution)/shard_map/all_to_all | solution.py:39
  450.1 1.2 copy-start.5
  506.3 5.7 copy-start.11
  508.5 20.8 %all-to-all-start.2 = ((f32[16,1,8193]{2,1,0:T(1,128)}), f32[16,1,8193]{2,1,0:T(1,128)S(1)}, u32[]{:S(2)}, u32[]{:S(2)}) async-start(f32[16,1,8193]{2,1,0:T(1,128)} %all_to_all.42), calls=%async_computation.2 | async-start | bytes 1064960 | tf_op jit(solution)/shard_map/all_to_all | solution.py:28
  530.6 21.2 %all-to-all-start.3 = ((f32[16,1,8193]{2,1,0:T(1,128)}), f32[16,1,8193]{2,1,0:T(1,128)S(1)}, u32[]{:S(2)}, u32[]{:S(2)}) async-start(f32[16,1,8193]{2,1,0:T(1,128)} %broadcast_in_dim.29), calls=%async_computation.3 | async-start | bytes 1064960 | tf_op jit(solution)/shard_map/all_to_all | solution.py:39
  536.0 142.6 %all-gather.8.cloned.1.call-start = ((), (), s32[]{:S(2)}) async-start(), calls=%async_computation.12 | async-start | bytes 4456448 | tf_op jit(solution)/shard_map/all_gather | solution.py:17
  553.4 125.2 %copy-start.3 = (f32[131088]{0:T(1024)}, f32[131088]{0:T(1024)S(1)}, u32[]{:S(2)}) copy-start(f32[131088]{0:T(1024)S(1)} %reshape.418) | copy-start | bytes 1573060
  562.3 40.8 %copy-start.12 = (bf16[2,128]{1,0:T(2,128)(2,1)S(1)}, bf16[2,128]{1,0:T(2,128)(2,1)}, u32[]{:S(2)}) copy-start(bf16[2,128]{1,0:T(2,128)(2,1)} %param.17) | copy-start | bytes 1540
  778.1 0.6 copy-start.9
  778.8 44.2 %copy-start.7 = (f32[131072]{0:T(1024)S(1)}, f32[131072]{0:T(1024)}, u32[]{:S(2)}) copy-start(f32[131072]{0:T(1024)} %get-tuple-element.362) | copy-start | bytes 1572868
  801.8 21.2 %all-to-all-start.10 = ((f32[16,64,128]{2,1,0:T(8,128)}), f32[16,64,128]{2,1,0:T(8,128)S(1)}, u32[]{:S(2)}, u32[]{:S(2)}) async-start(f32[16,64,128]{2,1,0:T(8,128)} %broadcast_in_dim.34), calls=%async_computation.10 | async-start | bytes 1048576 | tf_op jit(solution)/shard_map/all_to_all | solution.py:39
  823.0 1.7 copy-start.1
  880.9 7.1 copy-start.4
  880.9 8.2 copy-start.2
  880.9 56.9 %all-to-all-start.11 = ((f32[16,256,128]{2,1,0:T(8,128)}), f32[16,256,128]{2,1,0:T(8,128)S(1)}, u32[]{:S(2)}, u32[]{:S(2)}) async-start(f32[16,256,128]{2,1,0:T(8,128)} %bitcast.67), calls=%async_computation.11 | async-start | bytes 4194304 | tf_op jit(solution)/shard_map/all_to_all | solution.py:28
Sparse Core Ops, SparseCore 0:
  10.7 180.3 all-gather.9
  603.2 75.3 all-gather.7
where the time goes:
time: 951 us; the launch traced here: 947 us
  waiting for transfers between devices  313 us (33%)
  blocking collectives  310 us (33%)
  other arithmetic  115 us (12%)
  matrix products  85.2 us (9%)
  local copies, waits for them, and re-layouts  80.7 us (8%)
  starting transfers between devices  26.5 us (3%)
  between operations  16.2 us (2%)
    all_gather x2, waiting for transfers between devices, picked(): lax.all_gather(x, axis)  218 us
    all_to_all x4, blocking collectives, from_everyone(): return lax.all_to_all(copies, axis, split_axis=0, concat_axis=0, tiled=True)  116 us
    all_gather x2, blocking collectives, picked(): lax.all_gather(x, axis)  97.3 us
    all_to_all x3, blocking collectives, summed_on_arrival(): lax.all_to_all(blocks, axis, split_axis=0, concat_axis=0, tiled=True)  96.6 us
    scatter-add x18, other arithmetic, add_group(): return (total.at[tile_rows].add(contrib), None)  89.5 us
    dot_general x18, matrix products, add_group(): jnp.einsum('gij,gjr->gir', kernel, inputs[tile_cols], preferred_element_t...  64.9 us
    all_to_all x2, waiting for transfers between devices, summed_on_arrival(): lax.all_to_all(blocks, axis, split_axis=0, concat_axis=0, tiled=True)  64.4 us
    all_to_all x3, waiting for transfers between devices, from_everyone(): return lax.all_to_all(copies, axis, split_axis=0, concat_axis=0, tiled=True)  30 us
  transfers between devices with their start and end apart: 7, of which 6 were waited for; matrix products, arithmetic and copies ran while one was open for 0% of the time, Pallas kernels for 0%

commit v1 on v0

v1 whole, which is shorter than its diff:
```python
import jax
import jax.numpy as jnp
from jax import lax
from jax.experimental import pallas as pl
from jax.experimental.pallas import tpu as pltpu
from jax.sharding import Mesh
from jax.sharding import PartitionSpec as P

TILE = 128
SIDE = 16
BLOCK = 8
FEATURES = 16

support_fine = 0.35
support_mid = 0.55
support_coarse = 0.8

ROW = ("y", "zh", "k")
YZ = ("y", "zh")
COL = ("x", "zl")
ALL = ROW + COL

bf16 = jnp.bfloat16
f32 = jnp.float32

VMEM = pl.BlockSpec(memory_space=pltpu.VMEM)
SMEM = pl.BlockSpec(memory_space=pltpu.SMEM)
PARAMS = pltpu.CompilerParams(vmem_limit_bytes=56 * 1024 * 1024)


def turned(x):
    pairs = [(c * SIDE + r, r * SIDE + c) for r in range(SIDE) for c in range(SIDE)]
    return lax.ppermute(x, ALL, pairs)


def place_of_block(block, core):
    return ((block % 2) ^ core) * (SIDE // 2) + block // 2


def turned_blocks(x):
    pairs = [
        (c * SIDE + place_of_block(r, c % 2), r * SIDE + c) for r in range(SIDE) for c in range(SIDE)
    ]
    return lax.ppermute(x, ALL, pairs)


def from_partner(x):
    return lax.ppermute(x, "k", [(0, 1), (1, 0)])


def exchanged(x, axes):
    return lax.all_to_all(x, axes, split_axis=0, concat_axis=0, tiled=True)


def gathered(x, axes):
    return exchanged(jnp.broadcast_to(x, (lax.axis_size(axes), *x.shape)), axes)


def gathered_row(x):
    own = gathered(x, YZ)
    return own, from_partner(own)


def summed_row(own, other):
    pair = (own.astype(f32) + from_partner(other).astype(f32)).astype(bf16)
    return exchanged(pair, YZ).astype(f32).sum(axis=0)


def norm_parts(points):
    x = points.astype(f32)
    norm = x[0] * x[0] + x[1] * x[1]
    high = lax.reduce_precision(norm, 8, 7)
    rest = norm - high
    middle = lax.reduce_precision(rest, 8, 7)
    return [high, middle, rest - middle]


def row_features(points):
    one = jnp.ones(points.shape[1], f32)
    x = points.astype(f32)
    lines = [x[0], x[1], *norm_parts(points), one, one, one]
    lines += [jnp.zeros_like(one)] * (FEATURES - len(lines))
    return jnp.stack(lines).astype(bf16).T


def col_features(points):
    one = jnp.ones(points.shape[1], f32)
    x = points.astype(f32)
    lines = [-2.0 * x[0], -2.0 * x[1], one, one, one, *norm_parts(points)]
    lines += [jnp.zeros_like(one)] * (FEATURES - len(lines))
    return jnp.stack(lines).astype(bf16)


def wendland(left, right, support):
    square = jnp.maximum(jnp.dot(left, right, preferred_element_type=f32), 1e-30)
    margin = jnp.maximum(support - square * lax.rsqrt(square), 0.0)
    margin2 = margin * margin
    line = 5.0 / support**4 - (4.0 / support**5) * margin
    return (margin2 * margin2 * line).astype(bf16)


def at_tile(i):
    return pl.ds(pl.multiple_of(i * TILE, TILE), TILE)


def dot_turned(a, b):
    return lax.dot_general(a, b, (((1,), (1,)), ((), ())), preferred_element_type=f32)


def product_a0(listing, core, left, right, vector):
    listed = listing.shape[1]
    group = 8
    rows = left.shape[0] // TILE

    def kernel(list_ref, core_ref, left_ref, right_ref, vector_ref, own_ref, other_ref, total):
        total[...] = jnp.zeros_like(total)

        def step(g, carry):
            products = []
            for u in range(group):
                i, j = list_ref[0, g * group + u], list_ref[1, g * group + u]
                tile = wendland(left_ref[at_tile(i), :], right_ref[:, at_tile(j)], support_fine)
                products.append((i, dot_turned(vector_ref[:, at_tile(j)], tile)))
            for i, product in products:
                total[i] += product.reshape(SIDE, BLOCK, TILE)
            return carry

        lax.fori_loop(0, listed // group, step, 0)
        me = core_ref[0]
        for half in range(SIDE // 2):
            for i in range(rows):
                at = pl.ds(i * TILE, TILE)
                own_ref[half, :, at] = total[i, 2 * half + me].astype(bf16)
                other_ref[half, :, at] = total[i, 2 * half + 1 - me].astype(bf16)

    half = jax.ShapeDtypeStruct((SIDE // 2, BLOCK, left.shape[0]), bf16)
    return pl.pallas_call(
        kernel,
        out_shape=(half, half),
        in_specs=[SMEM, SMEM, VMEM, VMEM, VMEM],
        out_specs=(VMEM, VMEM),
        scratch_shapes=[pltpu.VMEM((rows, SIDE, BLOCK, TILE), f32)],
        compiler_params=PARAMS,
        name="product_a0",
    )(listing, core, left, right, vector)


def listed_tiles(listing, left, right, support):
    listed = listing.shape[1]
    group = 16

    def kernel(list_ref, left_ref, right_ref, out_ref):
        g = pl.program_id(0)
        for u in range(group):
            i, j = list_ref[0, g * group + u], list_ref[1, g * group + u]
            out_ref[u] = wendland(left_ref[at_tile(i), :], right_ref[:, at_tile(j)], support)

    return pl.pallas_call(
        kernel,
        out_shape=jax.ShapeDtypeStruct((listed, TILE, TILE), bf16),
        grid=(listed // group,),
        in_specs=[SMEM, VMEM, VMEM],
        out_specs=pl.BlockSpec((group, TILE, TILE), lambda g: (g, 0, 0)),
        compiler_params=PARAMS,
        name="listed_tiles",
    )(listing, left, right)


def all_pairs(left, right, support):
    def kernel(left_ref, right_ref, out_ref):
        for j in range(right.shape[1] // TILE):
            at = pl.ds(j * TILE, TILE)
            out_ref[:, at] = wendland(left_ref[...], right_ref[:, at], support)

    return pl.pallas_call(
        kernel,
        out_shape=jax.ShapeDtypeStruct((left.shape[0], right.shape[1]), bf16),
        grid=(left.shape[0] // TILE,),
        in_specs=[pl.BlockSpec((TILE, FEATURES), lambda i: (i, 0)), VMEM],
        out_specs=pl.BlockSpec((TILE, right.shape[1]), lambda i: (i, 0)),
        compiler_params=PARAMS,
        name="all_pairs",
    )(left, right)


def product_of_tiles(listing, tiles, halves, outs, flipped, shares):
    listed = listing.shape[1]
    group = 16
    steps = listed // group

    def kernel(list_ref, tile_ref, own_ref, other_ref, out_ref, vector, total):
        g = pl.program_id(0)

        @pl.when(g == 0)
        def _():
            total[...] = jnp.zeros_like(total)
            fields = SIDE * BLOCK // 2
            for ref, first in ((own_ref, 0), (other_ref, fields)):
                vector[pl.ds(first, fields), :] = ref[...].reshape(fields, ref.shape[2])

        products = []
        for u in range(group):
            i, j = list_ref[0, g * group + u], list_ref[1, g * group + u]
            if flipped:
                part = jnp.dot(vector[:, at_tile(i)], tile_ref[u], preferred_element_type=f32)
                products.append((j, part))
            else:
                products.append((i, dot_turned(vector[:, at_tile(j)], tile_ref[u])))
        for at, product in products:
            total[at] += product

        @pl.when(g == steps - 1)
        def _():
            for i in range(outs // TILE):
                if shares:
                    each = outs // SIDE // TILE
                    at = pl.ds(i % each * TILE, TILE)
                    out_ref[i // each, :, at] = total[i].astype(bf16)
                else:
                    out_ref[:, :, pl.ds(i * TILE, TILE)] = (
                        total[i].astype(bf16).reshape(SIDE, BLOCK, TILE)
                    )

    fields = SIDE * BLOCK
    shape = (SIDE, fields, outs // SIDE) if shares else (SIDE, BLOCK, outs)
    return pl.pallas_call(
        kernel,
        out_shape=jax.ShapeDtypeStruct(shape, bf16),
        grid=(steps,),
        in_specs=[SMEM, pl.BlockSpec((group, TILE, TILE), lambda g: (g, 0, 0)), VMEM, VMEM],
        out_specs=VMEM,
        scratch_shapes=[
            pltpu.VMEM((fields, halves[0].shape[2]), bf16),
            pltpu.VMEM((outs // TILE, fields, TILE), f32),
        ],
        compiler_params=PARAMS,
        name="product_of_tiles",
    )(listing, tiles, *halves)


def in_field_order(x, core):
    n = x.shape[-1]
    x = jnp.where(core == 0, x, x[::-1])
    return x.transpose(3, 1, 0, 2).reshape(n, SIDE * BLOCK)


def per_device(values, points0, points1, points2, tiles_a0, tiles_e1, tiles_a1, factor):
    core = lax.axis_index("k")
    col_id = lax.axis_index(COL)
    rows_fine, fields = values.shape
    rows_mid = points1.shape[1]
    coarse = points2.shape[1] * SIDE
    share = rows_fine // SIDE
    half = SIDE // 2
    list_a0, list_e1, list_a1 = tiles_a0[0, 0], tiles_e1[0, 0], tiles_a1[0, 0]
    ends = (list_a0.shape[1], list_a0.shape[1] + list_e1.shape[1])
    scale_a0 = (rows_fine / (SIDE * list_a0.shape[1] * TILE * TILE)) ** 0.5
    scale_e1 = (rows_fine / (SIDE * list_e1.shape[1] * TILE * TILE)) ** 0.5
    scale_a1 = (rows_mid / (SIDE * list_a1.shape[1] * TILE * TILE)) ** 0.5
    scale_e2 = (1.0 / (rows_mid * SIDE)) ** 0.5

    lists = turned(jnp.concatenate([list_a0, list_e1, list_a1], axis=1))
    turned_a0, turned_e1, turned_a1 = jnp.split(lists, ends, axis=1)
    points = turned(jnp.concatenate([points0, points1], axis=1))
    fine_there, mid_there = points[:, :rows_fine], points[:, rows_fine:]
    vector = values.T
    data_share = turned(
        lax.dynamic_index_in_dim(vector.reshape(SIDE, BLOCK, rows_fine), col_id, 0, keepdims=False)
    )
    left_fine = row_features(fine_there)

    own, other = product_a0(
        turned_a0, core.astype(jnp.int32).reshape(1), left_fine, col_features(points0), vector
    )

    right_there = col_features(mid_there)
    right_here = col_features(points1)
    tiles_back = listed_tiles(turned_e1, left_fine, right_here, support_mid)
    tiles_mid = listed_tiles(turned_a1, row_features(mid_there), right_here, support_mid)
    tiles_out = listed_tiles(list_e1, row_features(points0), right_there, support_mid)
    points2_all = exchanged(jnp.broadcast_to(points2, (SIDE, *points2.shape)), ROW)
    points2_all = points2_all.transpose(1, 0, 2).reshape(2, coarse)
    coarse_kernel = all_pairs(row_features(points2_all), right_there, support_coarse)
    factors = exchanged(
        jnp.broadcast_to(jnp.stack([factor, turned(factor)]), (SIDE, 2, *factor.shape)), ROW
    )
    factor_down = factors[:, 0].reshape(coarse, -1)
    factor_across = factors[:, 1]

    residual = data_share.astype(f32) - (0.5 * scale_a0) * summed_row(own, other)
    squares = jnp.sum(residual * residual, axis=0).reshape(-1, TILE).sum(axis=0)
    residual_halves = gathered_row(residual.astype(bf16))

    restricted = product_of_tiles(turned_e1, tiles_back, residual_halves, rows_mid, True, False)
    mid_share = scale_e1 * exchanged(restricted, COL).astype(f32).sum(axis=0)
    mid_all = gathered(mid_share.astype(bf16), COL)
    mid_data = turned_blocks(mid_share)

    mid_part = product_of_tiles(
        turned_a1, tiles_mid, (mid_all[:half], mid_all[half:]), rows_mid, False, False
    )
    mid_prod = scale_a1 * summed_row(mid_part[:half], mid_part[half:])
    mid_residual = mid_data - 0.5 * mid_prod.astype(bf16).astype(f32)

    coarse_part = dot_turned(mid_residual.astype(bf16), coarse_kernel)
    coarse_part = coarse_part.reshape(BLOCK, SIDE, -1).transpose(1, 0, 2)
    coarse_data = (scale_e2 * exchanged(coarse_part, COL).sum(axis=0)).astype(bf16)
    coarse_data = gathered(coarse_data, COL).transpose(1, 0, 2).reshape(BLOCK, coarse)
    halfway = jnp.dot(coarse_data, factor_down, preferred_element_type=f32).astype(bf16)
    halfway = gathered(halfway, COL)
    coarse_here = jnp.einsum("kfj,kij->fi", halfway, factor_across, preferred_element_type=f32)
    coarse_low = gathered(coarse_here.astype(bf16), COL).transpose(1, 0, 2).reshape(BLOCK, coarse)
    correction = jnp.dot(coarse_low, coarse_kernel, preferred_element_type=f32)
    mid_new = 0.5 * mid_data + scale_e2 * correction

    new_halves = gathered_row(mid_new.astype(bf16))
    fine_part = product_of_tiles(list_e1, tiles_out, new_halves, rows_fine, False, True)
    fine_sum = exchanged(fine_part, COL).astype(f32).sum(axis=0)
    fine_sum = in_field_order(fine_sum.reshape(2, half, BLOCK, share), core)
    own_data = lax.dynamic_slice_in_dim(values, col_id * share, share, 0).astype(f32)
    fine_coef = 0.5 * own_data + scale_e1 * fine_sum

    mid_coef = in_field_order(jnp.stack(gathered_row(mid_new)), core)
    coarse_coef = gathered(turned(coarse_here), COL).transpose(2, 0, 1).reshape(-1, fields)
    total = gathered(squares[None], ALL).sum()
    norm = total / (rows_fine * SIDE * fields)
    return (fine_coef, mid_coef, coarse_coef, jnp.stack([norm]))


def solution(mesh):
    fine_mesh = Mesh(mesh.devices.reshape(4, 2, 2, 4, 4), ALL)
    return jax.shard_map(
        per_device,
        mesh=fine_mesh,
        in_specs=(
            P(ROW, None),
            P(None, ROW),
            P(None, ROW),
            P(None, ROW),
            P(ROW, COL, None, None),
            P(ROW, COL, None, None),
            P(ROW, COL, None, None),
            P(ROW, COL),
        ),
        out_specs=(P(ALL, None), P(COL, None), P(ROW, None), P()),
        check_vma=False,
    )
```

time: 951 us -> 437 us (0.46)
  blocking collectives: 310 us -> 36 us
  waiting for transfers between devices: 313 us -> 121 us
  other arithmetic: 115 us -> 8.12 us
  starting transfers between devices: 26.5 us -> 131 us
  Pallas kernels: 0 us -> 101 us
  matrix products: 85.2 us -> 7.26 us
  local copies, waits for them, and re-layouts: 80.7 us -> 26.1 us
  between operations: 16.2 us -> 2.93 us
    all_gather x2 -> x0, waiting for transfers between devices: 218 us -> none  [picked(): lax.all_gather(x, axis)]
    all_to_all x7 -> x2, blocking collectives: 212 us -> 36 us  [exchanged(): return lax.all_to_all(x, axes, split_axis=0, concat_axis=0, tiled=True)]
    scatter-add x23 -> x0, other arithmetic: 103 us -> none  [the longest x18 89.5 us: add_group(): return (total.at[tile_rows].add(contrib), None)]
    pallas_call x0 -> x8, Pallas kernels: none -> 101 us  [the longest x1 48.8 us: product_a0(): pl.pallas_call(kernel, out_shape=(half, half), in_specs=[SMEM, SMEM, VMEM...]
    all_gather x2 -> x0, blocking collectives: 97.3 us -> none  [picked(): lax.all_gather(x, axis)]
    dot_general x27 -> x4, matrix products: 85.2 us -> 7.26 us  [the longest x1 4.01 us: dot_turned(): lax.dot_general(a, b, (((1,), (1,)), ((), ())), preferred_element_type=f32)]
    all_to_all x5 -> x14, starting transfers between devices: 26.2 us -> 104 us  [exchanged(): return lax.all_to_all(x, axes, split_axis=0, concat_axis=0, tiled=True)]
    gather x69 -> x0, local copies, waits for them, and re-layouts: 67.7 us -> none  [the longest x46 27.7 us: add_group(): kernel = wendland(row_tiles[:, tile_rows], col_tiles[:, tile_cols], support)]
  transfers between devices with their start and end apart: 7 -> 25, of which waited for: 6 -> 15; matrix products, arithmetic and copies ran while one was open for 0% -> 7% of each run, Pallas kernels for 0% -> 12%
where the time goes in v1:
time: 437 us; the launch traced here: 434 us
  starting transfers between devices  131 us (30%)
  waiting for transfers between devices  121 us (28%)
  Pallas kernels  101 us (23%)
  blocking collectives  36 us (8%)
  local copies, waits for them, and re-layouts  26.1 us (6%)
  other arithmetic  8.12 us (2%)
  matrix products  7.26 us (2%)
    all_to_all x14, waiting for transfers between devices, exchanged(): return lax.all_to_all(x, axes, split_axis=0, concat_axis=0, tiled=True)  112 us
    all_to_all x14, starting transfers between devices, exchanged(): return lax.all_to_all(x, axes, split_axis=0, concat_axis=0, tiled=True)  104 us
    pallas_call x1, Pallas kernels, product_a0(): pl.pallas_call(kernel, out_shape=(half, half), in_specs=[SMEM, SMEM, VMEM...  48.8 us
    all_to_all x2, blocking collectives, exchanged(): return lax.all_to_all(x, axes, split_axis=0, concat_axis=0, tiled=True)  36 us
    pallas_call x3, Pallas kernels, product_of_tiles(): pl.pallas_call(kernel, out_shape=jax.ShapeDtypeStruct(shape, bf16), grid=...  21.3 us
    pallas_call x3, Pallas kernels, listed_tiles(): pl.pallas_call(kernel, out_shape=jax.ShapeDtypeStruct((listed, TILE, TILE...  20.1 us
    ppermute x5, starting transfers between devices, turned(): return lax.ppermute(x, ALL, pairs)  18.8 us
    pallas_call x1, Pallas kernels, all_pairs(): pl.pallas_call(kernel, out_shape=jax.ShapeDtypeStruct((left.shape[0], rig...  10.9 us
  transfers between devices with their start and end apart: 25, of which 15 were waited for; matrix products, arithmetic and copies ran while one was open for 7% of the time, Pallas kernels for 12%

profile of v1, /device:TPU:1, one launch (start us, length us, event | category | flops | bytes accessed | tf_op | source)
XLA Modules:
  0.0 433.7 jit_solution(13411456693546900231)
XLA Ops:
  1.4 4.9 %collective-permute-start = (bf16[2,5120]{1,0:T(2,128)(2,1)S(1)}, bf16[2,5120]{1,0:T(2,128)(2,1)S(1)}, u32[]{:S(2)}, u32[]{:S(2)}) collective-permute-start(bf16[2,5120]{1,0:T(2,128)(2,1)S(1)} %pad_maximum_fusion.2), channel_id=1, source_target_pairs={{0,0},{16,1},{32,2},{48,3},{64,4},{80,5},{96,6},{112,7},{128,8},{1... | collective-permute-start | bytes 61448 | tf_op jit(solution)/shard_map/ppermute | solution.py:33
  15.9 48.8 %product_a0.1 = (bf16[8,8,4096]{2,1,0:T(8,128)(2,1)}, bf16[8,8,4096]{2,1,0:T(8,128)(2,1)}) custom-call(s32[2,384]{1,0:T(2,128)} %split.13.list_ref, s32[1]{0:T(128)} %bitcast.8.core_ref, bf16[4096,16]{1,0:T(8,128)(2,1)} %copy.65.left_ref, bf16[16,4096]{1,0:T(8,128)(2,1)} %stack.90.right_ref, bf16[128,4096]{1,0:T(8,128)(2,1)} %bitcast.74), custom_call_target="tpu_custom_call" | custom-call | tf_op jit(solution)/shard_map/product_a0/pallas_call | solution.py:137
  68.8 17.8 %all-to-all-start = ((bf16[8,8,4096]{2,1,0:T(8,128)(2,1)}), bf16[8,8,4096]{2,1,0:T(8,128)(2,1)S(1)}, u32[]{:S(2)}, u32[]{:S(2)}) async-start(bf16[8,8,4096]{2,1,0:T(8,128)(2,1)} %add_convert_fusion), calls=%async_computation | async-start | bytes 1048576 | tf_op jit(solution)/shard_map/all_to_all | solution.py:52
  91.2 10.2 %all-to-all-done = bf16[8,8,4096]{2,1,0:T(8,128)(2,1)S(1)} async-done(((bf16[8,8,4096]{2,1,0:T(8,128)(2,1)}), bf16[8,8,4096]{2,1,0:T(8,128)(2,1)S(1)}, u32[]{:S(2)}, u32[]{:S(2)}) %all-to-all-start) | async-done | bytes 524320 | tf_op jit(solution)/shard_map/all_to_all | solution.py:52
  101.7 24.1 %all_to_all.80.own_ref = bf16[8,8,4096]{2,1,0:T(8,128)(2,1)S(1)} all-to-all(bf16[8,8,4096]{2,1,0:T(8,128)(2,1)S(1)} %broadcast_in_dim.34), channel_id=1, replica_groups=mesh['y'=4,'zh'=2,'k'=2,'x'=4,'zl'=4] {'y','zh'}, dimensions={0} | all-to-all | bytes 1048576 | tf_op jit(solution)/shard_map/all_to_all | solution.py:52
  133.7 8.6 %listed_tiles.4.tile_ref = bf16[160,128,128]{2,1,0:T(8,128)(2,1)} custom-call(s32[2,160]{1,0:T(2,128)} %split.12.list_ref, bf16[4096,16]{1,0:T(8,128)(2,1)} %copy.65.left_ref, bf16[16,1024]{1,0:T(8,128)(2,1)} %stack.89.right_ref), custom_call_target="tpu_custom_call" | custom-call | tf_op jit(solution)/shard_map/listed_tiles/pallas_call | solution.py:158
  143.1 8.6 %product_of_tiles.3 = bf16[16,8,1024]{2,1,0:T(8,128)(2,1)} custom-call(s32[2,160]{1,0:T(2,128)} %split.12.list_ref, bf16[160,128,128]{2,1,0:T(8,128)(2,1)} %listed_tiles.4.tile_ref, bf16[8,8,4096]{2,1,0:T(8,128)(2,1)} %copy-done, bf16[8,8,4096]{2,1,0:T(8,128)(2,1)} %copy-done.1), custom_call_target="tpu_custom_call" | custom-call | tf_op jit(solution)/shard_map/product_of_tiles/pallas_call | solution.py:226
  151.7 7.6 %all-to-all-start.2 = ((bf16[16,8,1024]{2,1,0:T(8,128)(2,1)}), bf16[16,8,1024]{2,1,0:T(8,128)(2,1)S(1)}, u32[]{:S(2)}, u32[]{:S(2)}) async-start(bf16[16,8,1024]{2,1,0:T(8,128)(2,1)} %product_of_tiles.3), calls=%async_computation.2 | async-start | bytes 524288 | tf_op jit(solution)/shard_map/all_to_all | solution.py:52
  159.3 3.9 collective-permute-start.7
  163.9 5.4 %all-to-all-done.2 = bf16[16,8,1024]{2,1,0:T(8,128)(2,1)S(1)} async-done(((bf16[16,8,1024]{2,1,0:T(8,128)(2,1)}), bf16[16,8,1024]{2,1,0:T(8,128)(2,1)S(1)}, u32[]{:S(2)}, u32[]{:S(2)}) %all-to-all-start.2) | async-done | bytes 262176 | tf_op jit(solution)/shard_map/all_to_all | solution.py:52
  170.1 6.3 %all-to-all-start.3 = ((bf16[16,8,1024]{2,1,0:T(8,128)(2,1)}), bf16[16,8,1024]{2,1,0:T(8,128)(2,1)S(1)}, u32[]{:S(2)}, u32[]{:S(2)}) async-start(bf16[16,8,1024]{2,1,0:T(8,128)(2,1)} %broadcast_in_dim.35), calls=%async_computation.3 | async-start | bytes 524288 | tf_op jit(solution)/shard_map/all_to_all | solution.py:52
  180.2 7.1 %all-to-all-done.3 = bf16[16,8,1024]{2,1,0:T(8,128)(2,1)S(1)} async-done(((bf16[16,8,1024]{2,1,0:T(8,128)(2,1)}), bf16[16,8,1024]{2,1,0:T(8,128)(2,1)S(1)}, u32[]{:S(2)}, u32[]{:S(2)}) %all-to-all-start.3) | async-done | bytes 262176 | tf_op jit(solution)/shard_map/all_to_all | solution.py:52
  195.0 6.8 %all-to-all-start.4 = ((bf16[8,8,1024]{2,1,0:T(8,128)(2,1)}), bf16[8,8,1024]{2,1,0:T(8,128)(2,1)S(1)}, u32[]{:S(2)}, u32[]{:S(2)}) async-start(bf16[8,8,1024]{2,1,0:T(8,128)(2,1)} %add_convert_fusion.1), calls=%async_computation.4 | async-start | bytes 262144 | tf_op jit(solution)/shard_map/all_to_all | solution.py:52
  204.2 10.9 %all_pairs.1 = bf16[2048,1024]{1,0:T(8,128)(2,1)} custom-call(bf16[2048,16]{1,0:T(8,128)(2,1)} %bitcast.76, bf16[16,1024]{1,0:T(8,128)(2,1)} %stack.87.right_ref), custom_call_target="tpu_custom_call" | custom-call | tf_op jit(solution)/shard_map/all_pairs/pallas_call | solution.py:175
  217.0 4.8 %collective-permute-done.5 = f32[8,1024]{1,0:T(8,128)S(1)} collective-permute-done((f32[8,1024]{1,0:T(8,128)S(1)}, f32[8,1024]{1,0:T(8,128)S(1)}, u32[]{:S(2)}, u32[]{:S(2)}) %collective-permute-start.5) | collective-permute-done | bytes 32800 | tf_op jit(solution)/shard_map/ppermute | solution.py:44
  221.8 4.0 convolution_bitcast_fusion
  225.8 8.3 %all-to-all-start.6 = ((f32[16,8,128]{2,1,0:T(8,128)}), f32[16,8,128]{2,1,0:T(8,128)S(1)}, u32[]{:S(2)}, u32[]{:S(2)}) async-start(f32[16,8,128]{2,1,0:T(8,128)} %convolution_bitcast_fusion), calls=%async_computation.6 | async-start | bytes 131072 | tf_op jit(solution)/shard_map/all_to_all | solution.py:52
  234.2 7.0 %all-to-all-done.6 = f32[16,8,128]{2,1,0:T(8,128)S(1)} async-done(((f32[16,8,128]{2,1,0:T(8,128)}), f32[16,8,128]{2,1,0:T(8,128)S(1)}, u32[]{:S(2)}, u32[]{:S(2)}) %all-to-all-start.6) | async-done | bytes 65568 | tf_op jit(solution)/shard_map/all_to_all | solution.py:52
  242.4 11.9 %all-to-all-start.8 = ((bf16[16,2,128,128]{3,2,1,0:T(8,128)(2,1)}), bf16[16,2,128,128]{3,2,1,0:T(8,128)(2,1)S(1)}, u32[]{:S(2)}, u32[]{:S(2)}) async-start(bf16[16,2,128,128]{3,2,1,0:T(8,128)(2,1)} %broadcast_in_dim.38), calls=%async_computation.8 | async-start | bytes 2097152 | tf_op jit(solution)/shard_map/all_to_all | solution.py:52
  254.3 25.9 %all-to-all-done.8 = bf16[16,2,128,128]{3,2,1,0:T(8,128)(2,1)S(1)} async-done(((bf16[16,2,128,128]{3,2,1,0:T(8,128)(2,1)}), bf16[16,2,128,128]{3,2,1,0:T(8,128)(2,1)S(1)}, u32[]{:S(2)}, u32[]{:S(2)}) %all-to-all-start.8) | async-done | bytes 1048608 | tf_op jit(solution)/shard_map/all_to_all | solution.py:52
  280.9 7.4 %all-to-all-start.7 = ((bf16[16,8,128]{2,1,0:T(8,128)(2,1)}), bf16[16,8,128]{2,1,0:T(8,128)(2,1)S(1)}, u32[]{:S(2)}, u32[]{:S(2)}) async-start(bf16[16,8,128]{2,1,0:T(8,128)(2,1)} %broadcast_in_dim.37), calls=%async_computation.7 | async-start | bytes 65536 | tf_op jit(solution)/shard_map/all_to_all | solution.py:52
  288.3 6.8 %all-to-all-done.7 = bf16[16,8,128]{2,1,0:T(8,128)(2,1)S(1)} async-done(((bf16[16,8,128]{2,1,0:T(8,128)(2,1)}), bf16[16,8,128]{2,1,0:T(8,128)(2,1)S(1)}, u32[]{:S(2)}, u32[]{:S(2)}) %all-to-all-start.7) | async-done | bytes 32800 | tf_op jit(solution)/shard_map/all_to_all | solution.py:52
  299.4 6.8 %all-to-all-done.9 = bf16[16,8,128]{2,1,0:T(8,128)(2,1)S(1)} async-done(((bf16[16,8,128]{2,1,0:T(8,128)(2,1)}), bf16[16,8,128]{2,1,0:T(8,128)(2,1)S(1)}, u32[]{:S(2)}, u32[]{:S(2)}) %all-to-all-start.9) | async-done | bytes 32800 | tf_op jit(solution)/shard_map/all_to_all | solution.py:52
  306.9 8.6 %all-to-all-start.15 = ((f32[256,1,128]{2,1,0:T(1,128)}), f32[256,1,128]{2,1,0:T(1,128)S(1)}, u32[]{:S(2)}, u32[]{:S(2)}) async-start(f32[256,1,128]{2,1,0:T(1,128)} %broadcast_in_dim.44), calls=%async_computation.15 | async-start | bytes 262144 | tf_op jit(solution)/shard_map/all_to_all | solution.py:52
  315.8 12.6 %all-to-all-done.15 = f32[256,1,128]{2,1,0:T(1,128)S(1)} async-done(((f32[256,1,128]{2,1,0:T(1,128)}), f32[256,1,128]{2,1,0:T(1,128)S(1)}, u32[]{:S(2)}, u32[]{:S(2)}) %all-to-all-start.15) | async-done | bytes 131104 | tf_op jit(solution)/shard_map/all_to_all | solution.py:52
  332.5 4.3 collective-permute-start.10
  340.0 11.9 %all-to-all-start.14 = ((f32[16,8,128]{2,1,0:T(8,128)}), f32[16,8,128]{2,1,0:T(8,128)S(1)}, u32[]{:S(2)}, u32[]{:S(2)}) async-start(f32[16,8,128]{2,1,0:T(8,128)} %broadcast_in_dim.43), calls=%async_computation.14 | async-start | bytes 131072 | tf_op jit(solution)/shard_map/all_to_all | solution.py:52
  354.8 4.1 all-to-all-done.14
  358.9 11.8 %all_to_all.81.own_ref = bf16[8,8,1024]{2,1,0:T(8,128)(2,1)S(1)} all-to-all(bf16[8,8,1024]{2,1,0:T(8,128)(2,1)S(1)} %broadcast_in_dim.41), channel_id=1, replica_groups=mesh['y'=4,'zh'=2,'k'=2,'x'=4,'zl'=4] {'y','zh'}, dimensions={0} | all-to-all | bytes 262144 | tf_op jit(solution)/shard_map/all_to_all | solution.py:52
  380.2 8.6 %listed_tiles.3.tile_ref = bf16[160,128,128]{2,1,0:T(8,128)(2,1)} custom-call(s32[2,160]{1,0:T(2,128)} %bitcast.92, bf16[4096,16]{1,0:T(8,128)(2,1)} %copy.64.left_ref, bf16[16,1024]{1,0:T(8,128)(2,1)} %stack.87.right_ref), custom_call_target="tpu_custom_call" | custom-call | tf_op jit(solution)/shard_map/listed_tiles/pallas_call | solution.py:158
  389.5 9.8 %product_of_tiles.5 = bf16[16,128,256]{2,1,0:T(8,128)(2,1)} custom-call(s32[2,160]{1,0:T(2,128)} %bitcast.93, bf16[160,128,128]{2,1,0:T(8,128)(2,1)} %listed_tiles.3.tile_ref, bf16[8,8,1024]{2,1,0:T(8,128)(2,1)} %copy-done.2, bf16[8,8,1024]{2,1,0:T(8,128)(2,1)} %copy-done.4), custom_call_target="tpu_custom_call" | custom-call | tf_op jit(solution)/shard_map/product_of_tiles/pallas_call | solution.py:226
  406.1 24.7 %all-to-all-done.12 = bf16[16,128,256]{2,1,0:T(8,128)(2,1)S(1)} async-done(((bf16[16,128,256]{2,1,0:T(8,128)(2,1)}), bf16[16,128,256]{2,1,0:T(8,128)(2,1)S(1)}, u32[]{:S(2)}, u32[]{:S(2)}) %all-to-all-start.12) | async-done | bytes 1048608 | tf_op jit(solution)/shard_map/all_to_all | solution.py:52
  (126 shorter events, 80.3 us)
Async XLA Ops:
  1.4 12.9 %collective-permute-start = (bf16[2,5120]{1,0:T(2,128)(2,1)S(1)}, bf16[2,5120]{1,0:T(2,128)(2,1)S(1)}, u32[]{:S(2)}, u32[]{:S(2)}) collective-permute-start(bf16[2,5120]{1,0:T(2,128)(2,1)S(1)} %pad_maximum_fusion.2), channel_id=1, source_target_pairs={{0,0},{16,1},{32,2},{48,3},{64,4},{80,5},{96,6},{112,7},{128,8},{1... | collective-permute-start | bytes 61448 | tf_op jit(solution)/shard_map/ppermute | solution.py:33
  7.1 6.5 %collective-permute-start.1 = (s32[2,576]{1,0:T(2,128)S(1)}, s32[2,576]{1,0:T(2,128)S(1)}, u32[]{:S(2)}, u32[]{:S(2)}) collective-permute-start(s32[2,576]{1,0:T(2,128)S(1)} %pad_add_fusion), channel_id=1, source_target_pairs={{0,0},{16,1},{32,2},{48,3},{64,4},{80,5},{96,6},{112,7},{128,8},{1... | collective-permute-start | bytes 13832 | tf_op jit(solution)/shard_map/ppermute | solution.py:33
  14.5 113.2 %copy-start.7 = (bf16[2,128]{1,0:T(2,128)(2,1)S(1)}, bf16[2,128]{1,0:T(2,128)(2,1)}, u32[]{:S(2)}) copy-start(bf16[2,128]{1,0:T(2,128)(2,1)} %param.11) | copy-start | bytes 1540
  14.5 117.2 %copy-start.6 = (bf16[2,1024]{1,0:T(2,128)(2,1)S(1)}, bf16[2,1024]{1,0:T(2,128)(2,1)}, u32[]{:S(2)}) copy-start(bf16[2,1024]{1,0:T(2,128)(2,1)} %param.10) | copy-start | bytes 12292
  64.7 2.1 collective-permute-start.3
  68.8 32.7 %all-to-all-start = ((bf16[8,8,4096]{2,1,0:T(8,128)(2,1)}), bf16[8,8,4096]{2,1,0:T(8,128)(2,1)S(1)}, u32[]{:S(2)}, u32[]{:S(2)}) async-start(bf16[8,8,4096]{2,1,0:T(8,128)(2,1)} %add_convert_fusion), calls=%async_computation | async-start | bytes 1048576 | tf_op jit(solution)/shard_map/all_to_all | solution.py:52
  87.5 14.1 %collective-permute-start.2 = (bf16[8,4096]{1,0:T(8,128)(2,1)S(1)}, bf16[8,4096]{1,0:T(8,128)(2,1)S(1)}, u32[]{:S(2)}, u32[]{:S(2)}) collective-permute-start(bf16[8,4096]{1,0:T(8,128)(2,1)S(1)} %dynamic-slice_bitcast_fusion), channel_id=1, source_target_pairs={{0,0},{16,1},{32,2},{48,3},{64,4},{80,5},{96,6},{112,7},{128,8},{1... | collective-permute-start | bytes 196616 | tf_op jit(solution)/shard_map/ppermute | solution.py:33
  125.8 16.5 %copy-start = (bf16[8,8,4096]{2,1,0:T(8,128)(2,1)}, bf16[8,8,4096]{2,1,0:T(8,128)(2,1)S(1)}, u32[]{:S(2)}) copy-start(bf16[8,8,4096]{2,1,0:T(8,128)(2,1)S(1)} %all_to_all.80.own_ref) | copy-start | bytes 1572868
  125.8 16.5 %collective-permute-start.4 = (bf16[8,8,4096]{2,1,0:T(8,128)(2,1)S(1)}, bf16[8,8,4096]{2,1,0:T(8,128)(2,1)S(1)}, u32[]{:S(2)}, u32[]{:S(2)}) collective-permute-start(bf16[8,8,4096]{2,1,0:T(8,128)(2,1)S(1)} %all_to_all.80.own_ref), channel_id=1, source_target_pairs={{0,16},{16,0},{1,17},{17,1},{2,18},{18,2},{3,19},{19,3},{4,20},{20... | collective-permute-start | bytes 1572872 | tf_op jit(solution)/shard_map/ppermute | solution.py:48
  128.4 23.3 %all-to-all-start.5 = ((bf16[16,2,128]{2,1,0:T(2,128)(2,1)}), bf16[16,2,128]{2,1,0:T(2,128)(2,1)S(1)}, u32[]{:S(2)}, u32[]{:S(2)}) async-start(bf16[16,2,128]{2,1,0:T(2,128)(2,1)} %broadcast_in_dim.36), calls=%async_computation.5 | async-start | bytes 16384 | tf_op jit(solution)/shard_map/all_to_all | solution.py:52
  142.3 17.0 %copy-start.5 = (bf16[128,128]{1,0:T(8,128)(2,1)S(1)}, bf16[128,128]{1,0:T(8,128)(2,1)}, u32[]{:S(2)}) copy-start(bf16[128,128]{1,0:T(8,128)(2,1)} %param.15) | copy-start | bytes 98308
  142.3 0.8 copy-start.1
  151.7 17.6 %all-to-all-start.2 = ((bf16[16,8,1024]{2,1,0:T(8,128)(2,1)}), bf16[16,8,1024]{2,1,0:T(8,128)(2,1)S(1)}, u32[]{:S(2)}, u32[]{:S(2)}) async-start(bf16[16,8,1024]{2,1,0:T(8,128)(2,1)} %product_of_tiles.3), calls=%async_computation.2 | async-start | bytes 524288 | tf_op jit(solution)/shard_map/all_to_all | solution.py:52
  159.3 74.8 %collective-permute-start.7 = (bf16[128,128]{1,0:T(8,128)(2,1)S(1)}, bf16[128,128]{1,0:T(8,128)(2,1)S(1)}, u32[]{:S(2)}, u32[]{:S(2)}) collective-permute-start(bf16[128,128]{1,0:T(8,128)(2,1)S(1)} %copy-done.5), channel_id=1, source_target_pairs={{0,0},{16,1},{32,2},{48,3},{64,4},{80,5},{96,6},{112,7},{128,8},{1... | collective-permute-start | bytes 98312 | tf_op jit(solution)/shard_map/ppermute | solution.py:33
  170.1 17.3 %all-to-all-start.3 = ((bf16[16,8,1024]{2,1,0:T(8,128)(2,1)}), bf16[16,8,1024]{2,1,0:T(8,128)(2,1)S(1)}, u32[]{:S(2)}, u32[]{:S(2)}) async-start(bf16[16,8,1024]{2,1,0:T(8,128)(2,1)} %broadcast_in_dim.35), calls=%async_computation.3 | async-start | bytes 524288 | tf_op jit(solution)/shard_map/all_to_all | solution.py:52
  191.9 1.5 collective-permute-start.6
  195.0 22.0 %all-to-all-start.4 = ((bf16[8,8,1024]{2,1,0:T(8,128)(2,1)}), bf16[8,8,1024]{2,1,0:T(8,128)(2,1)S(1)}, u32[]{:S(2)}, u32[]{:S(2)}) async-start(bf16[8,8,1024]{2,1,0:T(8,128)(2,1)} %add_convert_fusion.1), calls=%async_computation.4 | async-start | bytes 262144 | tf_op jit(solution)/shard_map/all_to_all | solution.py:52
  215.1 6.7 %collective-permute-start.5 = (f32[8,1024]{1,0:T(8,128)S(1)}, f32[8,1024]{1,0:T(8,128)S(1)}, u32[]{:S(2)}, u32[]{:S(2)}) collective-permute-start(f32[8,1024]{1,0:T(8,128)S(1)} %get-tuple-element.37), channel_id=1, source_target_pairs={{0,0},{24,1},{32,2},{56,3},{64,4},{88,5},{96,6},{120,7},{128,8},{1... | collective-permute-start | bytes 98312 | tf_op jit(solution)/shard_map/ppermute | solution.py:44
  225.8 15.3 %all-to-all-start.6 = ((f32[16,8,128]{2,1,0:T(8,128)}), f32[16,8,128]{2,1,0:T(8,128)S(1)}, u32[]{:S(2)}, u32[]{:S(2)}) async-start(f32[16,8,128]{2,1,0:T(8,128)} %convolution_bitcast_fusion), calls=%async_computation.6 | async-start | bytes 131072 | tf_op jit(solution)/shard_map/all_to_all | solution.py:52
  242.4 37.8 %all-to-all-start.8 = ((bf16[16,2,128,128]{3,2,1,0:T(8,128)(2,1)}), bf16[16,2,128,128]{3,2,1,0:T(8,128)(2,1)S(1)}, u32[]{:S(2)}, u32[]{:S(2)}) async-start(bf16[16,2,128,128]{3,2,1,0:T(8,128)(2,1)} %broadcast_in_dim.38), calls=%async_computation.8 | async-start | bytes 2097152 | tf_op jit(solution)/shard_map/all_to_all | solution.py:52
  280.9 14.2 %all-to-all-start.7 = ((bf16[16,8,128]{2,1,0:T(8,128)(2,1)}), bf16[16,8,128]{2,1,0:T(8,128)(2,1)S(1)}, u32[]{:S(2)}, u32[]{:S(2)}) async-start(bf16[16,8,128]{2,1,0:T(8,128)(2,1)} %broadcast_in_dim.37), calls=%async_computation.7 | async-start | bytes 65536 | tf_op jit(solution)/shard_map/all_to_all | solution.py:52
  288.2 90.5 %copy-start.3 = (bf16[2,4096]{1,0:T(2,128)(2,1)S(1)}, bf16[2,4096]{1,0:T(2,128)(2,1)}, u32[]{:S(2)}) copy-start(bf16[2,4096]{1,0:T(2,128)(2,1)} %param.9) | copy-start | bytes 49156
  295.9 10.3 %all-to-all-start.9 = ((bf16[16,8,128]{2,1,0:T(8,128)(2,1)}), bf16[16,8,128]{2,1,0:T(8,128)(2,1)S(1)}, u32[]{:S(2)}, u32[]{:S(2)}) async-start(bf16[16,8,128]{2,1,0:T(8,128)(2,1)} %broadcast_in_dim.39), calls=%async_computation.9 | async-start | bytes 65536 | tf_op jit(solution)/shard_map/all_to_all | solution.py:52
  306.9 21.5 %all-to-all-start.15 = ((f32[256,1,128]{2,1,0:T(1,128)}), f32[256,1,128]{2,1,0:T(1,128)S(1)}, u32[]{:S(2)}, u32[]{:S(2)}) async-start(f32[256,1,128]{2,1,0:T(1,128)} %broadcast_in_dim.44), calls=%async_computation.15 | async-start | bytes 262144 | tf_op jit(solution)/shard_map/all_to_all | solution.py:52
  329.0 10.3 %all-to-all-start.10 = ((bf16[16,8,128]{2,1,0:T(8,128)(2,1)}), bf16[16,8,128]{2,1,0:T(8,128)(2,1)S(1)}, u32[]{:S(2)}, u32[]{:S(2)}) async-start(bf16[16,8,128]{2,1,0:T(8,128)(2,1)} %broadcast_in_dim.40), calls=%async_computation.10 | async-start | bytes 65536 | tf_op jit(solution)/shard_map/all_to_all | solution.py:52
  332.5 5.9 %collective-permute-start.10 = (f32[8,128]{1,0:T(8,128)S(1)}, f32[8,128]{1,0:T(8,128)S(1)}, u32[]{:S(2)}, u32[]{:S(2)}) collective-permute-start(f32[8,128]{1,0:T(8,128)S(1)} %get-tuple-element.62), channel_id=1, source_target_pairs={{0,0},{16,1},{32,2},{48,3},{64,4},{80,5},{96,6},{112,7},{128,8},{1... | collective-permute-start | bytes 12296 | tf_op jit(solution)/shard_map/ppermute | solution.py:33
  340.0 18.9 %all-to-all-start.14 = ((f32[16,8,128]{2,1,0:T(8,128)}), f32[16,8,128]{2,1,0:T(8,128)S(1)}, u32[]{:S(2)}, u32[]{:S(2)}) async-start(f32[16,8,128]{2,1,0:T(8,128)} %broadcast_in_dim.43), calls=%async_computation.14 | async-start | bytes 131072 | tf_op jit(solution)/shard_map/all_to_all | solution.py:52
  370.8 18.0 %copy-start.2 = (bf16[8,8,1024]{2,1,0:T(8,128)(2,1)}, bf16[8,8,1024]{2,1,0:T(8,128)(2,1)S(1)}, u32[]{:S(2)}) copy-start(bf16[8,8,1024]{2,1,0:T(8,128)(2,1)S(1)} %all_to_all.81.own_ref) | copy-start | bytes 393220
  371.5 27.7 %all-to-all-start.13 = ((f32[8,8,1024]{2,1,0:T(8,128)}), f32[8,8,1024]{2,1,0:T(8,128)S(1)}, u32[]{:S(2)}, u32[]{:S(2)}) async-start(f32[8,8,1024]{2,1,0:T(8,128)} %broadcast_in_dim.42), calls=%async_computation.13 | async-start | bytes 524288 | tf_op jit(solution)/shard_map/all_to_all | solution.py:52
  374.9 13.9 %collective-permute-start.8 = (bf16[8,8,1024]{2,1,0:T(8,128)(2,1)S(1)}, bf16[8,8,1024]{2,1,0:T(8,128)(2,1)S(1)}, u32[]{:S(2)}, u32[]{:S(2)}) collective-permute-start(bf16[8,8,1024]{2,1,0:T(8,128)(2,1)S(1)} %all_to_all.81.own_ref), channel_id=1, source_target_pairs={{0,16},{16,0},{1,17},{17,1},{2,18},{18,2},{3,19},{19,3},{4,20},{20... | collective-permute-start | bytes 393224 | tf_op jit(solution)/shard_map/ppermute | solution.py:48
  399.2 31.6 %all-to-all-start.12 = ((bf16[16,128,256]{2,1,0:T(8,128)(2,1)}), bf16[16,128,256]{2,1,0:T(8,128)(2,1)S(1)}, u32[]{:S(2)}, u32[]{:S(2)}) async-start(bf16[16,128,256]{2,1,0:T(8,128)(2,1)} %product_of_tiles.5), calls=%async_computation.12 | async-start | bytes 2097152 | tf_op jit(solution)/shard_map/all_to_all | solution.py:52
  402.9 2.1 collective-permute-start.9
  (1 other events, 0.7 us)

commit v2 on v1

v2 whole, which is shorter than its diff:
```python
import jax
import jax.numpy as jnp
from jax import lax
from jax.experimental import pallas as pl
from jax.experimental.pallas import tpu as pltpu
from jax.sharding import Mesh
from jax.sharding import PartitionSpec as P

TILE = 128
SIDE = 16
HALF = 8
BLOCK = 8
FIELDS = SIDE * BLOCK
GROUP = 16

support_fine = 0.35
support_mid = 0.55
support_coarse = 0.8

ROW = ("y", "zh", "k")
YZ = ("y", "zh")
COL = ("x", "zl")
ALL = ROW + COL

bf16 = jnp.bfloat16
f32 = jnp.float32

VMEM = pl.BlockSpec(memory_space=pltpu.VMEM)
SMEM = pl.BlockSpec(memory_space=pltpu.SMEM)


def room(mebibytes):
    return pltpu.CompilerParams(vmem_limit_bytes=mebibytes * 1024 * 1024)


def hint(microseconds):
    return pl.CostEstimate(
        flops=0, transcendentals=0, bytes_accessed=int(microseconds * 3.0e6)
    )


def turned(x):
    pairs = [(c * SIDE + r, r * SIDE + c) for r in range(SIDE) for c in range(SIDE)]
    return lax.ppermute(x, ALL, pairs)


def place_of_block(block, core):
    return ((block % 2) ^ core) * HALF + block // 2


def turned_blocks(x):
    pairs = [
        (c * SIDE + place_of_block(r, c % 2), r * SIDE + c) for r in range(SIDE) for c in range(SIDE)
    ]
    return lax.ppermute(x, ALL, pairs)


def from_partner(x):
    return lax.ppermute(x, "k", [(0, 1), (1, 0)])


def exchanged(x, axes):
    return lax.all_to_all(x, axes, split_axis=0, concat_axis=0, tiled=True)


def gathered(x, axes):
    return exchanged(jnp.broadcast_to(x, (lax.axis_size(axes), *x.shape)), axes)


def pair_sum(own, other):
    return (own.astype(f32) + from_partner(other).astype(f32)).astype(bf16)


def after(x, *others):
    return lax.optimization_barrier((x, *others))[0]


def parts_of(x):
    high = lax.reduce_precision(x, 8, 7)
    rest = x - high
    middle = lax.reduce_precision(rest, 8, 7)
    return jnp.stack([high, middle, rest - middle]).astype(bf16)


def stretch_of(support):
    return (4.0 / support**5) ** 0.2


def along(points, support):
    return (points.astype(f32) * stretch_of(support)).reshape(2, -1, 1, TILE)


def wendland(left, right, support):
    across, upward = left[0] - right[0], left[1] - right[1]
    square = jnp.maximum(across * across + upward * upward, 1e-30)
    edge = support * stretch_of(support)
    margin = jnp.maximum(edge - square * lax.rsqrt(square), 0.0)
    margin2 = margin * margin
    ratio = 5.0 / edge**4
    return (margin2 * margin2 * (ratio - margin)).astype(bf16)


def at_tile(i):
    return pl.ds(pl.multiple_of(i * TILE, TILE), TILE)


def spread(points, support):
    rows = along(points, support)
    tiles = rows.shape[1]

    def kernel(row_ref, out_ref):
        for axis in range(2):
            for t in range(tiles):
                out_ref[axis, t] = jnp.broadcast_to(row_ref[axis, t], (TILE, TILE)).T

    return pl.pallas_call(
        kernel,
        out_shape=jax.ShapeDtypeStruct((2, tiles, TILE, TILE), f32),
        in_specs=[VMEM],
        out_specs=VMEM,
        compiler_params=room(12),
        cost_estimate=hint(tiles / 8),
        name="spread",
    )(rows)


def add_tiles(list_ref, contracted, left_ref, right_ref, vector, total, support):
    listed = list_ref.shape[1]

    def step(g, carry):
        products = []
        for u in range(GROUP):
            j = list_ref[contracted, g * GROUP + u]
            i = list_ref[1 - contracted, g * GROUP + u]
            tile = wendland(
                (left_ref[0, j], left_ref[1, j]), (right_ref[0, i], right_ref[1, i]), support
            )
            product = jnp.dot(vector[:, at_tile(j)], tile, preferred_element_type=f32)
            products.append((i, product))
        for i, product in products:
            total[i] += product
        return carry

    lax.fori_loop(0, listed // GROUP, step, 0)


def product_a0(listing, place, left, right, vector):
    listed = listing.shape[1]
    tiles = right.shape[1]

    def kernel(list_ref, place_ref, left_ref, right_ref, vector_ref, own_ref, other_ref, total):
        me = place_ref[0]
        weight = jnp.where(place_ref[1] == place_ref[2], -2.0 / scale_of(tiles, listed), 0.0)
        for i in range(tiles):
            at = pl.ds(i * TILE, TILE)
            total[i] = vector_ref[:, at].astype(f32) * weight
        add_tiles(list_ref, 1, left_ref, right_ref, vector_ref, total, support_fine)
        for half in range(HALF):
            for i in range(tiles):
                at = pl.ds(i * TILE, TILE)
                own = pl.ds(pl.multiple_of((2 * half + me) * BLOCK, BLOCK), BLOCK)
                other = pl.ds(pl.multiple_of((2 * half + 1 - me) * BLOCK, BLOCK), BLOCK)
                own_ref[half, :, at] = total[i, own, :].astype(bf16)
                other_ref[half, :, at] = total[i, other, :].astype(bf16)

    half = jax.ShapeDtypeStruct((HALF, BLOCK, tiles * TILE), bf16)
    return pl.pallas_call(
        kernel,
        out_shape=(half, half),
        in_specs=[SMEM, SMEM, VMEM, VMEM, VMEM],
        out_specs=(VMEM, VMEM),
        scratch_shapes=[pltpu.VMEM((tiles, FIELDS, TILE), f32)],
        compiler_params=room(18),
        cost_estimate=hint(20),
        name="product_a0",
    )(listing, place, left, right, vector)


def product(listing, contracted, left, right, halves, support, form):
    listed = listing.shape[1]
    tiles = right.shape[1]
    length = left.shape[1] * TILE

    def kernel(list_ref, left_ref, right_ref, own_ref, other_ref, *rest):
        *outs, vector, total = rest
        total[...] = jnp.zeros_like(total)
        for ref, first in ((own_ref, 0), (other_ref, FIELDS // 2)):
            rows = ref[:, :, pl.ds(0, length)].reshape(FIELDS // 2, length)
            vector[pl.ds(first, FIELDS // 2), :] = rows.astype(bf16)
        add_tiles(list_ref, contracted, left_ref, right_ref, vector, total, support)
        for i in range(tiles):
            low = total[i].astype(bf16)
            if form == "shares":
                each = tiles // SIDE
                outs[0][i // each, :, pl.ds(i % each * TILE, TILE)] = low
            elif form == "blocks":
                outs[0][:, :, pl.ds(i * TILE, TILE)] = low.reshape(SIDE, BLOCK, TILE)
            else:
                pair = low.reshape(2, HALF, BLOCK, TILE)
                outs[0][:, :, pl.ds(i * TILE, TILE)] = pair[0]
                outs[1][:, :, pl.ds(i * TILE, TILE)] = pair[1]

    size = tiles * TILE
    if form == "shares":
        shapes = [(SIDE, FIELDS, size // SIDE)]
    elif form == "blocks":
        shapes = [(SIDE, BLOCK, size)]
    else:
        shapes = [(HALF, BLOCK, size)] * 2
    return pl.pallas_call(
        kernel,
        out_shape=[jax.ShapeDtypeStruct(shape, bf16) for shape in shapes],
        in_specs=[SMEM, VMEM, VMEM, VMEM, VMEM],
        out_specs=[VMEM] * len(shapes),
        scratch_shapes=[
            pltpu.VMEM((FIELDS, length), bf16),
            pltpu.VMEM((tiles, FIELDS, TILE), f32),
        ],
        compiler_params=room(18),
        cost_estimate=hint(listed / 18),
        name="product_" + form,
    )(listing, left, right, *halves)


def all_pairs(left, right, support):
    rows, cols = left.shape[1], right.shape[1]

    def kernel(left_ref, right_ref, out_ref):
        for j in range(cols):
            out_ref[:, pl.ds(j * TILE, TILE)] = wendland(
                (left_ref[0, 0], left_ref[1, 0]), (right_ref[0, j], right_ref[1, j]), support
            )

    return pl.pallas_call(
        kernel,
        out_shape=jax.ShapeDtypeStruct((rows * TILE, cols * TILE), bf16),
        grid=(rows,),
        in_specs=[pl.BlockSpec((2, 1, TILE, TILE), lambda i: (0, i, 0, 0)), VMEM],
        out_specs=pl.BlockSpec((TILE, cols * TILE), lambda i: (i, 0)),
        compiler_params=room(16),
        cost_estimate=hint(8),
        name="all_pairs",
    )(left, right)


def coarse_product(matrix, vector):
    rows, cols = matrix.shape

    def kernel(matrix_ref, vector_ref, out_ref, turned_ref):
        for t in range(cols // TILE):
            at = pl.ds(t * TILE, TILE)
            lines = vector_ref[:, at]
            full = jnp.concatenate([lines, jnp.zeros((TILE - BLOCK, TILE), f32)], axis=0)
            turned_ref[at, :] = full.T.astype(bf16)
        for q in range(rows // TILE):
            at = pl.ds(q * TILE, TILE)
            part = jnp.dot(matrix_ref[at, :], turned_ref[...], preferred_element_type=f32)
            out_ref[q] = part.T[:BLOCK, :]

    return pl.pallas_call(
        kernel,
        out_shape=jax.ShapeDtypeStruct((rows // TILE, BLOCK, TILE), f32),
        in_specs=[VMEM, VMEM],
        out_specs=VMEM,
        scratch_shapes=[pltpu.VMEM((cols, TILE), bf16)],
        compiler_params=room(12),
        cost_estimate=hint(3),
        name="coarse_product",
    )(matrix, vector)


def prolong(matrix, coarse_coef, mid_data, scale):
    rows, cols = matrix.shape
    two = 2 * TILE

    def kernel(matrix_ref, coef_ref, mid_ref, out_ref):
        total = jnp.zeros((BLOCK, cols), f32)
        for q in range(rows // two):
            pair = jnp.concatenate([coef_ref[2 * q], coef_ref[2 * q + 1]], axis=1)
            out_ref[q, :, pl.ds(cols, two)] = pair
            total += jnp.dot(
                pair.astype(bf16), matrix_ref[pl.ds(q * two, two), :], preferred_element_type=f32
            )
        coef = 0.5 * mid_ref[...] + scale * total
        for q in range(rows // two):
            out_ref[q, :, pl.ds(0, cols)] = coef

    return pl.pallas_call(
        kernel,
        out_shape=jax.ShapeDtypeStruct((rows // two, BLOCK, cols + two), f32),
        in_specs=[VMEM, VMEM, VMEM],
        out_specs=VMEM,
        compiler_params=room(12),
        cost_estimate=hint(3),
        name="prolong",
    )(matrix, coarse_coef, mid_data)


def in_field_order(x, core):
    n = x.shape[-1]
    x = jnp.where(core == 0, x, x[::-1])
    return x.transpose(3, 1, 0, 2).reshape(n, FIELDS)


def scale_of(tiles, listed):
    return (tiles * TILE / (SIDE * listed * TILE * TILE)) ** 0.5


def per_device(values, points0, points1, points2, tiles_a0, tiles_e1, tiles_a1, factor):
    core = lax.axis_index("k")
    col_id = lax.axis_index(COL)
    row_id = lax.axis_index(ROW)
    rows_fine, fields = values.shape
    rows_mid = points1.shape[1]
    rows_coarse = points2.shape[1]
    coarse = rows_coarse * SIDE
    share = rows_fine // SIDE
    tiles_fine, tiles_mid = rows_fine // TILE, rows_mid // TILE
    list_a0, list_e1, list_a1 = tiles_a0[0, 0], tiles_e1[0, 0], tiles_a1[0, 0]
    scale_a0 = scale_of(tiles_fine, list_a0.shape[1])
    scale_e1 = scale_of(tiles_fine, list_e1.shape[1])
    scale_a1 = scale_of(tiles_mid, list_a1.shape[1])
    scale_e2 = (1.0 / (rows_mid * SIDE)) ** 0.5

    lists = jnp.concatenate([list_a0, list_e1, list_a1], axis=1)
    sent = [points0, points1, lists, factor]
    lines = [a.astype(bf16).reshape(-1, TILE) for a in sent]
    ends = [0]
    for a in lines:
        ends.append(ends[-1] + a.shape[0])
    there = turned(jnp.concatenate(lines, axis=0))
    came = [there[b:e].reshape(a.shape) for a, b, e in zip(sent, ends, ends[1:])]
    fine_there, mid_there, lists, factor_there = came
    cuts = (list_a0.shape[1], list_a0.shape[1] + list_e1.shape[1])
    turned_a0, turned_e1, turned_a1 = jnp.split(lists.astype(jnp.int32), cuts, axis=1)
    place = jnp.stack([core, row_id, col_id]).astype(jnp.int32)

    centres = jnp.pad(points2, ((0, 2 * BLOCK - 2), (0, 0)))
    common = gathered(jnp.concatenate([factor, factor_there, centres], axis=0), YZ)
    own, other = product_a0(
        turned_a0, place, spread(points0, support_fine), along(fine_there, support_fine), values.T
    )
    own, other, common = lax.optimization_barrier((own, other, common))
    pair = pair_sum(own, other)

    arrived = exchanged(pair, YZ)
    fine_later, mid_here, mid_later, common, pair = lax.optimization_barrier(
        (fine_there, points1, mid_there, common, pair)
    )
    spread_fine = spread(fine_later, support_mid)
    spread_here = spread(mid_here, support_mid)
    spread_there = spread(mid_later, support_mid)
    residual = (-0.5 * scale_a0) * arrived.astype(f32).sum(axis=0)
    residual, spread_fine, spread_here, spread_there, common, mid_later = lax.optimization_barrier(
        (residual, spread_fine, spread_here, spread_there, common, mid_later)
    )
    partner = from_partner(common)

    def in_row_order(first, size):
        mine, its = common[:, first : first + size], partner[:, first : first + size]
        return jnp.stack([jnp.where(core == 0, mine, its), jnp.where(core == 0, its, mine)], axis=1)

    factor_down = in_row_order(0, rows_coarse).reshape(coarse, -1)
    factor_across = in_row_order(rows_coarse, rows_coarse).reshape(SIDE, rows_coarse, -1)
    centres = in_row_order(2 * rows_coarse, 2 * BLOCK).reshape(SIDE, 2 * BLOCK, -1)[:, :2]
    centres = centres.transpose(1, 0, 2).reshape(2, coarse)
    coarse_kernel = all_pairs(
        spread(centres, support_coarse), along(mid_later, support_coarse), support_coarse
    )

    squares = jnp.sum(residual * residual, axis=0).reshape(-1, TILE).sum(axis=0)
    squares = jnp.pad(parts_of(squares), ((0, BLOCK - 3), (0, 0)))
    fine_own = gathered(jnp.concatenate([residual.astype(bf16), squares], axis=1), YZ)
    fine_own, coarse_kernel, factor_down, factor_across = lax.optimization_barrier(
        (fine_own, coarse_kernel, factor_down, factor_across)
    )
    fine_other = from_partner(fine_own)
    squares = sum(h[:, :, rows_fine:].astype(f32).sum(axis=(0, 1)) for h in (fine_own, fine_other))

    (restricted,) = product(
        turned_e1, 0, spread_fine, along(points1, support_mid), (fine_own, fine_other), support_mid, "blocks"
    )
    mid_share = scale_e1 * exchanged(restricted, COL).astype(f32).sum(axis=0)
    mid_all = gathered(mid_share.astype(bf16), COL)
    mid_data = turned_blocks(mid_share)

    mid_own, mid_other = product(
        turned_a1,
        1,
        spread_here,
        along(mid_there, support_mid),
        (mid_all[:HALF], mid_all[HALF:]),
        support_mid,
        "halves",
    )
    mid_prod = scale_a1 * exchanged(pair_sum(mid_own, mid_other), YZ).astype(f32).sum(axis=0)
    mid_residual = mid_data - 0.5 * mid_prod.astype(bf16).astype(f32)

    coarse_part = coarse_product(coarse_kernel, mid_residual)
    coarse_data = (scale_e2 * exchanged(coarse_part, COL).sum(axis=0)).astype(bf16)
    squares = jnp.pad(parts_of(squares), ((0, BLOCK - 3), (0, 0)))
    coarse_data = gathered(jnp.concatenate([coarse_data, squares], axis=0), COL)
    norm = coarse_data[:, BLOCK:].astype(f32).sum() / (rows_fine * SIDE * fields)
    coarse_data = coarse_data[:, :BLOCK].transpose(1, 0, 2).reshape(BLOCK, coarse)
    halfway = jnp.dot(coarse_data, factor_down, preferred_element_type=f32).astype(bf16)
    halfway = gathered(halfway, COL)
    coarse_here = jnp.einsum("kfj,kij->fi", halfway, factor_across, preferred_element_type=f32)
    coarse_all = gathered(coarse_here, COL)

    new = prolong(coarse_kernel, coarse_all, mid_data, scale_e2)
    new_own = exchanged(new, YZ)
    new_other = from_partner(new_own)
    (fine_part,) = product(
        list_e1,
        1,
        spread_there,
        along(points0, support_mid),
        (new_own, new_other),
        support_mid,
        "shares",
    )
    fine_sum = exchanged(fine_part, COL).astype(f32).sum(axis=0)
    fine_sum = in_field_order(fine_sum.reshape(2, HALF, BLOCK, share), core)
    own_data = lax.dynamic_slice_in_dim(values, col_id * share, share, 0).astype(f32)
    fine_coef = 0.5 * own_data + scale_e1 * fine_sum

    both = jnp.stack([new_own, new_other])
    mid_coef = in_field_order(both[..., :rows_mid], core)
    coarse_coef = lax.dynamic_slice_in_dim(both, rows_mid + core * rows_coarse, rows_coarse, 3)
    coarse_coef = in_field_order(coarse_coef, core)
    return (fine_coef, mid_coef, coarse_coef, jnp.stack([norm]))


def solution(mesh):
    fine_mesh = Mesh(mesh.devices.reshape(4, 2, 2, 4, 4), ALL)
    return jax.shard_map(
        per_device,
        mesh=fine_mesh,
        in_specs=(
            P(ROW, None),
            P(None, ROW),
            P(None, ROW),
            P(None, ROW),
            P(ROW, COL, None, None),
            P(ROW, COL, None, None),
            P(ROW, COL, None, None),
            P(ROW, COL),
        ),
        out_specs=(P(ALL, None), P(COL, None), P(ROW, None), P()),
        check_vma=False,
    )
```

time: 437 us -> 293 us (0.67)
  starting transfers between devices: 131 us -> 73.1 us
  Pallas kernels: 101 us -> 46.5 us
  waiting for transfers between devices: 121 us -> 69.1 us
  blocking collectives: 36 us -> 62.8 us
  matrix products: 7.26 us -> 0.41 us
    all_to_all x14 -> x7, starting transfers between devices: 104 us -> 51.9 us  [exchanged(): return lax.all_to_all(x, axes, split_axis=0, concat_axis=0, tiled=True)]
    all_to_all x14 -> x7, waiting for transfers between devices: 112 us -> 61.7 us  [exchanged(): return lax.all_to_all(x, axes, split_axis=0, concat_axis=0, tiled=True)]
    pallas_call x1, Pallas kernels: 48.8 us -> 17 us  [product_a0(): pl.pallas_call(kernel, out_shape=(half, half), in_specs=[SMEM, SMEM, VMEM...]
    all_to_all x2 -> x5, blocking collectives: 36 us -> 62.8 us  [exchanged(): return lax.all_to_all(x, axes, split_axis=0, concat_axis=0, tiled=True)]
    pallas_call x7 -> x11, Pallas kernels: 52.3 us -> 29.4 us  [the longest x3 18.7 us: product(): pl.pallas_call(kernel, out_shape=[jax.ShapeDtypeStruct(shape, bf16) for s...]
    ppermute x5 -> x1, starting transfers between devices: 18.8 us -> 4.94 us  [turned(): return lax.ppermute(x, ALL, pairs)]
    unnamed x21 -> x30, local copies, waits for them, and re-layouts: 6.26 us -> 17.6 us
    ppermute x5, starting transfers between devices: 6.36 us -> 14.4 us  [from_partner(): return lax.ppermute(x, 'k', [(0, 1), (1, 0)])]
  transfers between devices with their start and end apart: 25 -> 14, of which waited for: 15 -> 11; matrix products, arithmetic and copies ran while one was open for 7% -> 4% of each run, Pallas kernels for 12% -> 9%
where the time goes in v2:
time: 293 us; the launch traced here: 291 us
  starting transfers between devices  73.1 us (25%)
  waiting for transfers between devices  69.1 us (24%)
  blocking collectives  62.8 us (21%)
  Pallas kernels  46.5 us (16%)
  local copies, waits for them, and re-layouts  24 us (8%)
  other arithmetic  12.1 us (4%)
  between operations  2.97 us (1%)
    all_to_all x5, blocking collectives, exchanged(): return lax.all_to_all(x, axes, split_axis=0, concat_axis=0, tiled=True)  62.8 us
    all_to_all x7, waiting for transfers between devices, exchanged(): return lax.all_to_all(x, axes, split_axis=0, concat_axis=0, tiled=True)  61.7 us
    all_to_all x7, starting transfers between devices, exchanged(): return lax.all_to_all(x, axes, split_axis=0, concat_axis=0, tiled=True)  51.9 us
    pallas_call x3, Pallas kernels, product(): pl.pallas_call(kernel, out_shape=[jax.ShapeDtypeStruct(shape, bf16) for s...  18.7 us
    unnamed x30, local copies, waits for them, and re-layouts  17.6 us
    pallas_call x1, Pallas kernels, product_a0(): pl.pallas_call(kernel, out_shape=(half, half), in_specs=[SMEM, SMEM, VMEM...  17 us
    ppermute x5, starting transfers between devices, from_partner(): return lax.ppermute(x, 'k', [(0, 1), (1, 0)])  14.4 us
  transfers between devices with their start and end apart: 14, of which 11 were waited for; matrix products, arithmetic and copies ran while one was open for 4% of the time, Pallas kernels for 9%

profile of v2, /device:TPU:1, one launch (start us, length us, event | category | flops | bytes accessed | tf_op | source)
XLA Modules:
  0.0 291.1 jit_solution(15290270992302175785)
XLA Ops:
  5.2 4.9 %collective-permute-start = (bf16[217,128]{1,0:T(8,128)(2,1)S(1)}, bf16[217,128]{1,0:T(8,128)(2,1)S(1)}, u32[]{:S(2)}, u32[]{:S(2)}) collective-permute-start(bf16[217,128]{1,0:T(8,128)(2,1)S(1)} %pad_maximum_fusion.4), channel_id=1, source_target_pairs={{0,0},{16,1},{32,2},{48,3},{64,4},{80,5},{96,6},{112,7},{128,8},{1... | collective-permute-start | bytes 166664 | tf_op jit(solution)/shard_map/ppermute | solution.py:44
  13.6 16.9 %all-to-all-start = ((bf16[8,272,128]{2,1,0:T(8,128)(2,1)}), bf16[8,272,128]{2,1,0:T(8,128)(2,1)S(1)}, u32[]{:S(2)}, u32[]{:S(2)}) async-start(bf16[8,272,128]{2,1,0:T(8,128)(2,1)} %broadcast_in_dim.18), calls=%async_computation | async-start | bytes 1114112 | tf_op jit(solution)/shard_map/all_to_all | solution.py:63
  35.2 2.2 copy-done.6
  37.4 17.0 %product_a0.1 = (bf16[8,8,4096]{2,1,0:T(8,128)(2,1)S(1)}, bf16[8,8,4096]{2,1,0:T(8,128)(2,1)S(1)}) custom-call(s32[2,384]{1,0:T(2,128)S(1)} %split.12.list_ref, s32[3]{0:T(128)S(1)} %pad_add_fusion.place_ref, f32[2,32,128,128]{3,2,1,0:T(8,128)S(1)} %copy-done.6, f32[2,32,1,128]{3,2,1,0:T(1,128)S(1)} %bitcast.75, bf16[128,4096]{1,0:T(8,128)(2,1)S(1)} %bitcast.72), custom_call_target="tpu_custom_call" | custom-call | bytes 60000000 | tf_op jit(solution)/shard_map/product_a0/pallas_call | solution.py:167
  54.5 2.5 collective-permute-start.1
  59.4 9.3 %all-to-all-start.1 = ((bf16[8,8,4096]{2,1,0:T(8,128)(2,1)}), bf16[8,8,4096]{2,1,0:T(8,128)(2,1)}, u32[]{:S(2)}, u32[]{:S(2)}) async-start(bf16[8,8,4096]{2,1,0:T(8,128)(2,1)} %add_convert_fusion), calls=%async_computation.1 | async-start | bytes 1048576 | tf_op jit(solution)/shard_map/all_to_all | solution.py:63
  72.7 11.8 %all-to-all-done.1 = bf16[8,8,4096]{2,1,0:T(8,128)(2,1)} async-done(((bf16[8,8,4096]{2,1,0:T(8,128)(2,1)}), bf16[8,8,4096]{2,1,0:T(8,128)(2,1)}, u32[]{:S(2)}, u32[]{:S(2)}) %all-to-all-start.1) | async-done | bytes 524320 | tf_op jit(solution)/shard_map/all_to_all | solution.py:63
  88.5 5.1 %all-to-all-start.2 = ((bf16[8,8,4224]{2,1,0:T(8,128)(2,1)}), bf16[8,8,4224]{2,1,0:T(8,128)(2,1)}, u32[]{:S(2)}, u32[]{:S(2)}) async-start(bf16[8,8,4224]{2,1,0:T(8,128)(2,1)} %broadcast_in_dim.19), calls=%async_computation.2 | async-start | bytes 1081344 | tf_op jit(solution)/shard_map/all_to_all | solution.py:63
  98.1 4.6 %all_pairs.1.matrix_ref = bf16[2048,1024]{1,0:T(8,128)(2,1)S(1)} custom-call(f32[2,16,128,128]{3,2,1,0:T(8,128)S(1)} %spread.9.left_ref, f32[2,8,1,128]{3,2,1,0:T(1,128)S(1)} %reshape.188.right_ref), custom_call_target="tpu_custom_call" | custom-call | bytes 24000000 | tf_op jit(solution)/shard_map/all_pairs/pallas_call | solution.py:234
  104.7 4.5 %all-to-all-done.2.own_ref = bf16[8,8,4224]{2,1,0:T(8,128)(2,1)} async-done(((bf16[8,8,4224]{2,1,0:T(8,128)(2,1)}), bf16[8,8,4224]{2,1,0:T(8,128)(2,1)}, u32[]{:S(2)}, u32[]{:S(2)}) %all-to-all-start.2) | async-done | bytes 540704 | tf_op jit(solution)/shard_map/all_to_all | solution.py:63
  111.7 2.2 copy-done.4
  113.9 8.1 %product_blocks.1 = bf16[16,8,1024]{2,1,0:T(8,128)(2,1)S(1)} custom-call(s32[2,160]{1,0:T(2,128)S(1)} %split.13.list_ref, f32[2,32,128,128]{3,2,1,0:T(8,128)S(1)} %copy-done.4, f32[2,8,1,128]{3,2,1,0:T(1,128)S(1)} %reshape.191.right_ref, bf16[8,8,4224]{2,1,0:T(8,128)(2,1)} %all-to-all-done.2.own_ref, bf16[8,8,4224]{2,1,0:T(8,128)(2,1)} %collective-permute-done.3.other_ref), custom_call_target="tpu_custom_call" | custom-call | bytes 26666666 | tf_op jit(solution)/shard_map/product_blocks/pallas_call | solution.py:210
  122.0 13.5 %all_to_all.60 = bf16[16,8,1024]{2,1,0:T(8,128)(2,1)S(1)} all-to-all(bf16[16,8,1024]{2,1,0:T(8,128)(2,1)S(1)} %product_blocks.1), channel_id=1, replica_groups=mesh['y'=4,'zh'=2,'k'=2,'x'=4,'zl'=4] {'x','zl'}, dimensions={0} | all-to-all | bytes 524288 | tf_op jit(solution)/shard_map/all_to_all | solution.py:63
  136.3 3.7 %all-to-all-start.4 = ((bf16[16,8,1024]{2,1,0:T(8,128)(2,1)}), bf16[16,8,1024]{2,1,0:T(8,128)(2,1)S(1)}, u32[]{:S(2)}, u32[]{:S(2)}) async-start(bf16[16,8,1024]{2,1,0:T(8,128)(2,1)} %broadcast_in_dim.20), calls=%async_computation.4 | async-start | bytes 524288 | tf_op jit(solution)/shard_map/all_to_all | solution.py:63
  140.1 8.5 %all-to-all-done.4 = bf16[16,8,1024]{2,1,0:T(8,128)(2,1)S(1)} async-done(((bf16[16,8,1024]{2,1,0:T(8,128)(2,1)}), bf16[16,8,1024]{2,1,0:T(8,128)(2,1)S(1)}, u32[]{:S(2)}, u32[]{:S(2)}) %all-to-all-start.4) | async-done | bytes 262176 | tf_op jit(solution)/shard_map/all_to_all | solution.py:63
  148.6 2.0 product_halves.1
  150.6 3.4 %collective-permute-start.5 = (bf16[8,8,1024]{2,1,0:T(8,128)(2,1)S(1)}, bf16[8,8,1024]{2,1,0:T(8,128)(2,1)S(1)}, u32[]{:S(2)}, u32[]{:S(2)}) collective-permute-start(bf16[8,8,1024]{2,1,0:T(8,128)(2,1)S(1)} %get-tuple-element.43), channel_id=1, source_target_pairs={{0,16},{16,0},{1,17},{17,1},{2,18},{18,2},{3,19},{19,3},{4,20},{20... | collective-permute-start | bytes 393224 | tf_op jit(solution)/shard_map/ppermute | solution.py:59
  155.7 5.7 %all-to-all-start.5 = ((bf16[8,8,1024]{2,1,0:T(8,128)(2,1)}), bf16[8,8,1024]{2,1,0:T(8,128)(2,1)S(1)}, u32[]{:S(2)}, u32[]{:S(2)}) async-start(bf16[8,8,1024]{2,1,0:T(8,128)(2,1)} %add_convert_fusion.1), calls=%async_computation.5 | async-start | bytes 262144 | tf_op jit(solution)/shard_map/all_to_all | solution.py:63
  164.8 6.1 %all-to-all-done.5 = bf16[8,8,1024]{2,1,0:T(8,128)(2,1)S(1)} async-done(((bf16[8,8,1024]{2,1,0:T(8,128)(2,1)}), bf16[8,8,1024]{2,1,0:T(8,128)(2,1)S(1)}, u32[]{:S(2)}, u32[]{:S(2)}) %all-to-all-start.5) | async-done | bytes 131104 | tf_op jit(solution)/shard_map/all_to_all | solution.py:63
  170.9 2.2 copy-done.1
  173.1 2.0 coarse_product.1
  175.2 7.2 %all-to-all-start.6 = ((f32[16,8,128]{2,1,0:T(8,128)}), f32[16,8,128]{2,1,0:T(8,128)S(1)}, u32[]{:S(2)}, u32[]{:S(2)}) async-start(f32[16,8,128]{2,1,0:T(8,128)} %coarse_product.1), calls=%async_computation.6 | async-start | bytes 131072 | tf_op jit(solution)/shard_map/all_to_all | solution.py:63
  182.4 7.0 %all-to-all-done.6 = f32[16,8,128]{2,1,0:T(8,128)S(1)} async-done(((f32[16,8,128]{2,1,0:T(8,128)}), f32[16,8,128]{2,1,0:T(8,128)S(1)}, u32[]{:S(2)}, u32[]{:S(2)}) %all-to-all-start.6) | async-done | bytes 65568 | tf_op jit(solution)/shard_map/all_to_all | solution.py:63
  189.4 9.7 %all_to_all.61 = bf16[16,16,128]{2,1,0:T(8,128)(2,1)S(1)} all-to-all(bf16[16,16,128]{2,1,0:T(8,128)(2,1)S(1)} %broadcast_in_dim.21), channel_id=1, replica_groups=mesh['y'=4,'zh'=2,'k'=2,'x'=4,'zl'=4] {'x','zl'}, dimensions={0} | all-to-all | bytes 131072 | tf_op jit(solution)/shard_map/all_to_all | solution.py:63
  199.3 9.4 %all_to_all.62 = bf16[16,8,128]{2,1,0:T(8,128)(2,1)S(1)} all-to-all(bf16[16,8,128]{2,1,0:T(8,128)(2,1)S(1)} %broadcast_in_dim.22), channel_id=1, replica_groups=mesh['y'=4,'zh'=2,'k'=2,'x'=4,'zl'=4] {'x','zl'}, dimensions={0} | all-to-all | bytes 65536 | tf_op jit(solution)/shard_map/all_to_all | solution.py:63
  209.0 9.6 %all_to_all.63.coef_ref = f32[16,8,128]{2,1,0:T(8,128)S(1)} all-to-all(f32[16,8,128]{2,1,0:T(8,128)S(1)} %broadcast_in_dim.23), channel_id=1, replica_groups=mesh['y'=4,'zh'=2,'k'=2,'x'=4,'zl'=4] {'x','zl'}, dimensions={0} | all-to-all | bytes 131072 | tf_op jit(solution)/shard_map/all_to_all | solution.py:63
  218.5 2.2 copy-done.2
  221.4 20.6 %all_to_all.64.own_ref = f32[8,8,1280]{2,1,0:T(8,128)S(1)} all-to-all(f32[8,8,1280]{2,1,0:T(8,128)S(1)} %prolong.1), channel_id=1, replica_groups=mesh['y'=4,'zh'=2,'k'=2,'x'=4,'zl'=4] {'y','zh'}, dimensions={0} | all-to-all | bytes 655360 | tf_op jit(solution)/shard_map/all_to_all | solution.py:63
  242.0 6.2 %collective-permute-start.6 = (f32[8,8,1280]{2,1,0:T(8,128)S(1)}, f32[8,8,1280]{2,1,0:T(8,128)S(1)}, u32[]{:S(2)}, u32[]{:S(2)}) collective-permute-start(f32[8,8,1280]{2,1,0:T(8,128)S(1)} %all_to_all.64.own_ref), channel_id=1, source_target_pairs={{0,16},{16,0},{1,17},{17,1},{2,18},{18,2},{3,19},{19,3},{4,20},{20... | collective-permute-start | bytes 983048 | tf_op jit(solution)/shard_map/ppermute | solution.py:59
  249.5 8.6 %product_shares.1 = bf16[16,128,256]{2,1,0:T(8,128)(2,1)} custom-call(s32[2,160]{1,0:T(2,128)S(1)} %bitcast.78, f32[2,8,128,128]{3,2,1,0:T(8,128)S(1)} %spread.8.left_ref, f32[2,32,1,128]{3,2,1,0:T(1,128)S(1)} %reshape.185.right_ref, f32[8,8,1280]{2,1,0:T(8,128)S(1)} %all_to_all.64.own_ref, f32[8,8,1280]{2,1,0:T(8,128)S(1)} %collective-permute-done.6.other_ref), custom_call_target="tpu_custom_call" | custom-call | bytes 26666666 | tf_op jit(solution)/shard_map/product_shares/pallas_call | solution.py:210
  258.1 3.9 %all-to-all-start.11 = ((bf16[16,128,256]{2,1,0:T(8,128)(2,1)}), bf16[16,128,256]{2,1,0:T(8,128)(2,1)S(1)}, u32[]{:S(2)}, u32[]{:S(2)}) async-start(bf16[16,128,256]{2,1,0:T(8,128)(2,1)} %product_shares.1), calls=%async_computation.11 | async-start | bytes 2097152 | tf_op jit(solution)/shard_map/all_to_all | solution.py:63
  265.2 23.8 %all-to-all-done.11 = bf16[16,128,256]{2,1,0:T(8,128)(2,1)S(1)} async-done(((bf16[16,128,256]{2,1,0:T(8,128)(2,1)}), bf16[16,128,256]{2,1,0:T(8,128)(2,1)S(1)}, u32[]{:S(2)}, u32[]{:S(2)}) %all-to-all-start.11) | async-done | bytes 1048608 | tf_op jit(solution)/shard_map/all_to_all | solution.py:63
  (126 shorter events, 43.7 us)
Async XLA Ops:
  0.6 33.8 %copy-start.11 = (bf16[4096,128]{1,0:T(8,128)(2,1)S(1)}, bf16[4096,128]{1,0:T(8,128)(2,1)}, u32[]{:S(2)}) copy-start(bf16[4096,128]{1,0:T(8,128)(2,1)} %param.8) | copy-start | bytes 3145732
  5.2 6.8 %collective-permute-start = (bf16[217,128]{1,0:T(8,128)(2,1)S(1)}, bf16[217,128]{1,0:T(8,128)(2,1)S(1)}, u32[]{:S(2)}, u32[]{:S(2)}) collective-permute-start(bf16[217,128]{1,0:T(8,128)(2,1)S(1)} %pad_maximum_fusion.4), channel_id=1, source_target_pairs={{0,0},{16,1},{32,2},{48,3},{64,4},{80,5},{96,6},{112,7},{128,8},{1... | collective-permute-start | bytes 166664 | tf_op jit(solution)/shard_map/ppermute | solution.py:44
  13.6 40.8 %all-to-all-start = ((bf16[8,272,128]{2,1,0:T(8,128)(2,1)}), bf16[8,272,128]{2,1,0:T(8,128)(2,1)S(1)}, u32[]{:S(2)}, u32[]{:S(2)}) async-start(bf16[8,272,128]{2,1,0:T(8,128)(2,1)} %broadcast_in_dim.18), calls=%async_computation | async-start | bytes 1114112 | tf_op jit(solution)/shard_map/all_to_all | solution.py:63
  32.5 2.0 copy-start.5
  35.0 33.7 %copy-start.12 = (bf16[2,1024]{1,0:T(2,128)(2,1)S(1)}, bf16[2,1024]{1,0:T(2,128)(2,1)}, u32[]{:S(2)}) copy-start(bf16[2,1024]{1,0:T(2,128)(2,1)} %param.10) | copy-start | bytes 12292
  35.2 2.2 copy-start.6
  54.5 14.3 %copy-start.8 = (bf16[8,272,128]{2,1,0:T(8,128)(2,1)}, bf16[8,272,128]{2,1,0:T(8,128)(2,1)S(1)}, u32[]{:S(2)}) copy-start(bf16[8,272,128]{2,1,0:T(8,128)(2,1)S(1)} %all-to-all-done) | copy-start | bytes 1671172
  54.5 4.0 %collective-permute-start.1 = (bf16[8,8,4096]{2,1,0:T(8,128)(2,1)S(1)}, bf16[8,8,4096]{2,1,0:T(8,128)(2,1)S(1)}, u32[]{:S(2)}, u32[]{:S(2)}) collective-permute-start(bf16[8,8,4096]{2,1,0:T(8,128)(2,1)S(1)} %get-tuple-element.28), channel_id=1, source_target_pairs={{0,16},{16,0},{1,17},{17,1},{2,18},{18,2},{3,19},{19,3},{4,20},{20... | collective-permute-start | bytes 1572872 | tf_op jit(solution)/shard_map/ppermute | solution.py:59
  59.4 25.1 %all-to-all-start.1 = ((bf16[8,8,4096]{2,1,0:T(8,128)(2,1)}), bf16[8,8,4096]{2,1,0:T(8,128)(2,1)}, u32[]{:S(2)}, u32[]{:S(2)}) async-start(bf16[8,8,4096]{2,1,0:T(8,128)(2,1)} %add_convert_fusion), calls=%async_computation.1 | async-start | bytes 1048576 | tf_op jit(solution)/shard_map/all_to_all | solution.py:63
  70.7 2.0 copy-start.3
  85.6 7.9 %collective-permute-start.2 = (bf16[8,272,128]{2,1,0:T(8,128)(2,1)}, bf16[8,272,128]{2,1,0:T(8,128)(2,1)}, u32[]{:S(2)}, u32[]{:S(2)}) collective-permute-start(bf16[8,272,128]{2,1,0:T(8,128)(2,1)} %copy-done.8), channel_id=1, source_target_pairs={{0,16},{16,0},{1,17},{17,1},{2,18},{18,2},{3,19},{19,3},{4,20},{20... | collective-permute-start | bytes 1671176 | tf_op jit(solution)/shard_map/ppermute | solution.py:59
  88.5 20.8 %all-to-all-start.2 = ((bf16[8,8,4224]{2,1,0:T(8,128)(2,1)}), bf16[8,8,4224]{2,1,0:T(8,128)(2,1)}, u32[]{:S(2)}, u32[]{:S(2)}) async-start(bf16[8,8,4224]{2,1,0:T(8,128)(2,1)} %broadcast_in_dim.19), calls=%async_computation.2 | async-start | bytes 1081344 | tf_op jit(solution)/shard_map/all_to_all | solution.py:63
  102.7 2.0 copy-start
  109.2 2.5 collective-permute-start.3
  111.7 2.2 copy-start.4
  136.3 12.3 %all-to-all-start.4 = ((bf16[16,8,1024]{2,1,0:T(8,128)(2,1)}), bf16[16,8,1024]{2,1,0:T(8,128)(2,1)S(1)}, u32[]{:S(2)}, u32[]{:S(2)}) async-start(bf16[16,8,1024]{2,1,0:T(8,128)(2,1)} %broadcast_in_dim.20), calls=%async_computation.4 | async-start | bytes 524288 | tf_op jit(solution)/shard_map/all_to_all | solution.py:63
  150.6 58.1 %copy-start.9 = (bf16[8,2,128,128]{3,2,1,0:T(8,128)(2,1)S(1)}, bf16[8,2,128,128]{3,2,1,0:T(8,128)(2,1)}, u32[]{:S(2)}) copy-start(bf16[8,2,128,128]{3,2,1,0:T(8,128)(2,1)} %copy.40) | copy-start | bytes 1572868
  150.6 4.4 %collective-permute-start.5 = (bf16[8,8,1024]{2,1,0:T(8,128)(2,1)S(1)}, bf16[8,8,1024]{2,1,0:T(8,128)(2,1)S(1)}, u32[]{:S(2)}, u32[]{:S(2)}) collective-permute-start(bf16[8,8,1024]{2,1,0:T(8,128)(2,1)S(1)} %get-tuple-element.43), channel_id=1, source_target_pairs={{0,16},{16,0},{1,17},{17,1},{2,18},{18,2},{3,19},{19,3},{4,20},{20... | collective-permute-start | bytes 393224 | tf_op jit(solution)/shard_map/ppermute | solution.py:59
  155.7 15.2 %all-to-all-start.5 = ((bf16[8,8,1024]{2,1,0:T(8,128)(2,1)}), bf16[8,8,1024]{2,1,0:T(8,128)(2,1)S(1)}, u32[]{:S(2)}, u32[]{:S(2)}) async-start(bf16[8,8,1024]{2,1,0:T(8,128)(2,1)} %add_convert_fusion.1), calls=%async_computation.5 | async-start | bytes 262144 | tf_op jit(solution)/shard_map/all_to_all | solution.py:63
  162.9 8.0 %collective-permute-start.4 = (f32[8,1024]{1,0:T(8,128)S(1)}, f32[8,1024]{1,0:T(8,128)S(1)}, u32[]{:S(2)}, u32[]{:S(2)}) collective-permute-start(f32[8,1024]{1,0:T(8,128)S(1)} %get-tuple-element.69), channel_id=1, source_target_pairs={{0,0},{24,1},{32,2},{56,3},{64,4},{88,5},{96,6},{120,7},{128,8},{1... | collective-permute-start | bytes 98312 | tf_op jit(solution)/shard_map/ppermute | solution.py:55
  170.9 2.2 copy-start.1
  173.1 26.0 %copy-start.10 = (bf16[8,2,128,128]{3,2,1,0:T(8,128)(2,1)S(1)}, bf16[8,2,128,128]{3,2,1,0:T(8,128)(2,1)}, u32[]{:S(2)}) copy-start(bf16[8,2,128,128]{3,2,1,0:T(8,128)(2,1)} %copy.39) | copy-start | bytes 1572868
  175.2 74.3 %copy-start.7 = (s32[1,1,2,160]{3,2,1,0:T(2,128)S(1)}, s32[1,1,2,160]{3,2,1,0:T(2,128)}, u32[]{:S(2)}) copy-start(s32[1,1,2,160]{3,2,1,0:T(2,128)} %param.13) | copy-start | bytes 3844
  175.2 14.2 %all-to-all-start.6 = ((f32[16,8,128]{2,1,0:T(8,128)}), f32[16,8,128]{2,1,0:T(8,128)S(1)}, u32[]{:S(2)}, u32[]{:S(2)}) async-start(f32[16,8,128]{2,1,0:T(8,128)} %coarse_product.1), calls=%async_computation.6 | async-start | bytes 131072 | tf_op jit(solution)/shard_map/all_to_all | solution.py:63
  218.5 2.2 copy-start.2
  242.0 7.5 %collective-permute-start.6 = (f32[8,8,1280]{2,1,0:T(8,128)S(1)}, f32[8,8,1280]{2,1,0:T(8,128)S(1)}, u32[]{:S(2)}, u32[]{:S(2)}) collective-permute-start(f32[8,8,1280]{2,1,0:T(8,128)S(1)} %all_to_all.64.own_ref), channel_id=1, source_target_pairs={{0,16},{16,0},{1,17},{17,1},{2,18},{18,2},{3,19},{19,3},{4,20},{20... | collective-permute-start | bytes 983048 | tf_op jit(solution)/shard_map/ppermute | solution.py:59
  258.1 30.9 %all-to-all-start.11 = ((bf16[16,128,256]{2,1,0:T(8,128)(2,1)}), bf16[16,128,256]{2,1,0:T(8,128)(2,1)S(1)}, u32[]{:S(2)}, u32[]{:S(2)}) async-start(bf16[16,128,256]{2,1,0:T(8,128)(2,1)} %product_shares.1), calls=%async_computation.11 | async-start | bytes 2097152 | tf_op jit(solution)/shard_map/all_to_all | solution.py:63

commit v3 on v2

v3 whole, which is shorter than its diff:
```python
import jax
import jax.numpy as jnp
from jax import lax
from jax.experimental import pallas as pl
from jax.experimental.pallas import tpu as pltpu
from jax.sharding import Mesh
from jax.sharding import PartitionSpec as P

TILE = 128
SIDE = 16
HALF = 8
BLOCK = 8
FIELDS = SIDE * BLOCK
GROUP = 16

support_fine = 0.35
support_mid = 0.55
support_coarse = 0.8

ROW = ("y", "zh", "k")
YZ = ("y", "zh")
COL = ("x", "zl")
ALL = ROW + COL

bf16 = jnp.bfloat16
f32 = jnp.float32

VMEM = pl.BlockSpec(memory_space=pltpu.VMEM)
SMEM = pl.BlockSpec(memory_space=pltpu.SMEM)


def room(mebibytes):
    return pltpu.CompilerParams(vmem_limit_bytes=mebibytes * 1024 * 1024)


def hint(microseconds):
    return pl.CostEstimate(
        flops=0, transcendentals=0, bytes_accessed=int(microseconds * 3.0e6)
    )


def turned(x):
    pairs = [(c * SIDE + r, r * SIDE + c) for r in range(SIDE) for c in range(SIDE)]
    return lax.ppermute(x, ALL, pairs)


def place_of_block(block, core):
    return ((block % 2) ^ core) * HALF + block // 2


def turned_blocks(x):
    pairs = [
        (c * SIDE + place_of_block(r, c % 2), r * SIDE + c) for r in range(SIDE) for c in range(SIDE)
    ]
    return lax.ppermute(x, ALL, pairs)


def from_partner(x):
    return lax.ppermute(x, "k", [(0, 1), (1, 0)])


def exchanged(x, axes):
    return lax.all_to_all(x, axes, split_axis=0, concat_axis=0, tiled=True)


def pair_sum(own, other):
    return (own.astype(f32) + from_partner(other).astype(f32)).astype(bf16)


def stretch_of(support):
    return (4.0 / support**5) ** 0.2


def wendland(left, right, support):
    across, upward = left[0] - right[0], left[1] - right[1]
    square = jnp.maximum(across * across + upward * upward, 1e-30)
    edge = support * stretch_of(support)
    margin = jnp.maximum(edge - square * lax.rsqrt(square), 0.0)
    margin2 = margin * margin
    ratio = 5.0 / edge**4
    return (margin2 * margin2 * (ratio - margin)).astype(bf16)


def at_tile(i):
    return pl.ds(pl.multiple_of(i * TILE, TILE), TILE)


def call(kernel, shapes, operands, name, mebibytes, microseconds, scratch=(), scalars=0):
    out = pl.pallas_call(
        kernel,
        out_shape=[jax.ShapeDtypeStruct(shape, kind) for shape, kind in shapes],
        in_specs=[SMEM] * scalars + [VMEM] * (len(operands) - scalars),
        out_specs=[VMEM] * len(shapes),
        scratch_shapes=list(scratch),
        compiler_params=room(mebibytes),
        cost_estimate=hint(microseconds),
        name=name,
    )(*operands)
    return out if len(shapes) > 1 else out[0]


def rows_of(listed):
    return -(-listed // TILE)


def in_rows(listing):
    rows = rows_of(listing.shape[1])
    padded = jnp.pad(listing, ((0, 0), (0, rows * TILE - listing.shape[1])))
    return padded.reshape(2 * rows, TILE)


def packed(points0, points1, lists, factor):
    fine, mid = points0.shape[1] // TILE, points1.shape[1] // TILE
    used = 2 * (fine + mid) + lists.shape[0]
    above = -(-used // SIDE) * SIDE

    def kernel(fine_ref, mid_ref, list_ref, factor_ref, out_ref):
        lines = []
        for ref, tiles in ((fine_ref, fine), (mid_ref, mid)):
            whole = ref[...].astype(f32)
            lines += [
                whole[a : a + 1, t * TILE : (t + 1) * TILE] for a in range(2) for t in range(tiles)
            ]
        lines.append(list_ref[...].astype(f32))
        if above > used:
            lines.append(jnp.zeros((above - used, TILE), f32))
        out_ref[pl.ds(0, above), :] = jnp.concatenate(lines, axis=0).astype(bf16)
        out_ref[pl.ds(above, TILE), :] = factor_ref[...]

    shapes = [((above + TILE, TILE), bf16)]
    return call(kernel, shapes, (points0, points1, lists, factor), "packed", 8, 1)


def unpacked(there, factor, centres, fine, mid, listed):
    used = 2 * (fine + mid) + listed
    above = -(-used // SIDE) * SIDE
    size = 2 * TILE + SIDE

    def kernel(there_ref, factor_ref, centre_ref, fine_ref, mid_ref, list_ref, common_ref):
        lines = there_ref[pl.ds(0, above), :].astype(f32)
        at = 0
        for ref, tiles in ((fine_ref, fine), (mid_ref, mid)):
            for a in range(2):
                for t in range(tiles):
                    ref[a, t] = lines[at : at + 1]
                    at += 1
        list_ref[...] = lines[at : at + listed].astype(jnp.int32)
        for chip in range(HALF):
            common_ref[chip, pl.ds(0, TILE), :] = factor_ref[...]
            common_ref[chip, pl.ds(TILE, TILE), :] = there_ref[pl.ds(above, TILE), :]
            common_ref[chip, pl.ds(2 * TILE, SIDE), :] = centre_ref[...]

    shapes = [
        ((2, fine, 1, TILE), f32),
        ((2, mid, 1, TILE), f32),
        ((listed, TILE), jnp.int32),
        ((HALF, size, TILE), bf16),
    ]
    return call(kernel, shapes, (there, factor, centres), "unpacked", 8, 1)


def set_points(left_ref, right_ref, left, right, support):
    stretch = stretch_of(support)
    for axis in range(2):
        for t in range(left.shape[1]):
            row = left_ref[axis, t] * stretch
            left[axis, t] = jnp.broadcast_to(row, (TILE, TILE)).T
        for t in range(right.shape[1]):
            right[axis, t] = right_ref[axis, t] * stretch


def point_scratch(left, right):
    return [pltpu.VMEM((2, left, TILE, TILE), f32), pltpu.VMEM((2, right, 1, TILE), f32)]


def add_tiles(list_ref, listed, first, contracted, left, right, vector, total, support):
    rows = rows_of(listed)
    steps = TILE // GROUP
    line_j = first + contracted * rows
    line_i = first + (1 - contracted) * rows

    def step(g, carry):
        row, lane = g // steps, g % steps * GROUP
        products = []
        for u in range(GROUP):
            j = list_ref[line_j + row, lane + u]
            i = list_ref[line_i + row, lane + u]
            tile = wendland((left[0, j], left[1, j]), (right[0, i], right[1, i]), support)
            product = jnp.dot(vector[:, at_tile(j)], tile, preferred_element_type=f32)
            products.append((i, product))
        for i, product in products:
            total[i] += product
        return carry

    lax.fori_loop(0, listed // GROUP, step, 0)


def product_a0(lists, place, left, right, vector, listed):
    tiles = right.shape[1]

    def kernel(
        list_ref, place_ref, left_ref, right_ref, vector_ref, own_ref, other_ref, left, right, total
    ):
        set_points(left_ref, right_ref, left, right, support_fine)
        me = place_ref[0]
        weight = jnp.where(place_ref[1] == place_ref[2], -2.0 / scale_of(tiles, listed), 0.0)
        for i in range(tiles):
            at = pl.ds(i * TILE, TILE)
            total[i] = vector_ref[:, at].astype(f32) * weight
        add_tiles(list_ref, listed, 0, 1, left, right, vector_ref, total, support_fine)
        for half in range(HALF):
            for i in range(tiles):
                at = pl.ds(i * TILE, TILE)
                own = pl.ds(pl.multiple_of((2 * half + me) * BLOCK, BLOCK), BLOCK)
                other = pl.ds(pl.multiple_of((2 * half + 1 - me) * BLOCK, BLOCK), BLOCK)
                own_ref[half, :, at] = total[i, own, :].astype(bf16)
                other_ref[half, :, at] = total[i, other, :].astype(bf16)

    half = ((HALF, BLOCK, tiles * TILE), bf16)
    scratch = [*point_scratch(left.shape[1], tiles), pltpu.VMEM((tiles, FIELDS, TILE), f32)]
    operands = (lists, place, left, right, vector)
    return call(kernel, [half, half], operands, "product_a0", 16, 20, scratch, 2)


def product(lists, listed, first, contracted, left, right, halves, support, form):
    tiles = right.shape[1]
    length = left.shape[1] * TILE

    def kernel(list_ref, left_ref, right_ref, own_ref, other_ref, *rest):
        *outs, left, right, vector, total = rest
        set_points(left_ref, right_ref, left, right, support)
        total[...] = jnp.zeros_like(total)
        for ref, at in ((own_ref, 0), (other_ref, FIELDS // 2)):
            rows = ref[:, :, pl.ds(0, length)].reshape(FIELDS // 2, length)
            vector[pl.ds(at, FIELDS // 2), :] = rows
        add_tiles(list_ref, listed, first, contracted, left, right, vector, total, support)
        for i in range(tiles):
            low = total[i].astype(bf16)
            if form == "shares":
                each = tiles // SIDE
                outs[0][i // each, :, pl.ds(i % each * TILE, TILE)] = low
            elif form == "blocks":
                outs[0][:, :, pl.ds(i * TILE, TILE)] = low.reshape(SIDE, BLOCK, TILE)
            else:
                pair = low.reshape(2, HALF, BLOCK, TILE)
                outs[0][:, :, pl.ds(i * TILE, TILE)] = pair[0]
                outs[1][:, :, pl.ds(i * TILE, TILE)] = pair[1]

    size = tiles * TILE
    if form == "shares":
        shapes = [((SIDE, FIELDS, size // SIDE), bf16)]
    elif form == "blocks":
        shapes = [((SIDE, BLOCK, size), bf16)]
    else:
        shapes = [((HALF, BLOCK, size), bf16)] * 2
    scratch = [
        *point_scratch(left.shape[1], tiles),
        pltpu.VMEM((FIELDS, length), bf16),
        pltpu.VMEM((tiles, FIELDS, TILE), f32),
    ]
    operands = (lists, left, right, *halves)
    return call(kernel, shapes, operands, "product_" + form, 16, listed / 18, scratch, 1)


def all_pairs(left, right, support):
    rows, cols = left.shape[1], right.shape[1]

    def kernel(left_ref, right_ref, out_ref):
        stretch = stretch_of(support)
        ys = [jnp.broadcast_to(left_ref[a, 0] * stretch, (TILE, TILE)).T for a in range(2)]
        for j in range(cols):
            out_ref[:, pl.ds(j * TILE, TILE)] = wendland(
                ys, (right_ref[0, j] * stretch, right_ref[1, j] * stretch), support
            )

    return pl.pallas_call(
        kernel,
        out_shape=jax.ShapeDtypeStruct((rows * TILE, cols * TILE), bf16),
        grid=(rows,),
        in_specs=[pl.BlockSpec((2, 1, 1, TILE), lambda i: (0, i, 0, 0)), VMEM],
        out_specs=pl.BlockSpec((TILE, cols * TILE), lambda i: (i, 0)),
        compiler_params=room(8),
        cost_estimate=hint(6),
        name="all_pairs",
    )(left, right)


def residual_of(arrived, scale):
    chips, _, n = arrived.shape

    def kernel(arrived_ref, out_ref):
        squares = jnp.zeros((1, TILE), f32)
        for t in range(n // TILE):
            at = pl.ds(t * TILE, TILE)
            part = scale * arrived_ref[:, :, at].astype(f32).sum(axis=0)
            squares += jnp.sum(part * part, axis=0, keepdims=True)
            low = part.astype(bf16)
            for chip in range(chips):
                out_ref[chip, :, at] = low
        tail = three_rows(squares)
        for chip in range(chips):
            out_ref[chip, :, pl.ds(n, TILE)] = tail

    return call(kernel, [((chips, BLOCK, n + TILE), bf16)], (arrived,), "residual_of", 8, 1)


def three_rows(x):
    high = x.astype(bf16).astype(f32)
    rest = x - high
    middle = rest.astype(bf16).astype(f32)
    rows = [high, middle, rest - middle, jnp.zeros((BLOCK - 3, TILE), f32)]
    return jnp.concatenate(rows, axis=0).astype(bf16)


def mid_of(arrived, scale):
    peers, _, n = arrived.shape

    def kernel(arrived_ref, out_ref, low_ref):
        part = scale * arrived_ref[...].astype(f32).sum(axis=0)
        out_ref[...] = part
        low = part.astype(bf16)
        for peer in range(peers):
            low_ref[peer] = low

    shapes = [((BLOCK, n), f32), ((peers, BLOCK, n), bf16)]
    return call(kernel, shapes, (arrived,), "mid_of", 8, 1)


def coarse_product(matrix, arrived, mid_data, scale):
    rows, cols = matrix.shape

    def kernel(matrix_ref, arrived_ref, mid_ref, out_ref, turned_ref):
        @pl.when(pl.program_id(0) == 0)
        def _():
            whole = (scale * arrived_ref[...].astype(f32).sum(axis=0)).astype(bf16).astype(f32)
            whole = mid_ref[...] - 0.5 * whole
            for t in range(cols // TILE):
                lines = whole[:, t * TILE : (t + 1) * TILE]
                full = jnp.concatenate([lines, jnp.zeros((TILE - BLOCK, TILE), f32)], axis=0)
                turned_ref[pl.ds(t * TILE, TILE), :] = full.T.astype(bf16)

        for q in range(2):
            at = pl.ds(q * TILE, TILE)
            part = jnp.dot(matrix_ref[at, :], turned_ref[...], preferred_element_type=f32)
            out_ref[q] = part.T[:BLOCK, :]

    return pl.pallas_call(
        kernel,
        out_shape=jax.ShapeDtypeStruct((rows // TILE, BLOCK, TILE), f32),
        grid=(rows // TILE // 2,),
        in_specs=[pl.BlockSpec((2 * TILE, cols), lambda q: (q, 0)), VMEM, VMEM],
        out_specs=pl.BlockSpec((2, BLOCK, TILE), lambda q: (q, 0, 0)),
        scratch_shapes=[pltpu.VMEM((cols, TILE), bf16)],
        compiler_params=room(8),
        cost_estimate=hint(3),
        name="coarse_product",
    )(matrix, arrived, mid_data)


def coarse_data_of(arrived, own, other, scale):
    peers = arrived.shape[0]
    n = own.shape[2] - TILE

    def kernel(arrived_ref, own_ref, other_ref, out_ref):
        data = (scale * arrived_ref[...].sum(axis=0)).astype(bf16)
        squares = jnp.zeros((1, TILE), f32)
        for ref in (own_ref, other_ref):
            tails = ref[...].astype(f32).sum(axis=0)
            squares += jnp.sum(tails, axis=0, keepdims=True)
        tail = three_rows(squares)
        for peer in range(peers):
            out_ref[peer, 0] = data
            out_ref[peer, 1] = tail

    tails = (own[:, :, n:], other[:, :, n:])
    shapes = [((peers, 2, BLOCK, TILE), bf16)]
    return call(kernel, shapes, (arrived, *tails), "coarse_data_of", 8, 1)


def halfway_of(gathered_data, factor_down):
    peers = gathered_data.shape[0]

    def kernel(data_ref, factor_ref, out_ref):
        total = jnp.zeros((BLOCK, TILE), f32)
        for q in range(peers // 2):
            pair = jnp.concatenate([data_ref[2 * q, 0], data_ref[2 * q + 1, 0]], axis=1)
            rows = factor_ref[pl.ds(q * 2 * TILE, 2 * TILE), :]
            total += jnp.dot(pair, rows, preferred_element_type=f32)
        low = total.astype(bf16)
        for peer in range(peers):
            out_ref[peer] = low

    shapes = [((peers, BLOCK, TILE), bf16)]
    return call(kernel, shapes, (gathered_data, factor_down), "halfway_of", 8, 1)


def coarse_coef_of(halfway, factor_across):
    peers = halfway.shape[0]

    def kernel(half_ref, factor_ref, out_ref):
        total = jnp.zeros((BLOCK, TILE), f32)
        for q in range(peers):
            total += lax.dot_general(
                half_ref[q], factor_ref[q], (((1,), (1,)), ((), ())), preferred_element_type=f32
            )
        for peer in range(peers):
            out_ref[peer] = total

    shapes = [((peers, BLOCK, TILE), f32)]
    return call(kernel, shapes, (halfway, factor_across), "coarse_coef_of", 8, 1)


def prolong(matrix, coarse_coef, mid_data, scale):
    rows, cols = matrix.shape
    two = 2 * TILE
    steps = rows // two

    def kernel(matrix_ref, coef_ref, mid_ref, out_ref, total):
        q = pl.program_id(0)

        @pl.when(q == 0)
        def _():
            total[...] = jnp.zeros_like(total)

        pair = jnp.concatenate([coef_ref[0], coef_ref[1]], axis=1).astype(bf16)
        out_ref[q, :, pl.ds(cols, two)] = pair
        total[...] += jnp.dot(pair, matrix_ref[...], preferred_element_type=f32)

        @pl.when(q == steps - 1)
        def _():
            low = (0.5 * mid_ref[...] + scale * total[...]).astype(bf16)
            for chip in range(steps):
                out_ref[chip, :, pl.ds(0, cols)] = low

    return pl.pallas_call(
        kernel,
        out_shape=jax.ShapeDtypeStruct((steps, BLOCK, cols + two), bf16),
        grid=(steps,),
        in_specs=[
            pl.BlockSpec((two, cols), lambda q: (q, 0)),
            pl.BlockSpec((2, BLOCK, TILE), lambda q: (q, 0, 0)),
            VMEM,
        ],
        out_specs=VMEM,
        scratch_shapes=[pltpu.VMEM((BLOCK, cols), f32)],
        compiler_params=room(8),
        cost_estimate=hint(3),
        name="prolong",
    )(matrix, coarse_coef, mid_data)


def fine_of(arrived, data, core, scale):
    n = arrived.shape[2]

    def kernel(core_ref, arrived_ref, data_ref, out_ref, summed):
        me = core_ref[0]
        summed[...] = arrived_ref[...].astype(f32).sum(axis=0)
        rows = []
        for block in range(SIDE):
            at = ((block % 2) ^ me) * HALF + block // 2
            rows.append(summed[pl.ds(pl.multiple_of(at * BLOCK, BLOCK), BLOCK), :])
        whole = jnp.concatenate(rows, axis=0)
        for t in range(n // TILE):
            at = pl.ds(t * TILE, TILE)
            data = data_ref[at, :].astype(f32)
            out_ref[at, :] = 0.5 * data + scale * whole[:, t * TILE : (t + 1) * TILE].T

    scratch = [pltpu.VMEM((FIELDS, n), f32)]
    return call(kernel, [((n, FIELDS), f32)], (core, arrived, data), "fine_of", 8, 2, scratch, 1)


def in_field_order(x, core):
    n = x.shape[-1]
    x = jnp.where(core == 0, x, x[::-1])
    return x.transpose(3, 1, 0, 2).reshape(n, FIELDS)


def scale_of(tiles, listed):
    return (tiles * TILE / (SIDE * listed * TILE * TILE)) ** 0.5


def per_device(values, points0, points1, points2, tiles_a0, tiles_e1, tiles_a1, factor):
    core = lax.axis_index("k")
    col_id = lax.axis_index(COL)
    row_id = lax.axis_index(ROW)
    rows_fine, fields = values.shape
    rows_mid = points1.shape[1]
    rows_coarse = points2.shape[1]
    coarse = rows_coarse * SIDE
    share = rows_fine // SIDE
    tiles_fine, tiles_mid = rows_fine // TILE, rows_mid // TILE
    list_a0, list_e1, list_a1 = tiles_a0[0, 0], tiles_e1[0, 0], tiles_a1[0, 0]
    scale_a0 = scale_of(tiles_fine, list_a0.shape[1])
    scale_e1 = scale_of(tiles_fine, list_e1.shape[1])
    scale_a1 = scale_of(tiles_mid, list_a1.shape[1])
    scale_e2 = (1.0 / (rows_mid * SIDE)) ** 0.5

    listed_a0, listed_e1, listed_a1 = (a.shape[1] for a in (list_a0, list_e1, list_a1))

    own_e1 = in_rows(list_e1)
    lists = jnp.concatenate([in_rows(list_a0), own_e1, in_rows(list_a1)], axis=0)
    there = turned(packed(points0, points1, lists, factor))
    centres = jnp.pad(points2, ((0, 2 * BLOCK - 2), (0, 0)))
    place = jnp.stack([core, row_id, col_id]).astype(jnp.int32)
    fine_here = points0.astype(f32).reshape(2, tiles_fine, 1, TILE)
    mid_here = points1.astype(f32).reshape(2, tiles_mid, 1, TILE)
    there, vector, centres, fine_here, mid_here = lax.optimization_barrier(
        (there, values.T, centres, fine_here, mid_here)
    )
    fine_there, mid_there, lists, common = unpacked(
        there, factor, centres, tiles_fine, tiles_mid, lists.shape[0]
    )
    first_e1 = 2 * rows_of(listed_a0)
    first_a1 = first_e1 + 2 * rows_of(listed_e1)

    common = exchanged(common, YZ)
    own, other = product_a0(lists, place, fine_here, fine_there, vector, listed_a0)
    own, other, common = lax.optimization_barrier((own, other, common))
    arrived = exchanged(pair_sum(own, other), YZ)

    fine_all, common, mid_later = lax.optimization_barrier(
        (residual_of(arrived, -0.5 * scale_a0), common, mid_there)
    )
    partner = from_partner(common)

    def in_row_order(at, size):
        mine, its = common[:, at : at + size], partner[:, at : at + size]
        return jnp.stack([jnp.where(core == 0, mine, its), jnp.where(core == 0, its, mine)], axis=1)

    factor_down = in_row_order(0, rows_coarse).reshape(coarse, -1)
    factor_across = in_row_order(rows_coarse, rows_coarse).reshape(SIDE, rows_coarse, -1)
    centres = in_row_order(2 * rows_coarse, 2 * BLOCK).reshape(SIDE, 2 * BLOCK, -1)[:, :2]
    centres = centres.astype(f32).transpose(1, 0, 2)[:, :, None]
    coarse_kernel = all_pairs(centres, mid_later, support_coarse)
    fine_own, coarse_kernel, factor_down, factor_across = lax.optimization_barrier(
        (exchanged(fine_all, YZ), coarse_kernel, factor_down, factor_across)
    )
    fine_other = from_partner(fine_own)

    restricted = product(
        lists, listed_e1, first_e1, 0, fine_there, mid_here, (fine_own, fine_other), support_mid, "blocks"
    )
    mid_share, mid_all = mid_of(exchanged(restricted, COL), scale_e1)
    mid_all = exchanged(mid_all, COL)
    mid_data = turned_blocks(mid_share)

    mid_halves = (mid_all[:HALF], mid_all[HALF:])
    mid_own, mid_other = product(
        lists, listed_a1, first_a1, 1, mid_here, mid_there, mid_halves, support_mid, "halves"
    )
    arrived = exchanged(pair_sum(mid_own, mid_other), YZ)

    coarse_part = coarse_product(coarse_kernel, arrived, mid_data, scale_a1)
    coarse_data = coarse_data_of(exchanged(coarse_part, COL), fine_own, fine_other, scale_e2)
    coarse_data = exchanged(coarse_data, COL)
    halfway = exchanged(halfway_of(coarse_data, factor_down), COL)
    coarse_all = exchanged(coarse_coef_of(halfway, factor_across), COL)

    new_own = exchanged(prolong(coarse_kernel, coarse_all, mid_data, scale_e2), YZ)
    new_other = from_partner(new_own)
    fine_part = product(
        own_e1, listed_e1, 0, 1, mid_there, fine_here, (new_own, new_other), support_mid, "shares"
    )
    own_data = lax.dynamic_slice_in_dim(values, col_id * share, share, 0)
    fine_coef = fine_of(exchanged(fine_part, COL), own_data, place, scale_e1)

    both = jnp.stack([new_own, new_other]).astype(f32)
    mid_coef = in_field_order(both[..., :rows_mid], core)
    coarse_coef = lax.dynamic_slice_in_dim(both, rows_mid + core * rows_coarse, rows_coarse, 3)
    coarse_coef = in_field_order(coarse_coef, core)
    norm = coarse_data[:, 1].astype(f32).sum() / (rows_fine * SIDE * fields)
    return (fine_coef, mid_coef, coarse_coef, jnp.stack([norm]))


def solution(mesh):
    fine_mesh = Mesh(mesh.devices.reshape(4, 2, 2, 4, 4), ALL)
    return jax.shard_map(
        per_device,
        mesh=fine_mesh,
        in_specs=(
            P(ROW, None),
            P(None, ROW),
            P(None, ROW),
            P(None, ROW),
            P(ROW, COL, None, None),
            P(ROW, COL, None, None),
            P(ROW, COL, None, None),
            P(ROW, COL),
        ),
        out_specs=(P(ALL, None), P(COL, None), P(ROW, None), P()),
        check_vma=False,
    )
```

time: 293 us -> 282 us (0.962)
  blocking collectives: 62.8 us -> 99.3 us
  waiting for transfers between devices: 69.1 us -> 49.3 us
  starting transfers between devices: 73.1 us -> 56.3 us
  other arithmetic: 12.1 us -> 2.5 us
  Pallas kernels: 46.5 us -> 53.4 us
  local copies, waits for them, and re-layouts: 24 us -> 17.1 us
    all_to_all x5 -> x7, blocking collectives: 62.8 us -> 99.3 us  [exchanged(): return lax.all_to_all(x, axes, split_axis=0, concat_axis=0, tiled=True)]
    all_to_all x7 -> x5, waiting for transfers between devices: 61.7 us -> 39.3 us  [exchanged(): return lax.all_to_all(x, axes, split_axis=0, concat_axis=0, tiled=True)]
    all_to_all x7 -> x5, starting transfers between devices: 51.9 us -> 35.8 us  [exchanged(): return lax.all_to_all(x, axes, split_axis=0, concat_axis=0, tiled=True)]
    unnamed x30 -> x17, local copies, waits for them, and re-layouts: 17.6 us -> 12.5 us
    ppermute x1, waiting for transfers between devices: 0.01 us -> 4.81 us  [turned_blocks(): return lax.ppermute(x, ALL, pairs)]
    pallas_call x10 -> x13, Pallas kernels: 39.9 us -> 43.7 us  [the longest x12 42.2 us: call(): pl.pallas_call(kernel, out_shape=[jax.ShapeDtypeStruct(shape, kind) for s...]
  transfers between devices with their start and end apart: 14 -> 12, of which waited for: 11 -> 9; matrix products, arithmetic and copies ran while one was open for 4% -> 3% of each run, Pallas kernels for 9% -> 8%
where the time goes in v3:
time: 282 us; the launch traced here: 281 us
  blocking collectives  99.3 us (35%)
  starting transfers between devices  56.3 us (20%)
  Pallas kernels  53.4 us (19%)
  waiting for transfers between devices  49.3 us (17%)
  local copies, waits for them, and re-layouts  17.1 us (6%)
    all_to_all x7, blocking collectives, exchanged(): return lax.all_to_all(x, axes, split_axis=0, concat_axis=0, tiled=True)  99.3 us
    pallas_call x12, Pallas kernels, call(): pl.pallas_call(kernel, out_shape=[jax.ShapeDtypeStruct(shape, kind) for s...  42.2 us
    all_to_all x5, waiting for transfers between devices, exchanged(): return lax.all_to_all(x, axes, split_axis=0, concat_axis=0, tiled=True)  39.3 us
    all_to_all x5, starting transfers between devices, exchanged(): return lax.all_to_all(x, axes, split_axis=0, concat_axis=0, tiled=True)  35.8 us
    ppermute x5, starting transfers between devices, from_partner(): return lax.ppermute(x, 'k', [(0, 1), (1, 0)])  13.6 us
    unnamed x17, local copies, waits for them, and re-layouts  12.5 us
  transfers between devices with their start and end apart: 12, of which 9 were waited for; matrix products, arithmetic and copies ran while one was open for 3% of the time, Pallas kernels for 8%

profile of v3, /device:TPU:1, one launch (start us, length us, event | category | flops | bytes accessed | tf_op | source)
XLA Modules:
  0.0 280.6 jit_solution(11259209731524157398)
XLA Ops:
  4.9 4.9 %collective-permute-start = (bf16[224,128]{1,0:T(8,128)(2,1)S(1)}, bf16[224,128]{1,0:T(8,128)(2,1)S(1)}, u32[]{:S(2)}, u32[]{:S(2)}) collective-permute-start(bf16[224,128]{1,0:T(8,128)(2,1)S(1)} %packed.1), channel_id=1, source_target_pairs={{0,0},{16,1},{32,2},{48,3},{64,4},{80,5},{96,6},{112,7},{128,8},{1... | collective-permute-start | bytes 172040 | tf_op jit(solution)/shard_map/ppermute | solution.py:44
  15.1 15.1 %all-to-all-start = ((bf16[8,272,128]{2,1,0:T(8,128)(2,1)}), bf16[8,272,128]{2,1,0:T(8,128)(2,1)S(1)}, u32[]{:S(2)}, u32[]{:S(2)}) async-start(bf16[8,272,128]{2,1,0:T(8,128)(2,1)} %get-tuple-element.38), calls=%async_computation | async-start | bytes 1114112 | tf_op jit(solution)/shard_map/all_to_all | solution.py:63
  30.4 18.3 %product_a0.1 = (bf16[8,8,4096]{2,1,0:T(8,128)(2,1)S(1)}, bf16[8,8,4096]{2,1,0:T(8,128)(2,1)S(1)}) custom-call(s32[12,128]{1,0:T(8,128)S(1)} %get-tuple-element.33.list_ref, s32[3]{0:T(128)S(1)} %pad_add_fusion.1.place_ref.core_ref, f32[2,32,1,128]{3,2,1,0:T(1,128)S(1)} %reshape.55.left_ref.right_ref, ...), custom_call_target="tpu_custom_call" | custom-call | bytes 60000000 | tf_op jit(solution)/shard_map/product_a0/pallas_call | solution.py:89
  48.7 2.4 collective-permute-start.1
  52.8 24.8 %all_to_all.60.arrived_ref = bf16[8,8,4096]{2,1,0:T(8,128)(2,1)S(1)} all-to-all(bf16[8,8,4096]{2,1,0:T(8,128)(2,1)S(1)} %add_convert_fusion), channel_id=1, replica_groups=mesh['y'=4,'zh'=2,'k'=2,'x'=4,'zl'=4] {'y','zh'}, dimensions={0} | all-to-all | bytes 1048576 | tf_op jit(solution)/shard_map/all_to_all | solution.py:63
  78.6 1.7 collective-permute-start.2
  80.3 5.3 %all-to-all-start.2 = ((bf16[8,8,4224]{2,1,0:T(8,128)(2,1)}), bf16[8,8,4224]{2,1,0:T(8,128)(2,1)S(1)}, u32[]{:S(2)}, u32[]{:S(2)}) async-start(bf16[8,8,4224]{2,1,0:T(8,128)(2,1)} %residual_of.1), calls=%async_computation.2 | async-start | bytes 1081344 | tf_op jit(solution)/shard_map/all_to_all | solution.py:63
  86.1 5.5 %all_pairs.1.matrix_ref = bf16[2048,1024]{1,0:T(8,128)(2,1)S(1)} custom-call(f32[2,16,1,128]{3,2,1,0:T(1,128)S(1)} %bitcast.38, f32[2,8,1,128]{3,2,1,0:T(1,128)S(1)} %get-tuple-element.44.right_ref.left_ref), custom_call_target="tpu_custom_call" | custom-call | bytes 18000000 | tf_op jit(solution)/shard_map/all_pairs/pallas_call | solution.py:276
  91.6 1.9 copy-done
  93.5 6.5 %all-to-all-done.2.own_ref = bf16[8,8,4224]{2,1,0:T(8,128)(2,1)S(1)} async-done(((bf16[8,8,4224]{2,1,0:T(8,128)(2,1)}), bf16[8,8,4224]{2,1,0:T(8,128)(2,1)S(1)}, u32[]{:S(2)}, u32[]{:S(2)}) %all-to-all-start.2) | async-done | bytes 540704 | tf_op jit(solution)/shard_map/all_to_all | solution.py:63
  102.6 8.6 %product_blocks.1 = bf16[16,8,1024]{2,1,0:T(8,128)(2,1)S(1)} custom-call(s32[12,128]{1,0:T(8,128)S(1)} %get-tuple-element.33.list_ref, f32[2,32,1,128]{3,2,1,0:T(1,128)S(1)} %get-tuple-element.34.right_ref.left_ref, f32[2,8,1,128]{3,2,1,0:T(1,128)S(1)} %reshape.57.right_ref.left_ref, bf16[8,8,4224]{2,1,0:T(8,128)(2,1)S(1)} %all-to-all-done.2.own_ref, ...), custom_call_target="tpu_custom_call" | custom-call | bytes 26666666 | tf_op jit(solution)/shard_map/product_blocks/pallas_call | solution.py:89
  111.2 14.1 %all_to_all.61.arrived_ref = bf16[16,8,1024]{2,1,0:T(8,128)(2,1)S(1)} all-to-all(bf16[16,8,1024]{2,1,0:T(8,128)(2,1)S(1)} %product_blocks.1), channel_id=1, replica_groups=mesh['y'=4,'zh'=2,'k'=2,'x'=4,'zl'=4] {'x','zl'}, dimensions={0} | all-to-all | bytes 524288 | tf_op jit(solution)/shard_map/all_to_all | solution.py:63
  125.3 13.1 %all_to_all.62 = bf16[16,8,1024]{2,1,0:T(8,128)(2,1)S(1)} all-to-all(bf16[16,8,1024]{2,1,0:T(8,128)(2,1)S(1)} %get-tuple-element.48), channel_id=1, replica_groups=mesh['y'=4,'zh'=2,'k'=2,'x'=4,'zl'=4] {'x','zl'}, dimensions={0} | all-to-all | bytes 524288 | tf_op jit(solution)/shard_map/all_to_all | solution.py:63
  138.5 2.4 product_halves.1
  140.9 2.3 collective-permute-start.4
  144.9 5.2 %all-to-all-start.5 = ((bf16[8,8,1024]{2,1,0:T(8,128)(2,1)}), bf16[8,8,1024]{2,1,0:T(8,128)(2,1)S(1)}, u32[]{:S(2)}, u32[]{:S(2)}) async-start(bf16[8,8,1024]{2,1,0:T(8,128)(2,1)} %add_convert_fusion.1), calls=%async_computation.5 | async-start | bytes 262144 | tf_op jit(solution)/shard_map/all_to_all | solution.py:63
  150.1 1.9 collective-permute-start.5
  152.0 4.8 %collective-permute-done.5.mid_ref = f32[8,1024]{1,0:T(8,128)S(1)} collective-permute-done((f32[8,1024]{1,0:T(8,128)S(1)}, f32[8,1024]{1,0:T(8,128)S(1)}, u32[]{:S(2)}, u32[]{:S(2)}) %collective-permute-start.5) | collective-permute-done | bytes 32800 | tf_op jit(solution)/shard_map/ppermute | solution.py:55
  156.8 2.7 all-to-all-done.5.arrived_ref
  159.5 2.2 copy-done.1
  161.7 4.2 %coarse_product.1 = f32[16,8,128]{2,1,0:T(8,128)} custom-call(bf16[2048,1024]{1,0:T(8,128)(2,1)S(1)} %copy-done.1, bf16[8,8,1024]{2,1,0:T(8,128)(2,1)S(1)} %all-to-all-done.5.arrived_ref, f32[8,1024]{1,0:T(8,128)S(1)} %collective-permute-done.5.mid_ref), custom_call_target="tpu_custom_call" | custom-call | bytes 9000000 | tf_op jit(solution)/shard_map/coarse_product/pallas_call | solution.py:347
  165.9 6.5 %all-to-all-start.6 = ((f32[16,8,128]{2,1,0:T(8,128)}), f32[16,8,128]{2,1,0:T(8,128)S(1)}, u32[]{:S(2)}, u32[]{:S(2)}) async-start(f32[16,8,128]{2,1,0:T(8,128)} %coarse_product.1), calls=%async_computation.6 | async-start | bytes 131072 | tf_op jit(solution)/shard_map/all_to_all | solution.py:63
  172.5 7.0 %all-to-all-done.6.arrived_ref = f32[16,8,128]{2,1,0:T(8,128)S(1)} async-done(((f32[16,8,128]{2,1,0:T(8,128)}), f32[16,8,128]{2,1,0:T(8,128)S(1)}, u32[]{:S(2)}, u32[]{:S(2)}) %all-to-all-start.6) | async-done | bytes 65568 | tf_op jit(solution)/shard_map/all_to_all | solution.py:63
  179.5 9.6 %all_to_all.63.data_ref = bf16[16,2,8,128]{3,2,1,0:T(8,128)(2,1)S(1)} all-to-all(bf16[16,2,8,128]{3,2,1,0:T(8,128)(2,1)S(1)} %coarse_data_of.1), channel_id=1, replica_groups=mesh['y'=4,'zh'=2,'k'=2,'x'=4,'zl'=4] {'x','zl'}, dimensions={0} | all-to-all | bytes 131072 | tf_op jit(solution)/shard_map/all_to_all | solution.py:63
  189.3 9.4 %all_to_all.64.half_ref = bf16[16,8,128]{2,1,0:T(8,128)(2,1)S(1)} all-to-all(bf16[16,8,128]{2,1,0:T(8,128)(2,1)S(1)} %halfway_of.1), channel_id=1, replica_groups=mesh['y'=4,'zh'=2,'k'=2,'x'=4,'zl'=4] {'x','zl'}, dimensions={0} | all-to-all | bytes 65536 | tf_op jit(solution)/shard_map/all_to_all | solution.py:63
  199.0 9.6 %all_to_all.65.coef_ref = f32[16,8,128]{2,1,0:T(8,128)S(1)} all-to-all(f32[16,8,128]{2,1,0:T(8,128)S(1)} %coarse_coef_of.1), channel_id=1, replica_groups=mesh['y'=4,'zh'=2,'k'=2,'x'=4,'zl'=4] {'x','zl'}, dimensions={0} | all-to-all | bytes 131072 | tf_op jit(solution)/shard_map/all_to_all | solution.py:63
  208.6 2.2 copy-done.2
  212.3 18.7 %all_to_all.66.own_ref = bf16[8,8,1280]{2,1,0:T(8,128)(2,1)S(1)} all-to-all(bf16[8,8,1280]{2,1,0:T(8,128)(2,1)S(1)} %prolong.1), channel_id=1, replica_groups=mesh['y'=4,'zh'=2,'k'=2,'x'=4,'zl'=4] {'y','zh'}, dimensions={0} | all-to-all | bytes 327680 | tf_op jit(solution)/shard_map/all_to_all | solution.py:63
  231.0 6.2 %collective-permute-start.6 = (bf16[8,8,1280]{2,1,0:T(8,128)(2,1)S(1)}, bf16[8,8,1280]{2,1,0:T(8,128)(2,1)S(1)}, u32[]{:S(2)}, u32[]{:S(2)}) collective-permute-start(bf16[8,8,1280]{2,1,0:T(8,128)(2,1)S(1)} %all_to_all.66.own_ref), channel_id=1, source_target_pairs={{0,16},{16,0},{1,17},{17,1},{2,18},{18,2},{3,19},{19,3},{4,20},{20... | collective-permute-start | bytes 491528 | tf_op jit(solution)/shard_map/ppermute | solution.py:59
  238.3 8.9 %product_shares.1 = bf16[16,128,256]{2,1,0:T(8,128)(2,1)} custom-call(s32[4,128]{1,0:T(4,128)S(1)} %reshape.43.list_ref, f32[2,8,1,128]{3,2,1,0:T(1,128)S(1)} %get-tuple-element.44.right_ref.left_ref, f32[2,32,1,128]{3,2,1,0:T(1,128)S(1)} %reshape.55.left_ref.right_ref, bf16[8,8,1280]{2,1,0:T(8,128)(2,1)S(1)} %all_to_all.66.own_ref, ...), custom_call_target="tpu_custom_call" | custom-call | bytes 26666666 | tf_op jit(solution)/shard_map/product_shares/pallas_call | solution.py:89
  247.2 3.7 %all-to-all-start.11 = ((bf16[16,128,256]{2,1,0:T(8,128)(2,1)}), bf16[16,128,256]{2,1,0:T(8,128)(2,1)S(1)}, u32[]{:S(2)}, u32[]{:S(2)}) async-start(bf16[16,128,256]{2,1,0:T(8,128)(2,1)} %product_shares.1), calls=%async_computation.11 | async-start | bytes 2097152 | tf_op jit(solution)/shard_map/all_to_all | solution.py:63
  254.9 23.1 %all-to-all-done.11.arrived_ref = bf16[16,128,256]{2,1,0:T(8,128)(2,1)S(1)} async-done(((bf16[16,128,256]{2,1,0:T(8,128)(2,1)}), bf16[16,128,256]{2,1,0:T(8,128)(2,1)S(1)}, u32[]{:S(2)}, u32[]{:S(2)}) %all-to-all-start.11) | async-done | bytes 1048608 | tf_op jit(solution)/shard_map/all_to_all | solution.py:63
  (61 shorter events, 24.8 us)
Async XLA Ops:
  2.7 0.8 copy-start.3
  3.5 0.7 copy-start.5
  4.2 0.7 copy-start.6
  4.9 8.6 %collective-permute-start = (bf16[224,128]{1,0:T(8,128)(2,1)S(1)}, bf16[224,128]{1,0:T(8,128)(2,1)S(1)}, u32[]{:S(2)}, u32[]{:S(2)}) collective-permute-start(bf16[224,128]{1,0:T(8,128)(2,1)S(1)} %packed.1), channel_id=1, source_target_pairs={{0,0},{16,1},{32,2},{48,3},{64,4},{80,5},{96,6},{112,7},{128,8},{1... | collective-permute-start | bytes 172040 | tf_op jit(solution)/shard_map/ppermute | solution.py:44
  13.5 0.8 copy-start.4
  15.1 33.6 %all-to-all-start = ((bf16[8,272,128]{2,1,0:T(8,128)(2,1)}), bf16[8,272,128]{2,1,0:T(8,128)(2,1)S(1)}, u32[]{:S(2)}, u32[]{:S(2)}) async-start(bf16[8,272,128]{2,1,0:T(8,128)(2,1)} %get-tuple-element.38), calls=%async_computation | async-start | bytes 1114112 | tf_op jit(solution)/shard_map/all_to_all | solution.py:63
  48.7 4.0 %collective-permute-start.1 = (bf16[8,8,4096]{2,1,0:T(8,128)(2,1)S(1)}, bf16[8,8,4096]{2,1,0:T(8,128)(2,1)S(1)}, u32[]{:S(2)}, u32[]{:S(2)}) collective-permute-start(bf16[8,8,4096]{2,1,0:T(8,128)(2,1)S(1)} %get-tuple-element.40), channel_id=1, source_target_pairs={{0,16},{16,0},{1,17},{17,1},{2,18},{18,2},{3,19},{19,3},{4,20},{20... | collective-permute-start | bytes 1572872 | tf_op jit(solution)/shard_map/ppermute | solution.py:59
  78.6 7.0 %collective-permute-start.2 = (bf16[8,272,128]{2,1,0:T(8,128)(2,1)S(1)}, bf16[8,272,128]{2,1,0:T(8,128)(2,1)S(1)}, u32[]{:S(2)}, u32[]{:S(2)}) collective-permute-start(bf16[8,272,128]{2,1,0:T(8,128)(2,1)S(1)} %all-to-all-done), channel_id=1, source_target_pairs={{0,16},{16,0},{1,17},{17,1},{2,18},{18,2},{3,19},{19,3},{4,20},{20... | collective-permute-start | bytes 1671176 | tf_op jit(solution)/shard_map/ppermute | solution.py:59
  80.3 19.7 %all-to-all-start.2 = ((bf16[8,8,4224]{2,1,0:T(8,128)(2,1)}), bf16[8,8,4224]{2,1,0:T(8,128)(2,1)S(1)}, u32[]{:S(2)}, u32[]{:S(2)}) async-start(bf16[8,8,4224]{2,1,0:T(8,128)(2,1)} %residual_of.1), calls=%async_computation.2 | async-start | bytes 1081344 | tf_op jit(solution)/shard_map/all_to_all | solution.py:63
  91.5 2.0 copy-start
  100.0 2.5 collective-permute-start.3
  140.9 3.3 %collective-permute-start.4 = (bf16[8,8,1024]{2,1,0:T(8,128)(2,1)S(1)}, bf16[8,8,1024]{2,1,0:T(8,128)(2,1)S(1)}, u32[]{:S(2)}, u32[]{:S(2)}) collective-permute-start(bf16[8,8,1024]{2,1,0:T(8,128)(2,1)S(1)} %get-tuple-element.50), channel_id=1, source_target_pairs={{0,16},{16,0},{1,17},{17,1},{2,18},{18,2},{3,19},{19,3},{4,20},{20... | collective-permute-start | bytes 393224 | tf_op jit(solution)/shard_map/ppermute | solution.py:59
  144.9 14.6 %all-to-all-start.5 = ((bf16[8,8,1024]{2,1,0:T(8,128)(2,1)}), bf16[8,8,1024]{2,1,0:T(8,128)(2,1)S(1)}, u32[]{:S(2)}, u32[]{:S(2)}) async-start(bf16[8,8,1024]{2,1,0:T(8,128)(2,1)} %add_convert_fusion.1), calls=%async_computation.5 | async-start | bytes 262144 | tf_op jit(solution)/shard_map/all_to_all | solution.py:63
  150.1 6.7 %collective-permute-start.5 = (f32[8,1024]{1,0:T(8,128)S(1)}, f32[8,1024]{1,0:T(8,128)S(1)}, u32[]{:S(2)}, u32[]{:S(2)}) collective-permute-start(f32[8,1024]{1,0:T(8,128)S(1)} %get-tuple-element.51), channel_id=1, source_target_pairs={{0,0},{24,1},{32,2},{56,3},{64,4},{88,5},{96,6},{120,7},{128,8},{1... | collective-permute-start | bytes 98312 | tf_op jit(solution)/shard_map/ppermute | solution.py:55
  159.5 2.2 copy-start.1
  165.9 13.5 %all-to-all-start.6 = ((f32[16,8,128]{2,1,0:T(8,128)}), f32[16,8,128]{2,1,0:T(8,128)S(1)}, u32[]{:S(2)}, u32[]{:S(2)}) async-start(f32[16,8,128]{2,1,0:T(8,128)} %coarse_product.1), calls=%async_computation.6 | async-start | bytes 131072 | tf_op jit(solution)/shard_map/all_to_all | solution.py:63
  208.6 2.2 copy-start.2
  231.0 7.2 %collective-permute-start.6 = (bf16[8,8,1280]{2,1,0:T(8,128)(2,1)S(1)}, bf16[8,8,1280]{2,1,0:T(8,128)(2,1)S(1)}, u32[]{:S(2)}, u32[]{:S(2)}) collective-permute-start(bf16[8,8,1280]{2,1,0:T(8,128)(2,1)S(1)} %all_to_all.66.own_ref), channel_id=1, source_target_pairs={{0,16},{16,0},{1,17},{17,1},{2,18},{18,2},{3,19},{19,3},{4,20},{20... | collective-permute-start | bytes 491528 | tf_op jit(solution)/shard_map/ppermute | solution.py:59
  247.2 30.9 %all-to-all-start.11 = ((bf16[16,128,256]{2,1,0:T(8,128)(2,1)}), bf16[16,128,256]{2,1,0:T(8,128)(2,1)S(1)}, u32[]{:S(2)}, u32[]{:S(2)}) async-start(bf16[16,128,256]{2,1,0:T(8,128)(2,1)} %product_shares.1), calls=%async_computation.11 | async-start | bytes 2097152 | tf_op jit(solution)/shard_map/all_to_all | solution.py:63

commit v4 on v3

--- a/solution.py
+++ b/solution.py
@@ -9,6 +9,8 @@
 TILE = 128
 SIDE = 16
 HALF = 8
+LINE = 4
+QUARTER = 8
 BLOCK = 8
 FIELDS = SIDE * BLOCK
 GROUP = 16
@@ -19,6 +21,7 @@
 
 ROW = ("y", "zh", "k")
 YZ = ("y", "zh")
+YZL = ("y", "zh", "zl")
 COL = ("x", "zl")
 ALL = ROW + COL
 
@@ -27,6 +30,7 @@
 
 VMEM = pl.BlockSpec(memory_space=pltpu.VMEM)
 SMEM = pl.BlockSpec(memory_space=pltpu.SMEM)
+HBM = pl.BlockSpec(memory_space=pltpu.HBM)
 
 
 def room(mebibytes):
@@ -131,12 +135,12 @@
     return call(kernel, shapes, (points0, points1, lists, factor), "packed", 8, 1)
 
 
-def unpacked(there, factor, centres, fine, mid, listed):
+def unpacked(there, factor, local, fine, mid, listed):
     used = 2 * (fine + mid) + listed
     above = -(-used // SIDE) * SIDE
-    size = 2 * TILE + SIDE
-
-    def kernel(there_ref, factor_ref, centre_ref, fine_ref, mid_ref, list_ref, common_ref):
+    size = 2 * TILE + local.shape[0]
+
+    def kernel(there_ref, factor_ref, local_ref, fine_ref, mid_ref, list_ref, common_ref):
         lines = there_ref[pl.ds(0, above), :].astype(f32)
         at = 0
         for ref, tiles in ((fine_ref, fine), (mid_ref, mid)):
@@ -148,7 +152,7 @@
         for chip in range(HALF):
             common_ref[chip, pl.ds(0, TILE), :] = factor_ref[...]
             common_ref[chip, pl.ds(TILE, TILE), :] = there_ref[pl.ds(above, TILE), :]
-            common_ref[chip, pl.ds(2 * TILE, SIDE), :] = centre_ref[...]
+            common_ref[chip, pl.ds(2 * TILE, local.shape[0]), :] = local_ref[...]
 
     shapes = [
         ((2, fine, 1, TILE), f32),
@@ -156,7 +160,7 @@
         ((listed, TILE), jnp.int32),
         ((HALF, size, TILE), bf16),
     ]
-    return call(kernel, shapes, (there, factor, centres), "unpacked", 8, 1)
+    return call(kernel, shapes, (there, factor, local), "unpacked", 8, 1)
 
 
 def set_points(left_ref, right_ref, left, right, support):
@@ -222,12 +226,13 @@
     return call(kernel, [half, half], operands, "product_a0", 16, 20, scratch, 2)
 
 
-def product(lists, listed, first, contracted, left, right, halves, support, form):
+def product(lists, listed, first, contracted, left, right, halves, support, tail=None):
     tiles = right.shape[1]
     length = left.shape[1] * TILE
+    size = tiles * TILE
 
     def kernel(list_ref, left_ref, right_ref, own_ref, other_ref, *rest):
-        *outs, left, right, vector, total = rest
+        *given, left, right, vector, total = rest
         set_points(left_ref, right_ref, left, right, support)
         total[...] = jnp.zeros_like(total)
         for ref, at in ((own_ref, 0), (other_ref, FIELDS // 2)):
@@ -236,30 +241,113 @@
         add_tiles(list_ref, listed, first, contracted, left, right, vector, total, support)
         for i in range(tiles):
             low = total[i].astype(bf16)
-            if form == "shares":
-                each = tiles // SIDE
-                outs[0][i // each, :, pl.ds(i % each * TILE, TILE)] = low
-            elif form == "blocks":
-                outs[0][:, :, pl.ds(i * TILE, TILE)] = low.reshape(SIDE, BLOCK, TILE)
+            at = pl.ds(i * TILE, TILE)
+            if tail is not None:
+                given[1][:, :, at] = low.reshape(SIDE, BLOCK, TILE)
             else:
                 pair = low.reshape(2, HALF, BLOCK, TILE)
-                outs[0][:, :, pl.ds(i * TILE, TILE)] = pair[0]
-                outs[1][:, :, pl.ds(i * TILE, TILE)] = pair[1]
-
-    size = tiles * TILE
-    if form == "shares":
-        shapes = [((SIDE, FIELDS, size // SIDE), bf16)]
-    elif form == "blocks":
-        shapes = [((SIDE, BLOCK, size), bf16)]
-    else:
-        shapes = [((HALF, BLOCK, size), bf16)] * 2
+                given[0][:, :, at] = pair[0]
+                given[1][:, :, at] = pair[1]
+        if tail is not None:
+            for peer in range(SIDE):
+                given[1][peer, :, pl.ds(size, TILE)] = given[0][...]
+
     scratch = [
         *point_scratch(left.shape[1], tiles),
         pltpu.VMEM((FIELDS, length), bf16),
         pltpu.VMEM((tiles, FIELDS, TILE), f32),
     ]
     operands = (lists, left, right, *halves)
-    return call(kernel, shapes, operands, "product_" + form, 16, listed / 18, scratch, 1)
+    if tail is not None:
+        shapes = [((SIDE, BLOCK, size + TILE), bf16)]
+        operands = (*operands, tail)
+    else:
+        shapes = [((HALF, BLOCK, size), bf16)] * 2
+    return call(kernel, shapes, operands, "product", 16, listed / 18, scratch, 1)
+
+
+def quarter_of(lists, place, blocks, rows):
+    listed, tiles = rows
+    lines = rows_of(LINE * QUARTER * tiles)
+    held = rows_of(listed)
+
+    def kernel(list_ref, place_ref, out_ref):
+        zl = place_ref[3]
+
+        def put(at, i, j):
+            out_ref[at // TILE, at % TILE] = i
+            out_ref[lines + at // TILE, at % TILE] = j
+
+        count = jnp.int32(0)
+        for block in range(blocks):
+
+            def step(t, count):
+                for u in range(GROUP):
+                    e = t * GROUP + u
+                    i = list_ref[block * 2 * held + e // TILE, e % TILE]
+                    j = list_ref[block * 2 * held + held + e // TILE, e % TILE]
+                    put(count, i // (2 * LINE) * 2 + i % 2, block * tiles + j)
+                    count = count + (i // 2 % LINE == zl).astype(jnp.int32)
+                return count
+
+            count = lax.fori_loop(0, listed // GROUP, step, count)
+        for u in range(GROUP):
+            put(count + u, jnp.int32(QUARTER), jnp.int32(0))
+        out_ref[2 * lines, 0] = (count + GROUP - 1) // GROUP
+
+    lines = lines + 1
+    return pl.pallas_call(
+        kernel,
+        out_shape=jax.ShapeDtypeStruct((2 * lines + 1, TILE), jnp.int32),
+        in_specs=[SMEM, SMEM],
+        out_specs=SMEM,
+        compiler_params=room(4),
+        cost_estimate=hint(7),
+        name="quarter_of",
+    )(lists, place)
+
+
+def product_quarter(lists, left, right, own, other, support):
+    lines = (lists.shape[0] - 1) // 2
+    tiles = right.shape[1]
+    length = left.shape[1] * TILE // LINE
+    steps = TILE // GROUP
+
+    def kernel(list_ref, left_ref, right_ref, own_ref, other_ref, out_ref, left, right, vector, total):
+        set_points(left_ref, right_ref, left, right, support)
+        total[...] = jnp.zeros_like(total)
+        for ref, first in ((own_ref, 0), (other_ref, FIELDS // 2)):
+            for chip in range(HALF):
+                for zl in range(LINE):
+                    at = pl.ds(first + chip * BLOCK, BLOCK)
+                    part = ref[chip * LINE + zl, :, pl.ds(0, length)]
+                    vector[at, pl.ds(zl * length, length)] = part
+
+        def step(g, carry):
+            row, lane = g // steps, g % steps * GROUP
+            products = []
+            for u in range(GROUP):
+                i = list_ref[row, lane + u]
+                j = list_ref[lines + row, lane + u]
+                tile = wendland((left[0, j], left[1, j]), (right[0, i], right[1, i]), support)
+                product = jnp.dot(vector[:, at_tile(j)], tile, preferred_element_type=f32)
+                products.append((i, product))
+            for i, product in products:
+                total[i] += product
+            return carry
+
+        lax.fori_loop(0, list_ref[2 * lines, 0], step, 0)
+        for i in range(QUARTER):
+            out_ref[i // 2, :, pl.ds(i % 2 * TILE, TILE)] = total[i].astype(bf16)
+
+    scratch = [
+        *point_scratch(left.shape[1], tiles),
+        pltpu.VMEM((FIELDS, length * LINE), bf16),
+        pltpu.VMEM((tiles, FIELDS, TILE), f32),
+    ]
+    operands = (lists, left, right, own, other)
+    shapes = [((QUARTER // 2, FIELDS, 2 * TILE), bf16)]
+    return call(kernel, shapes, operands, "product_quarter", 20, 10, scratch, 1)
 
 
 def all_pairs(left, right, support):
@@ -314,9 +402,10 @@
 
 def mid_of(arrived, scale):
     peers, _, n = arrived.shape
+    n = n - TILE
 
     def kernel(arrived_ref, out_ref, low_ref):
-        part = scale * arrived_ref[...].astype(f32).sum(axis=0)
+        part = scale * arrived_ref[:, :, pl.ds(0, n)].astype(f32).sum(axis=0)
         out_ref[...] = part
         low = part.astype(bf16)
         for peer in range(peers):
@@ -326,35 +415,59 @@
     return call(kernel, shapes, (arrived,), "mid_of", 8, 1)
 
 
+def chunks_of(matrix_ref, held, sems):
+    chunks = sems.shape[0]
+    size = matrix_ref.shape[0] // chunks
+    rows = [pl.ds(q * size, size) for q in range(chunks)]
+    return [
+        pltpu.make_async_copy(matrix_ref.at[r], held.at[r], sems.at[q]) for q, r in enumerate(rows)
+    ]
+
+
+def call_on_matrix(kernel, shape, kind, matrix, operands, name, scratch):
+    chunks = 4
+    return pl.pallas_call(
+        kernel,
+        out_shape=jax.ShapeDtypeStruct(shape, kind),
+        in_specs=[HBM] + [VMEM] * len(operands),
+        out_specs=VMEM,
+        scratch_shapes=[
+            pltpu.VMEM(matrix.shape, bf16),
+            pltpu.SemaphoreType.DMA((chunks,)),
+            *scratch,
+        ],
+        compiler_params=room(12),
+        cost_estimate=hint(3),
+        name=name,
+    )(pltpu.with_memory_space_constraint(matrix, pltpu.HBM), *operands)
+
+
 def coarse_product(matrix, arrived, mid_data, scale):
     rows, cols = matrix.shape
 
-    def kernel(matrix_ref, arrived_ref, mid_ref, out_ref, turned_ref):
-        @pl.when(pl.program_id(0) == 0)
-        def _():
-            whole = (scale * arrived_ref[...].astype(f32).sum(axis=0)).astype(bf16).astype(f32)
-            whole = mid_ref[...] - 0.5 * whole
-            for t in range(cols // TILE):
-                lines = whole[:, t * TILE : (t + 1) * TILE]
-                full = jnp.concatenate([lines, jnp.zeros((TILE - BLOCK, TILE), f32)], axis=0)
-                turned_ref[pl.ds(t * TILE, TILE), :] = full.T.astype(bf16)
-
-        for q in range(2):
-            at = pl.ds(q * TILE, TILE)
-            part = jnp.dot(matrix_ref[at, :], turned_ref[...], preferred_element_type=f32)
-            out_ref[q] = part.T[:BLOCK, :]
-
-    return pl.pallas_call(
-        kernel,
-        out_shape=jax.ShapeDtypeStruct((rows // TILE, BLOCK, TILE), f32),
-        grid=(rows // TILE // 2,),
-        in_specs=[pl.BlockSpec((2 * TILE, cols), lambda q: (q, 0)), VMEM, VMEM],
-        out_specs=pl.BlockSpec((2, BLOCK, TILE), lambda q: (q, 0, 0)),
-        scratch_shapes=[pltpu.VMEM((cols, TILE), bf16)],
-        compiler_params=room(8),
-        cost_estimate=hint(3),
-        name="coarse_product",
-    )(matrix, arrived, mid_data)
+    def kernel(matrix_ref, arrived_ref, mid_ref, out_ref, held, sems, turned_ref):
+        copies = chunks_of(matrix_ref, held, sems)
+        for copy in copies:
+            copy.start()
+        whole = (scale * arrived_ref[...].astype(f32).sum(axis=0)).astype(bf16).astype(f32)
+        whole = mid_ref[...] - 0.5 * whole
+        for t in range(cols // TILE):
+            lines = whole[:, t * TILE : (t + 1) * TILE]
+            full = jnp.concatenate([lines, jnp.zeros((TILE - BLOCK, TILE), f32)], axis=0)
+            turned_ref[pl.ds(t * TILE, TILE), :] = full.T.astype(bf16)
+        each = rows // TILE // len(copies)
+        for c, copy in enumerate(copies):
+            copy.wait()
+            for q in range(c * each, (c + 1) * each):
+                part = jnp.dot(
+                    held[pl.ds(q * TILE, TILE), :], turned_ref[...], preferred_element_type=f32
+                )
+                out_ref[q] = part.T[:BLOCK, :]
+
+    shape = (rows // TILE, BLOCK, TILE)
+    scratch = [pltpu.VMEM((cols, TILE), bf16)]
+    operands = (arrived, mid_data)
+    return call_on_matrix(kernel, shape, f32, matrix, operands, "coarse_product", scratch)
 
 
 def coarse_data_of(arrived, own, other, scale):
@@ -410,43 +523,35 @@
     return call(kernel, shapes, (halfway, factor_across), "coarse_coef_of", 8, 1)
 
 
-def prolong(matrix, coarse_coef, mid_data, scale):
+def prolong(matrix, coarse_coef, place, mid_data, scale):
     rows, cols = matrix.shape
     two = 2 * TILE
-    steps = rows // two
-
-    def kernel(matrix_ref, coef_ref, mid_ref, out_ref, total):
-        q = pl.program_id(0)
-
-        @pl.when(q == 0)
-        def _():
-            total[...] = jnp.zeros_like(total)
-
-        pair = jnp.concatenate([coef_ref[0], coef_ref[1]], axis=1).astype(bf16)
-        out_ref[q, :, pl.ds(cols, two)] = pair
-        total[...] += jnp.dot(pair, matrix_ref[...], preferred_element_type=f32)
-
-        @pl.when(q == steps - 1)
-        def _():
-            low = (0.5 * mid_ref[...] + scale * total[...]).astype(bf16)
-            for chip in range(steps):
-                out_ref[chip, :, pl.ds(0, cols)] = low
-
-    return pl.pallas_call(
-        kernel,
-        out_shape=jax.ShapeDtypeStruct((steps, BLOCK, cols + two), bf16),
-        grid=(steps,),
-        in_specs=[
-            pl.BlockSpec((two, cols), lambda q: (q, 0)),
-            pl.BlockSpec((2, BLOCK, TILE), lambda q: (q, 0, 0)),
-            VMEM,
-        ],
-        out_specs=VMEM,
-        scratch_shapes=[pltpu.VMEM((BLOCK, cols), f32)],
-        compiler_params=room(8),
-        cost_estimate=hint(3),
-        name="prolong",
-    )(matrix, coarse_coef, mid_data)
+
+    def kernel(matrix_ref, coef_ref, low_ref, mid_ref, out_ref, held, sems):
+        copies = chunks_of(matrix_ref, held, sems)
+        for copy in copies:
+            copy.start()
+        for chip in range(HALF):
+            for zl in range(LINE):
+                out_ref[chip * LINE + zl, :, pl.ds(cols, TILE)] = low_ref[chip]
+        total = jnp.zeros((BLOCK, cols), f32)
+        each = rows // two // len(copies)
+        for c, copy in enumerate(copies):
+            copy.wait()
+            for q in range(c * each, (c + 1) * each):
+                pair = jnp.concatenate([coef_ref[2 * q], coef_ref[2 * q + 1]], axis=1)
+                total += jnp.dot(
+                    pair.astype(bf16), held[pl.ds(q * two, two), :], preferred_element_type=f32
+                )
+        low = (0.5 * mid_ref[...] + scale * total).astype(bf16)
+        for chip in range(HALF * LINE):
+            out_ref[chip, :, pl.ds(0, cols)] = low
+
+    sent = coarse_coef.reshape(HALF, 2, BLOCK, TILE).astype(bf16)
+    sent = jnp.where(place[3] % 2 == 0, sent[:, 0], sent[:, 1])
+    shape = (HALF * LINE, BLOCK, cols + TILE)
+    operands = (coarse_coef, sent, mid_data)
+    return call_on_matrix(kernel, shape, bf16, matrix, operands, "prolong", ())
 
 
 def fine_of(arrived, data, core, scale):
@@ -500,15 +605,18 @@
     own_e1 = in_rows(list_e1)
     lists = jnp.concatenate([in_rows(list_a0), own_e1, in_rows(list_a1)], axis=0)
     there = turned(packed(points0, points1, lists, factor))
-    centres = jnp.pad(points2, ((0, 2 * BLOCK - 2), (0, 0)))
-    place = jnp.stack([core, row_id, col_id]).astype(jnp.int32)
+    local = [points2, jnp.zeros((SIDE - 2, TILE), bf16), points1.reshape(2 * tiles_mid, TILE)]
+    local = jnp.concatenate(local, axis=0)
+    x_id, zl_id = lax.axis_index("x"), lax.axis_index("zl")
+    place = jnp.stack([core, row_id, col_id, zl_id]).astype(jnp.int32)
     fine_here = points0.astype(f32).reshape(2, tiles_fine, 1, TILE)
     mid_here = points1.astype(f32).reshape(2, tiles_mid, 1, TILE)
-    there, vector, centres, fine_here, mid_here = lax.optimization_barrier(
-        (there, values.T, centres, fine_here, mid_here)
+    tail = jnp.pad(own_e1, ((0, BLOCK - own_e1.shape[0]), (0, 0))).astype(bf16)
+    there, vector, local, fine_here, mid_here, tail = lax.optimization_barrier(
+        (there, values.T, local, fine_here, mid_here, tail)
     )
     fine_there, mid_there, lists, common = unpacked(
-        there, factor, centres, tiles_fine, tiles_mid, lists.shape[0]
+        there, factor, local, tiles_fine, tiles_mid, lists.shape[0]
     )
     first_e1 = 2 * rows_of(listed_a0)
     first_a1 = first_e1 + 2 * rows_of(listed_e1)
@@ -518,8 +626,8 @@
     own, other, common = lax.optimization_barrier((own, other, common))
     arrived = exchanged(pair_sum(own, other), YZ)
 
-    fine_all, common, mid_later = lax.optimization_barrier(
-        (residual_of(arrived, -0.5 * scale_a0), common, mid_there)
+    fine_all, common, mid_later, fine_later = lax.optimization_barrier(
+        (residual_of(arrived, -0.5 * scale_a0), common, mid_there, fine_here)
     )
     partner = from_partner(common)
 
@@ -529,24 +637,39 @@
 
     factor_down = in_row_order(0, rows_coarse).reshape(coarse, -1)
     factor_across = in_row_order(rows_coarse, rows_coarse).reshape(SIDE, rows_coarse, -1)
-    centres = in_row_order(2 * rows_coarse, 2 * BLOCK).reshape(SIDE, 2 * BLOCK, -1)[:, :2]
+    centres = in_row_order(2 * rows_coarse, SIDE).reshape(SIDE, SIDE, -1)[:, :2]
     centres = centres.astype(f32).transpose(1, 0, 2)[:, :, None]
+    mid_line = in_row_order(2 * rows_coarse + SIDE, 2 * tiles_mid)
+    mid_line = mid_line.reshape(SIDE, 2, tiles_mid, 1, TILE)
+    mid_line = lax.dynamic_slice_in_dim(mid_line, x_id * LINE, LINE, 0).astype(f32)
+    mid_line = mid_line.transpose(1, 0, 2, 3, 4).reshape(2, LINE * tiles_mid, 1, TILE)
+    fine_quarter = fine_later.reshape(2, QUARTER // 2, LINE, 2, 1, TILE)
+    fine_quarter = lax.dynamic_index_in_dim(fine_quarter, zl_id, 2, keepdims=False)
+    fine_quarter = fine_quarter.reshape(2, QUARTER, 1, TILE)
+    fine_quarter = jnp.pad(fine_quarter, ((0, 0), (0, 1), (0, 0), (0, 0)), constant_values=8.0)
     coarse_kernel = all_pairs(centres, mid_later, support_coarse)
-    fine_own, coarse_kernel, factor_down, factor_across = lax.optimization_barrier(
-        (exchanged(fine_all, YZ), coarse_kernel, factor_down, factor_across)
+    fine_own, coarse_kernel, factor_down, factor_across, mid_line, fine_quarter = (
+        lax.optimization_barrier(
+            (exchanged(fine_all, YZ), coarse_kernel, factor_down, factor_across, mid_line, fine_quarter)
+        )
     )
     fine_other = from_partner(fine_own)
 
     restricted = product(
-        lists, listed_e1, first_e1, 0, fine_there, mid_here, (fine_own, fine_other), support_mid, "blocks"
-    )
-    mid_share, mid_all = mid_of(exchanged(restricted, COL), scale_e1)
-    mid_all = exchanged(mid_all, COL)
-    mid_data = turned_blocks(mid_share)
+        lists, listed_e1, first_e1, 0, fine_there, mid_here, (fine_own, fine_other), support_mid, tail
+    )
+    restricted = exchanged(restricted, COL)
+    mid_share, mid_all = mid_of(restricted, scale_e1)
+    line_lists = lax.dynamic_slice_in_dim(restricted[:, :, rows_mid:], x_id * LINE, LINE, 0)
+    line_lists = line_lists[:, : own_e1.shape[0]].reshape(-1, TILE).astype(jnp.int32)
+    line_lists = quarter_of(line_lists, place, LINE, (listed_e1, tiles_mid))
+    mid_all, mid_data, line_lists = lax.optimization_barrier(
+        (exchanged(mid_all, COL), turned_blocks(mid_share), line_lists)
+    )
 
     mid_halves = (mid_all[:HALF], mid_all[HALF:])
     mid_own, mid_other = product(
-        lists, listed_a1, first_a1, 1, mid_here, mid_there, mid_halves, support_mid, "halves"
+        lists, listed_a1, first_a1, 1, mid_here, mid_there, mid_halves, support_mid
     )
     arrived = exchanged(pair_sum(mid_own, mid_other), YZ)
 
@@ -556,18 +679,22 @@
     halfway = exchanged(halfway_of(coarse_data, factor_down), COL)
     coarse_all = exchanged(coarse_coef_of(halfway, factor_across), COL)
 
-    new_own = exchanged(prolong(coarse_kernel, coarse_all, mid_data, scale_e2), YZ)
+    new_own = exchanged(prolong(coarse_kernel, coarse_all, place, mid_data, scale_e2), YZL)
     new_other = from_partner(new_own)
-    fine_part = product(
-        own_e1, listed_e1, 0, 1, mid_there, fine_here, (new_own, new_other), support_mid, "shares"
+    fine_part = product_quarter(
+        line_lists, mid_line, fine_quarter, new_own, new_other, support_mid
     )
     own_data = lax.dynamic_slice_in_dim(values, col_id * share, share, 0)
-    fine_coef = fine_of(exchanged(fine_part, COL), own_data, place, scale_e1)
-
-    both = jnp.stack([new_own, new_other]).astype(f32)
-    mid_coef = in_field_order(both[..., :rows_mid], core)
-    coarse_coef = lax.dynamic_slice_in_dim(both, rows_mid + core * rows_coarse, rows_coarse, 3)
-    coarse_coef = in_field_order(coarse_coef, core)
+    fine_coef = fine_of(exchanged(fine_part, "x"), own_data, place, scale_e1)
+
+    def from_line(zl, at, size):
+        both = jnp.stack([new_own, new_other])[..., at : at + size]
+        both = both.reshape(2, HALF, LINE, BLOCK, size)
+        both = lax.dynamic_index_in_dim(both, zl, 2, keepdims=False)
+        return in_field_order(both.astype(f32), core)
+
+    mid_coef = from_line(zl_id, 0, rows_mid)
+    coarse_coef = from_line(core, rows_mid, rows_coarse)
     norm = coarse_data[:, 1].astype(f32).sum() / (rows_fine * SIDE * fields)
     return (fine_coef, mid_coef, coarse_coef, jnp.stack([norm]))
 

time: 282 us -> 275 us (0.975)
  Pallas kernels: 53.4 us -> 75.4 us
  waiting for transfers between devices: 49.3 us -> 30.6 us
  local copies, waits for them, and re-layouts: 17.1 us -> 12 us
  blocking collectives: 99.3 us -> 95.7 us
    pallas_call x2 -> x3, Pallas kernels: 5.69 us -> 25.5 us  [the longest x1 19.3 us: quarter_of(): pl.pallas_call(kernel, out_shape=jax.ShapeDtypeStruct((2 * lines + 1, TIL...]
    all_to_all x5 -> x6, waiting for transfers between devices: 39.3 us -> 26.1 us  [exchanged(): return lax.all_to_all(x, axes, split_axis=0, concat_axis=0, tiled=True)]
    unnamed x17 -> x13, local copies, waits for them, and re-layouts: 12.5 us -> 7.32 us
    ppermute x1, waiting for transfers between devices: 4.81 us -> 0.01 us  [turned_blocks(): return lax.ppermute(x, ALL, pairs)]
    all_to_all x7 -> x6, blocking collectives: 99.3 us -> 95.7 us  [exchanged(): return lax.all_to_all(x, axes, split_axis=0, concat_axis=0, tiled=True)]
    all_to_all x5 -> x6, starting transfers between devices: 35.8 us -> 34.3 us  [exchanged(): return lax.all_to_all(x, axes, split_axis=0, concat_axis=0, tiled=True)]
  transfers between devices with their start and end apart: 12 -> 13, of which waited for: 9 -> 7; matrix products, arithmetic and copies ran while one was open for 3% -> 3% of each run, Pallas kernels for 8% -> 16%
where the time goes in v4:
time: 275 us; the launch traced here: 274 us
  blocking collectives  95.7 us (35%)
  Pallas kernels  75.4 us (27%)
  starting transfers between devices  54.8 us (20%)
  waiting for transfers between devices  30.6 us (11%)
  local copies, waits for them, and re-layouts  12 us (4%)
  between operations  2.85 us (1%)
    all_to_all x6, blocking collectives, exchanged(): return lax.all_to_all(x, axes, split_axis=0, concat_axis=0, tiled=True)  95.7 us
    pallas_call x12, Pallas kernels, call(): pl.pallas_call(kernel, out_shape=[jax.ShapeDtypeStruct(shape, kind) for s...  44.4 us
    all_to_all x6, starting transfers between devices, exchanged(): return lax.all_to_all(x, axes, split_axis=0, concat_axis=0, tiled=True)  34.3 us
    all_to_all x6, waiting for transfers between devices, exchanged(): return lax.all_to_all(x, axes, split_axis=0, concat_axis=0, tiled=True)  26.1 us
    pallas_call x1, Pallas kernels, quarter_of(): pl.pallas_call(kernel, out_shape=jax.ShapeDtypeStruct((2 * lines + 1, TIL...  19.3 us
    ppermute x5, starting transfers between devices, from_partner(): return lax.ppermute(x, 'k', [(0, 1), (1, 0)])  12.3 us
    unnamed x13, local copies, waits for them, and re-layouts  7.32 us
    pallas_call x2, Pallas kernels, call_on_matrix(): pl.pallas_call(kernel, out_shape=jax.ShapeDtypeStruct(shape, kind), in_sp...  6.22 us
  transfers between devices with their start and end apart: 13, of which 7 were waited for; matrix products, arithmetic and copies ran while one was open for 3% of the time, Pallas kernels for 16%

profile of v4, /device:TPU:1, one launch (start us, length us, event | category | flops | bytes accessed | tf_op | source)
XLA Modules:
  0.0 274.1 jit_solution(12543916097496436669)
XLA Ops:
  4.9 4.9 %collective-permute-start = (bf16[224,128]{1,0:T(8,128)(2,1)S(1)}, bf16[224,128]{1,0:T(8,128)(2,1)S(1)}, u32[]{:S(2)}, u32[]{:S(2)}) collective-permute-start(bf16[224,128]{1,0:T(8,128)(2,1)S(1)} %packed.1), channel_id=1, source_target_pairs={{0,0},{16,1},{32,2},{48,3},{64,4},{80,5},{96,6},{112,7},{128,8},{1... | collective-permute-start | bytes 172040 | tf_op jit(solution)/shard_map/ppermute | solution.py:48
  15.3 14.3 %all-to-all-start = ((bf16[8,288,128]{2,1,0:T(8,128)(2,1)}), bf16[8,288,128]{2,1,0:T(8,128)(2,1)S(1)}, u32[]{:S(2)}, u32[]{:S(2)}) async-start(bf16[8,288,128]{2,1,0:T(8,128)(2,1)} %get-tuple-element.45), calls=%async_computation | async-start | bytes 1179648 | tf_op jit(solution)/shard_map/all_to_all | solution.py:67
  29.6 18.3 %product_a0.1 = (bf16[8,8,4096]{2,1,0:T(8,128)(2,1)S(1)}, bf16[8,8,4096]{2,1,0:T(8,128)(2,1)S(1)}) custom-call(s32[12,128]{1,0:T(8,128)S(1)} %get-tuple-element.38.list_ref, s32[4]{0:T(128)S(1)} %pad_add_fusion.1.place_ref.core_ref, f32[2,32,1,128]{3,2,1,0:T(1,128)S(1)} %reshape.99.left_ref, f32[2,32,1,128]{3,2,1,0:T(1,128)S(1)} %get-tuple-element.39.right_ref.left_ref, ...), custom_call_target="tpu_custom_call" | custom-call | bytes 60000000 | tf_op jit(solution)/shard_map/product_a0/pallas_call | solution.py:93
  48.0 2.5 collective-permute-start.1
  50.4 1.5 collective-permute-done.1
  52.1 24.8 %all_to_all.60.arrived_ref = bf16[8,8,4096]{2,1,0:T(8,128)(2,1)S(1)} all-to-all(bf16[8,8,4096]{2,1,0:T(8,128)(2,1)S(1)} %add_convert_fusion), channel_id=1, replica_groups=mesh['y'=4,'zh'=2,'k'=2,'x'=4,'zl'=4] {'y','zh'}, dimensions={0} | all-to-all | bytes 1048576 | tf_op jit(solution)/shard_map/all_to_all | solution.py:67
  77.8 1.7 collective-permute-start.2
  79.6 5.3 %all-to-all-start.2 = ((bf16[8,8,4224]{2,1,0:T(8,128)(2,1)}), bf16[8,8,4224]{2,1,0:T(8,128)(2,1)S(1)}, u32[]{:S(2)}, u32[]{:S(2)}) async-start(bf16[8,8,4224]{2,1,0:T(8,128)(2,1)} %residual_of.1), calls=%async_computation.2 | async-start | bytes 1081344 | tf_op jit(solution)/shard_map/all_to_all | solution.py:67
  85.3 5.5 %all_pairs.1.matrix_ref = bf16[2048,1024]{1,0:T(8,128)(2,1)S(1)} custom-call(f32[2,16,1,128]{3,2,1,0:T(1,128)S(1)} %bitcast.82, f32[2,8,1,128]{3,2,1,0:T(1,128)S(1)} %get-tuple-element.52.right_ref), custom_call_target="tpu_custom_call" | custom-call | bytes 18000000 | tf_op jit(solution)/shard_map/all_pairs/pallas_call | solution.py:364
  90.8 1.9 copy-done
  92.8 6.5 %all-to-all-done.2.own_ref = bf16[8,8,4224]{2,1,0:T(8,128)(2,1)S(1)} async-done(((bf16[8,8,4224]{2,1,0:T(8,128)(2,1)}), bf16[8,8,4224]{2,1,0:T(8,128)(2,1)S(1)}, u32[]{:S(2)}, u32[]{:S(2)}) %all-to-all-start.2) | async-done | bytes 540704 | tf_op jit(solution)/shard_map/all_to_all | solution.py:67
  100.3 1.6 collective-permute-done.3.other_ref
  101.8 8.6 %product.2 = bf16[16,8,1152]{2,1,0:T(8,128)(2,1)S(1)} custom-call(s32[12,128]{1,0:T(8,128)S(1)} %get-tuple-element.38.list_ref, f32[2,32,1,128]{3,2,1,0:T(1,128)S(1)} %get-tuple-element.39.right_ref.left_ref, f32[2,8,1,128]{3,2,1,0:T(1,128)S(1)} %reshape.101.right_ref.left_ref, bf16[8,8,4224]{2,1,0:T(8,128)(2,1)S(1)} %all-to-all-done.2.own_ref, ...), custom_call_target="tpu_custom_call" | custom-call | bytes 26666666 | tf_op jit(solution)/shard_map/product/pallas_call | solution.py:93
  110.4 14.6 %all_to_all.61.arrived_ref = bf16[16,8,1152]{2,1,0:T(8,128)(2,1)S(1)} all-to-all(bf16[16,8,1152]{2,1,0:T(8,128)(2,1)S(1)} %product.2), channel_id=1, replica_groups=mesh['y'=4,'zh'=2,'k'=2,'x'=4,'zl'=4] {'x','zl'}, dimensions={0} | all-to-all | bytes 589824 | tf_op jit(solution)/shard_map/all_to_all | solution.py:67
  125.8 3.9 %all-to-all-start.4 = ((bf16[16,8,1024]{2,1,0:T(8,128)(2,1)}), bf16[16,8,1024]{2,1,0:T(8,128)(2,1)S(1)}, u32[]{:S(2)}, u32[]{:S(2)}) async-start(bf16[16,8,1024]{2,1,0:T(8,128)(2,1)} %get-tuple-element.56), calls=%async_computation.4 | async-start | bytes 524288 | tf_op jit(solution)/shard_map/all_to_all | solution.py:67
  129.7 3.3 %collective-permute-start.4 = (f32[8,1024]{1,0:T(8,128)S(1)}, f32[8,1024]{1,0:T(8,128)S(1)}, u32[]{:S(2)}, u32[]{:S(2)}) collective-permute-start(f32[8,1024]{1,0:T(8,128)S(1)} %get-tuple-element.57), channel_id=1, source_target_pairs={{0,0},{24,1},{32,2},{56,3},{64,4},{88,5},{96,6},{120,7},{128,8},{1... | collective-permute-start | bytes 98312 | tf_op jit(solution)/shard_map/ppermute | solution.py:59
  133.0 19.3 %quarter_of.1.list_ref = s32[7,128]{1,0:T(8,128)S(1)} custom-call(s32[16,128]{1,0:T(8,128)S(1)} %convert.16.list_ref, s32[4]{0:T(128)S(1)} %pad_add_fusion.1.place_ref.core_ref), custom_call_target="tpu_custom_call" | custom-call | bytes 21000000 | tf_op jit(solution)/shard_map/quarter_of/pallas_call | solution.py:299
  152.3 2.4 product.3
  156.2 21.5 %all_to_all.62.arrived_ref = bf16[8,8,1024]{2,1,0:T(8,128)(2,1)S(1)} all-to-all(bf16[8,8,1024]{2,1,0:T(8,128)(2,1)S(1)} %add_convert_fusion.1), channel_id=1, replica_groups=mesh['y'=4,'zh'=2,'k'=2,'x'=4,'zl'=4] {'y','zh'}, dimensions={0} | all-to-all | bytes 262144 | tf_op jit(solution)/shard_map/all_to_all | solution.py:67
  177.7 3.7 %coarse_product.1 = f32[16,8,128]{2,1,0:T(8,128)} custom-call(bf16[2048,1024]{1,0:T(8,128)(2,1)} %copy-done, bf16[8,8,1024]{2,1,0:T(8,128)(2,1)S(1)} %all_to_all.62.arrived_ref, f32[8,1024]{1,0:T(8,128)S(1)} %collective-permute-done.4.mid_ref), custom_call_target="tpu_custom_call" | custom-call | bytes 9000000 | tf_op jit(solution)/shard_map/coarse_product/pallas_call | solution.py:429
  181.4 4.0 %all-to-all-start.6 = ((f32[16,8,128]{2,1,0:T(8,128)}), f32[16,8,128]{2,1,0:T(8,128)S(1)}, u32[]{:S(2)}, u32[]{:S(2)}) async-start(f32[16,8,128]{2,1,0:T(8,128)} %coarse_product.1), calls=%async_computation.6 | async-start | bytes 131072 | tf_op jit(solution)/shard_map/all_to_all | solution.py:67
  185.5 7.0 %all-to-all-done.6.arrived_ref = f32[16,8,128]{2,1,0:T(8,128)S(1)} async-done(((f32[16,8,128]{2,1,0:T(8,128)}), f32[16,8,128]{2,1,0:T(8,128)S(1)}, u32[]{:S(2)}, u32[]{:S(2)}) %all-to-all-start.6) | async-done | bytes 65568 | tf_op jit(solution)/shard_map/all_to_all | solution.py:67
  192.5 9.5 %all_to_all.63.data_ref = bf16[16,2,8,128]{3,2,1,0:T(8,128)(2,1)S(1)} all-to-all(bf16[16,2,8,128]{3,2,1,0:T(8,128)(2,1)S(1)} %coarse_data_of.1), channel_id=1, replica_groups=mesh['y'=4,'zh'=2,'k'=2,'x'=4,'zl'=4] {'x','zl'}, dimensions={0} | all-to-all | bytes 131072 | tf_op jit(solution)/shard_map/all_to_all | solution.py:67
  202.2 9.4 %all_to_all.64.half_ref = bf16[16,8,128]{2,1,0:T(8,128)(2,1)S(1)} all-to-all(bf16[16,8,128]{2,1,0:T(8,128)(2,1)S(1)} %halfway_of.1), channel_id=1, replica_groups=mesh['y'=4,'zh'=2,'k'=2,'x'=4,'zl'=4] {'x','zl'}, dimensions={0} | all-to-all | bytes 65536 | tf_op jit(solution)/shard_map/all_to_all | solution.py:67
  212.6 3.5 %all-to-all-start.9 = ((f32[16,8,128]{2,1,0:T(8,128)}), f32[16,8,128]{2,1,0:T(8,128)S(1)}, u32[]{:S(2)}, u32[]{:S(2)}) async-start(f32[16,8,128]{2,1,0:T(8,128)} %coarse_coef_of.1), calls=%async_computation.9 | async-start | bytes 131072 | tf_op jit(solution)/shard_map/all_to_all | solution.py:67
  216.1 6.9 %all-to-all-done.9.coef_ref = f32[16,8,128]{2,1,0:T(8,128)S(1)} async-done(((f32[16,8,128]{2,1,0:T(8,128)}), f32[16,8,128]{2,1,0:T(8,128)S(1)}, u32[]{:S(2)}, u32[]{:S(2)}) %all-to-all-start.9) | async-done | bytes 65568 | tf_op jit(solution)/shard_map/all_to_all | solution.py:67
  223.1 2.5 prolong.1
  225.6 15.8 %all_to_all.65.own_ref = bf16[32,8,1152]{2,1,0:T(8,128)(2,1)S(1)} all-to-all(bf16[32,8,1152]{2,1,0:T(8,128)(2,1)S(1)} %prolong.1), channel_id=1, replica_groups=mesh['y'=4,'zh'=2,'k'=2,'x'=4,'zl'=4] {'y','zh','zl'}, dimensions={0} | all-to-all | bytes 1179648 | tf_op jit(solution)/shard_map/all_to_all | solution.py:67
  241.4 7.1 %collective-permute-start.6 = (bf16[32,8,1152]{2,1,0:T(8,128)(2,1)S(1)}, bf16[32,8,1152]{2,1,0:T(8,128)(2,1)S(1)}, u32[]{:S(2)}, u32[]{:S(2)}) collective-permute-start(bf16[32,8,1152]{2,1,0:T(8,128)(2,1)S(1)} %all_to_all.65.own_ref), channel_id=1, source_target_pairs={{0,16},{16,0},{1,17},{17,1},{2,18},{18,2},{3,19},{19,3},{4,20},{20... | collective-permute-start | bytes 1769480 | tf_op jit(solution)/shard_map/ppermute | solution.py:63
  251.5 9.9 %product_quarter.1 = bf16[4,128,256]{2,1,0:T(8,128)(2,1)} custom-call(s32[7,128]{1,0:T(8,128)S(1)} %quarter_of.1.list_ref, f32[2,32,1,128]{3,2,1,0:T(1,128)S(1)} %bitcast.81, f32[2,9,1,128]{3,2,1,0:T(1,128)S(1)} %pad.20.right_ref, bf16[32,8,1152]{2,1,0:T(8,128)(2,1)S(1)} %all_to_all.65.own_ref, bf16[32,8,1152]{2,1,0:T(8,128)(2,1)S(1)} %collective-permute-done.6.other_ref), custom_call_target="tpu_custom_call" | custom-call | bytes 30000000 | tf_op jit(solution)/shard_map/product_quarter/pallas_call | solution.py:93
  261.4 3.4 %all-to-all-start.11 = ((bf16[4,128,256]{2,1,0:T(8,128)(2,1)}), bf16[4,128,256]{2,1,0:T(8,128)(2,1)S(1)}, u32[]{:S(2)}, u32[]{:S(2)}) async-start(bf16[4,128,256]{2,1,0:T(8,128)(2,1)} %product_quarter.1), calls=%async_computation.11 | async-start | bytes 524288 | tf_op jit(solution)/shard_map/all_to_all | solution.py:67
  265.9 5.7 %all-to-all-done.11.arrived_ref = bf16[4,128,256]{2,1,0:T(8,128)(2,1)S(1)} async-done(((bf16[4,128,256]{2,1,0:T(8,128)(2,1)}), bf16[4,128,256]{2,1,0:T(8,128)(2,1)S(1)}, u32[]{:S(2)}, u32[]{:S(2)}) %all-to-all-start.11) | async-done | bytes 262176 | tf_op jit(solution)/shard_map/all_to_all | solution.py:67
  (73 shorter events, 20.4 us)
Async XLA Ops:
  0.6 13.7 %copy-start.2 = (bf16[128,128]{1,0:T(8,128)(2,1)S(1)}, bf16[128,128]{1,0:T(8,128)(2,1)}, u32[]{:S(2)}) copy-start(bf16[128,128]{1,0:T(8,128)(2,1)} %factor_ref.3) | copy-start | bytes 98308
  2.7 0.8 copy-start.1
  3.5 0.7 copy-start.3
  4.2 0.7 copy-start.4
  4.9 9.4 %collective-permute-start = (bf16[224,128]{1,0:T(8,128)(2,1)S(1)}, bf16[224,128]{1,0:T(8,128)(2,1)S(1)}, u32[]{:S(2)}, u32[]{:S(2)}) collective-permute-start(bf16[224,128]{1,0:T(8,128)(2,1)S(1)} %packed.1), channel_id=1, source_target_pairs={{0,0},{16,1},{32,2},{48,3},{64,4},{80,5},{96,6},{112,7},{128,8},{1... | collective-permute-start | bytes 172040 | tf_op jit(solution)/shard_map/ppermute | solution.py:48
  15.3 32.7 %all-to-all-start = ((bf16[8,288,128]{2,1,0:T(8,128)(2,1)}), bf16[8,288,128]{2,1,0:T(8,128)(2,1)S(1)}, u32[]{:S(2)}, u32[]{:S(2)}) async-start(bf16[8,288,128]{2,1,0:T(8,128)(2,1)} %get-tuple-element.45), calls=%async_computation | async-start | bytes 1179648 | tf_op jit(solution)/shard_map/all_to_all | solution.py:67
  48.0 4.0 %collective-permute-start.1 = (bf16[8,8,4096]{2,1,0:T(8,128)(2,1)S(1)}, bf16[8,8,4096]{2,1,0:T(8,128)(2,1)S(1)}, u32[]{:S(2)}, u32[]{:S(2)}) collective-permute-start(bf16[8,8,4096]{2,1,0:T(8,128)(2,1)S(1)} %get-tuple-element.47), channel_id=1, source_target_pairs={{0,16},{16,0},{1,17},{17,1},{2,18},{18,2},{3,19},{19,3},{4,20},{20... | collective-permute-start | bytes 1572872 | tf_op jit(solution)/shard_map/ppermute | solution.py:63
  77.8 7.0 %collective-permute-start.2 = (bf16[8,288,128]{2,1,0:T(8,128)(2,1)S(1)}, bf16[8,288,128]{2,1,0:T(8,128)(2,1)S(1)}, u32[]{:S(2)}, u32[]{:S(2)}) collective-permute-start(bf16[8,288,128]{2,1,0:T(8,128)(2,1)S(1)} %all-to-all-done), channel_id=1, source_target_pairs={{0,16},{16,0},{1,17},{17,1},{2,18},{18,2},{3,19},{19,3},{4,20},{20... | collective-permute-start | bytes 1769480 | tf_op jit(solution)/shard_map/ppermute | solution.py:63
  79.6 19.8 %all-to-all-start.2 = ((bf16[8,8,4224]{2,1,0:T(8,128)(2,1)}), bf16[8,8,4224]{2,1,0:T(8,128)(2,1)S(1)}, u32[]{:S(2)}, u32[]{:S(2)}) async-start(bf16[8,8,4224]{2,1,0:T(8,128)(2,1)} %residual_of.1), calls=%async_computation.2 | async-start | bytes 1081344 | tf_op jit(solution)/shard_map/all_to_all | solution.py:67
  90.8 2.0 copy-start
  99.3 2.5 collective-permute-start.3
  125.8 26.5 %all-to-all-start.4 = ((bf16[16,8,1024]{2,1,0:T(8,128)(2,1)}), bf16[16,8,1024]{2,1,0:T(8,128)(2,1)S(1)}, u32[]{:S(2)}, u32[]{:S(2)}) async-start(bf16[16,8,1024]{2,1,0:T(8,128)(2,1)} %get-tuple-element.56), calls=%async_computation.4 | async-start | bytes 524288 | tf_op jit(solution)/shard_map/all_to_all | solution.py:67
  129.7 22.6 %collective-permute-start.4 = (f32[8,1024]{1,0:T(8,128)S(1)}, f32[8,1024]{1,0:T(8,128)S(1)}, u32[]{:S(2)}, u32[]{:S(2)}) collective-permute-start(f32[8,1024]{1,0:T(8,128)S(1)} %get-tuple-element.57), channel_id=1, source_target_pairs={{0,0},{24,1},{32,2},{56,3},{64,4},{88,5},{96,6},{120,7},{128,8},{1... | collective-permute-start | bytes 98312 | tf_op jit(solution)/shard_map/ppermute | solution.py:59
  154.8 1.4 collective-permute-start.5
  181.4 11.0 %all-to-all-start.6 = ((f32[16,8,128]{2,1,0:T(8,128)}), f32[16,8,128]{2,1,0:T(8,128)S(1)}, u32[]{:S(2)}, u32[]{:S(2)}) async-start(f32[16,8,128]{2,1,0:T(8,128)} %coarse_product.1), calls=%async_computation.6 | async-start | bytes 131072 | tf_op jit(solution)/shard_map/all_to_all | solution.py:67
  212.6 10.4 %all-to-all-start.9 = ((f32[16,8,128]{2,1,0:T(8,128)}), f32[16,8,128]{2,1,0:T(8,128)S(1)}, u32[]{:S(2)}, u32[]{:S(2)}) async-start(f32[16,8,128]{2,1,0:T(8,128)} %coarse_coef_of.1), calls=%async_computation.9 | async-start | bytes 131072 | tf_op jit(solution)/shard_map/all_to_all | solution.py:67
  241.4 9.2 %collective-permute-start.6 = (bf16[32,8,1152]{2,1,0:T(8,128)(2,1)S(1)}, bf16[32,8,1152]{2,1,0:T(8,128)(2,1)S(1)}, u32[]{:S(2)}, u32[]{:S(2)}) collective-permute-start(bf16[32,8,1152]{2,1,0:T(8,128)(2,1)S(1)} %all_to_all.65.own_ref), channel_id=1, source_target_pairs={{0,16},{16,0},{1,17},{17,1},{2,18},{18,2},{3,19},{19,3},{4,20},{20... | collective-permute-start | bytes 1769480 | tf_op jit(solution)/shard_map/ppermute | solution.py:63
  261.4 10.2 %all-to-all-start.11 = ((bf16[4,128,256]{2,1,0:T(8,128)(2,1)}), bf16[4,128,256]{2,1,0:T(8,128)(2,1)S(1)}, u32[]{:S(2)}, u32[]{:S(2)}) async-start(bf16[4,128,256]{2,1,0:T(8,128)(2,1)} %product_quarter.1), calls=%async_computation.11 | async-start | bytes 524288 | tf_op jit(solution)/shard_map/all_to_all | solution.py:67

commit v5 on v4

--- a/solution.py
+++ b/solution.py
@@ -115,24 +115,27 @@
 
 def packed(points0, points1, lists, factor):
     fine, mid = points0.shape[1] // TILE, points1.shape[1] // TILE
-    used = 2 * (fine + mid) + lists.shape[0]
+    used = 2 * (fine + mid) + sum(2 * rows_of(a.shape[1]) for a in lists)
     above = -(-used // SIDE) * SIDE
 
-    def kernel(fine_ref, mid_ref, list_ref, factor_ref, out_ref):
+    def kernel(fine_ref, mid_ref, *rest):
+        *list_refs, factor_ref, out_ref = rest
         lines = []
-        for ref, tiles in ((fine_ref, fine), (mid_ref, mid)):
+        for ref in (fine_ref, mid_ref, *list_refs):
             whole = ref[...].astype(f32)
-            lines += [
-                whole[a : a + 1, t * TILE : (t + 1) * TILE] for a in range(2) for t in range(tiles)
-            ]
-        lines.append(list_ref[...].astype(f32))
+            length = whole.shape[1]
+            short = -length % TILE
+            if short:
+                whole = jnp.concatenate([whole, jnp.zeros((2, short), f32)], axis=1)
+            for a in range(2):
+                lines += [whole[a : a + 1, t : t + TILE] for t in range(0, length, TILE)]
         if above > used:
             lines.append(jnp.zeros((above - used, TILE), f32))
         out_ref[pl.ds(0, above), :] = jnp.concatenate(lines, axis=0).astype(bf16)
         out_ref[pl.ds(above, TILE), :] = factor_ref[...]
 
     shapes = [((above + TILE, TILE), bf16)]
-    return call(kernel, shapes, (points0, points1, lists, factor), "packed", 8, 1)
+    return call(kernel, shapes, (points0, points1, *lists, factor), "packed", 8, 1)
 
 
 def unpacked(there, factor, local, fine, mid, listed):
@@ -163,6 +166,38 @@
     return call(kernel, shapes, (there, factor, local), "unpacked", 8, 1)
 
 
+def in_row_order(place, common, partner, mid):
+    at_centres, at_mid = 2 * TILE, 2 * TILE + SIDE
+
+    def kernel(place_ref, own_ref, other_ref, down_ref, across_ref, centre_ref, line_ref):
+        core, x = place_ref[0], place_ref[4]
+
+        def rows(chip, of_core, at, size):
+            own, other = own_ref[chip, pl.ds(at, size), :], other_ref[chip, pl.ds(at, size), :]
+            return jnp.where(core == of_core, own.astype(f32), other.astype(f32))
+
+        for block in range(SIDE):
+            chip, of_core = block // 2, block % 2
+            down_ref[pl.ds(block * TILE, TILE), :] = rows(chip, of_core, 0, TILE).astype(bf16)
+            across_ref[block] = rows(chip, of_core, TILE, TILE).astype(bf16)
+            lines = rows(chip, of_core, at_centres, SIDE)
+            for a in range(2):
+                centre_ref[a, block] = lines[a : a + 1]
+        for q in range(LINE):
+            lines = rows(x * (LINE // 2) + q // 2, q % 2, at_mid, 2 * mid)
+            for a in range(2):
+                for t in range(mid):
+                    line_ref[a, q * mid + t] = lines[a * mid + t : a * mid + t + 1]
+
+    shapes = [
+        ((SIDE * TILE, TILE), bf16),
+        ((SIDE, TILE, TILE), bf16),
+        ((2, SIDE, 1, TILE), f32),
+        ((2, LINE * mid, 1, TILE), f32),
+    ]
+    return call(kernel, shapes, (place, common, partner), "in_row_order", 8, 2, (), 1)
+
+
 def set_points(left_ref, right_ref, left, right, support):
     stretch = stretch_of(support)
     for axis in range(2):
@@ -179,14 +214,15 @@
 
 def add_tiles(list_ref, listed, first, contracted, left, right, vector, total, support):
     rows = rows_of(listed)
-    steps = TILE // GROUP
+    group = 2 * GROUP
+    steps = TILE // group
     line_j = first + contracted * rows
     line_i = first + (1 - contracted) * rows
 
     def step(g, carry):
-        row, lane = g // steps, g % steps * GROUP
+        row, lane = g // steps, g % steps * group
         products = []
-        for u in range(GROUP):
+        for u in range(group):
             j = list_ref[line_j + row, lane + u]
             i = list_ref[line_i + row, lane + u]
             tile = wendland((left[0, j], left[1, j]), (right[0, i], right[1, i]), support)
@@ -196,7 +232,7 @@
             total[i] += product
         return carry
 
-    lax.fori_loop(0, listed // GROUP, step, 0)
+    lax.fori_loop(0, listed // group, step, 0)
 
 
 def product_a0(lists, place, left, right, vector, listed):
@@ -266,52 +302,53 @@
     return call(kernel, shapes, operands, "product", 16, listed / 18, scratch, 1)
 
 
-def quarter_of(lists, place, blocks, rows):
-    listed, tiles = rows
-    lines = rows_of(LINE * QUARTER * tiles)
+def quarter_of(lists, place, blocks, listed, tiles):
     held = rows_of(listed)
-
-    def kernel(list_ref, place_ref, out_ref):
+    size = rows_of(LINE * QUARTER * tiles) * TILE
+
+    def kernel(place_ref, list_ref, out_ref):
         zl = place_ref[3]
-
-        def put(at, i, j):
-            out_ref[at // TILE, at % TILE] = i
-            out_ref[lines + at // TILE, at % TILE] = j
-
-        count = jnp.int32(0)
+        row = lax.broadcasted_iota(jnp.int32, (TILE, TILE), 0)
+        col = lax.broadcasted_iota(jnp.int32, (TILE, TILE), 1)
+        before = (row < col).astype(bf16)
+        slot = lax.broadcasted_iota(jnp.int32, (size, TILE), 0).astype(f32)
+        lane = lax.broadcasted_iota(jnp.int32, (1, TILE), 1)
+        count = jnp.zeros((1, 1), f32)
+        total = jnp.zeros((BLOCK, size), f32)
         for block in range(blocks):
-
-            def step(t, count):
-                for u in range(GROUP):
-                    e = t * GROUP + u
-                    i = list_ref[block * 2 * held + e // TILE, e % TILE]
-                    j = list_ref[block * 2 * held + held + e // TILE, e % TILE]
-                    put(count, i // (2 * LINE) * 2 + i % 2, block * tiles + j)
-                    count = count + (i // 2 % LINE == zl).astype(jnp.int32)
-                return count
-
-            count = lax.fori_loop(0, listed // GROUP, step, count)
-        for u in range(GROUP):
-            put(count + u, jnp.int32(QUARTER), jnp.int32(0))
-        out_ref[2 * lines, 0] = (count + GROUP - 1) // GROUP
-
-    lines = lines + 1
-    return pl.pallas_call(
-        kernel,
-        out_shape=jax.ShapeDtypeStruct((2 * lines + 1, TILE), jnp.int32),
-        in_specs=[SMEM, SMEM],
-        out_specs=SMEM,
-        compiler_params=room(4),
-        cost_estimate=hint(7),
-        name="quarter_of",
-    )(lists, place)
+            for part in range(held):
+                at = block * 2 * held + part
+                i = list_ref[at : at + 1, :]
+                j = list_ref[at + held : at + held + 1, :] + block * tiles
+                real = jnp.where(lane + part * TILE < listed, 1.0, 0.0)
+                flag = jnp.where(((i >> 1) & (LINE - 1)) == zl, real, 0.0)
+                rank = count + jnp.dot(
+                    jnp.broadcast_to(flag, (BLOCK, TILE)).astype(bf16),
+                    before,
+                    preferred_element_type=f32,
+                )[:1]
+                here = jnp.where(slot == jnp.where(flag > 0.5, rank, -1.0), 1.0, 0.0).astype(bf16)
+                lines = [((i >> 3) * 2 + (i & 1)).astype(f32), j.astype(f32)]
+                lines.append(jnp.zeros((BLOCK - 2, TILE), f32))
+                lines = jnp.concatenate(lines, axis=0).astype(bf16)
+                total += lax.dot_general(
+                    lines, here, (((1,), (1,)), ((), ())), preferred_element_type=f32
+                )
+                count += jnp.sum(flag, axis=1, keepdims=True)
+        slots = lax.broadcasted_iota(jnp.int32, (1, size), 1).astype(f32)
+        out_ref[0:1, :] = jnp.where(slots < count, total[0:1], float(QUARTER)).astype(jnp.int32)
+        out_ref[1:2, :] = total[1:2].astype(jnp.int32)
+        groups = ((count + (GROUP - 1)) * (1.0 / GROUP)).astype(jnp.int32)
+        out_ref[2:3, :] = jnp.broadcast_to(groups, (1, size))
+        out_ref[3:, :] = jnp.zeros((BLOCK - 3, size), jnp.int32)
+
+    shapes = [((BLOCK, size), jnp.int32)]
+    return call(kernel, shapes, (place, lists), "quarter_of", 8, 3, (), 1)
 
 
 def product_quarter(lists, left, right, own, other, support):
-    lines = (lists.shape[0] - 1) // 2
     tiles = right.shape[1]
     length = left.shape[1] * TILE // LINE
-    steps = TILE // GROUP
 
     def kernel(list_ref, left_ref, right_ref, own_ref, other_ref, out_ref, left, right, vector, total):
         set_points(left_ref, right_ref, left, right, support)
@@ -324,11 +361,10 @@
                     vector[at, pl.ds(zl * length, length)] = part
 
         def step(g, carry):
-            row, lane = g // steps, g % steps * GROUP
             products = []
             for u in range(GROUP):
-                i = list_ref[row, lane + u]
-                j = list_ref[lines + row, lane + u]
+                i = list_ref[0, g * GROUP + u]
+                j = list_ref[1, g * GROUP + u]
                 tile = wendland((left[0, j], left[1, j]), (right[0, i], right[1, i]), support)
                 product = jnp.dot(vector[:, at_tile(j)], tile, preferred_element_type=f32)
                 products.append((i, product))
@@ -336,7 +372,7 @@
                 total[i] += product
             return carry
 
-        lax.fori_loop(0, list_ref[2 * lines, 0], step, 0)
+        lax.fori_loop(0, list_ref[2, 0], step, 0)
         for i in range(QUARTER):
             out_ref[i // 2, :, pl.ds(i % 2 * TILE, TILE)] = total[i].astype(bf16)
 
@@ -373,23 +409,36 @@
     )(left, right)
 
 
-def residual_of(arrived, scale):
-    chips, _, n = arrived.shape
+def sum_of(arrived):
+    _, rows, n = arrived.shape
 
     def kernel(arrived_ref, out_ref):
+        for t in range(0, n, 4 * TILE):
+            at = pl.ds(t, 4 * TILE)
+            out_ref[:, at] = arrived_ref[:, :, at].astype(f32).sum(axis=0).astype(bf16)
+
+    return call(kernel, [((rows, n), bf16)], (arrived,), "sum_of", 8, 1)
+
+
+def residual_of(here, there, scale):
+    rows, n = here.shape
+
+    def kernel(here_ref, there_ref, out_ref):
         squares = jnp.zeros((1, TILE), f32)
         for t in range(n // TILE):
             at = pl.ds(t * TILE, TILE)
-            part = scale * arrived_ref[:, :, at].astype(f32).sum(axis=0)
+            part = scale * (here_ref[:, at].astype(f32) + there_ref[:, at].astype(f32))
             squares += jnp.sum(part * part, axis=0, keepdims=True)
             low = part.astype(bf16)
-            for chip in range(chips):
+            for chip in range(LINE):
                 out_ref[chip, :, at] = low
         tail = three_rows(squares)
-        for chip in range(chips):
-            out_ref[chip, :, pl.ds(n, TILE)] = tail
-
-    return call(kernel, [((chips, BLOCK, n + TILE), bf16)], (arrived,), "residual_of", 8, 1)
+        for chip in range(LINE):
+            out_ref[chip, pl.ds(0, BLOCK), pl.ds(n, TILE)] = tail
+            out_ref[chip, pl.ds(BLOCK, BLOCK), pl.ds(n, TILE)] = jnp.zeros_like(tail)
+
+    shapes = [((LINE, rows, n + TILE), bf16)]
+    return call(kernel, shapes, (here, there), "residual_of", 8, 1)
 
 
 def three_rows(x):
@@ -602,13 +651,15 @@
 
     listed_a0, listed_e1, listed_a1 = (a.shape[1] for a in (list_a0, list_e1, list_a1))
 
+    first_e1 = 2 * rows_of(listed_a0)
+    first_a1 = first_e1 + 2 * rows_of(listed_e1)
+
     own_e1 = in_rows(list_e1)
-    lists = jnp.concatenate([in_rows(list_a0), own_e1, in_rows(list_a1)], axis=0)
-    there = turned(packed(points0, points1, lists, factor))
+    there = turned(packed(points0, points1, (list_a0, list_e1, list_a1), factor))
     local = [points2, jnp.zeros((SIDE - 2, TILE), bf16), points1.reshape(2 * tiles_mid, TILE)]
     local = jnp.concatenate(local, axis=0)
     x_id, zl_id = lax.axis_index("x"), lax.axis_index("zl")
-    place = jnp.stack([core, row_id, col_id, zl_id]).astype(jnp.int32)
+    place = jnp.stack([core, row_id, col_id, zl_id, x_id]).astype(jnp.int32)
     fine_here = points0.astype(f32).reshape(2, tiles_fine, 1, TILE)
     mid_here = points1.astype(f32).reshape(2, tiles_mid, 1, TILE)
     tail = jnp.pad(own_e1, ((0, BLOCK - own_e1.shape[0]), (0, 0))).astype(bf16)
@@ -616,43 +667,35 @@
         (there, values.T, local, fine_here, mid_here, tail)
     )
     fine_there, mid_there, lists, common = unpacked(
-        there, factor, local, tiles_fine, tiles_mid, lists.shape[0]
-    )
-    first_e1 = 2 * rows_of(listed_a0)
-    first_a1 = first_e1 + 2 * rows_of(listed_e1)
+        there, factor, local, tiles_fine, tiles_mid, first_a1 + 2 * rows_of(listed_a1)
+    )
 
     common = exchanged(common, YZ)
     own, other = product_a0(lists, place, fine_here, fine_there, vector, listed_a0)
     own, other, common = lax.optimization_barrier((own, other, common))
-    arrived = exchanged(pair_sum(own, other), YZ)
-
-    fine_all, common, mid_later, fine_later = lax.optimization_barrier(
-        (residual_of(arrived, -0.5 * scale_a0), common, mid_there, fine_here)
-    )
-    partner = from_partner(common)
-
-    def in_row_order(at, size):
-        mine, its = common[:, at : at + size], partner[:, at : at + size]
-        return jnp.stack([jnp.where(core == 0, mine, its), jnp.where(core == 0, its, mine)], axis=1)
-
-    factor_down = in_row_order(0, rows_coarse).reshape(coarse, -1)
-    factor_across = in_row_order(rows_coarse, rows_coarse).reshape(SIDE, rows_coarse, -1)
-    centres = in_row_order(2 * rows_coarse, SIDE).reshape(SIDE, SIDE, -1)[:, :2]
-    centres = centres.astype(f32).transpose(1, 0, 2)[:, :, None]
-    mid_line = in_row_order(2 * rows_coarse + SIDE, 2 * tiles_mid)
-    mid_line = mid_line.reshape(SIDE, 2, tiles_mid, 1, TILE)
-    mid_line = lax.dynamic_slice_in_dim(mid_line, x_id * LINE, LINE, 0).astype(f32)
-    mid_line = mid_line.transpose(1, 0, 2, 3, 4).reshape(2, LINE * tiles_mid, 1, TILE)
+    pair = pair_sum(own, other).reshape(LINE, 2 * BLOCK, rows_fine)
+    arrived = exchanged(pair, "y")
+
+    common, pair = lax.optimization_barrier((common, pair))
+    ordered = in_row_order(place, common, from_partner(common), tiles_mid)
+    arrived, ordered = lax.optimization_barrier((arrived, ordered))
+    factor_down, factor_across, centres, mid_line = ordered
+    summed = sum_of(arrived)
+    centres, mid_later, fine_later, summed = lax.optimization_barrier(
+        (centres, mid_there, fine_here, summed)
+    )
+    swapped = lax.ppermute(summed, "zh", [(0, 1), (1, 0)])
+    coarse_kernel = all_pairs(centres, mid_later, support_coarse)
+    swapped, coarse_kernel, fine_later = lax.optimization_barrier(
+        (swapped, coarse_kernel, fine_later)
+    )
+    fine_own = exchanged(residual_of(summed, swapped, -0.5 * scale_a0), "y")
     fine_quarter = fine_later.reshape(2, QUARTER // 2, LINE, 2, 1, TILE)
     fine_quarter = lax.dynamic_index_in_dim(fine_quarter, zl_id, 2, keepdims=False)
     fine_quarter = fine_quarter.reshape(2, QUARTER, 1, TILE)
     fine_quarter = jnp.pad(fine_quarter, ((0, 0), (0, 1), (0, 0), (0, 0)), constant_values=8.0)
-    coarse_kernel = all_pairs(centres, mid_later, support_coarse)
-    fine_own, coarse_kernel, factor_down, factor_across, mid_line, fine_quarter = (
-        lax.optimization_barrier(
-            (exchanged(fine_all, YZ), coarse_kernel, factor_down, factor_across, mid_line, fine_quarter)
-        )
-    )
+    fine_own, fine_quarter = lax.optimization_barrier((fine_own, fine_quarter))
+    fine_own = fine_own.reshape(HALF, BLOCK, rows_fine + TILE)
     fine_other = from_partner(fine_own)
 
     restricted = product(
@@ -662,7 +705,7 @@
     mid_share, mid_all = mid_of(restricted, scale_e1)
     line_lists = lax.dynamic_slice_in_dim(restricted[:, :, rows_mid:], x_id * LINE, LINE, 0)
     line_lists = line_lists[:, : own_e1.shape[0]].reshape(-1, TILE).astype(jnp.int32)
-    line_lists = quarter_of(line_lists, place, LINE, (listed_e1, tiles_mid))
+    line_lists = quarter_of(line_lists, place, LINE, listed_e1, tiles_mid)
     mid_all, mid_data, line_lists = lax.optimization_barrier(
         (exchanged(mid_all, COL), turned_blocks(mid_share), line_lists)
     )

time: 275 us -> 253 us (0.920)
  blocking collectives: 95.7 us -> 64.1 us
  Pallas kernels: 75.4 us -> 56.4 us
  starting transfers between devices: 54.8 us -> 69 us
  waiting for transfers between devices: 30.6 us -> 43.9 us
    all_to_all x6 -> x5, blocking collectives: 95.7 us -> 64.1 us  [exchanged(): return lax.all_to_all(x, axes, split_axis=0, concat_axis=0, tiled=True)]
    pallas_call x1 -> x0, Pallas kernels: 19.3 us -> none  [quarter_of(): pl.pallas_call(kernel, out_shape=jax.ShapeDtypeStruct((2 * lines + 1, TIL...]
    all_to_all x6 -> x7, waiting for transfers between devices: 26.1 us -> 35.7 us  [exchanged(): return lax.all_to_all(x, axes, split_axis=0, concat_axis=0, tiled=True)]
    ppermute x5, starting transfers between devices: 12.3 us -> 17.5 us  [from_partner(): return lax.ppermute(x, 'k', [(0, 1), (1, 0)])]
    ppermute x0 -> x1, starting transfers between devices: none -> 5.21 us  [per_device(): swapped = lax.ppermute(summed, 'zh', [(0, 1), (1, 0)])]
    ppermute x1, waiting for transfers between devices: 0.01 us -> 4.12 us  [turned_blocks(): return lax.ppermute(x, ALL, pairs)]
    all_to_all x6 -> x7, starting transfers between devices: 34.3 us -> 38 us  [exchanged(): return lax.all_to_all(x, axes, split_axis=0, concat_axis=0, tiled=True)]
    unnamed x13 -> x19, local copies, waits for them, and re-layouts: 7.32 us -> 9.36 us
  transfers between devices with their start and end apart: 13 -> 15, of which waited for: 7 -> 9; matrix products, arithmetic and copies ran while one was open for 3% -> 3% of each run, Pallas kernels for 16% -> 10%
where the time goes in v5:
time: 253 us; the launch traced here: 252 us
  starting transfers between devices  69 us (27%)
  blocking collectives  64.1 us (25%)
  Pallas kernels  56.4 us (22%)
  waiting for transfers between devices  43.9 us (17%)
  local copies, waits for them, and re-layouts  12.6 us (5%)
  other arithmetic  3.23 us (1%)
  between operations  2.77 us (1%)
    all_to_all x5, blocking collectives, exchanged(): return lax.all_to_all(x, axes, split_axis=0, concat_axis=0, tiled=True)  64.1 us
    pallas_call x15, Pallas kernels, call(): pl.pallas_call(kernel, out_shape=[jax.ShapeDtypeStruct(shape, kind) for s...  44.7 us
    all_to_all x7, starting transfers between devices, exchanged(): return lax.all_to_all(x, axes, split_axis=0, concat_axis=0, tiled=True)  38 us
    all_to_all x7, waiting for transfers between devices, exchanged(): return lax.all_to_all(x, axes, split_axis=0, concat_axis=0, tiled=True)  35.7 us
    ppermute x5, starting transfers between devices, from_partner(): return lax.ppermute(x, 'k', [(0, 1), (1, 0)])  17.5 us
    unnamed x19, local copies, waits for them, and re-layouts  9.36 us
    pallas_call x2, Pallas kernels, call_on_matrix(): pl.pallas_call(kernel, out_shape=jax.ShapeDtypeStruct(shape, kind), in_sp...  6.23 us
    pallas_call x1, Pallas kernels, all_pairs(): pl.pallas_call(kernel, out_shape=jax.ShapeDtypeStruct((rows * TILE, cols...  5.45 us
  transfers between devices with their start and end apart: 15, of which 9 were waited for; matrix products, arithmetic and copies ran while one was open for 3% of the time, Pallas kernels for 10%

profile of v5, /device:TPU:1, one launch (start us, length us, event | category | flops | bytes accessed | tf_op | source)
XLA Modules:
  0.0 252.1 jit_solution(2801296069494441506)
XLA Ops:
  4.9 4.9 %collective-permute-start = (bf16[224,128]{1,0:T(8,128)(2,1)S(1)}, bf16[224,128]{1,0:T(8,128)(2,1)S(1)}, u32[]{:S(2)}, u32[]{:S(2)}) collective-permute-start(bf16[224,128]{1,0:T(8,128)(2,1)S(1)} %packed.1), channel_id=1, source_target_pairs={{0,0},{16,1},{32,2},{48,3},{64,4},{80,5},{96,6},{112,7},{128,8},{1... | collective-permute-start | bytes 172040 | tf_op jit(solution)/shard_map/ppermute | solution.py:48
  15.9 13.6 %all-to-all-start = ((bf16[8,288,128]{2,1,0:T(8,128)(2,1)}), bf16[8,288,128]{2,1,0:T(8,128)(2,1)S(1)}, u32[]{:S(2)}, u32[]{:S(2)}) async-start(bf16[8,288,128]{2,1,0:T(8,128)(2,1)} %get-tuple-element.54), calls=%async_computation | async-start | bytes 1179648 | tf_op jit(solution)/shard_map/all_to_all | solution.py:67
  29.6 17.1 %product_a0.1 = (bf16[8,8,4096]{2,1,0:T(8,128)(2,1)S(1)}, bf16[8,8,4096]{2,1,0:T(8,128)(2,1)S(1)}) custom-call(s32[12,128]{1,0:T(8,128)S(1)} %get-tuple-element.47.list_ref, s32[5]{0:T(128)S(1)} %stack.38.place_ref.core_ref, f32[2,32,1,128]{3,2,1,0:T(1,128)S(1)} %reshape.79.left_ref, f32[2,32,1,128]{3,2,1,0:T(1,128)S(1)} %get-tuple-element.48.right_ref.left_ref, ...), custom_call_target="tpu_custom_call" | custom-call | bytes 60000000 | tf_op jit(solution)/shard_map/product_a0/pallas_call | solution.py:93
  46.7 2.8 %collective-permute-start.1 = (bf16[8,8,4096]{2,1,0:T(8,128)(2,1)S(1)}, bf16[8,8,4096]{2,1,0:T(8,128)(2,1)S(1)}, u32[]{:S(2)}, u32[]{:S(2)}) collective-permute-start(bf16[8,8,4096]{2,1,0:T(8,128)(2,1)S(1)} %get-tuple-element.56), channel_id=1, source_target_pairs={{0,16},{16,0},{1,17},{17,1},{2,18},{18,2},{3,19},{19,3},{4,20},{20... | collective-permute-start | bytes 1572872 | tf_op jit(solution)/shard_map/ppermute | solution.py:63
  52.4 4.1 %all-to-all-start.1 = ((bf16[4,16,4096]{2,1,0:T(8,128)(2,1)}), bf16[4,16,4096]{2,1,0:T(8,128)(2,1)S(1)}, u32[]{:S(2)}, u32[]{:S(2)}) async-start(bf16[4,16,4096]{2,1,0:T(8,128)(2,1)} %bitcast.9), calls=%async_computation.1 | async-start | bytes 1048576 | tf_op jit(solution)/shard_map/all_to_all | solution.py:67
  57.3 8.4 %all-to-all-done.1.arrived_ref = bf16[4,16,4096]{2,1,0:T(8,128)(2,1)S(1)} async-done(((bf16[4,16,4096]{2,1,0:T(8,128)(2,1)}), bf16[4,16,4096]{2,1,0:T(8,128)(2,1)S(1)}, u32[]{:S(2)}, u32[]{:S(2)}) %all-to-all-start.1) | async-done | bytes 524320 | tf_op jit(solution)/shard_map/all_to_all | solution.py:67
  65.7 5.2 %collective-permute-start.3 = (bf16[16,4096]{1,0:T(8,128)(2,1)S(1)}, bf16[16,4096]{1,0:T(8,128)(2,1)S(1)}, u32[]{:S(2)}, u32[]{:S(2)}) collective-permute-start(bf16[16,4096]{1,0:T(8,128)(2,1)S(1)} %sum_of.1.here_ref), channel_id=1, source_target_pairs={{0,32},{32,0},{1,33},{33,1},{2,34},{34,2},{3,35},{35,3},{4,36},{36... | collective-permute-start | bytes 393224 | tf_op jit(solution)/shard_map/ppermute | solution.py:687
  70.9 5.5 %all_pairs.1.matrix_ref = bf16[2048,1024]{1,0:T(8,128)(2,1)S(1)} custom-call(f32[2,16,1,128]{3,2,1,0:T(1,128)S(1)} %get-tuple-element.67.left_ref, f32[2,8,1,128]{3,2,1,0:T(1,128)S(1)} %get-tuple-element.68.right_ref), custom_call_target="tpu_custom_call" | custom-call | bytes 18000000 | tf_op jit(solution)/shard_map/all_pairs/pallas_call | solution.py:400
  79.3 3.5 %all-to-all-start.2 = ((bf16[4,16,4224]{2,1,0:T(8,128)(2,1)}), bf16[4,16,4224]{2,1,0:T(8,128)(2,1)S(1)}, u32[]{:S(2)}, u32[]{:S(2)}) async-start(bf16[4,16,4224]{2,1,0:T(8,128)(2,1)} %residual_of.1), calls=%async_computation.2 | async-start | bytes 1081344 | tf_op jit(solution)/shard_map/all_to_all | solution.py:67
  82.8 7.8 %all-to-all-done.2 = bf16[4,16,4224]{2,1,0:T(8,128)(2,1)S(1)} async-done(((bf16[4,16,4224]{2,1,0:T(8,128)(2,1)}), bf16[4,16,4224]{2,1,0:T(8,128)(2,1)S(1)}, u32[]{:S(2)}, u32[]{:S(2)}) %all-to-all-start.2) | async-done | bytes 540704 | tf_op jit(solution)/shard_map/all_to_all | solution.py:67
  90.6 2.8 %collective-permute-start.4 = (bf16[8,8,4224]{2,1,0:T(8,128)(2,1)S(1)}, bf16[8,8,4224]{2,1,0:T(8,128)(2,1)S(1)}, u32[]{:S(2)}, u32[]{:S(2)}) collective-permute-start(bf16[8,8,4224]{2,1,0:T(8,128)(2,1)S(1)} %bitcast.57), channel_id=1, source_target_pairs={{0,16},{16,0},{1,17},{17,1},{2,18},{18,2},{3,19},{19,3},{4,20},{20... | collective-permute-start | bytes 1622024 | tf_op jit(solution)/shard_map/ppermute | solution.py:63
  94.9 8.1 %product.2 = bf16[16,8,1152]{2,1,0:T(8,128)(2,1)S(1)} custom-call(s32[12,128]{1,0:T(8,128)S(1)} %get-tuple-element.47.list_ref, f32[2,32,1,128]{3,2,1,0:T(1,128)S(1)} %get-tuple-element.48.right_ref.left_ref, f32[2,8,1,128]{3,2,1,0:T(1,128)S(1)} %reshape.81.right_ref.left_ref, bf16[8,8,4224]{2,1,0:T(8,128)(2,1)S(1)} %bitcast.58, ...), custom_call_target="tpu_custom_call" | custom-call | bytes 26666666 | tf_op jit(solution)/shard_map/product/pallas_call | solution.py:93
  103.0 13.5 %all_to_all.60.arrived_ref = bf16[16,8,1152]{2,1,0:T(8,128)(2,1)S(1)} all-to-all(bf16[16,8,1152]{2,1,0:T(8,128)(2,1)S(1)} %product.2), channel_id=1, replica_groups=mesh['y'=4,'zh'=2,'k'=2,'x'=4,'zl'=4] {'x','zl'}, dimensions={0} | all-to-all | bytes 589824 | tf_op jit(solution)/shard_map/all_to_all | solution.py:67
  117.3 3.9 %all-to-all-start.4 = ((bf16[16,8,1024]{2,1,0:T(8,128)(2,1)}), bf16[16,8,1024]{2,1,0:T(8,128)(2,1)S(1)}, u32[]{:S(2)}, u32[]{:S(2)}) async-start(bf16[16,8,1024]{2,1,0:T(8,128)(2,1)} %get-tuple-element.74), calls=%async_computation.4 | async-start | bytes 524288 | tf_op jit(solution)/shard_map/all_to_all | solution.py:67
  121.1 3.3 %collective-permute-start.5 = (f32[8,1024]{1,0:T(8,128)S(1)}, f32[8,1024]{1,0:T(8,128)S(1)}, u32[]{:S(2)}, u32[]{:S(2)}) collective-permute-start(f32[8,1024]{1,0:T(8,128)S(1)} %get-tuple-element.75), channel_id=1, source_target_pairs={{0,0},{24,1},{32,2},{56,3},{64,4},{88,5},{96,6},{120,7},{128,8},{1... | collective-permute-start | bytes 98312 | tf_op jit(solution)/shard_map/ppermute | solution.py:59
  125.7 4.1 %collective-permute-done.5.mid_ref = f32[8,1024]{1,0:T(8,128)S(1)} collective-permute-done((f32[8,1024]{1,0:T(8,128)S(1)}, f32[8,1024]{1,0:T(8,128)S(1)}, u32[]{:S(2)}, u32[]{:S(2)}) %collective-permute-start.5) | collective-permute-done | bytes 32800 | tf_op jit(solution)/shard_map/ppermute | solution.py:59
  129.8 2.4 product.3
  132.2 3.6 %collective-permute-start.6 = (bf16[8,8,1024]{2,1,0:T(8,128)(2,1)S(1)}, bf16[8,8,1024]{2,1,0:T(8,128)(2,1)S(1)}, u32[]{:S(2)}, u32[]{:S(2)}) collective-permute-start(bf16[8,8,1024]{2,1,0:T(8,128)(2,1)S(1)} %get-tuple-element.82), channel_id=1, source_target_pairs={{0,16},{16,0},{1,17},{17,1},{2,18},{18,2},{3,19},{19,3},{4,20},{20... | collective-permute-start | bytes 393224 | tf_op jit(solution)/shard_map/ppermute | solution.py:63
  136.9 15.9 %all_to_all.61.arrived_ref = bf16[8,8,1024]{2,1,0:T(8,128)(2,1)S(1)} all-to-all(bf16[8,8,1024]{2,1,0:T(8,128)(2,1)S(1)} %add_convert_fusion.1), channel_id=1, replica_groups=mesh['y'=4,'zh'=2,'k'=2,'x'=4,'zl'=4] {'y','zh'}, dimensions={0} | all-to-all | bytes 262144 | tf_op jit(solution)/shard_map/all_to_all | solution.py:67
  152.8 3.7 %coarse_product.1 = f32[16,8,128]{2,1,0:T(8,128)} custom-call(bf16[2048,1024]{1,0:T(8,128)(2,1)} %copy-done, bf16[8,8,1024]{2,1,0:T(8,128)(2,1)S(1)} %all_to_all.61.arrived_ref, f32[8,1024]{1,0:T(8,128)S(1)} %collective-permute-done.5.mid_ref), custom_call_target="tpu_custom_call" | custom-call | bytes 9000000 | tf_op jit(solution)/shard_map/coarse_product/pallas_call | solution.py:478
  156.6 6.1 %all-to-all-start.6 = ((f32[16,8,128]{2,1,0:T(8,128)}), f32[16,8,128]{2,1,0:T(8,128)S(1)}, u32[]{:S(2)}, u32[]{:S(2)}) async-start(f32[16,8,128]{2,1,0:T(8,128)} %coarse_product.1), calls=%async_computation.6 | async-start | bytes 131072 | tf_op jit(solution)/shard_map/all_to_all | solution.py:67
  162.7 7.0 %all-to-all-done.6.arrived_ref = f32[16,8,128]{2,1,0:T(8,128)S(1)} async-done(((f32[16,8,128]{2,1,0:T(8,128)}), f32[16,8,128]{2,1,0:T(8,128)S(1)}, u32[]{:S(2)}, u32[]{:S(2)}) %all-to-all-start.6) | async-done | bytes 65568 | tf_op jit(solution)/shard_map/all_to_all | solution.py:67
  169.7 9.5 %all_to_all.62.data_ref = bf16[16,2,8,128]{3,2,1,0:T(8,128)(2,1)S(1)} all-to-all(bf16[16,2,8,128]{3,2,1,0:T(8,128)(2,1)S(1)} %coarse_data_of.1), channel_id=1, replica_groups=mesh['y'=4,'zh'=2,'k'=2,'x'=4,'zl'=4] {'x','zl'}, dimensions={0} | all-to-all | bytes 131072 | tf_op jit(solution)/shard_map/all_to_all | solution.py:67
  179.4 9.4 %all_to_all.63.half_ref = bf16[16,8,128]{2,1,0:T(8,128)(2,1)S(1)} all-to-all(bf16[16,8,128]{2,1,0:T(8,128)(2,1)S(1)} %halfway_of.1), channel_id=1, replica_groups=mesh['y'=4,'zh'=2,'k'=2,'x'=4,'zl'=4] {'x','zl'}, dimensions={0} | all-to-all | bytes 65536 | tf_op jit(solution)/shard_map/all_to_all | solution.py:67
  189.8 3.5 %all-to-all-start.9 = ((f32[16,8,128]{2,1,0:T(8,128)}), f32[16,8,128]{2,1,0:T(8,128)S(1)}, u32[]{:S(2)}, u32[]{:S(2)}) async-start(f32[16,8,128]{2,1,0:T(8,128)} %coarse_coef_of.1), calls=%async_computation.9 | async-start | bytes 131072 | tf_op jit(solution)/shard_map/all_to_all | solution.py:67
  193.4 6.9 %all-to-all-done.9.coef_ref = f32[16,8,128]{2,1,0:T(8,128)S(1)} async-done(((f32[16,8,128]{2,1,0:T(8,128)}), f32[16,8,128]{2,1,0:T(8,128)S(1)}, u32[]{:S(2)}, u32[]{:S(2)}) %all-to-all-start.9) | async-done | bytes 65568 | tf_op jit(solution)/shard_map/all_to_all | solution.py:67
  200.3 2.5 prolong.1
  202.8 15.7 %all_to_all.64.own_ref = bf16[32,8,1152]{2,1,0:T(8,128)(2,1)S(1)} all-to-all(bf16[32,8,1152]{2,1,0:T(8,128)(2,1)S(1)} %prolong.1), channel_id=1, replica_groups=mesh['y'=4,'zh'=2,'k'=2,'x'=4,'zl'=4] {'y','zh','zl'}, dimensions={0} | all-to-all | bytes 1179648 | tf_op jit(solution)/shard_map/all_to_all | solution.py:67
  218.5 8.0 %collective-permute-start.7 = (bf16[32,8,1152]{2,1,0:T(8,128)(2,1)S(1)}, bf16[32,8,1152]{2,1,0:T(8,128)(2,1)S(1)}, u32[]{:S(2)}, u32[]{:S(2)}) collective-permute-start(bf16[32,8,1152]{2,1,0:T(8,128)(2,1)S(1)} %all_to_all.64.own_ref), channel_id=1, source_target_pairs={{0,16},{16,0},{1,17},{17,1},{2,18},{18,2},{3,19},{19,3},{4,20},{20... | collective-permute-start | bytes 1769480 | tf_op jit(solution)/shard_map/ppermute | solution.py:63
  229.5 9.9 %product_quarter.1 = bf16[4,128,256]{2,1,0:T(8,128)(2,1)} custom-call(s32[8,256]{1,0:T(8,128)S(1)} %quarter_of.1.list_ref, f32[2,32,1,128]{3,2,1,0:T(1,128)S(1)} %get-tuple-element.77.left_ref, f32[2,9,1,128]{3,2,1,0:T(1,128)S(1)} %pad.16.right_ref, bf16[32,8,1152]{2,1,0:T(8,128)(2,1)S(1)} %all_to_all.64.own_ref, ...), custom_call_target="tpu_custom_call" | custom-call | bytes 30000000 | tf_op jit(solution)/shard_map/product_quarter/pallas_call | solution.py:93
  239.4 3.4 %all-to-all-start.11 = ((bf16[4,128,256]{2,1,0:T(8,128)(2,1)}), bf16[4,128,256]{2,1,0:T(8,128)(2,1)S(1)}, u32[]{:S(2)}, u32[]{:S(2)}) async-start(bf16[4,128,256]{2,1,0:T(8,128)(2,1)} %product_quarter.1), calls=%async_computation.11 | async-start | bytes 524288 | tf_op jit(solution)/shard_map/all_to_all | solution.py:67
  243.9 5.7 %all-to-all-done.11.arrived_ref = bf16[4,128,256]{2,1,0:T(8,128)(2,1)S(1)} async-done(((bf16[4,128,256]{2,1,0:T(8,128)(2,1)}), bf16[4,128,256]{2,1,0:T(8,128)(2,1)S(1)}, u32[]{:S(2)}, u32[]{:S(2)}) %all-to-all-start.11) | async-done | bytes 262176 | tf_op jit(solution)/shard_map/all_to_all | solution.py:67
  (71 shorter events, 27.5 us)
Async XLA Ops:
  0.6 0.8 copy-start.1
  1.4 0.7 copy-start.3
  2.1 0.7 copy-start.4
  2.8 0.7 copy-start.5
  3.5 0.7 copy-start.6
  4.2 0.7 copy-start.7
  4.8 10.2 %copy-start.2 = (bf16[128,128]{1,0:T(8,128)(2,1)S(1)}, bf16[128,128]{1,0:T(8,128)(2,1)}, u32[]{:S(2)}) copy-start(bf16[128,128]{1,0:T(8,128)(2,1)} %factor_ref.1) | copy-start | bytes 98308
  4.9 10.1 %collective-permute-start = (bf16[224,128]{1,0:T(8,128)(2,1)S(1)}, bf16[224,128]{1,0:T(8,128)(2,1)S(1)}, u32[]{:S(2)}, u32[]{:S(2)}) collective-permute-start(bf16[224,128]{1,0:T(8,128)(2,1)S(1)} %packed.1), channel_id=1, source_target_pairs={{0,0},{16,1},{32,2},{48,3},{64,4},{80,5},{96,6},{112,7},{128,8},{1... | collective-permute-start | bytes 172040 | tf_op jit(solution)/shard_map/ppermute | solution.py:48
  15.9 30.8 %all-to-all-start = ((bf16[8,288,128]{2,1,0:T(8,128)(2,1)}), bf16[8,288,128]{2,1,0:T(8,128)(2,1)S(1)}, u32[]{:S(2)}, u32[]{:S(2)}) async-start(bf16[8,288,128]{2,1,0:T(8,128)(2,1)} %get-tuple-element.54), calls=%async_computation | async-start | bytes 1179648 | tf_op jit(solution)/shard_map/all_to_all | solution.py:67
  46.7 4.4 %collective-permute-start.1 = (bf16[8,8,4096]{2,1,0:T(8,128)(2,1)S(1)}, bf16[8,8,4096]{2,1,0:T(8,128)(2,1)S(1)}, u32[]{:S(2)}, u32[]{:S(2)}) collective-permute-start(bf16[8,8,4096]{2,1,0:T(8,128)(2,1)S(1)} %get-tuple-element.56), channel_id=1, source_target_pairs={{0,16},{16,0},{1,17},{17,1},{2,18},{18,2},{3,19},{19,3},{4,20},{20... | collective-permute-start | bytes 1572872 | tf_op jit(solution)/shard_map/ppermute | solution.py:63
  52.0 4.5 %collective-permute-start.2 = (bf16[8,288,128]{2,1,0:T(8,128)(2,1)S(1)}, bf16[8,288,128]{2,1,0:T(8,128)(2,1)S(1)}, u32[]{:S(2)}, u32[]{:S(2)}) collective-permute-start(bf16[8,288,128]{2,1,0:T(8,128)(2,1)S(1)} %all-to-all-done.own_ref), channel_id=1, source_target_pairs={{0,16},{16,0},{1,17},{17,1},{2,18},{18,2},{3,19},{19,3},{4,20},{20... | collective-permute-start | bytes 1769480 | tf_op jit(solution)/shard_map/ppermute | solution.py:63
  52.4 13.3 %all-to-all-start.1 = ((bf16[4,16,4096]{2,1,0:T(8,128)(2,1)}), bf16[4,16,4096]{2,1,0:T(8,128)(2,1)S(1)}, u32[]{:S(2)}, u32[]{:S(2)}) async-start(bf16[4,16,4096]{2,1,0:T(8,128)(2,1)} %bitcast.9), calls=%async_computation.1 | async-start | bytes 1048576 | tf_op jit(solution)/shard_map/all_to_all | solution.py:67
  65.7 12.6 %collective-permute-start.3 = (bf16[16,4096]{1,0:T(8,128)(2,1)S(1)}, bf16[16,4096]{1,0:T(8,128)(2,1)S(1)}, u32[]{:S(2)}, u32[]{:S(2)}) collective-permute-start(bf16[16,4096]{1,0:T(8,128)(2,1)S(1)} %sum_of.1.here_ref), channel_id=1, source_target_pairs={{0,32},{32,0},{1,33},{33,1},{2,34},{34,2},{3,35},{35,3},{4,36},{36... | collective-permute-start | bytes 393224 | tf_op jit(solution)/shard_map/ppermute | solution.py:687
  76.4 2.0 copy-start
  79.3 11.3 %all-to-all-start.2 = ((bf16[4,16,4224]{2,1,0:T(8,128)(2,1)}), bf16[4,16,4224]{2,1,0:T(8,128)(2,1)S(1)}, u32[]{:S(2)}, u32[]{:S(2)}) async-start(bf16[4,16,4224]{2,1,0:T(8,128)(2,1)} %residual_of.1), calls=%async_computation.2 | async-start | bytes 1081344 | tf_op jit(solution)/shard_map/all_to_all | solution.py:67
  90.6 4.3 %collective-permute-start.4 = (bf16[8,8,4224]{2,1,0:T(8,128)(2,1)S(1)}, bf16[8,8,4224]{2,1,0:T(8,128)(2,1)S(1)}, u32[]{:S(2)}, u32[]{:S(2)}) collective-permute-start(bf16[8,8,4224]{2,1,0:T(8,128)(2,1)S(1)} %bitcast.57), channel_id=1, source_target_pairs={{0,16},{16,0},{1,17},{17,1},{2,18},{18,2},{3,19},{19,3},{4,20},{20... | collective-permute-start | bytes 1622024 | tf_op jit(solution)/shard_map/ppermute | solution.py:63
  117.3 12.5 %all-to-all-start.4 = ((bf16[16,8,1024]{2,1,0:T(8,128)(2,1)}), bf16[16,8,1024]{2,1,0:T(8,128)(2,1)S(1)}, u32[]{:S(2)}, u32[]{:S(2)}) async-start(bf16[16,8,1024]{2,1,0:T(8,128)(2,1)} %get-tuple-element.74), calls=%async_computation.4 | async-start | bytes 524288 | tf_op jit(solution)/shard_map/all_to_all | solution.py:67
  121.1 8.6 %collective-permute-start.5 = (f32[8,1024]{1,0:T(8,128)S(1)}, f32[8,1024]{1,0:T(8,128)S(1)}, u32[]{:S(2)}, u32[]{:S(2)}) collective-permute-start(f32[8,1024]{1,0:T(8,128)S(1)} %get-tuple-element.75), channel_id=1, source_target_pairs={{0,0},{24,1},{32,2},{56,3},{64,4},{88,5},{96,6},{120,7},{128,8},{1... | collective-permute-start | bytes 98312 | tf_op jit(solution)/shard_map/ppermute | solution.py:59
  132.2 4.6 %collective-permute-start.6 = (bf16[8,8,1024]{2,1,0:T(8,128)(2,1)S(1)}, bf16[8,8,1024]{2,1,0:T(8,128)(2,1)S(1)}, u32[]{:S(2)}, u32[]{:S(2)}) collective-permute-start(bf16[8,8,1024]{2,1,0:T(8,128)(2,1)S(1)} %get-tuple-element.82), channel_id=1, source_target_pairs={{0,16},{16,0},{1,17},{17,1},{2,18},{18,2},{3,19},{19,3},{4,20},{20... | collective-permute-start | bytes 393224 | tf_op jit(solution)/shard_map/ppermute | solution.py:63
  156.6 13.1 %all-to-all-start.6 = ((f32[16,8,128]{2,1,0:T(8,128)}), f32[16,8,128]{2,1,0:T(8,128)S(1)}, u32[]{:S(2)}, u32[]{:S(2)}) async-start(f32[16,8,128]{2,1,0:T(8,128)} %coarse_product.1), calls=%async_computation.6 | async-start | bytes 131072 | tf_op jit(solution)/shard_map/all_to_all | solution.py:67
  189.8 10.4 %all-to-all-start.9 = ((f32[16,8,128]{2,1,0:T(8,128)}), f32[16,8,128]{2,1,0:T(8,128)S(1)}, u32[]{:S(2)}, u32[]{:S(2)}) async-start(f32[16,8,128]{2,1,0:T(8,128)} %coarse_coef_of.1), calls=%async_computation.9 | async-start | bytes 131072 | tf_op jit(solution)/shard_map/all_to_all | solution.py:67
  218.5 10.1 %collective-permute-start.7 = (bf16[32,8,1152]{2,1,0:T(8,128)(2,1)S(1)}, bf16[32,8,1152]{2,1,0:T(8,128)(2,1)S(1)}, u32[]{:S(2)}, u32[]{:S(2)}) collective-permute-start(bf16[32,8,1152]{2,1,0:T(8,128)(2,1)S(1)} %all_to_all.64.own_ref), channel_id=1, source_target_pairs={{0,16},{16,0},{1,17},{17,1},{2,18},{18,2},{3,19},{19,3},{4,20},{20... | collective-permute-start | bytes 1769480 | tf_op jit(solution)/shard_map/ppermute | solution.py:63
  239.4 10.2 %all-to-all-start.11 = ((bf16[4,128,256]{2,1,0:T(8,128)(2,1)}), bf16[4,128,256]{2,1,0:T(8,128)(2,1)S(1)}, u32[]{:S(2)}, u32[]{:S(2)}) async-start(bf16[4,128,256]{2,1,0:T(8,128)(2,1)} %product_quarter.1), calls=%async_computation.11 | async-start | bytes 524288 | tf_op jit(solution)/shard_map/all_to_all | solution.py:67

commit v6 on v5

--- a/solution.py
+++ b/solution.py
@@ -118,10 +118,20 @@
     used = 2 * (fine + mid) + sum(2 * rows_of(a.shape[1]) for a in lists)
     above = -(-used // SIDE) * SIDE
 
-    def kernel(fine_ref, mid_ref, *rest):
-        *list_refs, factor_ref, out_ref = rest
+    operands = (points0, points1, *lists, factor)
+    count = len(operands)
+
+    def kernel(*refs):
+        given, out_ref, held, sems = refs[:count], refs[count], refs[count + 1 : -1], refs[-1]
+        copies = [
+            pltpu.make_async_copy(ref, to, sems.at[n]) for n, (ref, to) in enumerate(zip(given, held))
+        ]
+        for copy in copies:
+            copy.start()
+        for copy in copies:
+            copy.wait()
         lines = []
-        for ref in (fine_ref, mid_ref, *list_refs):
+        for ref in held[:-1]:
             whole = ref[...].astype(f32)
             length = whole.shape[1]
             short = -length % TILE
@@ -132,10 +142,19 @@
         if above > used:
             lines.append(jnp.zeros((above - used, TILE), f32))
         out_ref[pl.ds(0, above), :] = jnp.concatenate(lines, axis=0).astype(bf16)
-        out_ref[pl.ds(above, TILE), :] = factor_ref[...]
-
-    shapes = [((above + TILE, TILE), bf16)]
-    return call(kernel, shapes, (points0, points1, *lists, factor), "packed", 8, 1)
+        out_ref[pl.ds(above, TILE), :] = held[-1][...]
+
+    return pl.pallas_call(
+        kernel,
+        out_shape=jax.ShapeDtypeStruct((above + TILE, TILE), bf16),
+        in_specs=[HBM] * count,
+        out_specs=VMEM,
+        scratch_shapes=[pltpu.VMEM(a.shape, a.dtype) for a in operands]
+        + [pltpu.SemaphoreType.DMA((count,))],
+        compiler_params=room(8),
+        cost_estimate=hint(1),
+        name="packed",
+    )(*(pltpu.with_memory_space_constraint(a, pltpu.HBM) for a in operands))
 
 
 def unpacked(there, factor, local, fine, mid, listed):
@@ -399,7 +418,7 @@
 
     return pl.pallas_call(
         kernel,
-        out_shape=jax.ShapeDtypeStruct((rows * TILE, cols * TILE), bf16),
+        out_shape=pltpu.HBM((rows * TILE, cols * TILE), bf16),
         grid=(rows,),
         in_specs=[pl.BlockSpec((2, 1, 1, TILE), lambda i: (0, i, 0, 0)), VMEM],
         out_specs=pl.BlockSpec((TILE, cols * TILE), lambda i: (i, 0)),
@@ -507,11 +526,10 @@
         each = rows // TILE // len(copies)
         for c, copy in enumerate(copies):
             copy.wait()
-            for q in range(c * each, (c + 1) * each):
-                part = jnp.dot(
-                    held[pl.ds(q * TILE, TILE), :], turned_ref[...], preferred_element_type=f32
-                )
-                out_ref[q] = part.T[:BLOCK, :]
+            at = pl.ds(c * each * TILE, each * TILE)
+            part = jnp.dot(held[at, :], turned_ref[...], preferred_element_type=f32)
+            for q in range(each):
+                out_ref[c * each + q] = part[q * TILE : (q + 1) * TILE].T[:BLOCK, :]
 
     shape = (rows // TILE, BLOCK, TILE)
     scratch = [pltpu.VMEM((cols, TILE), bf16)]
@@ -565,10 +583,11 @@
             total += lax.dot_general(
                 half_ref[q], factor_ref[q], (((1,), (1,)), ((), ())), preferred_element_type=f32
             )
+        low = total.astype(bf16)
         for peer in range(peers):
-            out_ref[peer] = total
-
-    shapes = [((peers, BLOCK, TILE), f32)]
+            out_ref[peer] = low
+
+    shapes = [((peers, BLOCK, TILE), bf16)]
     return call(kernel, shapes, (halfway, factor_across), "coarse_coef_of", 8, 1)
 
 
@@ -589,14 +608,12 @@
             copy.wait()
             for q in range(c * each, (c + 1) * each):
                 pair = jnp.concatenate([coef_ref[2 * q], coef_ref[2 * q + 1]], axis=1)
-                total += jnp.dot(
-                    pair.astype(bf16), held[pl.ds(q * two, two), :], preferred_element_type=f32
-                )
+                total += jnp.dot(pair, held[pl.ds(q * two, two), :], preferred_element_type=f32)
         low = (0.5 * mid_ref[...] + scale * total).astype(bf16)
         for chip in range(HALF * LINE):
             out_ref[chip, :, pl.ds(0, cols)] = low
 
-    sent = coarse_coef.reshape(HALF, 2, BLOCK, TILE).astype(bf16)
+    sent = coarse_coef.reshape(HALF, 2, BLOCK, TILE)
     sent = jnp.where(place[3] % 2 == 0, sent[:, 0], sent[:, 1])
     shape = (HALF * LINE, BLOCK, cols + TILE)
     operands = (coarse_coef, sent, mid_data)
@@ -663,8 +680,8 @@
     fine_here = points0.astype(f32).reshape(2, tiles_fine, 1, TILE)
     mid_here = points1.astype(f32).reshape(2, tiles_mid, 1, TILE)
     tail = jnp.pad(own_e1, ((0, BLOCK - own_e1.shape[0]), (0, 0))).astype(bf16)
-    there, vector, local, fine_here, mid_here, tail = lax.optimization_barrier(
-        (there, values.T, local, fine_here, mid_here, tail)
+    there, vector, local, fine_here, mid_here, tail, place = lax.optimization_barrier(
+        (there, values.T, local, fine_here, mid_here, tail, place)
     )
     fine_there, mid_there, lists, common = unpacked(
         there, factor, local, tiles_fine, tiles_mid, first_a1 + 2 * rows_of(listed_a1)

time: 253 us -> 251 us (level)
  local copies, waits for them, and re-layouts: 12.6 us -> 7.06 us
  Pallas kernels: 56.4 us -> 60.8 us
  waiting for transfers between devices: 43.9 us -> 40.2 us
    unnamed x19 -> x5, local copies, waits for them, and re-layouts: 9.36 us -> 3.22 us
    pallas_call x1 -> x2, Pallas kernels: 5.45 us -> 9.58 us  [the longest x1 8.66 us: all_pairs(): pl.pallas_call(kernel, out_shape=pltpu.HBM((rows * TILE, cols * TILE), bf...]
    all_to_all x7, waiting for transfers between devices: 35.7 us -> 32 us  [exchanged(): return lax.all_to_all(x, axes, split_axis=0, concat_axis=0, tiled=True)]
    pallas_call x15 -> x14, Pallas kernels: 44.7 us -> 44 us  [call(): pl.pallas_call(kernel, out_shape=[jax.ShapeDtypeStruct(shape, kind) for s...]
  transfers between devices with their start and end apart: 15 -> 15, of which waited for: 9 -> 9; matrix products, arithmetic and copies ran while one was open for 3% -> 3% of each run, Pallas kernels for 10% -> 11%
where the time goes in v6:
time: 251 us; the launch traced here: 250 us
  starting transfers between devices  69.3 us (28%)
  blocking collectives  64.3 us (26%)
  Pallas kernels  60.8 us (24%)
  waiting for transfers between devices  40.2 us (16%)
  local copies, waits for them, and re-layouts  7.06 us (3%)
  between operations  4.71 us (2%)
  other arithmetic  3.22 us (1%)
    all_to_all x5, blocking collectives, exchanged(): return lax.all_to_all(x, axes, split_axis=0, concat_axis=0, tiled=True)  64.3 us
    pallas_call x14, Pallas kernels, call(): pl.pallas_call(kernel, out_shape=[jax.ShapeDtypeStruct(shape, kind) for s...  44 us
    all_to_all x7, starting transfers between devices, exchanged(): return lax.all_to_all(x, axes, split_axis=0, concat_axis=0, tiled=True)  37.9 us
    all_to_all x7, waiting for transfers between devices, exchanged(): return lax.all_to_all(x, axes, split_axis=0, concat_axis=0, tiled=True)  32 us
    ppermute x5, starting transfers between devices, from_partner(): return lax.ppermute(x, 'k', [(0, 1), (1, 0)])  18 us
    pallas_call x1, Pallas kernels, all_pairs(): pl.pallas_call(kernel, out_shape=pltpu.HBM((rows * TILE, cols * TILE), bf...  8.66 us
    pallas_call x2, Pallas kernels, call_on_matrix(): pl.pallas_call(kernel, out_shape=jax.ShapeDtypeStruct(shape, kind), in_sp...  7.28 us
    ppermute x1, starting transfers between devices, per_device(): swapped = lax.ppermute(summed, 'zh', [(0, 1), (1, 0)])  5.16 us
  transfers between devices with their start and end apart: 15, of which 9 were waited for; matrix products, arithmetic and copies ran while one was open for 3% of the time, Pallas kernels for 11%

profile of v6, /device:TPU:1, one launch (start us, length us, event | category | flops | bytes accessed | tf_op | source)
XLA Modules:
  0.0 249.6 jit_solution(15391803141930197785)
XLA Ops:
  1.6 4.9 %collective-permute-start = (bf16[224,128]{1,0:T(8,128)(2,1)S(1)}, bf16[224,128]{1,0:T(8,128)(2,1)S(1)}, u32[]{:S(2)}, u32[]{:S(2)}) collective-permute-start(bf16[224,128]{1,0:T(8,128)(2,1)S(1)} %packed.1), channel_id=1, source_target_pairs={{0,0},{16,1},{32,2},{48,3},{64,4},{80,5},{96,6},{112,7},{128,8},{1... | collective-permute-start | bytes 172040 | tf_op jit(solution)/shard_map/ppermute | solution.py:48
  12.8 13.5 %all-to-all-start = ((bf16[8,288,128]{2,1,0:T(8,128)(2,1)}), bf16[8,288,128]{2,1,0:T(8,128)(2,1)S(1)}, u32[]{:S(2)}, u32[]{:S(2)}) async-start(bf16[8,288,128]{2,1,0:T(8,128)(2,1)} %get-tuple-element.56), calls=%async_computation | async-start | bytes 1179648 | tf_op jit(solution)/shard_map/all_to_all | solution.py:67
  26.2 17.0 %product_a0.1 = (bf16[8,8,4096]{2,1,0:T(8,128)(2,1)S(1)}, bf16[8,8,4096]{2,1,0:T(8,128)(2,1)S(1)}) custom-call(s32[12,128]{1,0:T(8,128)S(1)} %get-tuple-element.49.list_ref, s32[5]{0:T(128)S(1)} %stack.38.place_ref.core_ref, f32[2,32,1,128]{3,2,1,0:T(1,128)S(1)} %reshape.81.left_ref, f32[2,32,1,128]{3,2,1,0:T(1,128)S(1)} %get-tuple-element.50.right_ref.left_ref, ...), custom_call_target="tpu_custom_call" | custom-call | bytes 60000000 | tf_op jit(solution)/shard_map/product_a0/pallas_call | solution.py:93
  43.3 3.0 %collective-permute-start.1 = (bf16[8,8,4096]{2,1,0:T(8,128)(2,1)S(1)}, bf16[8,8,4096]{2,1,0:T(8,128)(2,1)S(1)}, u32[]{:S(2)}, u32[]{:S(2)}) collective-permute-start(bf16[8,8,4096]{2,1,0:T(8,128)(2,1)S(1)} %get-tuple-element.58), channel_id=1, source_target_pairs={{0,16},{16,0},{1,17},{17,1},{2,18},{18,2},{3,19},{19,3},{4,20},{20... | collective-permute-start | bytes 1572872 | tf_op jit(solution)/shard_map/ppermute | solution.py:63
  49.1 4.0 %all-to-all-start.1 = ((bf16[4,16,4096]{2,1,0:T(8,128)(2,1)}), bf16[4,16,4096]{2,1,0:T(8,128)(2,1)S(1)}, u32[]{:S(2)}, u32[]{:S(2)}) async-start(bf16[4,16,4096]{2,1,0:T(8,128)(2,1)} %bitcast.9), calls=%async_computation.1 | async-start | bytes 1048576 | tf_op jit(solution)/shard_map/all_to_all | solution.py:67
  53.9 8.4 %all-to-all-done.1.arrived_ref = bf16[4,16,4096]{2,1,0:T(8,128)(2,1)S(1)} async-done(((bf16[4,16,4096]{2,1,0:T(8,128)(2,1)}), bf16[4,16,4096]{2,1,0:T(8,128)(2,1)S(1)}, u32[]{:S(2)}, u32[]{:S(2)}) %all-to-all-start.1) | async-done | bytes 524320 | tf_op jit(solution)/shard_map/all_to_all | solution.py:67
  62.3 5.2 %collective-permute-start.3 = (bf16[16,4096]{1,0:T(8,128)(2,1)S(1)}, bf16[16,4096]{1,0:T(8,128)(2,1)S(1)}, u32[]{:S(2)}, u32[]{:S(2)}) collective-permute-start(bf16[16,4096]{1,0:T(8,128)(2,1)S(1)} %sum_of.1.here_ref), channel_id=1, source_target_pairs={{0,32},{32,0},{1,33},{33,1},{2,34},{34,2},{3,35},{35,3},{4,36},{36... | collective-permute-start | bytes 393224 | tf_op jit(solution)/shard_map/ppermute | solution.py:704
  67.5 8.7 %all_pairs.1.matrix_ref = bf16[2048,1024]{1,0:T(8,128)(2,1)} custom-call(f32[2,16,1,128]{3,2,1,0:T(1,128)S(1)} %get-tuple-element.69.left_ref, f32[2,8,1,128]{3,2,1,0:T(1,128)S(1)} %get-tuple-element.70.right_ref), custom_call_target="tpu_custom_call" | custom-call | bytes 18000000 | tf_op jit(solution)/shard_map/all_pairs/pallas_call | solution.py:419
  77.1 3.5 %all-to-all-start.2 = ((bf16[4,16,4224]{2,1,0:T(8,128)(2,1)}), bf16[4,16,4224]{2,1,0:T(8,128)(2,1)S(1)}, u32[]{:S(2)}, u32[]{:S(2)}) async-start(bf16[4,16,4224]{2,1,0:T(8,128)(2,1)} %residual_of.1), calls=%async_computation.2 | async-start | bytes 1081344 | tf_op jit(solution)/shard_map/all_to_all | solution.py:67
  80.6 7.8 %all-to-all-done.2 = bf16[4,16,4224]{2,1,0:T(8,128)(2,1)S(1)} async-done(((bf16[4,16,4224]{2,1,0:T(8,128)(2,1)}), bf16[4,16,4224]{2,1,0:T(8,128)(2,1)S(1)}, u32[]{:S(2)}, u32[]{:S(2)}) %all-to-all-start.2) | async-done | bytes 540704 | tf_op jit(solution)/shard_map/all_to_all | solution.py:67
  88.4 2.8 %collective-permute-start.4 = (bf16[8,8,4224]{2,1,0:T(8,128)(2,1)S(1)}, bf16[8,8,4224]{2,1,0:T(8,128)(2,1)S(1)}, u32[]{:S(2)}, u32[]{:S(2)}) collective-permute-start(bf16[8,8,4224]{2,1,0:T(8,128)(2,1)S(1)} %bitcast.58), channel_id=1, source_target_pairs={{0,16},{16,0},{1,17},{17,1},{2,18},{18,2},{3,19},{19,3},{4,20},{20... | collective-permute-start | bytes 1622024 | tf_op jit(solution)/shard_map/ppermute | solution.py:63
  92.7 8.1 %product.2 = bf16[16,8,1152]{2,1,0:T(8,128)(2,1)S(1)} custom-call(s32[12,128]{1,0:T(8,128)S(1)} %get-tuple-element.49.list_ref, f32[2,32,1,128]{3,2,1,0:T(1,128)S(1)} %get-tuple-element.50.right_ref.left_ref, f32[2,8,1,128]{3,2,1,0:T(1,128)S(1)} %reshape.83.right_ref.left_ref, bf16[8,8,4224]{2,1,0:T(8,128)(2,1)S(1)} %bitcast.59, ...), custom_call_target="tpu_custom_call" | custom-call | bytes 26666666 | tf_op jit(solution)/shard_map/product/pallas_call | solution.py:93
  100.8 13.5 %all_to_all.60.arrived_ref = bf16[16,8,1152]{2,1,0:T(8,128)(2,1)S(1)} all-to-all(bf16[16,8,1152]{2,1,0:T(8,128)(2,1)S(1)} %product.2), channel_id=1, replica_groups=mesh['y'=4,'zh'=2,'k'=2,'x'=4,'zl'=4] {'x','zl'}, dimensions={0} | all-to-all | bytes 589824 | tf_op jit(solution)/shard_map/all_to_all | solution.py:67
  115.1 3.9 %all-to-all-start.4 = ((bf16[16,8,1024]{2,1,0:T(8,128)(2,1)}), bf16[16,8,1024]{2,1,0:T(8,128)(2,1)S(1)}, u32[]{:S(2)}, u32[]{:S(2)}) async-start(bf16[16,8,1024]{2,1,0:T(8,128)(2,1)} %get-tuple-element.76), calls=%async_computation.4 | async-start | bytes 524288 | tf_op jit(solution)/shard_map/all_to_all | solution.py:67
  119.0 3.3 %collective-permute-start.5 = (f32[8,1024]{1,0:T(8,128)S(1)}, f32[8,1024]{1,0:T(8,128)S(1)}, u32[]{:S(2)}, u32[]{:S(2)}) collective-permute-start(f32[8,1024]{1,0:T(8,128)S(1)} %get-tuple-element.77), channel_id=1, source_target_pairs={{0,0},{24,1},{32,2},{56,3},{64,4},{88,5},{96,6},{120,7},{128,8},{1... | collective-permute-start | bytes 98312 | tf_op jit(solution)/shard_map/ppermute | solution.py:59
  123.5 4.1 %collective-permute-done.5.mid_ref = f32[8,1024]{1,0:T(8,128)S(1)} collective-permute-done((f32[8,1024]{1,0:T(8,128)S(1)}, f32[8,1024]{1,0:T(8,128)S(1)}, u32[]{:S(2)}, u32[]{:S(2)}) %collective-permute-start.5) | collective-permute-done | bytes 32800 | tf_op jit(solution)/shard_map/ppermute | solution.py:59
  127.6 2.4 product.3
  130.1 3.6 %collective-permute-start.6 = (bf16[8,8,1024]{2,1,0:T(8,128)(2,1)S(1)}, bf16[8,8,1024]{2,1,0:T(8,128)(2,1)S(1)}, u32[]{:S(2)}, u32[]{:S(2)}) collective-permute-start(bf16[8,8,1024]{2,1,0:T(8,128)(2,1)S(1)} %get-tuple-element.84), channel_id=1, source_target_pairs={{0,16},{16,0},{1,17},{17,1},{2,18},{18,2},{3,19},{19,3},{4,20},{20... | collective-permute-start | bytes 393224 | tf_op jit(solution)/shard_map/ppermute | solution.py:63
  134.7 16.0 %all_to_all.61.arrived_ref = bf16[8,8,1024]{2,1,0:T(8,128)(2,1)S(1)} all-to-all(bf16[8,8,1024]{2,1,0:T(8,128)(2,1)S(1)} %add_convert_fusion.1), channel_id=1, replica_groups=mesh['y'=4,'zh'=2,'k'=2,'x'=4,'zl'=4] {'y','zh'}, dimensions={0} | all-to-all | bytes 262144 | tf_op jit(solution)/shard_map/all_to_all | solution.py:67
  150.7 4.8 %coarse_product.1 = f32[16,8,128]{2,1,0:T(8,128)} custom-call(bf16[2048,1024]{1,0:T(8,128)(2,1)} %all_pairs.1.matrix_ref, bf16[8,8,1024]{2,1,0:T(8,128)(2,1)S(1)} %all_to_all.61.arrived_ref, f32[8,1024]{1,0:T(8,128)S(1)} %collective-permute-done.5.mid_ref), custom_call_target="tpu_custom_call" | custom-call | bytes 9000000 | tf_op jit(solution)/shard_map/coarse_product/pallas_call | solution.py:497
  155.5 6.2 %all-to-all-start.6 = ((f32[16,8,128]{2,1,0:T(8,128)}), f32[16,8,128]{2,1,0:T(8,128)S(1)}, u32[]{:S(2)}, u32[]{:S(2)}) async-start(f32[16,8,128]{2,1,0:T(8,128)} %coarse_product.1), calls=%async_computation.6 | async-start | bytes 131072 | tf_op jit(solution)/shard_map/all_to_all | solution.py:67
  161.7 7.0 %all-to-all-done.6.arrived_ref = f32[16,8,128]{2,1,0:T(8,128)S(1)} async-done(((f32[16,8,128]{2,1,0:T(8,128)}), f32[16,8,128]{2,1,0:T(8,128)S(1)}, u32[]{:S(2)}, u32[]{:S(2)}) %all-to-all-start.6) | async-done | bytes 65568 | tf_op jit(solution)/shard_map/all_to_all | solution.py:67
  168.7 9.6 %all_to_all.62.data_ref = bf16[16,2,8,128]{3,2,1,0:T(8,128)(2,1)S(1)} all-to-all(bf16[16,2,8,128]{3,2,1,0:T(8,128)(2,1)S(1)} %coarse_data_of.1), channel_id=1, replica_groups=mesh['y'=4,'zh'=2,'k'=2,'x'=4,'zl'=4] {'x','zl'}, dimensions={0} | all-to-all | bytes 131072 | tf_op jit(solution)/shard_map/all_to_all | solution.py:67
  178.5 9.4 %all_to_all.63.half_ref = bf16[16,8,128]{2,1,0:T(8,128)(2,1)S(1)} all-to-all(bf16[16,8,128]{2,1,0:T(8,128)(2,1)S(1)} %halfway_of.1), channel_id=1, replica_groups=mesh['y'=4,'zh'=2,'k'=2,'x'=4,'zl'=4] {'x','zl'}, dimensions={0} | all-to-all | bytes 65536 | tf_op jit(solution)/shard_map/all_to_all | solution.py:67
  188.9 3.5 %all-to-all-start.9 = ((bf16[16,8,128]{2,1,0:T(8,128)(2,1)}), bf16[16,8,128]{2,1,0:T(8,128)(2,1)S(1)}, u32[]{:S(2)}, u32[]{:S(2)}) async-start(bf16[16,8,128]{2,1,0:T(8,128)(2,1)} %coarse_coef_of.1), calls=%async_computation.9 | async-start | bytes 65536 | tf_op jit(solution)/shard_map/all_to_all | solution.py:67
  194.9 4.3 %all-to-all-done.9.coef_ref = bf16[16,8,128]{2,1,0:T(8,128)(2,1)S(1)} async-done(((bf16[16,8,128]{2,1,0:T(8,128)(2,1)}), bf16[16,8,128]{2,1,0:T(8,128)(2,1)S(1)}, u32[]{:S(2)}, u32[]{:S(2)}) %all-to-all-start.9) | async-done | bytes 32800 | tf_op jit(solution)/shard_map/all_to_all | solution.py:67
  199.2 2.5 prolong.1
  201.7 15.8 %all_to_all.64.own_ref = bf16[32,8,1152]{2,1,0:T(8,128)(2,1)S(1)} all-to-all(bf16[32,8,1152]{2,1,0:T(8,128)(2,1)S(1)} %prolong.1), channel_id=1, replica_groups=mesh['y'=4,'zh'=2,'k'=2,'x'=4,'zl'=4] {'y','zh','zl'}, dimensions={0} | all-to-all | bytes 1179648 | tf_op jit(solution)/shard_map/all_to_all | solution.py:67
  217.4 8.2 %collective-permute-start.7 = (bf16[32,8,1152]{2,1,0:T(8,128)(2,1)S(1)}, bf16[32,8,1152]{2,1,0:T(8,128)(2,1)S(1)}, u32[]{:S(2)}, u32[]{:S(2)}) collective-permute-start(bf16[32,8,1152]{2,1,0:T(8,128)(2,1)S(1)} %all_to_all.64.own_ref), channel_id=1, source_target_pairs={{0,16},{16,0},{1,17},{17,1},{2,18},{18,2},{3,19},{19,3},{4,20},{20... | collective-permute-start | bytes 1769480 | tf_op jit(solution)/shard_map/ppermute | solution.py:63
  228.7 9.3 %product_quarter.1 = bf16[4,128,256]{2,1,0:T(8,128)(2,1)} custom-call(s32[8,256]{1,0:T(8,128)S(1)} %quarter_of.1.list_ref, f32[2,32,1,128]{3,2,1,0:T(1,128)S(1)} %get-tuple-element.79.left_ref, f32[2,9,1,128]{3,2,1,0:T(1,128)S(1)} %pad.16.right_ref, bf16[32,8,1152]{2,1,0:T(8,128)(2,1)S(1)} %all_to_all.64.own_ref, ...), custom_call_target="tpu_custom_call" | custom-call | bytes 30000000 | tf_op jit(solution)/shard_map/product_quarter/pallas_call | solution.py:93
  237.9 3.4 %all-to-all-start.11 = ((bf16[4,128,256]{2,1,0:T(8,128)(2,1)}), bf16[4,128,256]{2,1,0:T(8,128)(2,1)S(1)}, u32[]{:S(2)}, u32[]{:S(2)}) async-start(bf16[4,128,256]{2,1,0:T(8,128)(2,1)} %product_quarter.1), calls=%async_computation.11 | async-start | bytes 524288 | tf_op jit(solution)/shard_map/all_to_all | solution.py:67
  242.5 4.7 %all-to-all-done.11.arrived_ref = bf16[4,128,256]{2,1,0:T(8,128)(2,1)S(1)} async-done(((bf16[4,128,256]{2,1,0:T(8,128)(2,1)}), bf16[4,128,256]{2,1,0:T(8,128)(2,1)S(1)}, u32[]{:S(2)}, u32[]{:S(2)}) %all-to-all-start.11) | async-done | bytes 262176 | tf_op jit(solution)/shard_map/all_to_all | solution.py:67
  (57 shorter events, 22.9 us)
Async XLA Ops:
  0.6 11.2 %copy-start = (bf16[128,128]{1,0:T(8,128)(2,1)S(1)}, bf16[128,128]{1,0:T(8,128)(2,1)}, u32[]{:S(2)}) copy-start(bf16[128,128]{1,0:T(8,128)(2,1)} %factor_ref.1) | copy-start | bytes 98308
  1.6 10.2 %collective-permute-start = (bf16[224,128]{1,0:T(8,128)(2,1)S(1)}, bf16[224,128]{1,0:T(8,128)(2,1)S(1)}, u32[]{:S(2)}, u32[]{:S(2)}) collective-permute-start(bf16[224,128]{1,0:T(8,128)(2,1)S(1)} %packed.1), channel_id=1, source_target_pairs={{0,0},{16,1},{32,2},{48,3},{64,4},{80,5},{96,6},{112,7},{128,8},{1... | collective-permute-start | bytes 172040 | tf_op jit(solution)/shard_map/ppermute | solution.py:48
  12.8 30.5 %all-to-all-start = ((bf16[8,288,128]{2,1,0:T(8,128)(2,1)}), bf16[8,288,128]{2,1,0:T(8,128)(2,1)S(1)}, u32[]{:S(2)}, u32[]{:S(2)}) async-start(bf16[8,288,128]{2,1,0:T(8,128)(2,1)} %get-tuple-element.56), calls=%async_computation | async-start | bytes 1179648 | tf_op jit(solution)/shard_map/all_to_all | solution.py:67
  43.3 4.5 %collective-permute-start.1 = (bf16[8,8,4096]{2,1,0:T(8,128)(2,1)S(1)}, bf16[8,8,4096]{2,1,0:T(8,128)(2,1)S(1)}, u32[]{:S(2)}, u32[]{:S(2)}) collective-permute-start(bf16[8,8,4096]{2,1,0:T(8,128)(2,1)S(1)} %get-tuple-element.58), channel_id=1, source_target_pairs={{0,16},{16,0},{1,17},{17,1},{2,18},{18,2},{3,19},{19,3},{4,20},{20... | collective-permute-start | bytes 1572872 | tf_op jit(solution)/shard_map/ppermute | solution.py:63
  48.7 4.4 %collective-permute-start.2 = (bf16[8,288,128]{2,1,0:T(8,128)(2,1)S(1)}, bf16[8,288,128]{2,1,0:T(8,128)(2,1)S(1)}, u32[]{:S(2)}, u32[]{:S(2)}) collective-permute-start(bf16[8,288,128]{2,1,0:T(8,128)(2,1)S(1)} %all-to-all-done.own_ref), channel_id=1, source_target_pairs={{0,16},{16,0},{1,17},{17,1},{2,18},{18,2},{3,19},{19,3},{4,20},{20... | collective-permute-start | bytes 1769480 | tf_op jit(solution)/shard_map/ppermute | solution.py:63
  49.1 13.2 %all-to-all-start.1 = ((bf16[4,16,4096]{2,1,0:T(8,128)(2,1)}), bf16[4,16,4096]{2,1,0:T(8,128)(2,1)S(1)}, u32[]{:S(2)}, u32[]{:S(2)}) async-start(bf16[4,16,4096]{2,1,0:T(8,128)(2,1)} %bitcast.9), calls=%async_computation.1 | async-start | bytes 1048576 | tf_op jit(solution)/shard_map/all_to_all | solution.py:67
  62.3 13.8 %collective-permute-start.3 = (bf16[16,4096]{1,0:T(8,128)(2,1)S(1)}, bf16[16,4096]{1,0:T(8,128)(2,1)S(1)}, u32[]{:S(2)}, u32[]{:S(2)}) collective-permute-start(bf16[16,4096]{1,0:T(8,128)(2,1)S(1)} %sum_of.1.here_ref), channel_id=1, source_target_pairs={{0,32},{32,0},{1,33},{33,1},{2,34},{34,2},{3,35},{35,3},{4,36},{36... | collective-permute-start | bytes 393224 | tf_op jit(solution)/shard_map/ppermute | solution.py:704
  77.1 11.3 %all-to-all-start.2 = ((bf16[4,16,4224]{2,1,0:T(8,128)(2,1)}), bf16[4,16,4224]{2,1,0:T(8,128)(2,1)S(1)}, u32[]{:S(2)}, u32[]{:S(2)}) async-start(bf16[4,16,4224]{2,1,0:T(8,128)(2,1)} %residual_of.1), calls=%async_computation.2 | async-start | bytes 1081344 | tf_op jit(solution)/shard_map/all_to_all | solution.py:67
  88.4 4.3 %collective-permute-start.4 = (bf16[8,8,4224]{2,1,0:T(8,128)(2,1)S(1)}, bf16[8,8,4224]{2,1,0:T(8,128)(2,1)S(1)}, u32[]{:S(2)}, u32[]{:S(2)}) collective-permute-start(bf16[8,8,4224]{2,1,0:T(8,128)(2,1)S(1)} %bitcast.58), channel_id=1, source_target_pairs={{0,16},{16,0},{1,17},{17,1},{2,18},{18,2},{3,19},{19,3},{4,20},{20... | collective-permute-start | bytes 1622024 | tf_op jit(solution)/shard_map/ppermute | solution.py:63
  115.1 12.6 %all-to-all-start.4 = ((bf16[16,8,1024]{2,1,0:T(8,128)(2,1)}), bf16[16,8,1024]{2,1,0:T(8,128)(2,1)S(1)}, u32[]{:S(2)}, u32[]{:S(2)}) async-start(bf16[16,8,1024]{2,1,0:T(8,128)(2,1)} %get-tuple-element.76), calls=%async_computation.4 | async-start | bytes 524288 | tf_op jit(solution)/shard_map/all_to_all | solution.py:67
  119.0 8.6 %collective-permute-start.5 = (f32[8,1024]{1,0:T(8,128)S(1)}, f32[8,1024]{1,0:T(8,128)S(1)}, u32[]{:S(2)}, u32[]{:S(2)}) collective-permute-start(f32[8,1024]{1,0:T(8,128)S(1)} %get-tuple-element.77), channel_id=1, source_target_pairs={{0,0},{24,1},{32,2},{56,3},{64,4},{88,5},{96,6},{120,7},{128,8},{1... | collective-permute-start | bytes 98312 | tf_op jit(solution)/shard_map/ppermute | solution.py:59
  130.1 4.6 %collective-permute-start.6 = (bf16[8,8,1024]{2,1,0:T(8,128)(2,1)S(1)}, bf16[8,8,1024]{2,1,0:T(8,128)(2,1)S(1)}, u32[]{:S(2)}, u32[]{:S(2)}) collective-permute-start(bf16[8,8,1024]{2,1,0:T(8,128)(2,1)S(1)} %get-tuple-element.84), channel_id=1, source_target_pairs={{0,16},{16,0},{1,17},{17,1},{2,18},{18,2},{3,19},{19,3},{4,20},{20... | collective-permute-start | bytes 393224 | tf_op jit(solution)/shard_map/ppermute | solution.py:63
  155.5 13.2 %all-to-all-start.6 = ((f32[16,8,128]{2,1,0:T(8,128)}), f32[16,8,128]{2,1,0:T(8,128)S(1)}, u32[]{:S(2)}, u32[]{:S(2)}) async-start(f32[16,8,128]{2,1,0:T(8,128)} %coarse_product.1), calls=%async_computation.6 | async-start | bytes 131072 | tf_op jit(solution)/shard_map/all_to_all | solution.py:67
  188.9 10.3 %all-to-all-start.9 = ((bf16[16,8,128]{2,1,0:T(8,128)(2,1)}), bf16[16,8,128]{2,1,0:T(8,128)(2,1)S(1)}, u32[]{:S(2)}, u32[]{:S(2)}) async-start(bf16[16,8,128]{2,1,0:T(8,128)(2,1)} %coarse_coef_of.1), calls=%async_computation.9 | async-start | bytes 65536 | tf_op jit(solution)/shard_map/all_to_all | solution.py:67
  217.4 10.3 %collective-permute-start.7 = (bf16[32,8,1152]{2,1,0:T(8,128)(2,1)S(1)}, bf16[32,8,1152]{2,1,0:T(8,128)(2,1)S(1)}, u32[]{:S(2)}, u32[]{:S(2)}) collective-permute-start(bf16[32,8,1152]{2,1,0:T(8,128)(2,1)S(1)} %all_to_all.64.own_ref), channel_id=1, source_target_pairs={{0,16},{16,0},{1,17},{17,1},{2,18},{18,2},{3,19},{19,3},{4,20},{20... | collective-permute-start | bytes 1769480 | tf_op jit(solution)/shard_map/ppermute | solution.py:63
  237.9 9.2 %all-to-all-start.11 = ((bf16[4,128,256]{2,1,0:T(8,128)(2,1)}), bf16[4,128,256]{2,1,0:T(8,128)(2,1)S(1)}, u32[]{:S(2)}, u32[]{:S(2)}) async-start(bf16[4,128,256]{2,1,0:T(8,128)(2,1)} %product_quarter.1), calls=%async_computation.11 | async-start | bytes 524288 | tf_op jit(solution)/shard_map/all_to_all | solution.py:67

commit v7 on v6

--- a/solution.py
+++ b/solution.py
@@ -321,24 +321,23 @@
     return call(kernel, shapes, operands, "product", 16, listed / 18, scratch, 1)
 
 
-def quarter_of(lists, place, blocks, listed, tiles):
+def quarter_of(lists, place, blocks, listed):
     held = rows_of(listed)
-    size = rows_of(LINE * QUARTER * tiles) * TILE
 
     def kernel(place_ref, list_ref, out_ref):
         zl = place_ref[3]
         row = lax.broadcasted_iota(jnp.int32, (TILE, TILE), 0)
         col = lax.broadcasted_iota(jnp.int32, (TILE, TILE), 1)
         before = (row < col).astype(bf16)
-        slot = lax.broadcasted_iota(jnp.int32, (size, TILE), 0).astype(f32)
+        slot = row.astype(f32)
         lane = lax.broadcasted_iota(jnp.int32, (1, TILE), 1)
-        count = jnp.zeros((1, 1), f32)
-        total = jnp.zeros((BLOCK, size), f32)
         for block in range(blocks):
+            count = jnp.zeros((1, 1), f32)
+            total = jnp.zeros((BLOCK, TILE), f32)
             for part in range(held):
                 at = block * 2 * held + part
                 i = list_ref[at : at + 1, :]
-                j = list_ref[at + held : at + held + 1, :] + block * tiles
+                j = list_ref[at + held : at + held + 1, :]
                 real = jnp.where(lane + part * TILE < listed, 1.0, 0.0)
                 flag = jnp.where(((i >> 1) & (LINE - 1)) == zl, real, 0.0)
                 rank = count + jnp.dot(
@@ -354,55 +353,85 @@
                     lines, here, (((1,), (1,)), ((), ())), preferred_element_type=f32
                 )
                 count += jnp.sum(flag, axis=1, keepdims=True)
-        slots = lax.broadcasted_iota(jnp.int32, (1, size), 1).astype(f32)
-        out_ref[0:1, :] = jnp.where(slots < count, total[0:1], float(QUARTER)).astype(jnp.int32)
-        out_ref[1:2, :] = total[1:2].astype(jnp.int32)
-        groups = ((count + (GROUP - 1)) * (1.0 / GROUP)).astype(jnp.int32)
-        out_ref[2:3, :] = jnp.broadcast_to(groups, (1, size))
-        out_ref[3:, :] = jnp.zeros((BLOCK - 3, size), jnp.int32)
-
-    shapes = [((BLOCK, size), jnp.int32)]
+            at = pl.ds(block * TILE, TILE)
+            rows = jnp.where(lane.astype(f32) < count, total[0:1], float(QUARTER))
+            groups = jnp.broadcast_to((count + (GROUP - 1)) * (1.0 / GROUP), (1, TILE))
+            out_ref[0:1, at] = rows.astype(jnp.int32)
+            out_ref[1:2, at] = total[1:2].astype(jnp.int32)
+            out_ref[2:3, at] = groups.astype(jnp.int32)
+            out_ref[3:, at] = jnp.zeros((BLOCK - 3, TILE), jnp.int32)
+
+    shapes = [((BLOCK, blocks * TILE), jnp.int32)]
     return call(kernel, shapes, (place, lists), "quarter_of", 8, 3, (), 1)
 
 
-def product_quarter(lists, left, right, own, other, support):
-    tiles = right.shape[1]
-    length = left.shape[1] * TILE // LINE
-
-    def kernel(list_ref, left_ref, right_ref, own_ref, other_ref, out_ref, left, right, vector, total):
+def dense_block(lists, block, left, right, support):
+    cols, rows = left.shape[1], right.shape[1]
+
+    def kernel(list_ref, left_ref, right_ref, out_ref, left, right):
         set_points(left_ref, right_ref, left, right, support)
-        total[...] = jnp.zeros_like(total)
+        out_ref[...] = jnp.zeros_like(out_ref)
+
+        def step(g, carry):
+            for u in range(GROUP):
+                i = list_ref[0, block * TILE + g * GROUP + u]
+                j = list_ref[1, block * TILE + g * GROUP + u]
+                out_ref[at_tile(j), at_tile(i)] = wendland(
+                    (left[0, j], left[1, j]), (right[0, i], right[1, i]), support
+                )
+            return carry
+
+        lax.fori_loop(0, list_ref[2, block * TILE], step, 0)
+
+    shapes = [((cols * TILE, rows * TILE), bf16)]
+    scratch = point_scratch(cols, rows)
+    return call(kernel, shapes, (lists, left, right), "dense_block", 12, 3, scratch, 1)
+
+
+def product_dense(matrices, own, other):
+    count = len(matrices)
+    length, width = matrices[0].shape
+    size = QUARTER * TILE
+
+    def kernel(*refs):
+        given, (own_ref, other_ref, out_ref, held, sems, vector, total) = refs[:count], refs[count:]
+        copies = [pltpu.make_async_copy(given[q], held.at[q], sems.at[q]) for q in range(count)]
+        for copy in copies:
+            copy.start()
         for ref, first in ((own_ref, 0), (other_ref, FIELDS // 2)):
             for chip in range(HALF):
                 for zl in range(LINE):
                     at = pl.ds(first + chip * BLOCK, BLOCK)
                     part = ref[chip * LINE + zl, :, pl.ds(0, length)]
                     vector[at, pl.ds(zl * length, length)] = part
-
-        def step(g, carry):
-            products = []
-            for u in range(GROUP):
-                i = list_ref[0, g * GROUP + u]
-                j = list_ref[1, g * GROUP + u]
-                tile = wendland((left[0, j], left[1, j]), (right[0, i], right[1, i]), support)
-                product = jnp.dot(vector[:, at_tile(j)], tile, preferred_element_type=f32)
-                products.append((i, product))
-            for i, product in products:
-                total[i] += product
-            return carry
-
-        lax.fori_loop(0, list_ref[2, 0], step, 0)
-        for i in range(QUARTER):
-            out_ref[i // 2, :, pl.ds(i % 2 * TILE, TILE)] = total[i].astype(bf16)
-
-    scratch = [
-        *point_scratch(left.shape[1], tiles),
-        pltpu.VMEM((FIELDS, length * LINE), bf16),
-        pltpu.VMEM((tiles, FIELDS, TILE), f32),
-    ]
-    operands = (lists, left, right, own, other)
-    shapes = [((QUARTER // 2, FIELDS, 2 * TILE), bf16)]
-    return call(kernel, shapes, operands, "product_quarter", 20, 10, scratch, 1)
+        for q, copy in enumerate(copies):
+            copy.wait()
+            lines = vector[:, pl.ds(q * length, length)]
+            for t in range(0, size, 2 * TILE):
+                at = pl.ds(t, 2 * TILE)
+                part = jnp.dot(lines, held[q, :, at], preferred_element_type=f32)
+                if q == 0:
+                    total[:, at] = part
+                elif q < count - 1:
+                    total[:, at] += part
+                else:
+                    out_ref[t // (2 * TILE)] = (total[:, at] + part).astype(bf16)
+
+    return pl.pallas_call(
+        kernel,
+        out_shape=jax.ShapeDtypeStruct((QUARTER // 2, FIELDS, 2 * TILE), bf16),
+        in_specs=[HBM] * count + [VMEM] * 2,
+        out_specs=VMEM,
+        scratch_shapes=[
+            pltpu.VMEM((count, length, width), bf16),
+            pltpu.SemaphoreType.DMA((count,)),
+            pltpu.VMEM((FIELDS, count * length), bf16),
+            pltpu.VMEM((FIELDS, size), f32),
+        ],
+        compiler_params=room(20),
+        cost_estimate=hint(4),
+        name="product_dense",
+    )(*(pltpu.with_memory_space_constraint(m, pltpu.HBM) for m in matrices), own, other)
 
 
 def all_pairs(left, right, support):
@@ -418,7 +447,7 @@
 
     return pl.pallas_call(
         kernel,
-        out_shape=pltpu.HBM((rows * TILE, cols * TILE), bf16),
+        out_shape=jax.ShapeDtypeStruct((rows * TILE, cols * TILE), bf16),
         grid=(rows,),
         in_specs=[pl.BlockSpec((2, 1, 1, TILE), lambda i: (0, i, 0, 0)), VMEM],
         out_specs=pl.BlockSpec((TILE, cols * TILE), lambda i: (i, 0)),
@@ -526,10 +555,11 @@
         each = rows // TILE // len(copies)
         for c, copy in enumerate(copies):
             copy.wait()
-            at = pl.ds(c * each * TILE, each * TILE)
-            part = jnp.dot(held[at, :], turned_ref[...], preferred_element_type=f32)
-            for q in range(each):
-                out_ref[c * each + q] = part[q * TILE : (q + 1) * TILE].T[:BLOCK, :]
+            for q in range(c * each, (c + 1) * each):
+                part = jnp.dot(
+                    held[pl.ds(q * TILE, TILE), :], turned_ref[...], preferred_element_type=f32
+                )
+                out_ref[q] = part.T[:BLOCK, :]
 
     shape = (rows // TILE, BLOCK, TILE)
     scratch = [pltpu.VMEM((cols, TILE), bf16)]
@@ -722,7 +752,7 @@
     mid_share, mid_all = mid_of(restricted, scale_e1)
     line_lists = lax.dynamic_slice_in_dim(restricted[:, :, rows_mid:], x_id * LINE, LINE, 0)
     line_lists = line_lists[:, : own_e1.shape[0]].reshape(-1, TILE).astype(jnp.int32)
-    line_lists = quarter_of(line_lists, place, LINE, listed_e1, tiles_mid)
+    line_lists = quarter_of(line_lists, place, LINE, listed_e1)
     mid_all, mid_data, line_lists = lax.optimization_barrier(
         (exchanged(mid_all, COL), turned_blocks(mid_share), line_lists)
     )
@@ -731,19 +761,33 @@
     mid_own, mid_other = product(
         lists, listed_a1, first_a1, 1, mid_here, mid_there, mid_halves, support_mid
     )
-    arrived = exchanged(pair_sum(mid_own, mid_other), YZ)
-
-    coarse_part = coarse_product(coarse_kernel, arrived, mid_data, scale_a1)
-    coarse_data = coarse_data_of(exchanged(coarse_part, COL), fine_own, fine_other, scale_e2)
-    coarse_data = exchanged(coarse_data, COL)
+    def e1_block(lists, q):
+        points = mid_line[:, q * tiles_mid : (q + 1) * tiles_mid]
+        return dense_block(lists, q, points, fine_quarter, support_mid)
+
+    pair, lists_then = lax.optimization_barrier((pair_sum(mid_own, mid_other), line_lists))
+    arrived, *first_two = lax.optimization_barrier(
+        (exchanged(pair, YZ), e1_block(lists_then, 0), e1_block(lists_then, 1))
+    )
+    coarse_part, lists_then = lax.optimization_barrier(
+        (coarse_product(coarse_kernel, arrived, mid_data, scale_a1), line_lists)
+    )
+    arrived, third = lax.optimization_barrier(
+        (exchanged(coarse_part, COL), e1_block(lists_then, 2))
+    )
+    coarse_data, lists_then = lax.optimization_barrier(
+        (coarse_data_of(arrived, fine_own, fine_other, scale_e2), line_lists)
+    )
+    coarse_data, fourth = lax.optimization_barrier(
+        (exchanged(coarse_data, COL), e1_block(lists_then, 3))
+    )
     halfway = exchanged(halfway_of(coarse_data, factor_down), COL)
     coarse_all = exchanged(coarse_coef_of(halfway, factor_across), COL)
 
     new_own = exchanged(prolong(coarse_kernel, coarse_all, place, mid_data, scale_e2), YZL)
     new_other = from_partner(new_own)
-    fine_part = product_quarter(
-        line_lists, mid_line, fine_quarter, new_own, new_other, support_mid
-    )
+    fine_part = product_dense((*first_two, third, fourth), new_own, new_other)
+    fine_part, new_own, new_other = lax.optimization_barrier((fine_part, new_own, new_other))
     own_data = lax.dynamic_slice_in_dim(values, col_id * share, share, 0)
     fine_coef = fine_of(exchanged(fine_part, "x"), own_data, place, scale_e1)
 

time: 251 us -> 253 us (level)
  blocking collectives: 64.3 us -> 46.5 us
  starting transfers between devices: 69.3 us -> 77.2 us
  local copies, waits for them, and re-layouts: 7.06 us -> 14.8 us
  Pallas kernels: 60.8 us -> 64.8 us
    all_to_all x5 -> x3, blocking collectives: 64.3 us -> 46.5 us  [exchanged(): return lax.all_to_all(x, axes, split_axis=0, concat_axis=0, tiled=True)]
    all_to_all x7 -> x9, starting transfers between devices: 37.9 us -> 47.8 us  [exchanged(): return lax.all_to_all(x, axes, split_axis=0, concat_axis=0, tiled=True)]
    unnamed x5 -> x15, local copies, waits for them, and re-layouts: 3.22 us -> 10.9 us
    pallas_call x14 -> x17, Pallas kernels: 44 us -> 47.3 us  [call(): pl.pallas_call(kernel, out_shape=[jax.ShapeDtypeStruct(shape, kind) for s...]
    pallas_call x1 -> x2, Pallas kernels: 8.66 us -> 10.4 us  [the longest x1 5.45 us: all_pairs(): pl.pallas_call(kernel, out_shape=jax.ShapeDtypeStruct((rows * TILE, cols...]
    all_to_all x7 -> x9, waiting for transfers between devices: 32 us -> 30.9 us  [exchanged(): return lax.all_to_all(x, axes, split_axis=0, concat_axis=0, tiled=True)]
  transfers between devices with their start and end apart: 15 -> 17, of which waited for: 9 -> 11; matrix products, arithmetic and copies ran while one was open for 3% -> 4% of each run, Pallas kernels for 11% -> 14%
where the time goes in v7:
time: 253 us; the launch traced here: 251 us
  starting transfers between devices  77.2 us (31%)
  Pallas kernels  64.8 us (26%)
  blocking collectives  46.5 us (18%)
  waiting for transfers between devices  39.2 us (15%)
  local copies, waits for them, and re-layouts  14.8 us (6%)
  between operations  4.75 us (2%)
  other arithmetic  3.87 us (2%)
    all_to_all x9, starting transfers between devices, exchanged(): return lax.all_to_all(x, axes, split_axis=0, concat_axis=0, tiled=True)  47.8 us
    pallas_call x17, Pallas kernels, call(): pl.pallas_call(kernel, out_shape=[jax.ShapeDtypeStruct(shape, kind) for s...  47.3 us
    all_to_all x3, blocking collectives, exchanged(): return lax.all_to_all(x, axes, split_axis=0, concat_axis=0, tiled=True)  46.5 us
    all_to_all x9, waiting for transfers between devices, exchanged(): return lax.all_to_all(x, axes, split_axis=0, concat_axis=0, tiled=True)  30.9 us
    ppermute x5, starting transfers between devices, from_partner(): return lax.ppermute(x, 'k', [(0, 1), (1, 0)])  16 us
    unnamed x15, local copies, waits for them, and re-layouts  10.9 us
    pallas_call x2, Pallas kernels, call_on_matrix(): pl.pallas_call(kernel, out_shape=jax.ShapeDtypeStruct(shape, kind), in_sp...  6.23 us
    pallas_call x1, Pallas kernels, all_pairs(): pl.pallas_call(kernel, out_shape=jax.ShapeDtypeStruct((rows * TILE, cols...  5.45 us
  transfers between devices with their start and end apart: 17, of which 11 were waited for; matrix products, arithmetic and copies ran while one was open for 4% of the time, Pallas kernels for 14%

profile of v7, /device:TPU:1, one launch (start us, length us, event | category | flops | bytes accessed | tf_op | source)
XLA Modules:
  0.0 251.2 jit_solution(7116720416225745017)
XLA Ops:
  1.6 4.9 %collective-permute-start = (bf16[224,128]{1,0:T(8,128)(2,1)S(1)}, bf16[224,128]{1,0:T(8,128)(2,1)S(1)}, u32[]{:S(2)}, u32[]{:S(2)}) collective-permute-start(bf16[224,128]{1,0:T(8,128)(2,1)S(1)} %packed.1), channel_id=1, source_target_pairs={{0,0},{16,1},{32,2},{48,3},{64,4},{80,5},{96,6},{112,7},{128,8},{1... | collective-permute-start | bytes 172040 | tf_op jit(solution)/shard_map/ppermute | solution.py:48
  12.7 13.5 %all-to-all-start = ((bf16[8,288,128]{2,1,0:T(8,128)(2,1)}), bf16[8,288,128]{2,1,0:T(8,128)(2,1)S(1)}, u32[]{:S(2)}, u32[]{:S(2)}) async-start(bf16[8,288,128]{2,1,0:T(8,128)(2,1)} %get-tuple-element.73), calls=%async_computation | async-start | bytes 1179648 | tf_op jit(solution)/shard_map/all_to_all | solution.py:67
  26.2 17.0 %product_a0.1 = (bf16[8,8,4096]{2,1,0:T(8,128)(2,1)S(1)}, bf16[8,8,4096]{2,1,0:T(8,128)(2,1)S(1)}) custom-call(s32[12,128]{1,0:T(8,128)S(1)} %get-tuple-element.65.list_ref, s32[5]{0:T(128)S(1)} %stack.38.place_ref.core_ref, f32[2,32,1,128]{3,2,1,0:T(1,128)S(1)} %reshape.81.left_ref, f32[2,32,1,128]{3,2,1,0:T(1,128)S(1)} %get-tuple-element.68.right_ref.left_ref, ...), custom_call_target="tpu_custom_call" | custom-call | bytes 60000000 | tf_op jit(solution)/shard_map/product_a0/pallas_call | solution.py:93
  43.2 3.0 %collective-permute-start.1 = (bf16[8,8,4096]{2,1,0:T(8,128)(2,1)S(1)}, bf16[8,8,4096]{2,1,0:T(8,128)(2,1)S(1)}, u32[]{:S(2)}, u32[]{:S(2)}) collective-permute-start(bf16[8,8,4096]{2,1,0:T(8,128)(2,1)S(1)} %get-tuple-element.75), channel_id=1, source_target_pairs={{0,16},{16,0},{1,17},{17,1},{2,18},{18,2},{3,19},{19,3},{4,20},{20... | collective-permute-start | bytes 1572872 | tf_op jit(solution)/shard_map/ppermute | solution.py:63
  49.1 4.0 %all-to-all-start.1 = ((bf16[4,16,4096]{2,1,0:T(8,128)(2,1)}), bf16[4,16,4096]{2,1,0:T(8,128)(2,1)S(1)}, u32[]{:S(2)}, u32[]{:S(2)}) async-start(bf16[4,16,4096]{2,1,0:T(8,128)(2,1)} %bitcast.9), calls=%async_computation.1 | async-start | bytes 1048576 | tf_op jit(solution)/shard_map/all_to_all | solution.py:67
  53.8 8.4 %all-to-all-done.1.arrived_ref = bf16[4,16,4096]{2,1,0:T(8,128)(2,1)S(1)} async-done(((bf16[4,16,4096]{2,1,0:T(8,128)(2,1)}), bf16[4,16,4096]{2,1,0:T(8,128)(2,1)S(1)}, u32[]{:S(2)}, u32[]{:S(2)}) %all-to-all-start.1) | async-done | bytes 524320 | tf_op jit(solution)/shard_map/all_to_all | solution.py:67
  62.3 5.2 %collective-permute-start.3 = (bf16[16,4096]{1,0:T(8,128)(2,1)S(1)}, bf16[16,4096]{1,0:T(8,128)(2,1)S(1)}, u32[]{:S(2)}, u32[]{:S(2)}) collective-permute-start(bf16[16,4096]{1,0:T(8,128)(2,1)S(1)} %sum_of.1.here_ref), channel_id=1, source_target_pairs={{0,32},{32,0},{1,33},{33,1},{2,34},{34,2},{3,35},{35,3},{4,36},{36... | collective-permute-start | bytes 393224 | tf_op jit(solution)/shard_map/ppermute | solution.py:734
  67.5 5.5 %all_pairs.1.matrix_ref = bf16[2048,1024]{1,0:T(8,128)(2,1)S(1)} custom-call(f32[2,16,1,128]{3,2,1,0:T(1,128)S(1)} %get-tuple-element.85.left_ref, f32[2,8,1,128]{3,2,1,0:T(1,128)S(1)} %get-tuple-element.86.right_ref), custom_call_target="tpu_custom_call" | custom-call | bytes 18000000 | tf_op jit(solution)/shard_map/all_pairs/pallas_call | solution.py:448
  75.8 3.5 %all-to-all-start.2 = ((bf16[4,16,4224]{2,1,0:T(8,128)(2,1)}), bf16[4,16,4224]{2,1,0:T(8,128)(2,1)S(1)}, u32[]{:S(2)}, u32[]{:S(2)}) async-start(bf16[4,16,4224]{2,1,0:T(8,128)(2,1)} %residual_of.1), calls=%async_computation.2 | async-start | bytes 1081344 | tf_op jit(solution)/shard_map/all_to_all | solution.py:67
  79.3 7.8 %all-to-all-done.2 = bf16[4,16,4224]{2,1,0:T(8,128)(2,1)S(1)} async-done(((bf16[4,16,4224]{2,1,0:T(8,128)(2,1)}), bf16[4,16,4224]{2,1,0:T(8,128)(2,1)S(1)}, u32[]{:S(2)}, u32[]{:S(2)}) %all-to-all-start.2) | async-done | bytes 540704 | tf_op jit(solution)/shard_map/all_to_all | solution.py:67
  91.4 8.1 %product.2 = bf16[16,8,1152]{2,1,0:T(8,128)(2,1)S(1)} custom-call(s32[12,128]{1,0:T(8,128)S(1)} %get-tuple-element.65.list_ref, f32[2,32,1,128]{3,2,1,0:T(1,128)S(1)} %get-tuple-element.68.right_ref.left_ref, f32[2,8,1,128]{3,2,1,0:T(1,128)S(1)} %reshape.83.right_ref.left_ref, bf16[8,8,4224]{2,1,0:T(8,128)(2,1)S(1)} %bitcast.59, ...), custom_call_target="tpu_custom_call" | custom-call | bytes 26666666 | tf_op jit(solution)/shard_map/product/pallas_call | solution.py:93
  99.5 13.5 %all_to_all.60.arrived_ref = bf16[16,8,1152]{2,1,0:T(8,128)(2,1)S(1)} all-to-all(bf16[16,8,1152]{2,1,0:T(8,128)(2,1)S(1)} %product.2), channel_id=1, replica_groups=mesh['y'=4,'zh'=2,'k'=2,'x'=4,'zl'=4] {'x','zl'}, dimensions={0} | all-to-all | bytes 589824 | tf_op jit(solution)/shard_map/all_to_all | solution.py:67
  113.8 3.9 %all-to-all-start.4 = ((bf16[16,8,1024]{2,1,0:T(8,128)(2,1)}), bf16[16,8,1024]{2,1,0:T(8,128)(2,1)S(1)}, u32[]{:S(2)}, u32[]{:S(2)}) async-start(bf16[16,8,1024]{2,1,0:T(8,128)(2,1)} %get-tuple-element.92), calls=%async_computation.4 | async-start | bytes 524288 | tf_op jit(solution)/shard_map/all_to_all | solution.py:67
  117.7 3.3 %collective-permute-start.5 = (f32[8,1024]{1,0:T(8,128)S(1)}, f32[8,1024]{1,0:T(8,128)S(1)}, u32[]{:S(2)}, u32[]{:S(2)}) collective-permute-start(f32[8,1024]{1,0:T(8,128)S(1)} %get-tuple-element.93), channel_id=1, source_target_pairs={{0,0},{24,1},{32,2},{56,3},{64,4},{88,5},{96,6},{120,7},{128,8},{1... | collective-permute-start | bytes 98312 | tf_op jit(solution)/shard_map/ppermute | solution.py:59
  122.1 4.3 %collective-permute-done.5.mid_ref = f32[8,1024]{1,0:T(8,128)S(1)} collective-permute-done((f32[8,1024]{1,0:T(8,128)S(1)}, f32[8,1024]{1,0:T(8,128)S(1)}, u32[]{:S(2)}, u32[]{:S(2)}) %collective-permute-start.5) | collective-permute-done | bytes 32800 | tf_op jit(solution)/shard_map/ppermute | solution.py:59
  128.8 3.6 %collective-permute-start.6 = (bf16[8,8,1024]{2,1,0:T(8,128)(2,1)S(1)}, bf16[8,8,1024]{2,1,0:T(8,128)(2,1)S(1)}, u32[]{:S(2)}, u32[]{:S(2)}) collective-permute-start(bf16[8,8,1024]{2,1,0:T(8,128)(2,1)S(1)} %get-tuple-element.96), channel_id=1, source_target_pairs={{0,16},{16,0},{1,17},{17,1},{2,18},{18,2},{3,19},{19,3},{4,20},{20... | collective-permute-start | bytes 393224 | tf_op jit(solution)/shard_map/ppermute | solution.py:63
  134.1 6.7 %all-to-all-start.5 = ((bf16[8,8,1024]{2,1,0:T(8,128)(2,1)}), bf16[8,8,1024]{2,1,0:T(8,128)(2,1)S(1)}, u32[]{:S(2)}, u32[]{:S(2)}) async-start(bf16[8,8,1024]{2,1,0:T(8,128)(2,1)} %add_convert_fusion.1), calls=%async_computation.5 | async-start | bytes 262144 | tf_op jit(solution)/shard_map/all_to_all | solution.py:67
  140.8 3.2 %dense_block.4.refs_0_ = bf16[1024,1152]{1,0:T(8,128)(2,1)S(1)} custom-call(s32[8,512]{1,0:T(8,128)S(1)} %quarter_of.1.list_ref, f32[2,8,1,128]{3,2,1,0:T(1,128)S(1)} %get-tuple-element.129.left_ref, f32[2,9,1,128]{3,2,1,0:T(1,128)S(1)} %pad.16.right_ref), custom_call_target="tpu_custom_call" | custom-call | bytes 9000000 | tf_op jit(solution)/shard_map/dense_block/pallas_call | solution.py:93
  145.4 3.0 %dense_block.5.refs_1_ = bf16[1024,1152]{1,0:T(8,128)(2,1)S(1)} custom-call(s32[8,512]{1,0:T(8,128)S(1)} %quarter_of.1.list_ref, f32[2,8,1,128]{3,2,1,0:T(1,128)S(1)} %get-tuple-element.128.left_ref, f32[2,9,1,128]{3,2,1,0:T(1,128)S(1)} %pad.16.right_ref), custom_call_target="tpu_custom_call" | custom-call | bytes 9000000 | tf_op jit(solution)/shard_map/dense_block/pallas_call | solution.py:93
  150.2 3.7 %coarse_product.1 = f32[16,8,128]{2,1,0:T(8,128)} custom-call(bf16[2048,1024]{1,0:T(8,128)(2,1)} %copy-done, bf16[8,8,1024]{2,1,0:T(8,128)(2,1)S(1)} %all-to-all-done.5.arrived_ref, f32[8,1024]{1,0:T(8,128)S(1)} %collective-permute-done.5.mid_ref), custom_call_target="tpu_custom_call" | custom-call | bytes 9000000 | tf_op jit(solution)/shard_map/coarse_product/pallas_call | solution.py:526
  154.0 5.1 %all-to-all-start.6 = ((f32[16,8,128]{2,1,0:T(8,128)}), f32[16,8,128]{2,1,0:T(8,128)S(1)}, u32[]{:S(2)}, u32[]{:S(2)}) async-start(f32[16,8,128]{2,1,0:T(8,128)} %coarse_product.1), calls=%async_computation.6 | async-start | bytes 131072 | tf_op jit(solution)/shard_map/all_to_all | solution.py:67
  159.1 3.0 %dense_block.6.refs_2_ = bf16[1024,1152]{1,0:T(8,128)(2,1)S(1)} custom-call(s32[8,512]{1,0:T(8,128)S(1)} %quarter_of.1.list_ref, f32[2,8,1,128]{3,2,1,0:T(1,128)S(1)} %get-tuple-element.127.left_ref, f32[2,9,1,128]{3,2,1,0:T(1,128)S(1)} %pad.16.right_ref), custom_call_target="tpu_custom_call" | custom-call | bytes 9000000 | tf_op jit(solution)/shard_map/dense_block/pallas_call | solution.py:93
  166.7 4.3 %all-to-all-start.7 = ((bf16[16,2,8,128]{3,2,1,0:T(8,128)(2,1)}), bf16[16,2,8,128]{3,2,1,0:T(8,128)(2,1)S(1)}, u32[]{:S(2)}, u32[]{:S(2)}) async-start(bf16[16,2,8,128]{3,2,1,0:T(8,128)(2,1)} %coarse_data_of.1), calls=%async_computation.7 | async-start | bytes 131072 | tf_op jit(solution)/shard_map/all_to_all | solution.py:67
  171.1 3.0 %dense_block.7.refs_3_ = bf16[1024,1152]{1,0:T(8,128)(2,1)S(1)} custom-call(s32[8,512]{1,0:T(8,128)S(1)} %quarter_of.1.list_ref, f32[2,8,1,128]{3,2,1,0:T(1,128)S(1)} %get-tuple-element.126.left_ref, f32[2,9,1,128]{3,2,1,0:T(1,128)S(1)} %pad.16.right_ref), custom_call_target="tpu_custom_call" | custom-call | bytes 9000000 | tf_op jit(solution)/shard_map/dense_block/pallas_call | solution.py:93
  178.2 11.1 %all_to_all.61.half_ref = bf16[16,8,128]{2,1,0:T(8,128)(2,1)S(1)} all-to-all(bf16[16,8,128]{2,1,0:T(8,128)(2,1)S(1)} %halfway_of.1), channel_id=1, replica_groups=mesh['y'=4,'zh'=2,'k'=2,'x'=4,'zl'=4] {'x','zl'}, dimensions={0} | all-to-all | bytes 65536 | tf_op jit(solution)/shard_map/all_to_all | solution.py:67
  190.4 3.5 %all-to-all-start.9 = ((bf16[16,8,128]{2,1,0:T(8,128)(2,1)}), bf16[16,8,128]{2,1,0:T(8,128)(2,1)S(1)}, u32[]{:S(2)}, u32[]{:S(2)}) async-start(bf16[16,8,128]{2,1,0:T(8,128)(2,1)} %coarse_coef_of.1), calls=%async_computation.9 | async-start | bytes 65536 | tf_op jit(solution)/shard_map/all_to_all | solution.py:67
  196.4 4.3 %all-to-all-done.9.coef_ref = bf16[16,8,128]{2,1,0:T(8,128)(2,1)S(1)} async-done(((bf16[16,8,128]{2,1,0:T(8,128)(2,1)}), bf16[16,8,128]{2,1,0:T(8,128)(2,1)S(1)}, u32[]{:S(2)}, u32[]{:S(2)}) %all-to-all-start.9) | async-done | bytes 32800 | tf_op jit(solution)/shard_map/all_to_all | solution.py:67
  203.2 21.9 %all_to_all.62.refs_4_ = bf16[32,8,1152]{2,1,0:T(8,128)(2,1)S(1)} all-to-all(bf16[32,8,1152]{2,1,0:T(8,128)(2,1)S(1)} %prolong.1), channel_id=1, replica_groups=mesh['y'=4,'zh'=2,'k'=2,'x'=4,'zl'=4] {'y','zh','zl'}, dimensions={0} | all-to-all | bytes 1179648 | tf_op jit(solution)/shard_map/all_to_all | solution.py:67
  225.1 6.2 %collective-permute-start.7 = (bf16[32,8,1152]{2,1,0:T(8,128)(2,1)S(1)}, bf16[32,8,1152]{2,1,0:T(8,128)(2,1)S(1)}, u32[]{:S(2)}, u32[]{:S(2)}) collective-permute-start(bf16[32,8,1152]{2,1,0:T(8,128)(2,1)S(1)} %all_to_all.62.refs_4_), channel_id=1, source_target_pairs={{0,16},{16,0},{1,17},{17,1},{2,18},{18,2},{3,19},{19,3},{4,20},{20... | collective-permute-start | bytes 1769480 | tf_op jit(solution)/shard_map/ppermute | solution.py:63
  233.4 4.9 %product_dense.1 = bf16[4,128,256]{2,1,0:T(8,128)(2,1)} custom-call(bf16[1024,1152]{1,0:T(8,128)(2,1)} %copy-done.1, bf16[1024,1152]{1,0:T(8,128)(2,1)} %copy-done.2, bf16[1024,1152]{1,0:T(8,128)(2,1)} %copy-done.3, bf16[1024,1152]{1,0:T(8,128)(2,1)} %copy-done.4, bf16[32,8,1152]{2,1,0:T(8,128)(2,1)S(1)} %all_to_all.62.refs_4_, ...), custom_call_target="tpu_custom_call" | custom-call | bytes 12000000 | tf_op jit(solution)/shard_map/product_dense/pallas_call | solution.py:420
  238.5 3.4 %all-to-all-start.11 = ((bf16[4,128,256]{2,1,0:T(8,128)(2,1)}), bf16[4,128,256]{2,1,0:T(8,128)(2,1)S(1)}, u32[]{:S(2)}, u32[]{:S(2)}) async-start(bf16[4,128,256]{2,1,0:T(8,128)(2,1)} %product_dense.1), calls=%async_computation.11 | async-start | bytes 524288 | tf_op jit(solution)/shard_map/all_to_all | solution.py:67
  243.8 4.9 %all-to-all-done.11.arrived_ref = bf16[4,128,256]{2,1,0:T(8,128)(2,1)S(1)} async-done(((bf16[4,128,256]{2,1,0:T(8,128)(2,1)}), bf16[4,128,256]{2,1,0:T(8,128)(2,1)S(1)}, u32[]{:S(2)}, u32[]{:S(2)}) %all-to-all-start.11) | async-done | bytes 262176 | tf_op jit(solution)/shard_map/all_to_all | solution.py:67
  (74 shorter events, 44.9 us)
Async XLA Ops:
  0.6 11.2 %copy-start.5 = (bf16[128,128]{1,0:T(8,128)(2,1)S(1)}, bf16[128,128]{1,0:T(8,128)(2,1)}, u32[]{:S(2)}) copy-start(bf16[128,128]{1,0:T(8,128)(2,1)} %factor_ref.1) | copy-start | bytes 98308
  1.6 10.2 %collective-permute-start = (bf16[224,128]{1,0:T(8,128)(2,1)S(1)}, bf16[224,128]{1,0:T(8,128)(2,1)S(1)}, u32[]{:S(2)}, u32[]{:S(2)}) collective-permute-start(bf16[224,128]{1,0:T(8,128)(2,1)S(1)} %packed.1), channel_id=1, source_target_pairs={{0,0},{16,1},{32,2},{48,3},{64,4},{80,5},{96,6},{112,7},{128,8},{1... | collective-permute-start | bytes 172040 | tf_op jit(solution)/shard_map/ppermute | solution.py:48
  12.7 30.5 %all-to-all-start = ((bf16[8,288,128]{2,1,0:T(8,128)(2,1)}), bf16[8,288,128]{2,1,0:T(8,128)(2,1)S(1)}, u32[]{:S(2)}, u32[]{:S(2)}) async-start(bf16[8,288,128]{2,1,0:T(8,128)(2,1)} %get-tuple-element.73), calls=%async_computation | async-start | bytes 1179648 | tf_op jit(solution)/shard_map/all_to_all | solution.py:67
  43.2 4.5 %collective-permute-start.1 = (bf16[8,8,4096]{2,1,0:T(8,128)(2,1)S(1)}, bf16[8,8,4096]{2,1,0:T(8,128)(2,1)S(1)}, u32[]{:S(2)}, u32[]{:S(2)}) collective-permute-start(bf16[8,8,4096]{2,1,0:T(8,128)(2,1)S(1)} %get-tuple-element.75), channel_id=1, source_target_pairs={{0,16},{16,0},{1,17},{17,1},{2,18},{18,2},{3,19},{19,3},{4,20},{20... | collective-permute-start | bytes 1572872 | tf_op jit(solution)/shard_map/ppermute | solution.py:63
  48.7 4.4 %collective-permute-start.2 = (bf16[8,288,128]{2,1,0:T(8,128)(2,1)S(1)}, bf16[8,288,128]{2,1,0:T(8,128)(2,1)S(1)}, u32[]{:S(2)}, u32[]{:S(2)}) collective-permute-start(bf16[8,288,128]{2,1,0:T(8,128)(2,1)S(1)} %all-to-all-done.own_ref), channel_id=1, source_target_pairs={{0,16},{16,0},{1,17},{17,1},{2,18},{18,2},{3,19},{19,3},{4,20},{20... | collective-permute-start | bytes 1769480 | tf_op jit(solution)/shard_map/ppermute | solution.py:63
  49.1 13.2 %all-to-all-start.1 = ((bf16[4,16,4096]{2,1,0:T(8,128)(2,1)}), bf16[4,16,4096]{2,1,0:T(8,128)(2,1)S(1)}, u32[]{:S(2)}, u32[]{:S(2)}) async-start(bf16[4,16,4096]{2,1,0:T(8,128)(2,1)} %bitcast.9), calls=%async_computation.1 | async-start | bytes 1048576 | tf_op jit(solution)/shard_map/all_to_all | solution.py:67
  62.3 12.6 %collective-permute-start.3 = (bf16[16,4096]{1,0:T(8,128)(2,1)S(1)}, bf16[16,4096]{1,0:T(8,128)(2,1)S(1)}, u32[]{:S(2)}, u32[]{:S(2)}) collective-permute-start(bf16[16,4096]{1,0:T(8,128)(2,1)S(1)} %sum_of.1.here_ref), channel_id=1, source_target_pairs={{0,32},{32,0},{1,33},{33,1},{2,34},{34,2},{3,35},{35,3},{4,36},{36... | collective-permute-start | bytes 393224 | tf_op jit(solution)/shard_map/ppermute | solution.py:734
  72.9 2.0 copy-start
  75.8 11.3 %all-to-all-start.2 = ((bf16[4,16,4224]{2,1,0:T(8,128)(2,1)}), bf16[4,16,4224]{2,1,0:T(8,128)(2,1)S(1)}, u32[]{:S(2)}, u32[]{:S(2)}) async-start(bf16[4,16,4224]{2,1,0:T(8,128)(2,1)} %residual_of.1), calls=%async_computation.2 | async-start | bytes 1081344 | tf_op jit(solution)/shard_map/all_to_all | solution.py:67
  87.1 4.3 %collective-permute-start.4 = (bf16[8,8,4224]{2,1,0:T(8,128)(2,1)S(1)}, bf16[8,8,4224]{2,1,0:T(8,128)(2,1)S(1)}, u32[]{:S(2)}, u32[]{:S(2)}) collective-permute-start(bf16[8,8,4224]{2,1,0:T(8,128)(2,1)S(1)} %bitcast.58), channel_id=1, source_target_pairs={{0,16},{16,0},{1,17},{17,1},{2,18},{18,2},{3,19},{19,3},{4,20},{20... | collective-permute-start | bytes 1622024 | tf_op jit(solution)/shard_map/ppermute | solution.py:63
  113.8 12.5 %all-to-all-start.4 = ((bf16[16,8,1024]{2,1,0:T(8,128)(2,1)}), bf16[16,8,1024]{2,1,0:T(8,128)(2,1)S(1)}, u32[]{:S(2)}, u32[]{:S(2)}) async-start(bf16[16,8,1024]{2,1,0:T(8,128)(2,1)} %get-tuple-element.92), calls=%async_computation.4 | async-start | bytes 524288 | tf_op jit(solution)/shard_map/all_to_all | solution.py:67
  117.7 8.6 %collective-permute-start.5 = (f32[8,1024]{1,0:T(8,128)S(1)}, f32[8,1024]{1,0:T(8,128)S(1)}, u32[]{:S(2)}, u32[]{:S(2)}) collective-permute-start(f32[8,1024]{1,0:T(8,128)S(1)} %get-tuple-element.93), channel_id=1, source_target_pairs={{0,0},{24,1},{32,2},{56,3},{64,4},{88,5},{96,6},{120,7},{128,8},{1... | collective-permute-start | bytes 98312 | tf_op jit(solution)/shard_map/ppermute | solution.py:59
  128.8 4.6 %collective-permute-start.6 = (bf16[8,8,1024]{2,1,0:T(8,128)(2,1)S(1)}, bf16[8,8,1024]{2,1,0:T(8,128)(2,1)S(1)}, u32[]{:S(2)}, u32[]{:S(2)}) collective-permute-start(bf16[8,8,1024]{2,1,0:T(8,128)(2,1)S(1)} %get-tuple-element.96), channel_id=1, source_target_pairs={{0,16},{16,0},{1,17},{17,1},{2,18},{18,2},{3,19},{19,3},{4,20},{20... | collective-permute-start | bytes 393224 | tf_op jit(solution)/shard_map/ppermute | solution.py:63
  134.1 16.2 %all-to-all-start.5 = ((bf16[8,8,1024]{2,1,0:T(8,128)(2,1)}), bf16[8,8,1024]{2,1,0:T(8,128)(2,1)S(1)}, u32[]{:S(2)}, u32[]{:S(2)}) async-start(bf16[8,8,1024]{2,1,0:T(8,128)(2,1)} %add_convert_fusion.1), calls=%async_computation.5 | async-start | bytes 262144 | tf_op jit(solution)/shard_map/all_to_all | solution.py:67
  143.9 1.4 copy-start.1
  148.3 1.5 copy-start.2
  154.0 12.1 %all-to-all-start.6 = ((f32[16,8,128]{2,1,0:T(8,128)}), f32[16,8,128]{2,1,0:T(8,128)S(1)}, u32[]{:S(2)}, u32[]{:S(2)}) async-start(f32[16,8,128]{2,1,0:T(8,128)} %coarse_product.1), calls=%async_computation.6 | async-start | bytes 131072 | tf_op jit(solution)/shard_map/all_to_all | solution.py:67
  162.1 1.4 copy-start.3
  166.7 11.3 %all-to-all-start.7 = ((bf16[16,2,8,128]{3,2,1,0:T(8,128)(2,1)}), bf16[16,2,8,128]{3,2,1,0:T(8,128)(2,1)S(1)}, u32[]{:S(2)}, u32[]{:S(2)}) async-start(bf16[16,2,8,128]{3,2,1,0:T(8,128)(2,1)} %coarse_data_of.1), calls=%async_computation.7 | async-start | bytes 131072 | tf_op jit(solution)/shard_map/all_to_all | solution.py:67
  174.1 1.5 copy-start.4
  190.4 10.3 %all-to-all-start.9 = ((bf16[16,8,128]{2,1,0:T(8,128)(2,1)}), bf16[16,8,128]{2,1,0:T(8,128)(2,1)S(1)}, u32[]{:S(2)}, u32[]{:S(2)}) async-start(bf16[16,8,128]{2,1,0:T(8,128)(2,1)} %coarse_coef_of.1), calls=%async_computation.9 | async-start | bytes 65536 | tf_op jit(solution)/shard_map/all_to_all | solution.py:67
  225.1 8.3 %collective-permute-start.7 = (bf16[32,8,1152]{2,1,0:T(8,128)(2,1)S(1)}, bf16[32,8,1152]{2,1,0:T(8,128)(2,1)S(1)}, u32[]{:S(2)}, u32[]{:S(2)}) collective-permute-start(bf16[32,8,1152]{2,1,0:T(8,128)(2,1)S(1)} %all_to_all.62.refs_4_), channel_id=1, source_target_pairs={{0,16},{16,0},{1,17},{17,1},{2,18},{18,2},{3,19},{19,3},{4,20},{20... | collective-permute-start | bytes 1769480 | tf_op jit(solution)/shard_map/ppermute | solution.py:63
  238.5 10.2 %all-to-all-start.11 = ((bf16[4,128,256]{2,1,0:T(8,128)(2,1)}), bf16[4,128,256]{2,1,0:T(8,128)(2,1)S(1)}, u32[]{:S(2)}, u32[]{:S(2)}) async-start(bf16[4,128,256]{2,1,0:T(8,128)(2,1)} %product_dense.1), calls=%async_computation.11 | async-start | bytes 524288 | tf_op jit(solution)/shard_map/all_to_all | solution.py:67

commit v8 on v7

--- a/solution.py
+++ b/solution.py
@@ -171,39 +171,32 @@
                     ref[a, t] = lines[at : at + 1]
                     at += 1
         list_ref[...] = lines[at : at + listed].astype(jnp.int32)
-        for chip in range(HALF):
-            common_ref[chip, pl.ds(0, TILE), :] = factor_ref[...]
-            common_ref[chip, pl.ds(TILE, TILE), :] = there_ref[pl.ds(above, TILE), :]
-            common_ref[chip, pl.ds(2 * TILE, local.shape[0]), :] = local_ref[...]
+        common_ref[pl.ds(0, TILE), :] = factor_ref[...]
+        common_ref[pl.ds(TILE, TILE), :] = there_ref[pl.ds(above, TILE), :]
+        common_ref[pl.ds(2 * TILE, local.shape[0]), :] = local_ref[...]
 
     shapes = [
         ((2, fine, 1, TILE), f32),
         ((2, mid, 1, TILE), f32),
         ((listed, TILE), jnp.int32),
-        ((HALF, size, TILE), bf16),
+        ((size, TILE), bf16),
     ]
     return call(kernel, shapes, (there, factor, local), "unpacked", 8, 1)
 
 
-def in_row_order(place, common, partner, mid):
+def split_common(place, common, mid):
     at_centres, at_mid = 2 * TILE, 2 * TILE + SIDE
 
-    def kernel(place_ref, own_ref, other_ref, down_ref, across_ref, centre_ref, line_ref):
-        core, x = place_ref[0], place_ref[4]
-
-        def rows(chip, of_core, at, size):
-            own, other = own_ref[chip, pl.ds(at, size), :], other_ref[chip, pl.ds(at, size), :]
-            return jnp.where(core == of_core, own.astype(f32), other.astype(f32))
-
+    def kernel(place_ref, common_ref, down_ref, across_ref, centre_ref, line_ref):
+        x = place_ref[4]
         for block in range(SIDE):
-            chip, of_core = block // 2, block % 2
-            down_ref[pl.ds(block * TILE, TILE), :] = rows(chip, of_core, 0, TILE).astype(bf16)
-            across_ref[block] = rows(chip, of_core, TILE, TILE).astype(bf16)
-            lines = rows(chip, of_core, at_centres, SIDE)
+            down_ref[pl.ds(block * TILE, TILE), :] = common_ref[block, pl.ds(0, TILE), :]
+            across_ref[block] = common_ref[block, pl.ds(TILE, TILE), :]
+            lines = common_ref[block, pl.ds(at_centres, SIDE), :].astype(f32)
             for a in range(2):
                 centre_ref[a, block] = lines[a : a + 1]
         for q in range(LINE):
-            lines = rows(x * (LINE // 2) + q // 2, q % 2, at_mid, 2 * mid)
+            lines = common_ref[x * LINE + q, pl.ds(at_mid, 2 * mid), :].astype(f32)
             for a in range(2):
                 for t in range(mid):
                     line_ref[a, q * mid + t] = lines[a * mid + t : a * mid + t + 1]
@@ -214,7 +207,7 @@
         ((2, SIDE, 1, TILE), f32),
         ((2, LINE * mid, 1, TILE), f32),
     ]
-    return call(kernel, shapes, (place, common, partner), "in_row_order", 8, 2, (), 1)
+    return call(kernel, shapes, (place, common), "split_common", 8, 2, (), 1)
 
 
 def set_points(left_ref, right_ref, left, right, support):
@@ -717,38 +710,39 @@
         there, factor, local, tiles_fine, tiles_mid, first_a1 + 2 * rows_of(listed_a1)
     )
 
-    common = exchanged(common, YZ)
+    common = lax.all_gather(common, ROW, axis=0)
     own, other = product_a0(lists, place, fine_here, fine_there, vector, listed_a0)
-    own, other, common = lax.optimization_barrier((own, other, common))
     pair = pair_sum(own, other).reshape(LINE, 2 * BLOCK, rows_fine)
-    arrived = exchanged(pair, "y")
-
-    common, pair = lax.optimization_barrier((common, pair))
-    ordered = in_row_order(place, common, from_partner(common), tiles_mid)
-    arrived, ordered = lax.optimization_barrier((arrived, ordered))
-    factor_down, factor_across, centres, mid_line = ordered
-    summed = sum_of(arrived)
-    centres, mid_later, fine_later, summed = lax.optimization_barrier(
-        (centres, mid_there, fine_here, summed)
-    )
+    summed = sum_of(exchanged(pair, "y"))
     swapped = lax.ppermute(summed, "zh", [(0, 1), (1, 0)])
+    fine_own = exchanged(residual_of(summed, swapped, -0.5 * scale_a0), "y")
+    fine_own = fine_own.reshape(HALF, BLOCK, rows_fine + TILE)
+    fine_other = from_partner(fine_own)
+
+    restricted = product(
+        lists, listed_e1, first_e1, 0, fine_there, mid_here, (fine_own, fine_other), support_mid, tail
+    )
+    common, fine_later, mid_later = lax.optimization_barrier(
+        (common, fine_here, mid_there, restricted)
+    )[:3]
+    factor_down, factor_across, centres, mid_line = split_common(place, common, tiles_mid)
     coarse_kernel = all_pairs(centres, mid_later, support_coarse)
-    swapped, coarse_kernel, fine_later = lax.optimization_barrier(
-        (swapped, coarse_kernel, fine_later)
-    )
-    fine_own = exchanged(residual_of(summed, swapped, -0.5 * scale_a0), "y")
     fine_quarter = fine_later.reshape(2, QUARTER // 2, LINE, 2, 1, TILE)
     fine_quarter = lax.dynamic_index_in_dim(fine_quarter, zl_id, 2, keepdims=False)
     fine_quarter = fine_quarter.reshape(2, QUARTER, 1, TILE)
     fine_quarter = jnp.pad(fine_quarter, ((0, 0), (0, 1), (0, 0), (0, 0)), constant_values=8.0)
-    fine_own, fine_quarter = lax.optimization_barrier((fine_own, fine_quarter))
-    fine_own = fine_own.reshape(HALF, BLOCK, rows_fine + TILE)
-    fine_other = from_partner(fine_own)
-
-    restricted = product(
-        lists, listed_e1, first_e1, 0, fine_there, mid_here, (fine_own, fine_other), support_mid, tail
-    )
-    restricted = exchanged(restricted, COL)
+    restricted, coarse_kernel, factor_down, factor_across, mid_line, fine_quarter = (
+        lax.optimization_barrier(
+            (
+                exchanged(restricted, COL),
+                coarse_kernel,
+                factor_down,
+                factor_across,
+                mid_line,
+                fine_quarter,
+            )
+        )
+    )
     mid_share, mid_all = mid_of(restricted, scale_e1)
     line_lists = lax.dynamic_slice_in_dim(restricted[:, :, rows_mid:], x_id * LINE, LINE, 0)
     line_lists = line_lists[:, : own_e1.shape[0]].reshape(-1, TILE).astype(jnp.int32)
@@ -766,27 +760,28 @@
         return dense_block(lists, q, points, fine_quarter, support_mid)
 
     pair, lists_then = lax.optimization_barrier((pair_sum(mid_own, mid_other), line_lists))
-    arrived, *first_two = lax.optimization_barrier(
-        (exchanged(pair, YZ), e1_block(lists_then, 0), e1_block(lists_then, 1))
-    )
+    arrived, first = lax.optimization_barrier((exchanged(pair, YZ), e1_block(lists_then, 0)))
     coarse_part, lists_then = lax.optimization_barrier(
         (coarse_product(coarse_kernel, arrived, mid_data, scale_a1), line_lists)
     )
-    arrived, third = lax.optimization_barrier(
-        (exchanged(coarse_part, COL), e1_block(lists_then, 2))
+    arrived, second = lax.optimization_barrier(
+        (exchanged(coarse_part, COL), e1_block(lists_then, 1))
     )
     coarse_data, lists_then = lax.optimization_barrier(
         (coarse_data_of(arrived, fine_own, fine_other, scale_e2), line_lists)
     )
-    coarse_data, fourth = lax.optimization_barrier(
-        (exchanged(coarse_data, COL), e1_block(lists_then, 3))
-    )
-    halfway = exchanged(halfway_of(coarse_data, factor_down), COL)
+    coarse_data, third = lax.optimization_barrier(
+        (exchanged(coarse_data, COL), e1_block(lists_then, 2))
+    )
+    halfway, lists_then = lax.optimization_barrier(
+        (halfway_of(coarse_data, factor_down), line_lists)
+    )
+    halfway, fourth = lax.optimization_barrier((exchanged(halfway, COL), e1_block(lists_then, 3)))
     coarse_all = exchanged(coarse_coef_of(halfway, factor_across), COL)
 
     new_own = exchanged(prolong(coarse_kernel, coarse_all, place, mid_data, scale_e2), YZL)
     new_other = from_partner(new_own)
-    fine_part = product_dense((*first_two, third, fourth), new_own, new_other)
+    fine_part = product_dense((first, second, third, fourth), new_own, new_other)
     fine_part, new_own, new_other = lax.optimization_barrier((fine_part, new_own, new_other))
     own_data = lax.dynamic_slice_in_dim(values, col_id * share, share, 0)
     fine_coef = fine_of(exchanged(fine_part, "x"), own_data, place, scale_e1)

time: 253 us -> 255 us (level)
  between operations: 4.75 us -> 18.1 us
  starting transfers between devices: 77.2 us -> 66.4 us
    all_to_all x9 -> x8, starting transfers between devices: 47.8 us -> 38.1 us  [exchanged(): return lax.all_to_all(x, axes, split_axis=0, concat_axis=0, tiled=True)]
    all_to_all x9 -> x8, waiting for transfers between devices: 30.9 us -> 24.2 us  [exchanged(): return lax.all_to_all(x, axes, split_axis=0, concat_axis=0, tiled=True)]
    ppermute x5 -> x4, starting transfers between devices: 16 us -> 11 us  [from_partner(): return lax.ppermute(x, 'k', [(0, 1), (1, 0)])]
    all_gather x0 -> x1, waiting for transfers between devices: none -> 4.61 us  [per_device(): common = lax.all_gather(common, ROW, axis=0)]
    ppermute x1, starting transfers between devices: 5.18 us -> 9.03 us  [per_device(): swapped = lax.ppermute(summed, 'zh', [(0, 1), (1, 0)])]
    unnamed x15 -> x17, local copies, waits for them, and re-layouts: 10.9 us -> 12.2 us
  transfers between devices with their start and end apart: 17 -> 16, of which waited for: 11 -> 13; matrix products, arithmetic and copies ran while one was open for 4% -> 4% of each run, Pallas kernels for 14% -> 11%
where the time goes in v8:
time: 255 us; the launch traced here: 254 us
  starting transfers between devices  66.4 us (26%)
  Pallas kernels  65 us (25%)
  blocking collectives  46.8 us (18%)
  waiting for transfers between devices  38.7 us (15%)
  between operations  18.1 us (7%)
  local copies, waits for them, and re-layouts  16 us (6%)
  other arithmetic  3.08 us (1%)
    pallas_call x17, Pallas kernels, call(): pl.pallas_call(kernel, out_shape=[jax.ShapeDtypeStruct(shape, kind) for s...  47.5 us
    all_to_all x3, blocking collectives, exchanged(): return lax.all_to_all(x, axes, split_axis=0, concat_axis=0, tiled=True)  46.8 us
    all_to_all x8, starting transfers between devices, exchanged(): return lax.all_to_all(x, axes, split_axis=0, concat_axis=0, tiled=True)  38.1 us
    all_to_all x8, waiting for transfers between devices, exchanged(): return lax.all_to_all(x, axes, split_axis=0, concat_axis=0, tiled=True)  24.2 us
    unnamed x17, local copies, waits for them, and re-layouts  12.2 us
    ppermute x4, starting transfers between devices, from_partner(): return lax.ppermute(x, 'k', [(0, 1), (1, 0)])  11 us
    ppermute x1, starting transfers between devices, per_device(): swapped = lax.ppermute(summed, 'zh', [(0, 1), (1, 0)])  9.03 us
    pallas_call x2, Pallas kernels, call_on_matrix(): pl.pallas_call(kernel, out_shape=jax.ShapeDtypeStruct(shape, kind), in_sp...  6.24 us
  transfers between devices with their start and end apart: 16, of which 13 were waited for; matrix products, arithmetic and copies ran while one was open for 4% of the time, Pallas kernels for 11%

profile of v8, /device:TPU:1, one launch (start us, length us, event | category | flops | bytes accessed | tf_op | source)
XLA Modules:
  0.0 254.2 jit_solution(3902979550003902808)
XLA Ops:
  8.2 4.9 %collective-permute-start = (bf16[224,128]{1,0:T(8,128)(2,1)S(1)}, bf16[224,128]{1,0:T(8,128)(2,1)S(1)}, u32[]{:S(2)}, u32[]{:S(2)}) collective-permute-start(bf16[224,128]{1,0:T(8,128)(2,1)S(1)} %packed.1), channel_id=1, source_target_pairs={{0,0},{16,1},{32,2},{48,3},{64,4},{80,5},{96,6},{112,7},{128,8},{1... | collective-permute-start | bytes 172040 | tf_op jit(solution)/shard_map/ppermute | solution.py:48
  19.0 17.1 %product_a0.1 = (bf16[8,8,4096]{2,1,0:T(8,128)(2,1)S(1)}, bf16[8,8,4096]{2,1,0:T(8,128)(2,1)S(1)}) custom-call(s32[12,128]{1,0:T(8,128)S(1)} %get-tuple-element.59.list_ref, s32[5]{0:T(128)S(1)} %stack.38.place_ref.core_ref, f32[2,32,1,128]{3,2,1,0:T(1,128)S(1)} %reshape.81.left_ref, f32[2,32,1,128]{3,2,1,0:T(1,128)S(1)} %get-tuple-element.62.right_ref.left_ref, ...), custom_call_target="tpu_custom_call" | custom-call | bytes 60000000 | tf_op jit(solution)/shard_map/product_a0/pallas_call | solution.py:93
  38.2 15.3 %all_to_all.55.arrived_ref = bf16[4,16,4096]{2,1,0:T(8,128)(2,1)S(1)} all-to-all(bf16[4,16,4096]{2,1,0:T(8,128)(2,1)S(1)} %bitcast.65), channel_id=1, replica_groups=mesh['y'=4,'zh'=2,'k'=2,'x'=4,'zl'=4] {'y'}, dimensions={0} | all-to-all | bytes 1048576 | tf_op jit(solution)/shard_map/all_to_all | solution.py:67
  53.6 9.0 %collective-permute-start.2 = (bf16[16,4096]{1,0:T(8,128)(2,1)S(1)}, bf16[16,4096]{1,0:T(8,128)(2,1)S(1)}, u32[]{:S(2)}, u32[]{:S(2)}) collective-permute-start(bf16[16,4096]{1,0:T(8,128)(2,1)S(1)} %sum_of.1.here_ref), channel_id=1, source_target_pairs={{0,32},{32,0},{1,33},{33,1},{2,34},{34,2},{3,35},{35,3},{4,36},{36... | collective-permute-start | bytes 393224 | tf_op jit(solution)/shard_map/ppermute | solution.py:717
  65.2 15.5 %all_to_all.56 = bf16[4,16,4224]{2,1,0:T(8,128)(2,1)S(1)} all-to-all(bf16[4,16,4224]{2,1,0:T(8,128)(2,1)S(1)} %residual_of.1), channel_id=1, replica_groups=mesh['y'=4,'zh'=2,'k'=2,'x'=4,'zl'=4] {'y'}, dimensions={0} | all-to-all | bytes 1081344 | tf_op jit(solution)/shard_map/all_to_all | solution.py:67
  84.2 8.8 %product.2 = bf16[16,8,1152]{2,1,0:T(8,128)(2,1)} custom-call(s32[12,128]{1,0:T(8,128)S(1)} %get-tuple-element.59.list_ref, f32[2,32,1,128]{3,2,1,0:T(1,128)S(1)} %get-tuple-element.62.right_ref.left_ref, f32[2,8,1,128]{3,2,1,0:T(1,128)S(1)} %reshape.83.right_ref.left_ref, bf16[8,8,4224]{2,1,0:T(8,128)(2,1)S(1)} %bitcast.60, ...), custom_call_target="tpu_custom_call" | custom-call | bytes 26666666 | tf_op jit(solution)/shard_map/product/pallas_call | solution.py:93
  93.1 4.2 %all-to-all-start.2 = ((bf16[16,8,1152]{2,1,0:T(8,128)(2,1)}), bf16[16,8,1152]{2,1,0:T(8,128)(2,1)S(1)}, u32[]{:S(2)}, u32[]{:S(2)}) async-start(bf16[16,8,1152]{2,1,0:T(8,128)(2,1)} %product.2), calls=%async_computation.2 | async-start | bytes 589824 | tf_op jit(solution)/shard_map/all_to_all | solution.py:67
  97.2 4.6 %all-gather.3.cloned.1.call-done = bf16[4608,128]{1,0:T(8,128)(2,1)} async-done(((bf16[288,128]{1,0:T(8,128)(2,1)}), bf16[4608,128]{1,0:T(8,128)(2,1)}) %all-gather.3.cloned.1.call-update) | async-done | bytes 1179664 | tf_op jit(solution)/shard_map/all_gather | solution.py:713
  103.7 5.5 %all_pairs.1.matrix_ref = bf16[2048,1024]{1,0:T(8,128)(2,1)S(1)} custom-call(f32[2,16,1,128]{3,2,1,0:T(1,128)S(1)} %get-tuple-element.70.left_ref, f32[2,8,1,128]{3,2,1,0:T(1,128)S(1)} %get-tuple-element.71.right_ref), custom_call_target="tpu_custom_call" | custom-call | bytes 18000000 | tf_op jit(solution)/shard_map/all_pairs/pallas_call | solution.py:441
  112.0 4.5 %all-to-all-start.3 = ((bf16[16,8,1024]{2,1,0:T(8,128)(2,1)}), bf16[16,8,1024]{2,1,0:T(8,128)(2,1)S(1)}, u32[]{:S(2)}, u32[]{:S(2)}) async-start(bf16[16,8,1024]{2,1,0:T(8,128)(2,1)} %get-tuple-element.77), calls=%async_computation.3 | async-start | bytes 524288 | tf_op jit(solution)/shard_map/all_to_all | solution.py:67
  116.5 3.3 %collective-permute-start.4 = (f32[8,1024]{1,0:T(8,128)S(1)}, f32[8,1024]{1,0:T(8,128)S(1)}, u32[]{:S(2)}, u32[]{:S(2)}) collective-permute-start(f32[8,1024]{1,0:T(8,128)S(1)} %get-tuple-element.78), channel_id=1, source_target_pairs={{0,0},{24,1},{32,2},{56,3},{64,4},{88,5},{96,6},{120,7},{128,8},{1... | collective-permute-start | bytes 98312 | tf_op jit(solution)/shard_map/ppermute | solution.py:59
  120.8 3.0 %collective-permute-done.4.mid_ref = f32[8,1024]{1,0:T(8,128)S(1)} collective-permute-done((f32[8,1024]{1,0:T(8,128)S(1)}, f32[8,1024]{1,0:T(8,128)S(1)}, u32[]{:S(2)}, u32[]{:S(2)}) %collective-permute-start.4) | collective-permute-done | bytes 32800 | tf_op jit(solution)/shard_map/ppermute | solution.py:59
  123.8 2.5 %all-to-all-done.3 = bf16[16,8,1024]{2,1,0:T(8,128)(2,1)S(1)} async-done(((bf16[16,8,1024]{2,1,0:T(8,128)(2,1)}), bf16[16,8,1024]{2,1,0:T(8,128)(2,1)S(1)}, u32[]{:S(2)}, u32[]{:S(2)}) %all-to-all-start.3) | async-done | bytes 262176 | tf_op jit(solution)/shard_map/all_to_all | solution.py:67
  132.8 6.7 %all-to-all-start.4 = ((bf16[8,8,1024]{2,1,0:T(8,128)(2,1)}), bf16[8,8,1024]{2,1,0:T(8,128)(2,1)S(1)}, u32[]{:S(2)}, u32[]{:S(2)}) async-start(bf16[8,8,1024]{2,1,0:T(8,128)(2,1)} %add_convert_fusion.1), calls=%async_computation.4 | async-start | bytes 262144 | tf_op jit(solution)/shard_map/all_to_all | solution.py:67
  139.5 3.2 %dense_block.4.refs_0_ = bf16[1024,1152]{1,0:T(8,128)(2,1)S(1)} custom-call(s32[8,512]{1,0:T(8,128)S(1)} %quarter_of.1.list_ref, f32[2,8,1,128]{3,2,1,0:T(1,128)S(1)} %get-tuple-element.117.left_ref, f32[2,9,1,128]{3,2,1,0:T(1,128)S(1)} %pad.16.right_ref), custom_call_target="tpu_custom_call" | custom-call | bytes 9000000 | tf_op jit(solution)/shard_map/dense_block/pallas_call | solution.py:93
  144.1 4.9 %all-to-all-done.4.arrived_ref = bf16[8,8,1024]{2,1,0:T(8,128)(2,1)S(1)} async-done(((bf16[8,8,1024]{2,1,0:T(8,128)(2,1)}), bf16[8,8,1024]{2,1,0:T(8,128)(2,1)S(1)}, u32[]{:S(2)}, u32[]{:S(2)}) %all-to-all-start.4) | async-done | bytes 131104 | tf_op jit(solution)/shard_map/all_to_all | solution.py:67
  149.0 3.8 %coarse_product.1 = f32[16,8,128]{2,1,0:T(8,128)} custom-call(bf16[2048,1024]{1,0:T(8,128)(2,1)} %copy-done, bf16[8,8,1024]{2,1,0:T(8,128)(2,1)S(1)} %all-to-all-done.4.arrived_ref, f32[8,1024]{1,0:T(8,128)S(1)} %collective-permute-done.4.mid_ref), custom_call_target="tpu_custom_call" | custom-call | bytes 9000000 | tf_op jit(solution)/shard_map/coarse_product/pallas_call | solution.py:519
  152.8 6.1 %all-to-all-start.5 = ((f32[16,8,128]{2,1,0:T(8,128)}), f32[16,8,128]{2,1,0:T(8,128)S(1)}, u32[]{:S(2)}, u32[]{:S(2)}) async-start(f32[16,8,128]{2,1,0:T(8,128)} %coarse_product.1), calls=%async_computation.5 | async-start | bytes 131072 | tf_op jit(solution)/shard_map/all_to_all | solution.py:67
  158.9 3.0 %dense_block.5.refs_1_ = bf16[1024,1152]{1,0:T(8,128)(2,1)S(1)} custom-call(s32[8,512]{1,0:T(8,128)S(1)} %quarter_of.1.list_ref, f32[2,8,1,128]{3,2,1,0:T(1,128)S(1)} %get-tuple-element.116.left_ref, f32[2,9,1,128]{3,2,1,0:T(1,128)S(1)} %pad.16.right_ref), custom_call_target="tpu_custom_call" | custom-call | bytes 9000000 | tf_op jit(solution)/shard_map/dense_block/pallas_call | solution.py:93
  163.3 2.5 all-to-all-done.5.arrived_ref
  166.5 4.4 %all-to-all-start.6 = ((bf16[16,2,8,128]{3,2,1,0:T(8,128)(2,1)}), bf16[16,2,8,128]{3,2,1,0:T(8,128)(2,1)S(1)}, u32[]{:S(2)}, u32[]{:S(2)}) async-start(bf16[16,2,8,128]{3,2,1,0:T(8,128)(2,1)} %coarse_data_of.1), calls=%async_computation.6 | async-start | bytes 131072 | tf_op jit(solution)/shard_map/all_to_all | solution.py:67
  170.9 3.0 %dense_block.6.refs_2_ = bf16[1024,1152]{1,0:T(8,128)(2,1)S(1)} custom-call(s32[8,512]{1,0:T(8,128)S(1)} %quarter_of.1.list_ref, f32[2,8,1,128]{3,2,1,0:T(1,128)S(1)} %get-tuple-element.115.left_ref, f32[2,9,1,128]{3,2,1,0:T(1,128)S(1)} %pad.16.right_ref), custom_call_target="tpu_custom_call" | custom-call | bytes 9000000 | tf_op jit(solution)/shard_map/dense_block/pallas_call | solution.py:93
  175.3 2.6 %all-to-all-done.6.data_ref = bf16[16,2,8,128]{3,2,1,0:T(8,128)(2,1)S(1)} async-done(((bf16[16,2,8,128]{3,2,1,0:T(8,128)(2,1)}), bf16[16,2,8,128]{3,2,1,0:T(8,128)(2,1)S(1)}, u32[]{:S(2)}, u32[]{:S(2)}) %all-to-all-start.6) | async-done | bytes 65568 | tf_op jit(solution)/shard_map/all_to_all | solution.py:67
  178.7 4.3 %all-to-all-start.7 = ((bf16[16,8,128]{2,1,0:T(8,128)(2,1)}), bf16[16,8,128]{2,1,0:T(8,128)(2,1)S(1)}, u32[]{:S(2)}, u32[]{:S(2)}) async-start(bf16[16,8,128]{2,1,0:T(8,128)(2,1)} %halfway_of.1), calls=%async_computation.7 | async-start | bytes 65536 | tf_op jit(solution)/shard_map/all_to_all | solution.py:67
  183.1 3.0 %dense_block.7.refs_3_ = bf16[1024,1152]{1,0:T(8,128)(2,1)S(1)} custom-call(s32[8,512]{1,0:T(8,128)S(1)} %quarter_of.1.list_ref, f32[2,8,1,128]{3,2,1,0:T(1,128)S(1)} %get-tuple-element.114.left_ref, f32[2,9,1,128]{3,2,1,0:T(1,128)S(1)} %pad.16.right_ref), custom_call_target="tpu_custom_call" | custom-call | bytes 9000000 | tf_op jit(solution)/shard_map/dense_block/pallas_call | solution.py:93
  190.9 4.6 %all-to-all-start.8 = ((bf16[16,8,128]{2,1,0:T(8,128)(2,1)}), bf16[16,8,128]{2,1,0:T(8,128)(2,1)S(1)}, u32[]{:S(2)}, u32[]{:S(2)}) async-start(bf16[16,8,128]{2,1,0:T(8,128)(2,1)} %coarse_coef_of.1), calls=%async_computation.8 | async-start | bytes 65536 | tf_op jit(solution)/shard_map/all_to_all | solution.py:67
  198.1 4.3 %all-to-all-done.8.coef_ref = bf16[16,8,128]{2,1,0:T(8,128)(2,1)S(1)} async-done(((bf16[16,8,128]{2,1,0:T(8,128)(2,1)}), bf16[16,8,128]{2,1,0:T(8,128)(2,1)S(1)}, u32[]{:S(2)}, u32[]{:S(2)}) %all-to-all-start.8) | async-done | bytes 32800 | tf_op jit(solution)/shard_map/all_to_all | solution.py:67
  204.9 16.0 %all_to_all.57.refs_4_ = bf16[32,8,1152]{2,1,0:T(8,128)(2,1)S(1)} all-to-all(bf16[32,8,1152]{2,1,0:T(8,128)(2,1)S(1)} %prolong.1), channel_id=1, replica_groups=mesh['y'=4,'zh'=2,'k'=2,'x'=4,'zl'=4] {'y','zh','zl'}, dimensions={0} | all-to-all | bytes 1179648 | tf_op jit(solution)/shard_map/all_to_all | solution.py:67
  220.9 6.5 %collective-permute-start.6 = (bf16[32,8,1152]{2,1,0:T(8,128)(2,1)S(1)}, bf16[32,8,1152]{2,1,0:T(8,128)(2,1)S(1)}, u32[]{:S(2)}, u32[]{:S(2)}) collective-permute-start(bf16[32,8,1152]{2,1,0:T(8,128)(2,1)S(1)} %all_to_all.57.refs_4_), channel_id=1, source_target_pairs={{0,16},{16,0},{1,17},{17,1},{2,18},{18,2},{3,19},{19,3},{4,20},{20... | collective-permute-start | bytes 1769480 | tf_op jit(solution)/shard_map/ppermute | solution.py:63
  229.6 4.9 %product_dense.1 = bf16[4,128,256]{2,1,0:T(8,128)(2,1)} custom-call(bf16[1024,1152]{1,0:T(8,128)(2,1)} %copy-done.1, bf16[1024,1152]{1,0:T(8,128)(2,1)} %copy-done.2, bf16[1024,1152]{1,0:T(8,128)(2,1)} %copy-done.3, bf16[1024,1152]{1,0:T(8,128)(2,1)} %copy-done.4, bf16[32,8,1152]{2,1,0:T(8,128)(2,1)S(1)} %all_to_all.57.refs_4_, ...), custom_call_target="tpu_custom_call" | custom-call | bytes 12000000 | tf_op jit(solution)/shard_map/product_dense/pallas_call | solution.py:413
  234.6 3.4 %all-to-all-start.10 = ((bf16[4,128,256]{2,1,0:T(8,128)(2,1)}), bf16[4,128,256]{2,1,0:T(8,128)(2,1)S(1)}, u32[]{:S(2)}, u32[]{:S(2)}) async-start(bf16[4,128,256]{2,1,0:T(8,128)(2,1)} %product_dense.1), calls=%async_computation.10 | async-start | bytes 524288 | tf_op jit(solution)/shard_map/all_to_all | solution.py:67
  239.9 4.9 %all-to-all-done.10.arrived_ref = bf16[4,128,256]{2,1,0:T(8,128)(2,1)S(1)} async-done(((bf16[4,128,256]{2,1,0:T(8,128)(2,1)}), bf16[4,128,256]{2,1,0:T(8,128)(2,1)S(1)}, u32[]{:S(2)}, u32[]{:S(2)}) %all-to-all-start.10) | async-done | bytes 262176 | tf_op jit(solution)/shard_map/all_to_all | solution.py:67
  (75 shorter events, 45.7 us)
Async XLA Ops:
  7.2 11.2 %copy-start.6 = (bf16[128,128]{1,0:T(8,128)(2,1)S(1)}, bf16[128,128]{1,0:T(8,128)(2,1)}, u32[]{:S(2)}) copy-start(bf16[128,128]{1,0:T(8,128)(2,1)} %factor_ref.1) | copy-start | bytes 98308
  7.2 94.7 %all-gather.3.cloned.1.call-start = ((), (), s32[]{:S(2)}) async-start(), calls=%async_computation.11 | async-start | bytes 1253376 | tf_op jit(solution)/shard_map/all_gather | solution.py:713
  8.2 10.2 %collective-permute-start = (bf16[224,128]{1,0:T(8,128)(2,1)S(1)}, bf16[224,128]{1,0:T(8,128)(2,1)S(1)}, u32[]{:S(2)}, u32[]{:S(2)}) collective-permute-start(bf16[224,128]{1,0:T(8,128)(2,1)S(1)} %packed.1), channel_id=1, source_target_pairs={{0,0},{16,1},{32,2},{48,3},{64,4},{80,5},{96,6},{112,7},{128,8},{1... | collective-permute-start | bytes 172040 | tf_op jit(solution)/shard_map/ppermute | solution.py:48
  36.1 2.0 collective-permute-start.1
  53.6 11.5 %collective-permute-start.2 = (bf16[16,4096]{1,0:T(8,128)(2,1)S(1)}, bf16[16,4096]{1,0:T(8,128)(2,1)S(1)}, u32[]{:S(2)}, u32[]{:S(2)}) collective-permute-start(bf16[16,4096]{1,0:T(8,128)(2,1)S(1)} %sum_of.1.here_ref), channel_id=1, source_target_pairs={{0,32},{32,0},{1,33},{33,1},{2,34},{34,2},{3,35},{35,3},{4,36},{36... | collective-permute-start | bytes 393224 | tf_op jit(solution)/shard_map/ppermute | solution.py:717
  80.7 3.6 %collective-permute-start.3 = (bf16[8,8,4224]{2,1,0:T(8,128)(2,1)S(1)}, bf16[8,8,4224]{2,1,0:T(8,128)(2,1)S(1)}, u32[]{:S(2)}, u32[]{:S(2)}) collective-permute-start(bf16[8,8,4224]{2,1,0:T(8,128)(2,1)S(1)} %bitcast.59), channel_id=1, source_target_pairs={{0,16},{16,0},{1,17},{17,1},{2,18},{18,2},{3,19},{19,3},{4,20},{20... | collective-permute-start | bytes 1622024 | tf_op jit(solution)/shard_map/ppermute | solution.py:63
  93.1 18.2 %all-to-all-start.2 = ((bf16[16,8,1152]{2,1,0:T(8,128)(2,1)}), bf16[16,8,1152]{2,1,0:T(8,128)(2,1)S(1)}, u32[]{:S(2)}, u32[]{:S(2)}) async-start(bf16[16,8,1152]{2,1,0:T(8,128)(2,1)} %product.2), calls=%async_computation.2 | async-start | bytes 589824 | tf_op jit(solution)/shard_map/all_to_all | solution.py:67
  101.8 1.3 copy-start.5
  109.2 2.0 copy-start
  112.0 14.4 %all-to-all-start.3 = ((bf16[16,8,1024]{2,1,0:T(8,128)(2,1)}), bf16[16,8,1024]{2,1,0:T(8,128)(2,1)S(1)}, u32[]{:S(2)}, u32[]{:S(2)}) async-start(bf16[16,8,1024]{2,1,0:T(8,128)(2,1)} %get-tuple-element.77), calls=%async_computation.3 | async-start | bytes 524288 | tf_op jit(solution)/shard_map/all_to_all | solution.py:67
  116.5 7.4 %collective-permute-start.4 = (f32[8,1024]{1,0:T(8,128)S(1)}, f32[8,1024]{1,0:T(8,128)S(1)}, u32[]{:S(2)}, u32[]{:S(2)}) collective-permute-start(f32[8,1024]{1,0:T(8,128)S(1)} %get-tuple-element.78), channel_id=1, source_target_pairs={{0,0},{24,1},{32,2},{56,3},{64,4},{88,5},{96,6},{120,7},{128,8},{1... | collective-permute-start | bytes 98312 | tf_op jit(solution)/shard_map/ppermute | solution.py:59
  128.8 3.3 %collective-permute-start.5 = (bf16[8,8,1024]{2,1,0:T(8,128)(2,1)S(1)}, bf16[8,8,1024]{2,1,0:T(8,128)(2,1)S(1)}, u32[]{:S(2)}, u32[]{:S(2)}) collective-permute-start(bf16[8,8,1024]{2,1,0:T(8,128)(2,1)S(1)} %get-tuple-element.81), channel_id=1, source_target_pairs={{0,16},{16,0},{1,17},{17,1},{2,18},{18,2},{3,19},{19,3},{4,20},{20... | collective-permute-start | bytes 393224 | tf_op jit(solution)/shard_map/ppermute | solution.py:63
  132.8 16.2 %all-to-all-start.4 = ((bf16[8,8,1024]{2,1,0:T(8,128)(2,1)}), bf16[8,8,1024]{2,1,0:T(8,128)(2,1)S(1)}, u32[]{:S(2)}, u32[]{:S(2)}) async-start(bf16[8,8,1024]{2,1,0:T(8,128)(2,1)} %add_convert_fusion.1), calls=%async_computation.4 | async-start | bytes 262144 | tf_op jit(solution)/shard_map/all_to_all | solution.py:67
  142.7 1.4 copy-start.1
  152.8 13.1 %all-to-all-start.5 = ((f32[16,8,128]{2,1,0:T(8,128)}), f32[16,8,128]{2,1,0:T(8,128)S(1)}, u32[]{:S(2)}, u32[]{:S(2)}) async-start(f32[16,8,128]{2,1,0:T(8,128)} %coarse_product.1), calls=%async_computation.5 | async-start | bytes 131072 | tf_op jit(solution)/shard_map/all_to_all | solution.py:67
  161.9 1.5 copy-start.2
  166.5 11.4 %all-to-all-start.6 = ((bf16[16,2,8,128]{3,2,1,0:T(8,128)(2,1)}), bf16[16,2,8,128]{3,2,1,0:T(8,128)(2,1)S(1)}, u32[]{:S(2)}, u32[]{:S(2)}) async-start(bf16[16,2,8,128]{3,2,1,0:T(8,128)(2,1)} %coarse_data_of.1), calls=%async_computation.6 | async-start | bytes 131072 | tf_op jit(solution)/shard_map/all_to_all | solution.py:67
  173.9 1.4 copy-start.3
  178.7 11.2 %all-to-all-start.7 = ((bf16[16,8,128]{2,1,0:T(8,128)(2,1)}), bf16[16,8,128]{2,1,0:T(8,128)(2,1)S(1)}, u32[]{:S(2)}, u32[]{:S(2)}) async-start(bf16[16,8,128]{2,1,0:T(8,128)(2,1)} %halfway_of.1), calls=%async_computation.7 | async-start | bytes 65536 | tf_op jit(solution)/shard_map/all_to_all | solution.py:67
  186.0 1.5 copy-start.4
  190.9 11.5 %all-to-all-start.8 = ((bf16[16,8,128]{2,1,0:T(8,128)(2,1)}), bf16[16,8,128]{2,1,0:T(8,128)(2,1)S(1)}, u32[]{:S(2)}, u32[]{:S(2)}) async-start(bf16[16,8,128]{2,1,0:T(8,128)(2,1)} %coarse_coef_of.1), calls=%async_computation.8 | async-start | bytes 65536 | tf_op jit(solution)/shard_map/all_to_all | solution.py:67
  220.9 8.7 %collective-permute-start.6 = (bf16[32,8,1152]{2,1,0:T(8,128)(2,1)S(1)}, bf16[32,8,1152]{2,1,0:T(8,128)(2,1)S(1)}, u32[]{:S(2)}, u32[]{:S(2)}) collective-permute-start(bf16[32,8,1152]{2,1,0:T(8,128)(2,1)S(1)} %all_to_all.57.refs_4_), channel_id=1, source_target_pairs={{0,16},{16,0},{1,17},{17,1},{2,18},{18,2},{3,19},{19,3},{4,20},{20... | collective-permute-start | bytes 1769480 | tf_op jit(solution)/shard_map/ppermute | solution.py:63
  234.6 10.2 %all-to-all-start.10 = ((bf16[4,128,256]{2,1,0:T(8,128)(2,1)}), bf16[4,128,256]{2,1,0:T(8,128)(2,1)S(1)}, u32[]{:S(2)}, u32[]{:S(2)}) async-start(bf16[4,128,256]{2,1,0:T(8,128)(2,1)} %product_dense.1), calls=%async_computation.10 | async-start | bytes 524288 | tf_op jit(solution)/shard_map/all_to_all | solution.py:67
Sparse Core Ops, SparseCore 0:
  36.4 65.4 all-gather.2

commit v9 on v8

--- a/solution.py
+++ b/solution.py
@@ -171,32 +171,39 @@
                     ref[a, t] = lines[at : at + 1]
                     at += 1
         list_ref[...] = lines[at : at + listed].astype(jnp.int32)
-        common_ref[pl.ds(0, TILE), :] = factor_ref[...]
-        common_ref[pl.ds(TILE, TILE), :] = there_ref[pl.ds(above, TILE), :]
-        common_ref[pl.ds(2 * TILE, local.shape[0]), :] = local_ref[...]
+        for chip in range(HALF):
+            common_ref[chip, pl.ds(0, TILE), :] = factor_ref[...]
+            common_ref[chip, pl.ds(TILE, TILE), :] = there_ref[pl.ds(above, TILE), :]
+            common_ref[chip, pl.ds(2 * TILE, local.shape[0]), :] = local_ref[...]
 
     shapes = [
         ((2, fine, 1, TILE), f32),
         ((2, mid, 1, TILE), f32),
         ((listed, TILE), jnp.int32),
-        ((size, TILE), bf16),
+        ((HALF, size, TILE), bf16),
     ]
     return call(kernel, shapes, (there, factor, local), "unpacked", 8, 1)
 
 
-def split_common(place, common, mid):
+def in_row_order(place, common, partner, mid):
     at_centres, at_mid = 2 * TILE, 2 * TILE + SIDE
 
-    def kernel(place_ref, common_ref, down_ref, across_ref, centre_ref, line_ref):
-        x = place_ref[4]
+    def kernel(place_ref, own_ref, other_ref, down_ref, across_ref, centre_ref, line_ref):
+        core, x = place_ref[0], place_ref[4]
+
+        def rows(chip, of_core, at, size):
+            own, other = own_ref[chip, pl.ds(at, size), :], other_ref[chip, pl.ds(at, size), :]
+            return jnp.where(core == of_core, own.astype(f32), other.astype(f32))
+
         for block in range(SIDE):
-            down_ref[pl.ds(block * TILE, TILE), :] = common_ref[block, pl.ds(0, TILE), :]
-            across_ref[block] = common_ref[block, pl.ds(TILE, TILE), :]
-            lines = common_ref[block, pl.ds(at_centres, SIDE), :].astype(f32)
+            chip, of_core = block // 2, block % 2
+            down_ref[pl.ds(block * TILE, TILE), :] = rows(chip, of_core, 0, TILE).astype(bf16)
+            across_ref[block] = rows(chip, of_core, TILE, TILE).astype(bf16)
+            lines = rows(chip, of_core, at_centres, SIDE)
             for a in range(2):
                 centre_ref[a, block] = lines[a : a + 1]
         for q in range(LINE):
-            lines = common_ref[x * LINE + q, pl.ds(at_mid, 2 * mid), :].astype(f32)
+            lines = rows(x * (LINE // 2) + q // 2, q % 2, at_mid, 2 * mid)
             for a in range(2):
                 for t in range(mid):
                     line_ref[a, q * mid + t] = lines[a * mid + t : a * mid + t + 1]
@@ -207,7 +214,7 @@
         ((2, SIDE, 1, TILE), f32),
         ((2, LINE * mid, 1, TILE), f32),
     ]
-    return call(kernel, shapes, (place, common), "split_common", 8, 2, (), 1)
+    return call(kernel, shapes, (place, common, partner), "in_row_order", 8, 2, (), 1)
 
 
 def set_points(left_ref, right_ref, left, right, support):
@@ -710,7 +717,6 @@
         there, factor, local, tiles_fine, tiles_mid, first_a1 + 2 * rows_of(listed_a1)
     )
 
-    common = lax.all_gather(common, ROW, axis=0)
     own, other = product_a0(lists, place, fine_here, fine_there, vector, listed_a0)
     pair = pair_sum(own, other).reshape(LINE, 2 * BLOCK, rows_fine)
     summed = sum_of(exchanged(pair, "y"))
@@ -719,48 +725,44 @@
     fine_own = fine_own.reshape(HALF, BLOCK, rows_fine + TILE)
     fine_other = from_partner(fine_own)
 
+    common, fine_own, fine_other = lax.optimization_barrier((common, fine_own, fine_other))
+    common = exchanged(common, YZ)
     restricted = product(
         lists, listed_e1, first_e1, 0, fine_there, mid_here, (fine_own, fine_other), support_mid, tail
     )
-    common, fine_later, mid_later = lax.optimization_barrier(
-        (common, fine_here, mid_there, restricted)
-    )[:3]
-    factor_down, factor_across, centres, mid_line = split_common(place, common, tiles_mid)
-    coarse_kernel = all_pairs(centres, mid_later, support_coarse)
-    fine_quarter = fine_later.reshape(2, QUARTER // 2, LINE, 2, 1, TILE)
+    restricted, common = lax.optimization_barrier((restricted, common))
+    ordered = in_row_order(place, common, from_partner(common), tiles_mid)
+    fine_quarter = fine_here.reshape(2, QUARTER // 2, LINE, 2, 1, TILE)
     fine_quarter = lax.dynamic_index_in_dim(fine_quarter, zl_id, 2, keepdims=False)
     fine_quarter = fine_quarter.reshape(2, QUARTER, 1, TILE)
     fine_quarter = jnp.pad(fine_quarter, ((0, 0), (0, 1), (0, 0), (0, 0)), constant_values=8.0)
-    restricted, coarse_kernel, factor_down, factor_across, mid_line, fine_quarter = (
-        lax.optimization_barrier(
-            (
-                exchanged(restricted, COL),
-                coarse_kernel,
-                factor_down,
-                factor_across,
-                mid_line,
-                fine_quarter,
-            )
-        )
-    )
+    restricted, ordered, fine_quarter = lax.optimization_barrier(
+        (exchanged(restricted, COL), ordered, fine_quarter)
+    )
+    factor_down, factor_across, centres, mid_line = ordered
     mid_share, mid_all = mid_of(restricted, scale_e1)
     line_lists = lax.dynamic_slice_in_dim(restricted[:, :, rows_mid:], x_id * LINE, LINE, 0)
     line_lists = line_lists[:, : own_e1.shape[0]].reshape(-1, TILE).astype(jnp.int32)
     line_lists = quarter_of(line_lists, place, LINE, listed_e1)
-    mid_all, mid_data, line_lists = lax.optimization_barrier(
-        (exchanged(mid_all, COL), turned_blocks(mid_share), line_lists)
+
+    def e1_block(lists, q):
+        points = mid_line[:, q * tiles_mid : (q + 1) * tiles_mid]
+        return dense_block(lists, q, points, fine_quarter, support_mid)
+
+    mid_all, mid_data, line_lists, first = lax.optimization_barrier(
+        (exchanged(mid_all, COL), turned_blocks(mid_share), line_lists, e1_block(line_lists, 0))
     )
 
     mid_halves = (mid_all[:HALF], mid_all[HALF:])
     mid_own, mid_other = product(
         lists, listed_a1, first_a1, 1, mid_here, mid_there, mid_halves, support_mid
     )
-    def e1_block(lists, q):
-        points = mid_line[:, q * tiles_mid : (q + 1) * tiles_mid]
-        return dense_block(lists, q, points, fine_quarter, support_mid)
-
-    pair, lists_then = lax.optimization_barrier((pair_sum(mid_own, mid_other), line_lists))
-    arrived, first = lax.optimization_barrier((exchanged(pair, YZ), e1_block(lists_then, 0)))
+    pair, centres, mid_later = lax.optimization_barrier(
+        (pair_sum(mid_own, mid_other), centres, mid_there)
+    )
+    arrived, coarse_kernel = lax.optimization_barrier(
+        (exchanged(pair, YZ), all_pairs(centres, mid_later, support_coarse))
+    )
     coarse_part, lists_then = lax.optimization_barrier(
         (coarse_product(coarse_kernel, arrived, mid_data, scale_a1), line_lists)
     )

time: 255 us -> 257 us (level)
  between operations: 18.1 us -> 4.78 us
  starting transfers between devices: 66.4 us -> 79.3 us
  waiting for transfers between devices: 38.7 us -> 43.4 us
  blocking collectives: 46.8 us -> 44.2 us
    all_to_all x8 -> x9, waiting for transfers between devices: 24.2 us -> 36.5 us  [exchanged(): return lax.all_to_all(x, axes, split_axis=0, concat_axis=0, tiled=True)]
    all_to_all x8 -> x9, starting transfers between devices: 38.1 us -> 45.2 us  [exchanged(): return lax.all_to_all(x, axes, split_axis=0, concat_axis=0, tiled=True)]
    ppermute x4 -> x5, starting transfers between devices: 11 us -> 17.2 us  [from_partner(): return lax.ppermute(x, 'k', [(0, 1), (1, 0)])]
    all_gather x1 -> x0, waiting for transfers between devices: 4.61 us -> none  [per_device(): common = lax.all_gather(common, ROW, axis=0)]
    ppermute x1, waiting for transfers between devices: 2.98 us -> 0.01 us  [turned_blocks(): return lax.ppermute(x, ALL, pairs)]
    all_to_all x3, blocking collectives: 46.8 us -> 44.2 us  [exchanged(): return lax.all_to_all(x, axes, split_axis=0, concat_axis=0, tiled=True)]
    unnamed x17 -> x19, local copies, waits for them, and re-layouts: 12.2 us -> 11.7 us
  transfers between devices with their start and end apart: 16 -> 17, of which waited for: 13 -> 13; matrix products, arithmetic and copies ran while one was open for 4% -> 4% of each run, Pallas kernels for 11% -> 11%
where the time goes in v9:
time: 257 us; the launch traced here: 256 us
  starting transfers between devices  79.3 us (31%)
  Pallas kernels  65.3 us (25%)
  blocking collectives  44.2 us (17%)
  waiting for transfers between devices  43.4 us (17%)
  local copies, waits for them, and re-layouts  15.6 us (6%)
  between operations  4.78 us (2%)
  other arithmetic  3.08 us (1%)
    pallas_call x17, Pallas kernels, call(): pl.pallas_call(kernel, out_shape=[jax.ShapeDtypeStruct(shape, kind) for s...  47.7 us
    all_to_all x9, starting transfers between devices, exchanged(): return lax.all_to_all(x, axes, split_axis=0, concat_axis=0, tiled=True)  45.2 us
    all_to_all x3, blocking collectives, exchanged(): return lax.all_to_all(x, axes, split_axis=0, concat_axis=0, tiled=True)  44.2 us
    all_to_all x9, waiting for transfers between devices, exchanged(): return lax.all_to_all(x, axes, split_axis=0, concat_axis=0, tiled=True)  36.5 us
    ppermute x5, starting transfers between devices, from_partner(): return lax.ppermute(x, 'k', [(0, 1), (1, 0)])  17.2 us
    unnamed x19, local copies, waits for them, and re-layouts  11.7 us
    ppermute x1, starting transfers between devices, per_device(): swapped = lax.ppermute(summed, 'zh', [(0, 1), (1, 0)])  8.7 us
    pallas_call x2, Pallas kernels, call_on_matrix(): pl.pallas_call(kernel, out_shape=jax.ShapeDtypeStruct(shape, kind), in_sp...  6.25 us
  transfers between devices with their start and end apart: 17, of which 13 were waited for; matrix products, arithmetic and copies ran while one was open for 4% of the time, Pallas kernels for 11%

profile of v9, /device:TPU:1, one launch (start us, length us, event | category | flops | bytes accessed | tf_op | source)
XLA Modules:
  0.0 255.7 jit_solution(10472348429282984601)
XLA Ops:
  1.6 4.9 %collective-permute-start = (bf16[224,128]{1,0:T(8,128)(2,1)S(1)}, bf16[224,128]{1,0:T(8,128)(2,1)S(1)}, u32[]{:S(2)}, u32[]{:S(2)}) collective-permute-start(bf16[224,128]{1,0:T(8,128)(2,1)S(1)} %packed.1), channel_id=1, source_target_pairs={{0,0},{16,1},{32,2},{48,3},{64,4},{80,5},{96,6},{112,7},{128,8},{1... | collective-permute-start | bytes 172040 | tf_op jit(solution)/shard_map/ppermute | solution.py:48
  12.7 17.1 %product_a0.1 = (bf16[8,8,4096]{2,1,0:T(8,128)(2,1)S(1)}, bf16[8,8,4096]{2,1,0:T(8,128)(2,1)S(1)}) custom-call(s32[12,128]{1,0:T(8,128)S(1)} %get-tuple-element.63.list_ref, s32[5]{0:T(128)S(1)} %stack.38.place_ref.core_ref, f32[2,32,1,128]{3,2,1,0:T(1,128)S(1)} %reshape.81.left_ref, f32[2,32,1,128]{3,2,1,0:T(1,128)S(1)} %get-tuple-element.64.right_ref.left_ref, ...), custom_call_target="tpu_custom_call" | custom-call | bytes 60000000 | tf_op jit(solution)/shard_map/product_a0/pallas_call | solution.py:93
  31.9 15.3 %all_to_all.60.arrived_ref = bf16[4,16,4096]{2,1,0:T(8,128)(2,1)S(1)} all-to-all(bf16[4,16,4096]{2,1,0:T(8,128)(2,1)S(1)} %bitcast.63), channel_id=1, replica_groups=mesh['y'=4,'zh'=2,'k'=2,'x'=4,'zl'=4] {'y'}, dimensions={0} | all-to-all | bytes 1048576 | tf_op jit(solution)/shard_map/all_to_all | solution.py:67
  47.2 8.7 %collective-permute-start.2 = (bf16[16,4096]{1,0:T(8,128)(2,1)S(1)}, bf16[16,4096]{1,0:T(8,128)(2,1)S(1)}, u32[]{:S(2)}, u32[]{:S(2)}) collective-permute-start(bf16[16,4096]{1,0:T(8,128)(2,1)S(1)} %sum_of.1.here_ref), channel_id=1, source_target_pairs={{0,32},{32,0},{1,33},{33,1},{2,34},{34,2},{3,35},{35,3},{4,36},{36... | collective-permute-start | bytes 393224 | tf_op jit(solution)/shard_map/ppermute | solution.py:723
  58.5 9.4 %all_to_all.61 = bf16[4,16,4224]{2,1,0:T(8,128)(2,1)S(1)} all-to-all(bf16[4,16,4224]{2,1,0:T(8,128)(2,1)S(1)} %residual_of.1), channel_id=1, replica_groups=mesh['y'=4,'zh'=2,'k'=2,'x'=4,'zl'=4] {'y'}, dimensions={0} | all-to-all | bytes 1081344 | tf_op jit(solution)/shard_map/all_to_all | solution.py:67
  67.9 6.1 %collective-permute-start.3 = (bf16[8,8,4224]{2,1,0:T(8,128)(2,1)S(1)}, bf16[8,8,4224]{2,1,0:T(8,128)(2,1)S(1)}, u32[]{:S(2)}, u32[]{:S(2)}) collective-permute-start(bf16[8,8,4224]{2,1,0:T(8,128)(2,1)S(1)} %bitcast.58), channel_id=1, source_target_pairs={{0,16},{16,0},{1,17},{17,1},{2,18},{18,2},{3,19},{19,3},{4,20},{20... | collective-permute-start | bytes 1622024 | tf_op jit(solution)/shard_map/ppermute | solution.py:63
  75.5 7.1 %all-to-all-start.2 = ((bf16[8,288,128]{2,1,0:T(8,128)(2,1)}), bf16[8,288,128]{2,1,0:T(8,128)(2,1)S(1)}, u32[]{:S(2)}, u32[]{:S(2)}) async-start(bf16[8,288,128]{2,1,0:T(8,128)(2,1)} %get-tuple-element.74), calls=%async_computation.2 | async-start | bytes 1179648 | tf_op jit(solution)/shard_map/all_to_all | solution.py:67
  82.7 8.9 %product.2 = bf16[16,8,1152]{2,1,0:T(8,128)(2,1)} custom-call(s32[12,128]{1,0:T(8,128)S(1)} %get-tuple-element.63.list_ref, f32[2,32,1,128]{3,2,1,0:T(1,128)S(1)} %get-tuple-element.64.right_ref.left_ref, f32[2,8,1,128]{3,2,1,0:T(1,128)S(1)} %reshape.83.right_ref.left_ref, bf16[8,8,4224]{2,1,0:T(8,128)(2,1)S(1)} %bitcast.59, ...), custom_call_target="tpu_custom_call" | custom-call | bytes 26666666 | tf_op jit(solution)/shard_map/product/pallas_call | solution.py:93
  91.5 7.5 %all-to-all-done.2.own_ref = bf16[8,288,128]{2,1,0:T(8,128)(2,1)S(1)} async-done(((bf16[8,288,128]{2,1,0:T(8,128)(2,1)}), bf16[8,288,128]{2,1,0:T(8,128)(2,1)S(1)}, u32[]{:S(2)}, u32[]{:S(2)}) %all-to-all-start.2) | async-done | bytes 589856 | tf_op jit(solution)/shard_map/all_to_all | solution.py:67
  100.7 4.7 %all-to-all-start.3 = ((bf16[16,8,1152]{2,1,0:T(8,128)(2,1)}), bf16[16,8,1152]{2,1,0:T(8,128)(2,1)S(1)}, u32[]{:S(2)}, u32[]{:S(2)}) async-start(bf16[16,8,1152]{2,1,0:T(8,128)(2,1)} %product.2), calls=%async_computation.3 | async-start | bytes 589824 | tf_op jit(solution)/shard_map/all_to_all | solution.py:67
  107.1 9.3 %all-to-all-done.3.arrived_ref = bf16[16,8,1152]{2,1,0:T(8,128)(2,1)S(1)} async-done(((bf16[16,8,1152]{2,1,0:T(8,128)(2,1)}), bf16[16,8,1152]{2,1,0:T(8,128)(2,1)S(1)}, u32[]{:S(2)}, u32[]{:S(2)}) %all-to-all-start.3) | async-done | bytes 294944 | tf_op jit(solution)/shard_map/all_to_all | solution.py:67
  117.2 3.9 %all-to-all-start.4 = ((bf16[16,8,1024]{2,1,0:T(8,128)(2,1)}), bf16[16,8,1024]{2,1,0:T(8,128)(2,1)S(1)}, u32[]{:S(2)}, u32[]{:S(2)}) async-start(bf16[16,8,1024]{2,1,0:T(8,128)(2,1)} %get-tuple-element.82), calls=%async_computation.4 | async-start | bytes 524288 | tf_op jit(solution)/shard_map/all_to_all | solution.py:67
  121.1 3.3 %collective-permute-start.5 = (f32[8,1024]{1,0:T(8,128)S(1)}, f32[8,1024]{1,0:T(8,128)S(1)}, u32[]{:S(2)}, u32[]{:S(2)}) collective-permute-start(f32[8,1024]{1,0:T(8,128)S(1)} %get-tuple-element.83), channel_id=1, source_target_pairs={{0,0},{24,1},{32,2},{56,3},{64,4},{88,5},{96,6},{120,7},{128,8},{1... | collective-permute-start | bytes 98312 | tf_op jit(solution)/shard_map/ppermute | solution.py:59
  125.5 3.0 %dense_block.4.refs_0_ = bf16[1024,1152]{1,0:T(8,128)(2,1)S(1)} custom-call(s32[8,512]{1,0:T(8,128)S(1)} %quarter_of.1.list_ref, f32[2,8,1,128]{3,2,1,0:T(1,128)S(1)} %get-tuple-element.125.left_ref, f32[2,9,1,128]{3,2,1,0:T(1,128)S(1)} %pad.16.right_ref), custom_call_target="tpu_custom_call" | custom-call | bytes 9000000 | tf_op jit(solution)/shard_map/dense_block/pallas_call | solution.py:93
  133.2 2.8 %collective-permute-start.6 = (bf16[8,8,1024]{2,1,0:T(8,128)(2,1)S(1)}, bf16[8,8,1024]{2,1,0:T(8,128)(2,1)S(1)}, u32[]{:S(2)}, u32[]{:S(2)}) collective-permute-start(bf16[8,8,1024]{2,1,0:T(8,128)(2,1)S(1)} %get-tuple-element.90), channel_id=1, source_target_pairs={{0,16},{16,0},{1,17},{17,1},{2,18},{18,2},{3,19},{19,3},{4,20},{20... | collective-permute-start | bytes 393224 | tf_op jit(solution)/shard_map/ppermute | solution.py:63
  137.6 8.7 %all-to-all-start.5 = ((bf16[8,8,1024]{2,1,0:T(8,128)(2,1)}), bf16[8,8,1024]{2,1,0:T(8,128)(2,1)S(1)}, u32[]{:S(2)}, u32[]{:S(2)}) async-start(bf16[8,8,1024]{2,1,0:T(8,128)(2,1)} %add_convert_fusion.1), calls=%async_computation.5 | async-start | bytes 262144 | tf_op jit(solution)/shard_map/all_to_all | solution.py:67
  146.3 5.5 %all_pairs.1.matrix_ref = bf16[2048,1024]{1,0:T(8,128)(2,1)S(1)} custom-call(f32[2,16,1,128]{3,2,1,0:T(1,128)S(1)} %get-tuple-element.93.left_ref, f32[2,8,1,128]{3,2,1,0:T(1,128)S(1)} %get-tuple-element.94.right_ref), custom_call_target="tpu_custom_call" | custom-call | bytes 18000000 | tf_op jit(solution)/shard_map/all_pairs/pallas_call | solution.py:448
  155.9 3.8 %coarse_product.1 = f32[16,8,128]{2,1,0:T(8,128)} custom-call(bf16[2048,1024]{1,0:T(8,128)(2,1)} %copy-done, bf16[8,8,1024]{2,1,0:T(8,128)(2,1)S(1)} %all-to-all-done.5.arrived_ref, f32[8,1024]{1,0:T(8,128)S(1)} %collective-permute-done.5.mid_ref), custom_call_target="tpu_custom_call" | custom-call | bytes 9000000 | tf_op jit(solution)/shard_map/coarse_product/pallas_call | solution.py:526
  159.6 4.1 %all-to-all-start.6 = ((f32[16,8,128]{2,1,0:T(8,128)}), f32[16,8,128]{2,1,0:T(8,128)S(1)}, u32[]{:S(2)}, u32[]{:S(2)}) async-start(f32[16,8,128]{2,1,0:T(8,128)} %coarse_product.1), calls=%async_computation.6 | async-start | bytes 131072 | tf_op jit(solution)/shard_map/all_to_all | solution.py:67
  163.7 3.0 %dense_block.5.refs_1_ = bf16[1024,1152]{1,0:T(8,128)(2,1)S(1)} custom-call(s32[8,512]{1,0:T(8,128)S(1)} %quarter_of.1.list_ref, f32[2,8,1,128]{3,2,1,0:T(1,128)S(1)} %get-tuple-element.124.left_ref, f32[2,9,1,128]{3,2,1,0:T(1,128)S(1)} %pad.16.right_ref), custom_call_target="tpu_custom_call" | custom-call | bytes 9000000 | tf_op jit(solution)/shard_map/dense_block/pallas_call | solution.py:93
  171.3 4.4 %all-to-all-start.7 = ((bf16[16,2,8,128]{3,2,1,0:T(8,128)(2,1)}), bf16[16,2,8,128]{3,2,1,0:T(8,128)(2,1)S(1)}, u32[]{:S(2)}, u32[]{:S(2)}) async-start(bf16[16,2,8,128]{3,2,1,0:T(8,128)(2,1)} %coarse_data_of.1), calls=%async_computation.7 | async-start | bytes 131072 | tf_op jit(solution)/shard_map/all_to_all | solution.py:67
  175.8 3.0 %dense_block.6.refs_2_ = bf16[1024,1152]{1,0:T(8,128)(2,1)S(1)} custom-call(s32[8,512]{1,0:T(8,128)S(1)} %quarter_of.1.list_ref, f32[2,8,1,128]{3,2,1,0:T(1,128)S(1)} %get-tuple-element.123.left_ref, f32[2,9,1,128]{3,2,1,0:T(1,128)S(1)} %pad.16.right_ref), custom_call_target="tpu_custom_call" | custom-call | bytes 9000000 | tf_op jit(solution)/shard_map/dense_block/pallas_call | solution.py:93
  180.2 2.6 %all-to-all-done.7.data_ref = bf16[16,2,8,128]{3,2,1,0:T(8,128)(2,1)S(1)} async-done(((bf16[16,2,8,128]{3,2,1,0:T(8,128)(2,1)}), bf16[16,2,8,128]{3,2,1,0:T(8,128)(2,1)S(1)}, u32[]{:S(2)}, u32[]{:S(2)}) %all-to-all-start.7) | async-done | bytes 65568 | tf_op jit(solution)/shard_map/all_to_all | solution.py:67
  183.6 4.3 %all-to-all-start.8 = ((bf16[16,8,128]{2,1,0:T(8,128)(2,1)}), bf16[16,8,128]{2,1,0:T(8,128)(2,1)S(1)}, u32[]{:S(2)}, u32[]{:S(2)}) async-start(bf16[16,8,128]{2,1,0:T(8,128)(2,1)} %halfway_of.1), calls=%async_computation.8 | async-start | bytes 65536 | tf_op jit(solution)/shard_map/all_to_all | solution.py:67
  187.9 3.0 %dense_block.7.refs_3_ = bf16[1024,1152]{1,0:T(8,128)(2,1)S(1)} custom-call(s32[8,512]{1,0:T(8,128)S(1)} %quarter_of.1.list_ref, f32[2,8,1,128]{3,2,1,0:T(1,128)S(1)} %get-tuple-element.122.left_ref, f32[2,9,1,128]{3,2,1,0:T(1,128)S(1)} %pad.16.right_ref), custom_call_target="tpu_custom_call" | custom-call | bytes 9000000 | tf_op jit(solution)/shard_map/dense_block/pallas_call | solution.py:93
  195.8 4.6 %all-to-all-start.9 = ((bf16[16,8,128]{2,1,0:T(8,128)(2,1)}), bf16[16,8,128]{2,1,0:T(8,128)(2,1)S(1)}, u32[]{:S(2)}, u32[]{:S(2)}) async-start(bf16[16,8,128]{2,1,0:T(8,128)(2,1)} %coarse_coef_of.1), calls=%async_computation.9 | async-start | bytes 65536 | tf_op jit(solution)/shard_map/all_to_all | solution.py:67
  202.9 4.3 %all-to-all-done.9.coef_ref = bf16[16,8,128]{2,1,0:T(8,128)(2,1)S(1)} async-done(((bf16[16,8,128]{2,1,0:T(8,128)(2,1)}), bf16[16,8,128]{2,1,0:T(8,128)(2,1)S(1)}, u32[]{:S(2)}, u32[]{:S(2)}) %all-to-all-start.9) | async-done | bytes 32800 | tf_op jit(solution)/shard_map/all_to_all | solution.py:67
  209.7 19.5 %all_to_all.62.refs_4_ = bf16[32,8,1152]{2,1,0:T(8,128)(2,1)S(1)} all-to-all(bf16[32,8,1152]{2,1,0:T(8,128)(2,1)S(1)} %prolong.1), channel_id=1, replica_groups=mesh['y'=4,'zh'=2,'k'=2,'x'=4,'zl'=4] {'y','zh','zl'}, dimensions={0} | all-to-all | bytes 1179648 | tf_op jit(solution)/shard_map/all_to_all | solution.py:67
  229.3 6.5 %collective-permute-start.7 = (bf16[32,8,1152]{2,1,0:T(8,128)(2,1)S(1)}, bf16[32,8,1152]{2,1,0:T(8,128)(2,1)S(1)}, u32[]{:S(2)}, u32[]{:S(2)}) collective-permute-start(bf16[32,8,1152]{2,1,0:T(8,128)(2,1)S(1)} %all_to_all.62.refs_4_), channel_id=1, source_target_pairs={{0,16},{16,0},{1,17},{17,1},{2,18},{18,2},{3,19},{19,3},{4,20},{20... | collective-permute-start | bytes 1769480 | tf_op jit(solution)/shard_map/ppermute | solution.py:63
  237.9 4.9 %product_dense.1 = bf16[4,128,256]{2,1,0:T(8,128)(2,1)} custom-call(bf16[1024,1152]{1,0:T(8,128)(2,1)} %copy-done.1, bf16[1024,1152]{1,0:T(8,128)(2,1)} %copy-done.2, bf16[1024,1152]{1,0:T(8,128)(2,1)} %copy-done.3, bf16[1024,1152]{1,0:T(8,128)(2,1)} %copy-done.4, bf16[32,8,1152]{2,1,0:T(8,128)(2,1)S(1)} %all_to_all.62.refs_4_, ...), custom_call_target="tpu_custom_call" | custom-call | bytes 12000000 | tf_op jit(solution)/shard_map/product_dense/pallas_call | solution.py:420
  243.0 3.4 %all-to-all-start.11 = ((bf16[4,128,256]{2,1,0:T(8,128)(2,1)}), bf16[4,128,256]{2,1,0:T(8,128)(2,1)S(1)}, u32[]{:S(2)}, u32[]{:S(2)}) async-start(bf16[4,128,256]{2,1,0:T(8,128)(2,1)} %product_dense.1), calls=%async_computation.11 | async-start | bytes 524288 | tf_op jit(solution)/shard_map/all_to_all | solution.py:67
  248.3 4.9 %all-to-all-done.11.arrived_ref = bf16[4,128,256]{2,1,0:T(8,128)(2,1)S(1)} async-done(((bf16[4,128,256]{2,1,0:T(8,128)(2,1)}), bf16[4,128,256]{2,1,0:T(8,128)(2,1)S(1)}, u32[]{:S(2)}, u32[]{:S(2)}) %all-to-all-start.11) | async-done | bytes 262176 | tf_op jit(solution)/shard_map/all_to_all | solution.py:67
  (78 shorter events, 48.4 us)
Async XLA Ops:
  0.6 11.2 %copy-start.7 = (bf16[128,128]{1,0:T(8,128)(2,1)S(1)}, bf16[128,128]{1,0:T(8,128)(2,1)}, u32[]{:S(2)}) copy-start(bf16[128,128]{1,0:T(8,128)(2,1)} %factor_ref.1) | copy-start | bytes 98308
  1.6 10.2 %collective-permute-start = (bf16[224,128]{1,0:T(8,128)(2,1)S(1)}, bf16[224,128]{1,0:T(8,128)(2,1)S(1)}, u32[]{:S(2)}, u32[]{:S(2)}) collective-permute-start(bf16[224,128]{1,0:T(8,128)(2,1)S(1)} %packed.1), channel_id=1, source_target_pairs={{0,0},{16,1},{32,2},{48,3},{64,4},{80,5},{96,6},{112,7},{128,8},{1... | collective-permute-start | bytes 172040 | tf_op jit(solution)/shard_map/ppermute | solution.py:48
  29.8 2.0 collective-permute-start.1
  47.2 11.2 %collective-permute-start.2 = (bf16[16,4096]{1,0:T(8,128)(2,1)S(1)}, bf16[16,4096]{1,0:T(8,128)(2,1)S(1)}, u32[]{:S(2)}, u32[]{:S(2)}) collective-permute-start(bf16[16,4096]{1,0:T(8,128)(2,1)S(1)} %sum_of.1.here_ref), channel_id=1, source_target_pairs={{0,32},{32,0},{1,33},{33,1},{2,34},{34,2},{3,35},{35,3},{4,36},{36... | collective-permute-start | bytes 393224 | tf_op jit(solution)/shard_map/ppermute | solution.py:723
  67.9 7.6 %collective-permute-start.3 = (bf16[8,8,4224]{2,1,0:T(8,128)(2,1)S(1)}, bf16[8,8,4224]{2,1,0:T(8,128)(2,1)S(1)}, u32[]{:S(2)}, u32[]{:S(2)}) collective-permute-start(bf16[8,8,4224]{2,1,0:T(8,128)(2,1)S(1)} %bitcast.58), channel_id=1, source_target_pairs={{0,16},{16,0},{1,17},{17,1},{2,18},{18,2},{3,19},{19,3},{4,20},{20... | collective-permute-start | bytes 1622024 | tf_op jit(solution)/shard_map/ppermute | solution.py:63
  75.5 23.5 %all-to-all-start.2 = ((bf16[8,288,128]{2,1,0:T(8,128)(2,1)}), bf16[8,288,128]{2,1,0:T(8,128)(2,1)S(1)}, u32[]{:S(2)}, u32[]{:S(2)}) async-start(bf16[8,288,128]{2,1,0:T(8,128)(2,1)} %get-tuple-element.74), calls=%async_computation.2 | async-start | bytes 1179648 | tf_op jit(solution)/shard_map/all_to_all | solution.py:67
  99.0 6.5 %collective-permute-start.4 = (bf16[8,288,128]{2,1,0:T(8,128)(2,1)S(1)}, bf16[8,288,128]{2,1,0:T(8,128)(2,1)S(1)}, u32[]{:S(2)}, u32[]{:S(2)}) collective-permute-start(bf16[8,288,128]{2,1,0:T(8,128)(2,1)S(1)} %all-to-all-done.2.own_ref), channel_id=1, source_target_pairs={{0,16},{16,0},{1,17},{17,1},{2,18},{18,2},{3,19},{19,3},{4,20},{20... | collective-permute-start | bytes 1769480 | tf_op jit(solution)/shard_map/ppermute | solution.py:63
  100.7 15.7 %all-to-all-start.3 = ((bf16[16,8,1152]{2,1,0:T(8,128)(2,1)}), bf16[16,8,1152]{2,1,0:T(8,128)(2,1)S(1)}, u32[]{:S(2)}, u32[]{:S(2)}) async-start(bf16[16,8,1152]{2,1,0:T(8,128)(2,1)} %product.2), calls=%async_computation.3 | async-start | bytes 589824 | tf_op jit(solution)/shard_map/all_to_all | solution.py:67
  106.3 0.8 copy-start.5
  117.2 13.6 %all-to-all-start.4 = ((bf16[16,8,1024]{2,1,0:T(8,128)(2,1)}), bf16[16,8,1024]{2,1,0:T(8,128)(2,1)S(1)}, u32[]{:S(2)}, u32[]{:S(2)}) async-start(bf16[16,8,1024]{2,1,0:T(8,128)(2,1)} %get-tuple-element.82), calls=%async_computation.4 | async-start | bytes 524288 | tf_op jit(solution)/shard_map/all_to_all | solution.py:67
  121.1 8.8 %collective-permute-start.5 = (f32[8,1024]{1,0:T(8,128)S(1)}, f32[8,1024]{1,0:T(8,128)S(1)}, u32[]{:S(2)}, u32[]{:S(2)}) collective-permute-start(f32[8,1024]{1,0:T(8,128)S(1)} %get-tuple-element.83), channel_id=1, source_target_pairs={{0,0},{24,1},{32,2},{56,3},{64,4},{88,5},{96,6},{120,7},{128,8},{1... | collective-permute-start | bytes 98312 | tf_op jit(solution)/shard_map/ppermute | solution.py:59
  128.5 1.4 copy-start.1
  133.2 3.8 %collective-permute-start.6 = (bf16[8,8,1024]{2,1,0:T(8,128)(2,1)S(1)}, bf16[8,8,1024]{2,1,0:T(8,128)(2,1)S(1)}, u32[]{:S(2)}, u32[]{:S(2)}) collective-permute-start(bf16[8,8,1024]{2,1,0:T(8,128)(2,1)S(1)} %get-tuple-element.90), channel_id=1, source_target_pairs={{0,16},{16,0},{1,17},{17,1},{2,18},{18,2},{3,19},{19,3},{4,20},{20... | collective-permute-start | bytes 393224 | tf_op jit(solution)/shard_map/ppermute | solution.py:63
  137.6 18.2 %all-to-all-start.5 = ((bf16[8,8,1024]{2,1,0:T(8,128)(2,1)}), bf16[8,8,1024]{2,1,0:T(8,128)(2,1)S(1)}, u32[]{:S(2)}, u32[]{:S(2)}) async-start(bf16[8,8,1024]{2,1,0:T(8,128)(2,1)} %add_convert_fusion.1), calls=%async_computation.5 | async-start | bytes 262144 | tf_op jit(solution)/shard_map/all_to_all | solution.py:67
  151.8 2.0 copy-start
  159.6 11.1 %all-to-all-start.6 = ((f32[16,8,128]{2,1,0:T(8,128)}), f32[16,8,128]{2,1,0:T(8,128)S(1)}, u32[]{:S(2)}, u32[]{:S(2)}) async-start(f32[16,8,128]{2,1,0:T(8,128)} %coarse_product.1), calls=%async_computation.6 | async-start | bytes 131072 | tf_op jit(solution)/shard_map/all_to_all | solution.py:67
  163.7 19.1 %copy-start.6 = (bf16[2048,128]{1,0:T(8,128)(2,1)S(1)}, bf16[2048,128]{1,0:T(8,128)(2,1)}, u32[]{:S(2)}) copy-start(bf16[2048,128]{1,0:T(8,128)(2,1)} %copy-done.5) | copy-start | bytes 1572868
  166.7 1.5 copy-start.2
  171.3 11.5 %all-to-all-start.7 = ((bf16[16,2,8,128]{3,2,1,0:T(8,128)(2,1)}), bf16[16,2,8,128]{3,2,1,0:T(8,128)(2,1)S(1)}, u32[]{:S(2)}, u32[]{:S(2)}) async-start(bf16[16,2,8,128]{3,2,1,0:T(8,128)(2,1)} %coarse_data_of.1), calls=%async_computation.7 | async-start | bytes 131072 | tf_op jit(solution)/shard_map/all_to_all | solution.py:67
  178.8 1.4 copy-start.3
  183.6 11.2 %all-to-all-start.8 = ((bf16[16,8,128]{2,1,0:T(8,128)(2,1)}), bf16[16,8,128]{2,1,0:T(8,128)(2,1)S(1)}, u32[]{:S(2)}, u32[]{:S(2)}) async-start(bf16[16,8,128]{2,1,0:T(8,128)(2,1)} %halfway_of.1), calls=%async_computation.8 | async-start | bytes 65536 | tf_op jit(solution)/shard_map/all_to_all | solution.py:67
  190.9 1.5 copy-start.4
  195.8 11.5 %all-to-all-start.9 = ((bf16[16,8,128]{2,1,0:T(8,128)(2,1)}), bf16[16,8,128]{2,1,0:T(8,128)(2,1)S(1)}, u32[]{:S(2)}, u32[]{:S(2)}) async-start(bf16[16,8,128]{2,1,0:T(8,128)(2,1)} %coarse_coef_of.1), calls=%async_computation.9 | async-start | bytes 65536 | tf_op jit(solution)/shard_map/all_to_all | solution.py:67
  229.3 8.6 %collective-permute-start.7 = (bf16[32,8,1152]{2,1,0:T(8,128)(2,1)S(1)}, bf16[32,8,1152]{2,1,0:T(8,128)(2,1)S(1)}, u32[]{:S(2)}, u32[]{:S(2)}) collective-permute-start(bf16[32,8,1152]{2,1,0:T(8,128)(2,1)S(1)} %all_to_all.62.refs_4_), channel_id=1, source_target_pairs={{0,16},{16,0},{1,17},{17,1},{2,18},{18,2},{3,19},{19,3},{4,20},{20... | collective-permute-start | bytes 1769480 | tf_op jit(solution)/shard_map/ppermute | solution.py:63
  243.0 10.2 %all-to-all-start.11 = ((bf16[4,128,256]{2,1,0:T(8,128)(2,1)}), bf16[4,128,256]{2,1,0:T(8,128)(2,1)S(1)}, u32[]{:S(2)}, u32[]{:S(2)}) async-start(bf16[4,128,256]{2,1,0:T(8,128)(2,1)} %product_dense.1), calls=%async_computation.11 | async-start | bytes 524288 | tf_op jit(solution)/shard_map/all_to_all | solution.py:67

commit v10 on v6

--- a/solution.py
+++ b/solution.py
@@ -171,39 +171,41 @@
                     ref[a, t] = lines[at : at + 1]
                     at += 1
         list_ref[...] = lines[at : at + listed].astype(jnp.int32)
-        for chip in range(HALF):
-            common_ref[chip, pl.ds(0, TILE), :] = factor_ref[...]
-            common_ref[chip, pl.ds(TILE, TILE), :] = there_ref[pl.ds(above, TILE), :]
-            common_ref[chip, pl.ds(2 * TILE, local.shape[0]), :] = local_ref[...]
+        common_ref[pl.ds(0, TILE), :] = factor_ref[...]
+        common_ref[pl.ds(TILE, TILE), :] = there_ref[pl.ds(above, TILE), :]
+        common_ref[pl.ds(2 * TILE, local.shape[0]), :] = local_ref[...]
 
     shapes = [
         ((2, fine, 1, TILE), f32),
         ((2, mid, 1, TILE), f32),
         ((listed, TILE), jnp.int32),
-        ((HALF, size, TILE), bf16),
+        ((size, TILE), bf16),
     ]
     return call(kernel, shapes, (there, factor, local), "unpacked", 8, 1)
 
 
 def in_row_order(place, common, partner, mid):
     at_centres, at_mid = 2 * TILE, 2 * TILE + SIDE
+    length = common.shape[1] // 2
 
     def kernel(place_ref, own_ref, other_ref, down_ref, across_ref, centre_ref, line_ref):
-        core, x = place_ref[0], place_ref[4]
-
-        def rows(chip, of_core, at, size):
-            own, other = own_ref[chip, pl.ds(at, size), :], other_ref[chip, pl.ds(at, size), :]
+        core, x, zh = place_ref[0], place_ref[4], place_ref[5]
+
+        def rows(y, of_zh, of_core, at, size):
+            first = jnp.where(zh == of_zh, 0, length)
+            lines = pl.ds(pl.multiple_of(first + at, SIDE), size)
+            own, other = own_ref[y, lines, :], other_ref[y, lines, :]
             return jnp.where(core == of_core, own.astype(f32), other.astype(f32))
 
         for block in range(SIDE):
-            chip, of_core = block // 2, block % 2
-            down_ref[pl.ds(block * TILE, TILE), :] = rows(chip, of_core, 0, TILE).astype(bf16)
-            across_ref[block] = rows(chip, of_core, TILE, TILE).astype(bf16)
-            lines = rows(chip, of_core, at_centres, SIDE)
+            chip = (block // LINE, block // 2 % 2, block % 2)
+            down_ref[pl.ds(block * TILE, TILE), :] = rows(*chip, 0, TILE).astype(bf16)
+            across_ref[block] = rows(*chip, TILE, TILE).astype(bf16)
+            lines = rows(*chip, at_centres, SIDE)
             for a in range(2):
                 centre_ref[a, block] = lines[a : a + 1]
         for q in range(LINE):
-            lines = rows(x * (LINE // 2) + q // 2, q % 2, at_mid, 2 * mid)
+            lines = rows(x, q // 2, q % 2, at_mid, 2 * mid)
             for a in range(2):
                 for t in range(mid):
                     line_ref[a, q * mid + t] = lines[a * mid + t : a * mid + t + 1]
@@ -418,7 +420,7 @@
 
     return pl.pallas_call(
         kernel,
-        out_shape=pltpu.HBM((rows * TILE, cols * TILE), bf16),
+        out_shape=jax.ShapeDtypeStruct((rows * TILE, cols * TILE), bf16),
         grid=(rows,),
         in_specs=[pl.BlockSpec((2, 1, 1, TILE), lambda i: (0, i, 0, 0)), VMEM],
         out_specs=pl.BlockSpec((TILE, cols * TILE), lambda i: (i, 0)),
@@ -526,10 +528,11 @@
         each = rows // TILE // len(copies)
         for c, copy in enumerate(copies):
             copy.wait()
-            at = pl.ds(c * each * TILE, each * TILE)
-            part = jnp.dot(held[at, :], turned_ref[...], preferred_element_type=f32)
-            for q in range(each):
-                out_ref[c * each + q] = part[q * TILE : (q + 1) * TILE].T[:BLOCK, :]
+            for q in range(c * each, (c + 1) * each):
+                part = jnp.dot(
+                    held[pl.ds(q * TILE, TILE), :], turned_ref[...], preferred_element_type=f32
+                )
+                out_ref[q] = part.T[:BLOCK, :]
 
     shape = (rows // TILE, BLOCK, TILE)
     scratch = [pltpu.VMEM((cols, TILE), bf16)]
@@ -676,7 +679,7 @@
     local = [points2, jnp.zeros((SIDE - 2, TILE), bf16), points1.reshape(2 * tiles_mid, TILE)]
     local = jnp.concatenate(local, axis=0)
     x_id, zl_id = lax.axis_index("x"), lax.axis_index("zl")
-    place = jnp.stack([core, row_id, col_id, zl_id, x_id]).astype(jnp.int32)
+    place = jnp.stack([core, row_id, col_id, zl_id, x_id, lax.axis_index("zh")]).astype(jnp.int32)
     fine_here = points0.astype(f32).reshape(2, tiles_fine, 1, TILE)
     mid_here = points1.astype(f32).reshape(2, tiles_mid, 1, TILE)
     tail = jnp.pad(own_e1, ((0, BLOCK - own_e1.shape[0]), (0, 0))).astype(bf16)
@@ -687,38 +690,46 @@
         there, factor, local, tiles_fine, tiles_mid, first_a1 + 2 * rows_of(listed_a1)
     )
 
-    common = exchanged(common, YZ)
     own, other = product_a0(lists, place, fine_here, fine_there, vector, listed_a0)
-    own, other, common = lax.optimization_barrier((own, other, common))
     pair = pair_sum(own, other).reshape(LINE, 2 * BLOCK, rows_fine)
-    arrived = exchanged(pair, "y")
-
-    common, pair = lax.optimization_barrier((common, pair))
+    summed = sum_of(exchanged(pair, "y"))
+    common, summed = lax.optimization_barrier((common, summed))
+    swapped = lax.ppermute(summed, "zh", [(0, 1), (1, 0)])
+    swapped, common, crossed = lax.optimization_barrier(
+        (swapped, common, lax.ppermute(common, "zh", [(0, 1), (1, 0)]))
+    )
+    common = jnp.concatenate([common, crossed], axis=0)
+    common = jnp.broadcast_to(common, (LINE, *common.shape))
+    fine_own = exchanged(residual_of(summed, swapped, -0.5 * scale_a0), "y")
+    fine_own, common = lax.optimization_barrier((fine_own, common))
+    fine_own = fine_own.reshape(HALF, BLOCK, rows_fine + TILE)
+    fine_other = from_partner(fine_own)
+
+    common, fine_own, fine_other = lax.optimization_barrier((common, fine_own, fine_other))
+    common = exchanged(common, "y")
+    restricted = product(
+        lists, listed_e1, first_e1, 0, fine_there, mid_here, (fine_own, fine_other), support_mid, tail
+    )
+    restricted, common = lax.optimization_barrier((restricted, common))
     ordered = in_row_order(place, common, from_partner(common), tiles_mid)
-    arrived, ordered = lax.optimization_barrier((arrived, ordered))
-    factor_down, factor_across, centres, mid_line = ordered
-    summed = sum_of(arrived)
-    centres, mid_later, fine_later, summed = lax.optimization_barrier(
-        (centres, mid_there, fine_here, summed)
-    )
-    swapped = lax.ppermute(summed, "zh", [(0, 1), (1, 0)])
-    coarse_kernel = all_pairs(centres, mid_later, support_coarse)
-    swapped, coarse_kernel, fine_later = lax.optimization_barrier(
-        (swapped, coarse_kernel, fine_later)
-    )
-    fine_own = exchanged(residual_of(summed, swapped, -0.5 * scale_a0), "y")
-    fine_quarter = fine_later.reshape(2, QUARTER // 2, LINE, 2, 1, TILE)
+    fine_quarter = fine_here.reshape(2, QUARTER // 2, LINE, 2, 1, TILE)
     fine_quarter = lax.dynamic_index_in_dim(fine_quarter, zl_id, 2, keepdims=False)
     fine_quarter = fine_quarter.reshape(2, QUARTER, 1, TILE)
     fine_quarter = jnp.pad(fine_quarter, ((0, 0), (0, 1), (0, 0), (0, 0)), constant_values=8.0)
-    fine_own, fine_quarter = lax.optimization_barrier((fine_own, fine_quarter))
-    fine_own = fine_own.reshape(HALF, BLOCK, rows_fine + TILE)
-    fine_other = from_partner(fine_own)
-
-    restricted = product(
-        lists, listed_e1, first_e1, 0, fine_there, mid_here, (fine_own, fine_other), support_mid, tail
-    )
-    restricted = exchanged(restricted, COL)
+    factor_down, factor_across, centres, mid_line = ordered
+    coarse_kernel = all_pairs(centres, mid_there, support_coarse)
+    restricted, coarse_kernel, factor_down, factor_across, mid_line, fine_quarter = (
+        lax.optimization_barrier(
+            (
+                exchanged(restricted, COL),
+                coarse_kernel,
+                factor_down,
+                factor_across,
+                mid_line,
+                fine_quarter,
+            )
+        )
+    )
     mid_share, mid_all = mid_of(restricted, scale_e1)
     line_lists = lax.dynamic_slice_in_dim(restricted[:, :, rows_mid:], x_id * LINE, LINE, 0)
     line_lists = line_lists[:, : own_e1.shape[0]].reshape(-1, TILE).astype(jnp.int32)
@@ -744,6 +755,7 @@
     fine_part = product_quarter(
         line_lists, mid_line, fine_quarter, new_own, new_other, support_mid
     )
+    fine_part, new_own, new_other = lax.optimization_barrier((fine_part, new_own, new_other))
     own_data = lax.dynamic_slice_in_dim(values, col_id * share, share, 0)
     fine_coef = fine_of(exchanged(fine_part, "x"), own_data, place, scale_e1)
 

time: 251 us -> 248 us (0.988)
  starting transfers between devices: 69.3 us -> 62.8 us
  Pallas kernels: 60.8 us -> 56.5 us
  local copies, waits for them, and re-layouts: 7.06 us -> 10.7 us
  waiting for transfers between devices: 40.2 us -> 43.2 us
    all_to_all x7, starting transfers between devices: 37.9 us -> 29.7 us  [exchanged(): return lax.all_to_all(x, axes, split_axis=0, concat_axis=0, tiled=True)]
    ppermute x0 -> x1, waiting for transfers between devices: none -> 7.46 us  [per_device(): lax.ppermute(common, 'zh', [(0, 1), (1, 0)])]
    all_to_all x7, waiting for transfers between devices: 32 us -> 28.2 us  [exchanged(): return lax.all_to_all(x, axes, split_axis=0, concat_axis=0, tiled=True)]
    ppermute x1, starting transfers between devices: 5.16 us -> 8.64 us  [per_device(): swapped = lax.ppermute(summed, 'zh', [(0, 1), (1, 0)])]
    pallas_call x1, Pallas kernels: 8.66 us -> 5.45 us  [all_pairs(): pl.pallas_call(kernel, out_shape=jax.ShapeDtypeStruct((rows * TILE, cols...]
    unnamed x5 -> x11, local copies, waits for them, and re-layouts: 3.22 us -> 5.96 us
  transfers between devices with their start and end apart: 15 -> 16, of which waited for: 9 -> 12; matrix products, arithmetic and copies ran while one was open for 3% -> 4% of each run, Pallas kernels for 11% -> 7%
where the time goes in v10:
time: 248 us; the launch traced here: 246 us
  blocking collectives  65.9 us (27%)
  starting transfers between devices  62.8 us (25%)
  Pallas kernels  56.5 us (23%)
  waiting for transfers between devices  43.2 us (17%)
  local copies, waits for them, and re-layouts  10.7 us (4%)
  between operations  4.75 us (2%)
    all_to_all x5, blocking collectives, exchanged(): return lax.all_to_all(x, axes, split_axis=0, concat_axis=0, tiled=True)  65.9 us
    pallas_call x14, Pallas kernels, call(): pl.pallas_call(kernel, out_shape=[jax.ShapeDtypeStruct(shape, kind) for s...  43.9 us
    all_to_all x7, starting transfers between devices, exchanged(): return lax.all_to_all(x, axes, split_axis=0, concat_axis=0, tiled=True)  29.7 us
    all_to_all x7, waiting for transfers between devices, exchanged(): return lax.all_to_all(x, axes, split_axis=0, concat_axis=0, tiled=True)  28.2 us
    ppermute x5, starting transfers between devices, from_partner(): return lax.ppermute(x, 'k', [(0, 1), (1, 0)])  16.2 us
    ppermute x1, starting transfers between devices, per_device(): swapped = lax.ppermute(summed, 'zh', [(0, 1), (1, 0)])  8.64 us
    ppermute x1, waiting for transfers between devices, per_device(): lax.ppermute(common, 'zh', [(0, 1), (1, 0)])  7.46 us
    pallas_call x2, Pallas kernels, call_on_matrix(): pl.pallas_call(kernel, out_shape=jax.ShapeDtypeStruct(shape, kind), in_sp...  6.3 us
  transfers between devices with their start and end apart: 16, of which 12 were waited for; matrix products, arithmetic and copies ran while one was open for 4% of the time, Pallas kernels for 7%

profile of v10, /device:TPU:1, one launch (start us, length us, event | category | flops | bytes accessed | tf_op | source)
XLA Modules:
  0.0 246.4 jit_solution(11800520784278494870)
XLA Ops:
  1.6 4.9 %collective-permute-start = (bf16[224,128]{1,0:T(8,128)(2,1)S(1)}, bf16[224,128]{1,0:T(8,128)(2,1)S(1)}, u32[]{:S(2)}, u32[]{:S(2)}) collective-permute-start(bf16[224,128]{1,0:T(8,128)(2,1)S(1)} %packed.1), channel_id=1, source_target_pairs={{0,0},{16,1},{32,2},{48,3},{64,4},{80,5},{96,6},{112,7},{128,8},{1... | collective-permute-start | bytes 172040 | tf_op jit(solution)/shard_map/ppermute | solution.py:48
  11.8 17.0 %product_a0.1 = (bf16[8,8,4096]{2,1,0:T(8,128)(2,1)S(1)}, bf16[8,8,4096]{2,1,0:T(8,128)(2,1)S(1)}) custom-call(s32[12,128]{1,0:T(8,128)S(1)} %get-tuple-element.52.list_ref, s32[6]{0:T(128)S(1)} %stack.42.place_ref.core_ref, f32[2,32,1,128]{3,2,1,0:T(1,128)S(1)} %reshape.81.left_ref, f32[2,32,1,128]{3,2,1,0:T(1,128)S(1)} %get-tuple-element.53.right_ref.left_ref, ...), custom_call_target="tpu_custom_call" | custom-call | bytes 60000000 | tf_op jit(solution)/shard_map/product_a0/pallas_call | solution.py:93
  31.0 15.3 %all_to_all.60.arrived_ref = bf16[4,16,4096]{2,1,0:T(8,128)(2,1)S(1)} all-to-all(bf16[4,16,4096]{2,1,0:T(8,128)(2,1)S(1)} %bitcast.64), channel_id=1, replica_groups=mesh['y'=4,'zh'=2,'k'=2,'x'=4,'zl'=4] {'y'}, dimensions={0} | all-to-all | bytes 1048576 | tf_op jit(solution)/shard_map/all_to_all | solution.py:67
  46.4 8.6 %collective-permute-start.2 = (bf16[16,4096]{1,0:T(8,128)(2,1)S(1)}, bf16[16,4096]{1,0:T(8,128)(2,1)S(1)}, u32[]{:S(2)}, u32[]{:S(2)}) collective-permute-start(bf16[16,4096]{1,0:T(8,128)(2,1)S(1)} %sum_of.1.here_ref), channel_id=1, source_target_pairs={{0,32},{32,0},{1,33},{33,1},{2,34},{34,2},{3,35},{35,3},{4,36},{36... | collective-permute-start | bytes 393224 | tf_op jit(solution)/shard_map/ppermute | solution.py:697
  55.2 7.5 %collective-permute-done.3 = bf16[288,128]{1,0:T(8,128)(2,1)S(1)} collective-permute-done((bf16[288,128]{1,0:T(8,128)(2,1)S(1)}, bf16[288,128]{1,0:T(8,128)(2,1)S(1)}, u32[]{:S(2)}, u32[]{:S(2)}) %collective-permute-start.3) | collective-permute-done | bytes 73760 | tf_op jit(solution)/shard_map/ppermute | solution.py:699
  63.6 3.5 %all-to-all-start.1 = ((bf16[4,16,4224]{2,1,0:T(8,128)(2,1)}), bf16[4,16,4224]{2,1,0:T(8,128)(2,1)S(1)}, u32[]{:S(2)}, u32[]{:S(2)}) async-start(bf16[4,16,4224]{2,1,0:T(8,128)(2,1)} %residual_of.1), calls=%async_computation.1 | async-start | bytes 1081344 | tf_op jit(solution)/shard_map/all_to_all | solution.py:67
  67.1 7.0 %all-to-all-done.1 = bf16[4,16,4224]{2,1,0:T(8,128)(2,1)S(1)} async-done(((bf16[4,16,4224]{2,1,0:T(8,128)(2,1)}), bf16[4,16,4224]{2,1,0:T(8,128)(2,1)S(1)}, u32[]{:S(2)}, u32[]{:S(2)}) %all-to-all-start.1) | async-done | bytes 540704 | tf_op jit(solution)/shard_map/all_to_all | solution.py:67
  74.9 4.1 %collective-permute-start.4 = (bf16[8,8,4224]{2,1,0:T(8,128)(2,1)S(1)}, bf16[8,8,4224]{2,1,0:T(8,128)(2,1)S(1)}, u32[]{:S(2)}, u32[]{:S(2)}) collective-permute-start(bf16[8,8,4224]{2,1,0:T(8,128)(2,1)S(1)} %bitcast.59), channel_id=1, source_target_pairs={{0,16},{16,0},{1,17},{17,1},{2,18},{18,2},{3,19},{19,3},{4,20},{20... | collective-permute-start | bytes 1622024 | tf_op jit(solution)/shard_map/ppermute | solution.py:63
  80.6 3.5 %all-to-all-start.2 = ((bf16[4,576,128]{2,1,0:T(8,128)(2,1)}), bf16[4,576,128]{2,1,0:T(8,128)(2,1)S(1)}, u32[]{:S(2)}, u32[]{:S(2)}) async-start(bf16[4,576,128]{2,1,0:T(8,128)(2,1)} %broadcast_in_dim.7), calls=%async_computation.2 | async-start | bytes 1179648 | tf_op jit(solution)/shard_map/all_to_all | solution.py:67
  84.1 8.8 %product.2 = bf16[16,8,1152]{2,1,0:T(8,128)(2,1)} custom-call(s32[12,128]{1,0:T(8,128)S(1)} %get-tuple-element.52.list_ref, f32[2,32,1,128]{3,2,1,0:T(1,128)S(1)} %get-tuple-element.53.right_ref.left_ref, f32[2,8,1,128]{3,2,1,0:T(1,128)S(1)} %reshape.83.right_ref.left_ref, bf16[8,8,4224]{2,1,0:T(8,128)(2,1)S(1)} %bitcast.60, ...), custom_call_target="tpu_custom_call" | custom-call | bytes 26666666 | tf_op jit(solution)/shard_map/product/pallas_call | solution.py:93
  95.2 5.9 %all-to-all-start.3 = ((bf16[16,8,1152]{2,1,0:T(8,128)(2,1)}), bf16[16,8,1152]{2,1,0:T(8,128)(2,1)S(1)}, u32[]{:S(2)}, u32[]{:S(2)}) async-start(bf16[16,8,1152]{2,1,0:T(8,128)(2,1)} %product.2), calls=%async_computation.3 | async-start | bytes 589824 | tf_op jit(solution)/shard_map/all_to_all | solution.py:67
  102.7 5.5 %all_pairs.1.matrix_ref = bf16[2048,1024]{1,0:T(8,128)(2,1)S(1)} custom-call(f32[2,16,1,128]{3,2,1,0:T(1,128)S(1)} %get-tuple-element.73.left_ref, f32[2,8,1,128]{3,2,1,0:T(1,128)S(1)} %get-tuple-element.74.right_ref), custom_call_target="tpu_custom_call" | custom-call | bytes 18000000 | tf_op jit(solution)/shard_map/all_pairs/pallas_call | solution.py:421
  112.8 5.0 %all-to-all-start.4 = ((bf16[16,8,1024]{2,1,0:T(8,128)(2,1)}), bf16[16,8,1024]{2,1,0:T(8,128)(2,1)S(1)}, u32[]{:S(2)}, u32[]{:S(2)}) async-start(bf16[16,8,1024]{2,1,0:T(8,128)(2,1)} %get-tuple-element.79), calls=%async_computation.4 | async-start | bytes 524288 | tf_op jit(solution)/shard_map/all_to_all | solution.py:67
  117.9 3.3 %collective-permute-start.6 = (f32[8,1024]{1,0:T(8,128)S(1)}, f32[8,1024]{1,0:T(8,128)S(1)}, u32[]{:S(2)}, u32[]{:S(2)}) collective-permute-start(f32[8,1024]{1,0:T(8,128)S(1)} %get-tuple-element.80), channel_id=1, source_target_pairs={{0,0},{24,1},{32,2},{56,3},{64,4},{88,5},{96,6},{120,7},{128,8},{1... | collective-permute-start | bytes 98312 | tf_op jit(solution)/shard_map/ppermute | solution.py:59
  122.4 3.0 %collective-permute-done.6.mid_ref = f32[8,1024]{1,0:T(8,128)S(1)} collective-permute-done((f32[8,1024]{1,0:T(8,128)S(1)}, f32[8,1024]{1,0:T(8,128)S(1)}, u32[]{:S(2)}, u32[]{:S(2)}) %collective-permute-start.6) | collective-permute-done | bytes 32800 | tf_op jit(solution)/shard_map/ppermute | solution.py:59
  125.4 2.1 all-to-all-done.4
  127.6 2.4 product.3
  130.0 2.7 %collective-permute-start.7 = (bf16[8,8,1024]{2,1,0:T(8,128)(2,1)S(1)}, bf16[8,8,1024]{2,1,0:T(8,128)(2,1)S(1)}, u32[]{:S(2)}, u32[]{:S(2)}) collective-permute-start(bf16[8,8,1024]{2,1,0:T(8,128)(2,1)S(1)} %get-tuple-element.87), channel_id=1, source_target_pairs={{0,16},{16,0},{1,17},{17,1},{2,18},{18,2},{3,19},{19,3},{4,20},{20... | collective-permute-start | bytes 393224 | tf_op jit(solution)/shard_map/ppermute | solution.py:63
  133.8 16.0 %all_to_all.61.arrived_ref = bf16[8,8,1024]{2,1,0:T(8,128)(2,1)S(1)} all-to-all(bf16[8,8,1024]{2,1,0:T(8,128)(2,1)S(1)} %add_convert_fusion.1), channel_id=1, replica_groups=mesh['y'=4,'zh'=2,'k'=2,'x'=4,'zl'=4] {'y','zh'}, dimensions={0} | all-to-all | bytes 262144 | tf_op jit(solution)/shard_map/all_to_all | solution.py:67
  149.7 3.8 %coarse_product.1 = f32[16,8,128]{2,1,0:T(8,128)} custom-call(bf16[2048,1024]{1,0:T(8,128)(2,1)} %copy-done, bf16[8,8,1024]{2,1,0:T(8,128)(2,1)S(1)} %all_to_all.61.arrived_ref, f32[8,1024]{1,0:T(8,128)S(1)} %collective-permute-done.6.mid_ref), custom_call_target="tpu_custom_call" | custom-call | bytes 9000000 | tf_op jit(solution)/shard_map/coarse_product/pallas_call | solution.py:499
  153.6 4.9 %all-to-all-start.6 = ((f32[16,8,128]{2,1,0:T(8,128)}), f32[16,8,128]{2,1,0:T(8,128)S(1)}, u32[]{:S(2)}, u32[]{:S(2)}) async-start(f32[16,8,128]{2,1,0:T(8,128)} %coarse_product.1), calls=%async_computation.6 | async-start | bytes 131072 | tf_op jit(solution)/shard_map/all_to_all | solution.py:67
  158.5 7.0 %all-to-all-done.6.arrived_ref = f32[16,8,128]{2,1,0:T(8,128)S(1)} async-done(((f32[16,8,128]{2,1,0:T(8,128)}), f32[16,8,128]{2,1,0:T(8,128)S(1)}, u32[]{:S(2)}, u32[]{:S(2)}) %all-to-all-start.6) | async-done | bytes 65568 | tf_op jit(solution)/shard_map/all_to_all | solution.py:67
  165.5 9.5 %all_to_all.62.data_ref = bf16[16,2,8,128]{3,2,1,0:T(8,128)(2,1)S(1)} all-to-all(bf16[16,2,8,128]{3,2,1,0:T(8,128)(2,1)S(1)} %coarse_data_of.1), channel_id=1, replica_groups=mesh['y'=4,'zh'=2,'k'=2,'x'=4,'zl'=4] {'x','zl'}, dimensions={0} | all-to-all | bytes 131072 | tf_op jit(solution)/shard_map/all_to_all | solution.py:67
  175.2 9.4 %all_to_all.63.half_ref = bf16[16,8,128]{2,1,0:T(8,128)(2,1)S(1)} all-to-all(bf16[16,8,128]{2,1,0:T(8,128)(2,1)S(1)} %halfway_of.1), channel_id=1, replica_groups=mesh['y'=4,'zh'=2,'k'=2,'x'=4,'zl'=4] {'x','zl'}, dimensions={0} | all-to-all | bytes 65536 | tf_op jit(solution)/shard_map/all_to_all | solution.py:67
  185.6 3.5 %all-to-all-start.9 = ((bf16[16,8,128]{2,1,0:T(8,128)(2,1)}), bf16[16,8,128]{2,1,0:T(8,128)(2,1)S(1)}, u32[]{:S(2)}, u32[]{:S(2)}) async-start(bf16[16,8,128]{2,1,0:T(8,128)(2,1)} %coarse_coef_of.1), calls=%async_computation.9 | async-start | bytes 65536 | tf_op jit(solution)/shard_map/all_to_all | solution.py:67
  191.7 4.3 %all-to-all-done.9.coef_ref = bf16[16,8,128]{2,1,0:T(8,128)(2,1)S(1)} async-done(((bf16[16,8,128]{2,1,0:T(8,128)(2,1)}), bf16[16,8,128]{2,1,0:T(8,128)(2,1)S(1)}, u32[]{:S(2)}, u32[]{:S(2)}) %all-to-all-start.9) | async-done | bytes 32800 | tf_op jit(solution)/shard_map/all_to_all | solution.py:67
  196.0 2.5 %prolong.1 = bf16[32,8,1152]{2,1,0:T(8,128)(2,1)S(1)} custom-call(bf16[2048,1024]{1,0:T(8,128)(2,1)} %copy-done, bf16[16,8,128]{2,1,0:T(8,128)(2,1)S(1)} %all-to-all-done.9.coef_ref, bf16[8,8,128]{2,1,0:T(8,128)(2,1)S(1)} %fusion.4.low_ref, f32[8,1024]{1,0:T(8,128)S(1)} %collective-permute-done.6.mid_ref), custom_call_target="tpu_custom_call" | custom-call | bytes 9000000 | tf_op jit(solution)/shard_map/prolong/pallas_call | solution.py:499
  198.4 15.7 %all_to_all.64.own_ref = bf16[32,8,1152]{2,1,0:T(8,128)(2,1)S(1)} all-to-all(bf16[32,8,1152]{2,1,0:T(8,128)(2,1)S(1)} %prolong.1), channel_id=1, replica_groups=mesh['y'=4,'zh'=2,'k'=2,'x'=4,'zl'=4] {'y','zh','zl'}, dimensions={0} | all-to-all | bytes 1179648 | tf_op jit(solution)/shard_map/all_to_all | solution.py:67
  214.1 8.0 %collective-permute-start.8 = (bf16[32,8,1152]{2,1,0:T(8,128)(2,1)S(1)}, bf16[32,8,1152]{2,1,0:T(8,128)(2,1)S(1)}, u32[]{:S(2)}, u32[]{:S(2)}) collective-permute-start(bf16[32,8,1152]{2,1,0:T(8,128)(2,1)S(1)} %all_to_all.64.own_ref), channel_id=1, source_target_pairs={{0,16},{16,0},{1,17},{17,1},{2,18},{18,2},{3,19},{19,3},{4,20},{20... | collective-permute-start | bytes 1769480 | tf_op jit(solution)/shard_map/ppermute | solution.py:63
  224.3 9.3 %product_quarter.1 = bf16[4,128,256]{2,1,0:T(8,128)(2,1)} custom-call(s32[8,256]{1,0:T(8,128)S(1)} %quarter_of.1.list_ref, f32[2,32,1,128]{3,2,1,0:T(1,128)S(1)} %get-tuple-element.82.left_ref, f32[2,9,1,128]{3,2,1,0:T(1,128)S(1)} %pad.16.right_ref, bf16[32,8,1152]{2,1,0:T(8,128)(2,1)S(1)} %all_to_all.64.own_ref, ...), custom_call_target="tpu_custom_call" | custom-call | bytes 30000000 | tf_op jit(solution)/shard_map/product_quarter/pallas_call | solution.py:93
  233.7 3.4 %all-to-all-start.11 = ((bf16[4,128,256]{2,1,0:T(8,128)(2,1)}), bf16[4,128,256]{2,1,0:T(8,128)(2,1)S(1)}, u32[]{:S(2)}, u32[]{:S(2)}) async-start(bf16[4,128,256]{2,1,0:T(8,128)(2,1)} %product_quarter.1), calls=%async_computation.11 | async-start | bytes 524288 | tf_op jit(solution)/shard_map/all_to_all | solution.py:67
  238.9 4.9 %all-to-all-done.11.arrived_ref = bf16[4,128,256]{2,1,0:T(8,128)(2,1)S(1)} async-done(((bf16[4,128,256]{2,1,0:T(8,128)(2,1)}), bf16[4,128,256]{2,1,0:T(8,128)(2,1)S(1)}, u32[]{:S(2)}, u32[]{:S(2)}) %all-to-all-start.11) | async-done | bytes 262176 | tf_op jit(solution)/shard_map/all_to_all | solution.py:67
  (67 shorter events, 29.2 us)
Async XLA Ops:
  0.6 11.2 %copy-start.3 = (bf16[128,128]{1,0:T(8,128)(2,1)S(1)}, bf16[128,128]{1,0:T(8,128)(2,1)}, u32[]{:S(2)}) copy-start(bf16[128,128]{1,0:T(8,128)(2,1)} %factor_ref.1) | copy-start | bytes 98308
  1.6 10.2 %collective-permute-start = (bf16[224,128]{1,0:T(8,128)(2,1)S(1)}, bf16[224,128]{1,0:T(8,128)(2,1)S(1)}, u32[]{:S(2)}, u32[]{:S(2)}) collective-permute-start(bf16[224,128]{1,0:T(8,128)(2,1)S(1)} %packed.1), channel_id=1, source_target_pairs={{0,0},{16,1},{32,2},{48,3},{64,4},{80,5},{96,6},{112,7},{128,8},{1... | collective-permute-start | bytes 172040 | tf_op jit(solution)/shard_map/ppermute | solution.py:48
  28.9 2.0 collective-permute-start.1
  46.4 16.2 %collective-permute-start.2 = (bf16[16,4096]{1,0:T(8,128)(2,1)S(1)}, bf16[16,4096]{1,0:T(8,128)(2,1)S(1)}, u32[]{:S(2)}, u32[]{:S(2)}) collective-permute-start(bf16[16,4096]{1,0:T(8,128)(2,1)S(1)} %sum_of.1.here_ref), channel_id=1, source_target_pairs={{0,32},{32,0},{1,33},{33,1},{2,34},{34,2},{3,35},{35,3},{4,36},{36... | collective-permute-start | bytes 393224 | tf_op jit(solution)/shard_map/ppermute | solution.py:697
  55.1 7.6 %collective-permute-start.3 = (bf16[288,128]{1,0:T(8,128)(2,1)S(1)}, bf16[288,128]{1,0:T(8,128)(2,1)S(1)}, u32[]{:S(2)}, u32[]{:S(2)}) collective-permute-start(bf16[288,128]{1,0:T(8,128)(2,1)S(1)} %get-tuple-element.63), channel_id=1, source_target_pairs={{0,32},{32,0},{1,33},{33,1},{2,34},{34,2},{3,35},{35,3},{4,36},{36... | collective-permute-start | bytes 221192 | tf_op jit(solution)/shard_map/ppermute | solution.py:699
  63.6 10.5 %all-to-all-start.1 = ((bf16[4,16,4224]{2,1,0:T(8,128)(2,1)}), bf16[4,16,4224]{2,1,0:T(8,128)(2,1)S(1)}, u32[]{:S(2)}, u32[]{:S(2)}) async-start(bf16[4,16,4224]{2,1,0:T(8,128)(2,1)} %residual_of.1), calls=%async_computation.1 | async-start | bytes 1081344 | tf_op jit(solution)/shard_map/all_to_all | solution.py:67
  74.9 5.7 %collective-permute-start.4 = (bf16[8,8,4224]{2,1,0:T(8,128)(2,1)S(1)}, bf16[8,8,4224]{2,1,0:T(8,128)(2,1)S(1)}, u32[]{:S(2)}, u32[]{:S(2)}) collective-permute-start(bf16[8,8,4224]{2,1,0:T(8,128)(2,1)S(1)} %bitcast.59), channel_id=1, source_target_pairs={{0,16},{16,0},{1,17},{17,1},{2,18},{18,2},{3,19},{19,3},{4,20},{20... | collective-permute-start | bytes 1622024 | tf_op jit(solution)/shard_map/ppermute | solution.py:63
  80.6 13.4 %all-to-all-start.2 = ((bf16[4,576,128]{2,1,0:T(8,128)(2,1)}), bf16[4,576,128]{2,1,0:T(8,128)(2,1)S(1)}, u32[]{:S(2)}, u32[]{:S(2)}) async-start(bf16[4,576,128]{2,1,0:T(8,128)(2,1)} %broadcast_in_dim.7), calls=%async_computation.2 | async-start | bytes 1179648 | tf_op jit(solution)/shard_map/all_to_all | solution.py:67
  94.0 7.1 %collective-permute-start.5 = (bf16[4,576,128]{2,1,0:T(8,128)(2,1)S(1)}, bf16[4,576,128]{2,1,0:T(8,128)(2,1)S(1)}, u32[]{:S(2)}, u32[]{:S(2)}) collective-permute-start(bf16[4,576,128]{2,1,0:T(8,128)(2,1)S(1)} %all-to-all-done.2.own_ref), channel_id=1, source_target_pairs={{0,16},{16,0},{1,17},{17,1},{2,18},{18,2},{3,19},{19,3},{4,20},{20... | collective-permute-start | bytes 1769480 | tf_op jit(solution)/shard_map/ppermute | solution.py:63
  95.2 16.8 %all-to-all-start.3 = ((bf16[16,8,1152]{2,1,0:T(8,128)(2,1)}), bf16[16,8,1152]{2,1,0:T(8,128)(2,1)S(1)}, u32[]{:S(2)}, u32[]{:S(2)}) async-start(bf16[16,8,1152]{2,1,0:T(8,128)(2,1)} %product.2), calls=%async_computation.3 | async-start | bytes 589824 | tf_op jit(solution)/shard_map/all_to_all | solution.py:67
  101.9 0.8 copy-start.1
  108.2 2.0 copy-start
  112.8 14.8 %all-to-all-start.4 = ((bf16[16,8,1024]{2,1,0:T(8,128)(2,1)}), bf16[16,8,1024]{2,1,0:T(8,128)(2,1)S(1)}, u32[]{:S(2)}, u32[]{:S(2)}) async-start(bf16[16,8,1024]{2,1,0:T(8,128)(2,1)} %get-tuple-element.79), calls=%async_computation.4 | async-start | bytes 524288 | tf_op jit(solution)/shard_map/all_to_all | solution.py:67
  117.9 7.6 %collective-permute-start.6 = (f32[8,1024]{1,0:T(8,128)S(1)}, f32[8,1024]{1,0:T(8,128)S(1)}, u32[]{:S(2)}, u32[]{:S(2)}) collective-permute-start(f32[8,1024]{1,0:T(8,128)S(1)} %get-tuple-element.80), channel_id=1, source_target_pairs={{0,0},{24,1},{32,2},{56,3},{64,4},{88,5},{96,6},{120,7},{128,8},{1... | collective-permute-start | bytes 98312 | tf_op jit(solution)/shard_map/ppermute | solution.py:59
  130.0 3.7 %collective-permute-start.7 = (bf16[8,8,1024]{2,1,0:T(8,128)(2,1)S(1)}, bf16[8,8,1024]{2,1,0:T(8,128)(2,1)S(1)}, u32[]{:S(2)}, u32[]{:S(2)}) collective-permute-start(bf16[8,8,1024]{2,1,0:T(8,128)(2,1)S(1)} %get-tuple-element.87), channel_id=1, source_target_pairs={{0,16},{16,0},{1,17},{17,1},{2,18},{18,2},{3,19},{19,3},{4,20},{20... | collective-permute-start | bytes 393224 | tf_op jit(solution)/shard_map/ppermute | solution.py:63
  149.7 25.3 %copy-start.2 = (bf16[2048,128]{1,0:T(8,128)(2,1)S(1)}, bf16[2048,128]{1,0:T(8,128)(2,1)}, u32[]{:S(2)}) copy-start(bf16[2048,128]{1,0:T(8,128)(2,1)} %copy-done.1) | copy-start | bytes 1572868
  153.6 11.9 %all-to-all-start.6 = ((f32[16,8,128]{2,1,0:T(8,128)}), f32[16,8,128]{2,1,0:T(8,128)S(1)}, u32[]{:S(2)}, u32[]{:S(2)}) async-start(f32[16,8,128]{2,1,0:T(8,128)} %coarse_product.1), calls=%async_computation.6 | async-start | bytes 131072 | tf_op jit(solution)/shard_map/all_to_all | solution.py:67
  185.6 10.3 %all-to-all-start.9 = ((bf16[16,8,128]{2,1,0:T(8,128)(2,1)}), bf16[16,8,128]{2,1,0:T(8,128)(2,1)S(1)}, u32[]{:S(2)}, u32[]{:S(2)}) async-start(bf16[16,8,128]{2,1,0:T(8,128)(2,1)} %coarse_coef_of.1), calls=%async_computation.9 | async-start | bytes 65536 | tf_op jit(solution)/shard_map/all_to_all | solution.py:67
  214.1 10.1 %collective-permute-start.8 = (bf16[32,8,1152]{2,1,0:T(8,128)(2,1)S(1)}, bf16[32,8,1152]{2,1,0:T(8,128)(2,1)S(1)}, u32[]{:S(2)}, u32[]{:S(2)}) collective-permute-start(bf16[32,8,1152]{2,1,0:T(8,128)(2,1)S(1)} %all_to_all.64.own_ref), channel_id=1, source_target_pairs={{0,16},{16,0},{1,17},{17,1},{2,18},{18,2},{3,19},{19,3},{4,20},{20... | collective-permute-start | bytes 1769480 | tf_op jit(solution)/shard_map/ppermute | solution.py:63
  233.7 10.2 %all-to-all-start.11 = ((bf16[4,128,256]{2,1,0:T(8,128)(2,1)}), bf16[4,128,256]{2,1,0:T(8,128)(2,1)S(1)}, u32[]{:S(2)}, u32[]{:S(2)}) async-start(bf16[4,128,256]{2,1,0:T(8,128)(2,1)} %product_quarter.1), calls=%async_computation.11 | async-start | bytes 524288 | tf_op jit(solution)/shard_map/all_to_all | solution.py:67

commit v11 on v10

--- a/solution.py
+++ b/solution.py
@@ -532,12 +532,12 @@
                 part = jnp.dot(
                     held[pl.ds(q * TILE, TILE), :], turned_ref[...], preferred_element_type=f32
                 )
-                out_ref[q] = part.T[:BLOCK, :]
+                out_ref[q] = part.T[:BLOCK, :].astype(bf16)
 
     shape = (rows // TILE, BLOCK, TILE)
     scratch = [pltpu.VMEM((cols, TILE), bf16)]
     operands = (arrived, mid_data)
-    return call_on_matrix(kernel, shape, f32, matrix, operands, "coarse_product", scratch)
+    return call_on_matrix(kernel, shape, bf16, matrix, operands, "coarse_product", scratch)
 
 
 def coarse_data_of(arrived, own, other, scale):
@@ -545,7 +545,7 @@
     n = own.shape[2] - TILE
 
     def kernel(arrived_ref, own_ref, other_ref, out_ref):
-        data = (scale * arrived_ref[...].sum(axis=0)).astype(bf16)
+        data = (scale * arrived_ref[...].astype(f32).sum(axis=0)).astype(bf16)
         squares = jnp.zeros((1, TILE), f32)
         for ref in (own_ref, other_ref):
             tails = ref[...].astype(f32).sum(axis=0)

time: 248 us -> 248 us (level)
  no operation moved by 1% of the time
where the time goes in v11:
time: 248 us; the launch traced here: 245 us
  blocking collectives  66 us (27%)
  starting transfers between devices  62.9 us (25%)
  Pallas kernels  56.5 us (23%)
  waiting for transfers between devices  42 us (17%)
  local copies, waits for them, and re-layouts  10.7 us (4%)
  between operations  4.75 us (2%)
    all_to_all x5, blocking collectives, exchanged(): return lax.all_to_all(x, axes, split_axis=0, concat_axis=0, tiled=True)  66 us
    pallas_call x14, Pallas kernels, call(): pl.pallas_call(kernel, out_shape=[jax.ShapeDtypeStruct(shape, kind) for s...  43.9 us
    all_to_all x7, starting transfers between devices, exchanged(): return lax.all_to_all(x, axes, split_axis=0, concat_axis=0, tiled=True)  29.8 us
    all_to_all x7, waiting for transfers between devices, exchanged(): return lax.all_to_all(x, axes, split_axis=0, concat_axis=0, tiled=True)  27 us
    ppermute x5, starting transfers between devices, from_partner(): return lax.ppermute(x, 'k', [(0, 1), (1, 0)])  16.2 us
    ppermute x1, starting transfers between devices, per_device(): swapped = lax.ppermute(summed, 'zh', [(0, 1), (1, 0)])  8.6 us
    ppermute x1, waiting for transfers between devices, per_device(): lax.ppermute(common, 'zh', [(0, 1), (1, 0)])  7.46 us
    pallas_call x2, Pallas kernels, call_on_matrix(): pl.pallas_call(kernel, out_shape=jax.ShapeDtypeStruct(shape, kind), in_sp...  6.28 us
  transfers between devices with their start and end apart: 16, of which 12 were waited for; matrix products, arithmetic and copies ran while one was open for 4% of the time, Pallas kernels for 7%

profile of v11, /device:TPU:1, one launch (start us, length us, event | category | flops | bytes accessed | tf_op | source)
XLA Modules:
  0.0 245.3 jit_solution(4877429812331157697)
XLA Ops:
  1.6 4.9 %collective-permute-start = (bf16[224,128]{1,0:T(8,128)(2,1)S(1)}, bf16[224,128]{1,0:T(8,128)(2,1)S(1)}, u32[]{:S(2)}, u32[]{:S(2)}) collective-permute-start(bf16[224,128]{1,0:T(8,128)(2,1)S(1)} %packed.1), channel_id=1, source_target_pairs={{0,0},{16,1},{32,2},{48,3},{64,4},{80,5},{96,6},{112,7},{128,8},{1... | collective-permute-start | bytes 172040 | tf_op jit(solution)/shard_map/ppermute | solution.py:48
  11.8 17.1 %product_a0.1 = (bf16[8,8,4096]{2,1,0:T(8,128)(2,1)S(1)}, bf16[8,8,4096]{2,1,0:T(8,128)(2,1)S(1)}) custom-call(s32[12,128]{1,0:T(8,128)S(1)} %get-tuple-element.52.list_ref, s32[6]{0:T(128)S(1)} %stack.42.place_ref.core_ref, f32[2,32,1,128]{3,2,1,0:T(1,128)S(1)} %reshape.81.left_ref, f32[2,32,1,128]{3,2,1,0:T(1,128)S(1)} %get-tuple-element.53.right_ref.left_ref, ...), custom_call_target="tpu_custom_call" | custom-call | bytes 60000000 | tf_op jit(solution)/shard_map/product_a0/pallas_call | solution.py:93
  31.1 15.3 %all_to_all.60.arrived_ref = bf16[4,16,4096]{2,1,0:T(8,128)(2,1)S(1)} all-to-all(bf16[4,16,4096]{2,1,0:T(8,128)(2,1)S(1)} %bitcast.64), channel_id=1, replica_groups=mesh['y'=4,'zh'=2,'k'=2,'x'=4,'zl'=4] {'y'}, dimensions={0} | all-to-all | bytes 1048576 | tf_op jit(solution)/shard_map/all_to_all | solution.py:67
  46.5 8.6 %collective-permute-start.2 = (bf16[16,4096]{1,0:T(8,128)(2,1)S(1)}, bf16[16,4096]{1,0:T(8,128)(2,1)S(1)}, u32[]{:S(2)}, u32[]{:S(2)}) collective-permute-start(bf16[16,4096]{1,0:T(8,128)(2,1)S(1)} %sum_of.1.here_ref), channel_id=1, source_target_pairs={{0,32},{32,0},{1,33},{33,1},{2,34},{34,2},{3,35},{35,3},{4,36},{36... | collective-permute-start | bytes 393224 | tf_op jit(solution)/shard_map/ppermute | solution.py:697
  55.2 7.5 %collective-permute-done.3 = bf16[288,128]{1,0:T(8,128)(2,1)S(1)} collective-permute-done((bf16[288,128]{1,0:T(8,128)(2,1)S(1)}, bf16[288,128]{1,0:T(8,128)(2,1)S(1)}, u32[]{:S(2)}, u32[]{:S(2)}) %collective-permute-start.3) | collective-permute-done | bytes 73760 | tf_op jit(solution)/shard_map/ppermute | solution.py:699
  63.6 3.5 %all-to-all-start.1 = ((bf16[4,16,4224]{2,1,0:T(8,128)(2,1)}), bf16[4,16,4224]{2,1,0:T(8,128)(2,1)S(1)}, u32[]{:S(2)}, u32[]{:S(2)}) async-start(bf16[4,16,4224]{2,1,0:T(8,128)(2,1)} %residual_of.1), calls=%async_computation.1 | async-start | bytes 1081344 | tf_op jit(solution)/shard_map/all_to_all | solution.py:67
  67.1 7.0 %all-to-all-done.1 = bf16[4,16,4224]{2,1,0:T(8,128)(2,1)S(1)} async-done(((bf16[4,16,4224]{2,1,0:T(8,128)(2,1)}), bf16[4,16,4224]{2,1,0:T(8,128)(2,1)S(1)}, u32[]{:S(2)}, u32[]{:S(2)}) %all-to-all-start.1) | async-done | bytes 540704 | tf_op jit(solution)/shard_map/all_to_all | solution.py:67
  74.9 4.1 %collective-permute-start.4 = (bf16[8,8,4224]{2,1,0:T(8,128)(2,1)S(1)}, bf16[8,8,4224]{2,1,0:T(8,128)(2,1)S(1)}, u32[]{:S(2)}, u32[]{:S(2)}) collective-permute-start(bf16[8,8,4224]{2,1,0:T(8,128)(2,1)S(1)} %bitcast.59), channel_id=1, source_target_pairs={{0,16},{16,0},{1,17},{17,1},{2,18},{18,2},{3,19},{19,3},{4,20},{20... | collective-permute-start | bytes 1622024 | tf_op jit(solution)/shard_map/ppermute | solution.py:63
  80.6 3.5 %all-to-all-start.2 = ((bf16[4,576,128]{2,1,0:T(8,128)(2,1)}), bf16[4,576,128]{2,1,0:T(8,128)(2,1)S(1)}, u32[]{:S(2)}, u32[]{:S(2)}) async-start(bf16[4,576,128]{2,1,0:T(8,128)(2,1)} %broadcast_in_dim.7), calls=%async_computation.2 | async-start | bytes 1179648 | tf_op jit(solution)/shard_map/all_to_all | solution.py:67
  84.1 8.8 %product.2 = bf16[16,8,1152]{2,1,0:T(8,128)(2,1)} custom-call(s32[12,128]{1,0:T(8,128)S(1)} %get-tuple-element.52.list_ref, f32[2,32,1,128]{3,2,1,0:T(1,128)S(1)} %get-tuple-element.53.right_ref.left_ref, f32[2,8,1,128]{3,2,1,0:T(1,128)S(1)} %reshape.83.right_ref.left_ref, bf16[8,8,4224]{2,1,0:T(8,128)(2,1)S(1)} %bitcast.60, ...), custom_call_target="tpu_custom_call" | custom-call | bytes 26666666 | tf_op jit(solution)/shard_map/product/pallas_call | solution.py:93
  95.2 6.0 %all-to-all-start.3 = ((bf16[16,8,1152]{2,1,0:T(8,128)(2,1)}), bf16[16,8,1152]{2,1,0:T(8,128)(2,1)S(1)}, u32[]{:S(2)}, u32[]{:S(2)}) async-start(bf16[16,8,1152]{2,1,0:T(8,128)(2,1)} %product.2), calls=%async_computation.3 | async-start | bytes 589824 | tf_op jit(solution)/shard_map/all_to_all | solution.py:67
  102.8 5.5 %all_pairs.1.matrix_ref = bf16[2048,1024]{1,0:T(8,128)(2,1)S(1)} custom-call(f32[2,16,1,128]{3,2,1,0:T(1,128)S(1)} %get-tuple-element.73.left_ref, f32[2,8,1,128]{3,2,1,0:T(1,128)S(1)} %get-tuple-element.74.right_ref), custom_call_target="tpu_custom_call" | custom-call | bytes 18000000 | tf_op jit(solution)/shard_map/all_pairs/pallas_call | solution.py:421
  112.9 5.0 %all-to-all-start.4 = ((bf16[16,8,1024]{2,1,0:T(8,128)(2,1)}), bf16[16,8,1024]{2,1,0:T(8,128)(2,1)S(1)}, u32[]{:S(2)}, u32[]{:S(2)}) async-start(bf16[16,8,1024]{2,1,0:T(8,128)(2,1)} %get-tuple-element.79), calls=%async_computation.4 | async-start | bytes 524288 | tf_op jit(solution)/shard_map/all_to_all | solution.py:67
  118.0 3.3 %collective-permute-start.6 = (f32[8,1024]{1,0:T(8,128)S(1)}, f32[8,1024]{1,0:T(8,128)S(1)}, u32[]{:S(2)}, u32[]{:S(2)}) collective-permute-start(f32[8,1024]{1,0:T(8,128)S(1)} %get-tuple-element.80), channel_id=1, source_target_pairs={{0,0},{24,1},{32,2},{56,3},{64,4},{88,5},{96,6},{120,7},{128,8},{1... | collective-permute-start | bytes 98312 | tf_op jit(solution)/shard_map/ppermute | solution.py:59
  122.5 3.0 %collective-permute-done.6.mid_ref = f32[8,1024]{1,0:T(8,128)S(1)} collective-permute-done((f32[8,1024]{1,0:T(8,128)S(1)}, f32[8,1024]{1,0:T(8,128)S(1)}, u32[]{:S(2)}, u32[]{:S(2)}) %collective-permute-start.6) | collective-permute-done | bytes 32800 | tf_op jit(solution)/shard_map/ppermute | solution.py:59
  125.5 2.1 all-to-all-done.4
  127.7 2.4 product.3
  130.1 2.8 %collective-permute-start.7 = (bf16[8,8,1024]{2,1,0:T(8,128)(2,1)S(1)}, bf16[8,8,1024]{2,1,0:T(8,128)(2,1)S(1)}, u32[]{:S(2)}, u32[]{:S(2)}) collective-permute-start(bf16[8,8,1024]{2,1,0:T(8,128)(2,1)S(1)} %get-tuple-element.87), channel_id=1, source_target_pairs={{0,16},{16,0},{1,17},{17,1},{2,18},{18,2},{3,19},{19,3},{4,20},{20... | collective-permute-start | bytes 393224 | tf_op jit(solution)/shard_map/ppermute | solution.py:63
  133.8 15.9 %all_to_all.61.arrived_ref = bf16[8,8,1024]{2,1,0:T(8,128)(2,1)S(1)} all-to-all(bf16[8,8,1024]{2,1,0:T(8,128)(2,1)S(1)} %add_convert_fusion.1), channel_id=1, replica_groups=mesh['y'=4,'zh'=2,'k'=2,'x'=4,'zl'=4] {'y','zh'}, dimensions={0} | all-to-all | bytes 262144 | tf_op jit(solution)/shard_map/all_to_all | solution.py:67
  149.8 3.8 %coarse_product.1 = bf16[16,8,128]{2,1,0:T(8,128)(2,1)} custom-call(bf16[2048,1024]{1,0:T(8,128)(2,1)} %copy-done, bf16[8,8,1024]{2,1,0:T(8,128)(2,1)S(1)} %all_to_all.61.arrived_ref, f32[8,1024]{1,0:T(8,128)S(1)} %collective-permute-done.6.mid_ref), custom_call_target="tpu_custom_call" | custom-call | bytes 9000000 | tf_op jit(solution)/shard_map/coarse_product/pallas_call | solution.py:499
  153.6 4.9 %all-to-all-start.6 = ((bf16[16,8,128]{2,1,0:T(8,128)(2,1)}), bf16[16,8,128]{2,1,0:T(8,128)(2,1)S(1)}, u32[]{:S(2)}, u32[]{:S(2)}) async-start(bf16[16,8,128]{2,1,0:T(8,128)(2,1)} %coarse_product.1), calls=%async_computation.6 | async-start | bytes 65536 | tf_op jit(solution)/shard_map/all_to_all | solution.py:67
  158.5 6.8 %all-to-all-done.6.arrived_ref = bf16[16,8,128]{2,1,0:T(8,128)(2,1)S(1)} async-done(((bf16[16,8,128]{2,1,0:T(8,128)(2,1)}), bf16[16,8,128]{2,1,0:T(8,128)(2,1)S(1)}, u32[]{:S(2)}, u32[]{:S(2)}) %all-to-all-start.6) | async-done | bytes 32800 | tf_op jit(solution)/shard_map/all_to_all | solution.py:67
  165.4 9.5 %all_to_all.62.data_ref = bf16[16,2,8,128]{3,2,1,0:T(8,128)(2,1)S(1)} all-to-all(bf16[16,2,8,128]{3,2,1,0:T(8,128)(2,1)S(1)} %coarse_data_of.1), channel_id=1, replica_groups=mesh['y'=4,'zh'=2,'k'=2,'x'=4,'zl'=4] {'x','zl'}, dimensions={0} | all-to-all | bytes 131072 | tf_op jit(solution)/shard_map/all_to_all | solution.py:67
  175.1 9.4 %all_to_all.63.half_ref = bf16[16,8,128]{2,1,0:T(8,128)(2,1)S(1)} all-to-all(bf16[16,8,128]{2,1,0:T(8,128)(2,1)S(1)} %halfway_of.1), channel_id=1, replica_groups=mesh['y'=4,'zh'=2,'k'=2,'x'=4,'zl'=4] {'x','zl'}, dimensions={0} | all-to-all | bytes 65536 | tf_op jit(solution)/shard_map/all_to_all | solution.py:67
  185.6 3.5 %all-to-all-start.9 = ((bf16[16,8,128]{2,1,0:T(8,128)(2,1)}), bf16[16,8,128]{2,1,0:T(8,128)(2,1)S(1)}, u32[]{:S(2)}, u32[]{:S(2)}) async-start(bf16[16,8,128]{2,1,0:T(8,128)(2,1)} %coarse_coef_of.1), calls=%async_computation.9 | async-start | bytes 65536 | tf_op jit(solution)/shard_map/all_to_all | solution.py:67
  191.6 4.3 %all-to-all-done.9.coef_ref = bf16[16,8,128]{2,1,0:T(8,128)(2,1)S(1)} async-done(((bf16[16,8,128]{2,1,0:T(8,128)(2,1)}), bf16[16,8,128]{2,1,0:T(8,128)(2,1)S(1)}, u32[]{:S(2)}, u32[]{:S(2)}) %all-to-all-start.9) | async-done | bytes 32800 | tf_op jit(solution)/shard_map/all_to_all | solution.py:67
  195.9 2.5 %prolong.1 = bf16[32,8,1152]{2,1,0:T(8,128)(2,1)S(1)} custom-call(bf16[2048,1024]{1,0:T(8,128)(2,1)} %copy-done, bf16[16,8,128]{2,1,0:T(8,128)(2,1)S(1)} %all-to-all-done.9.coef_ref, bf16[8,8,128]{2,1,0:T(8,128)(2,1)S(1)} %fusion.4.low_ref, f32[8,1024]{1,0:T(8,128)S(1)} %collective-permute-done.6.mid_ref), custom_call_target="tpu_custom_call" | custom-call | bytes 9000000 | tf_op jit(solution)/shard_map/prolong/pallas_call | solution.py:499
  198.4 15.7 %all_to_all.64.own_ref = bf16[32,8,1152]{2,1,0:T(8,128)(2,1)S(1)} all-to-all(bf16[32,8,1152]{2,1,0:T(8,128)(2,1)S(1)} %prolong.1), channel_id=1, replica_groups=mesh['y'=4,'zh'=2,'k'=2,'x'=4,'zl'=4] {'y','zh','zl'}, dimensions={0} | all-to-all | bytes 1179648 | tf_op jit(solution)/shard_map/all_to_all | solution.py:67
  214.1 8.1 %collective-permute-start.8 = (bf16[32,8,1152]{2,1,0:T(8,128)(2,1)S(1)}, bf16[32,8,1152]{2,1,0:T(8,128)(2,1)S(1)}, u32[]{:S(2)}, u32[]{:S(2)}) collective-permute-start(bf16[32,8,1152]{2,1,0:T(8,128)(2,1)S(1)} %all_to_all.64.own_ref), channel_id=1, source_target_pairs={{0,16},{16,0},{1,17},{17,1},{2,18},{18,2},{3,19},{19,3},{4,20},{20... | collective-permute-start | bytes 1769480 | tf_op jit(solution)/shard_map/ppermute | solution.py:63
  224.2 9.3 %product_quarter.1 = bf16[4,128,256]{2,1,0:T(8,128)(2,1)} custom-call(s32[8,256]{1,0:T(8,128)S(1)} %quarter_of.1.list_ref, f32[2,32,1,128]{3,2,1,0:T(1,128)S(1)} %get-tuple-element.82.left_ref, f32[2,9,1,128]{3,2,1,0:T(1,128)S(1)} %pad.16.right_ref, bf16[32,8,1152]{2,1,0:T(8,128)(2,1)S(1)} %all_to_all.64.own_ref, ...), custom_call_target="tpu_custom_call" | custom-call | bytes 30000000 | tf_op jit(solution)/shard_map/product_quarter/pallas_call | solution.py:93
  233.6 3.4 %all-to-all-start.11 = ((bf16[4,128,256]{2,1,0:T(8,128)(2,1)}), bf16[4,128,256]{2,1,0:T(8,128)(2,1)S(1)}, u32[]{:S(2)}, u32[]{:S(2)}) async-start(bf16[4,128,256]{2,1,0:T(8,128)(2,1)} %product_quarter.1), calls=%async_computation.11 | async-start | bytes 524288 | tf_op jit(solution)/shard_map/all_to_all | solution.py:67
  238.9 3.9 %all-to-all-done.11.arrived_ref = bf16[4,128,256]{2,1,0:T(8,128)(2,1)S(1)} async-done(((bf16[4,128,256]{2,1,0:T(8,128)(2,1)}), bf16[4,128,256]{2,1,0:T(8,128)(2,1)S(1)}, u32[]{:S(2)}, u32[]{:S(2)}) %all-to-all-start.11) | async-done | bytes 262176 | tf_op jit(solution)/shard_map/all_to_all | solution.py:67
  (67 shorter events, 29.2 us)
Async XLA Ops:
  0.6 11.2 %copy-start.3 = (bf16[128,128]{1,0:T(8,128)(2,1)S(1)}, bf16[128,128]{1,0:T(8,128)(2,1)}, u32[]{:S(2)}) copy-start(bf16[128,128]{1,0:T(8,128)(2,1)} %factor_ref.1) | copy-start | bytes 98308
  1.6 10.2 %collective-permute-start = (bf16[224,128]{1,0:T(8,128)(2,1)S(1)}, bf16[224,128]{1,0:T(8,128)(2,1)S(1)}, u32[]{:S(2)}, u32[]{:S(2)}) collective-permute-start(bf16[224,128]{1,0:T(8,128)(2,1)S(1)} %packed.1), channel_id=1, source_target_pairs={{0,0},{16,1},{32,2},{48,3},{64,4},{80,5},{96,6},{112,7},{128,8},{1... | collective-permute-start | bytes 172040 | tf_op jit(solution)/shard_map/ppermute | solution.py:48
  28.9 2.0 collective-permute-start.1
  46.5 16.2 %collective-permute-start.2 = (bf16[16,4096]{1,0:T(8,128)(2,1)S(1)}, bf16[16,4096]{1,0:T(8,128)(2,1)S(1)}, u32[]{:S(2)}, u32[]{:S(2)}) collective-permute-start(bf16[16,4096]{1,0:T(8,128)(2,1)S(1)} %sum_of.1.here_ref), channel_id=1, source_target_pairs={{0,32},{32,0},{1,33},{33,1},{2,34},{34,2},{3,35},{35,3},{4,36},{36... | collective-permute-start | bytes 393224 | tf_op jit(solution)/shard_map/ppermute | solution.py:697
  55.1 7.6 %collective-permute-start.3 = (bf16[288,128]{1,0:T(8,128)(2,1)S(1)}, bf16[288,128]{1,0:T(8,128)(2,1)S(1)}, u32[]{:S(2)}, u32[]{:S(2)}) collective-permute-start(bf16[288,128]{1,0:T(8,128)(2,1)S(1)} %get-tuple-element.63), channel_id=1, source_target_pairs={{0,32},{32,0},{1,33},{33,1},{2,34},{34,2},{3,35},{35,3},{4,36},{36... | collective-permute-start | bytes 221192 | tf_op jit(solution)/shard_map/ppermute | solution.py:699
  63.6 10.5 %all-to-all-start.1 = ((bf16[4,16,4224]{2,1,0:T(8,128)(2,1)}), bf16[4,16,4224]{2,1,0:T(8,128)(2,1)S(1)}, u32[]{:S(2)}, u32[]{:S(2)}) async-start(bf16[4,16,4224]{2,1,0:T(8,128)(2,1)} %residual_of.1), calls=%async_computation.1 | async-start | bytes 1081344 | tf_op jit(solution)/shard_map/all_to_all | solution.py:67
  74.9 5.7 %collective-permute-start.4 = (bf16[8,8,4224]{2,1,0:T(8,128)(2,1)S(1)}, bf16[8,8,4224]{2,1,0:T(8,128)(2,1)S(1)}, u32[]{:S(2)}, u32[]{:S(2)}) collective-permute-start(bf16[8,8,4224]{2,1,0:T(8,128)(2,1)S(1)} %bitcast.59), channel_id=1, source_target_pairs={{0,16},{16,0},{1,17},{17,1},{2,18},{18,2},{3,19},{19,3},{4,20},{20... | collective-permute-start | bytes 1622024 | tf_op jit(solution)/shard_map/ppermute | solution.py:63
  80.6 13.4 %all-to-all-start.2 = ((bf16[4,576,128]{2,1,0:T(8,128)(2,1)}), bf16[4,576,128]{2,1,0:T(8,128)(2,1)S(1)}, u32[]{:S(2)}, u32[]{:S(2)}) async-start(bf16[4,576,128]{2,1,0:T(8,128)(2,1)} %broadcast_in_dim.7), calls=%async_computation.2 | async-start | bytes 1179648 | tf_op jit(solution)/shard_map/all_to_all | solution.py:67
  94.0 7.2 %collective-permute-start.5 = (bf16[4,576,128]{2,1,0:T(8,128)(2,1)S(1)}, bf16[4,576,128]{2,1,0:T(8,128)(2,1)S(1)}, u32[]{:S(2)}, u32[]{:S(2)}) collective-permute-start(bf16[4,576,128]{2,1,0:T(8,128)(2,1)S(1)} %all-to-all-done.2.own_ref), channel_id=1, source_target_pairs={{0,16},{16,0},{1,17},{17,1},{2,18},{18,2},{3,19},{19,3},{4,20},{20... | collective-permute-start | bytes 1769480 | tf_op jit(solution)/shard_map/ppermute | solution.py:63
  95.2 16.9 %all-to-all-start.3 = ((bf16[16,8,1152]{2,1,0:T(8,128)(2,1)}), bf16[16,8,1152]{2,1,0:T(8,128)(2,1)S(1)}, u32[]{:S(2)}, u32[]{:S(2)}) async-start(bf16[16,8,1152]{2,1,0:T(8,128)(2,1)} %product.2), calls=%async_computation.3 | async-start | bytes 589824 | tf_op jit(solution)/shard_map/all_to_all | solution.py:67
  102.0 0.8 copy-start.1
  108.3 2.0 copy-start
  112.9 14.8 %all-to-all-start.4 = ((bf16[16,8,1024]{2,1,0:T(8,128)(2,1)}), bf16[16,8,1024]{2,1,0:T(8,128)(2,1)S(1)}, u32[]{:S(2)}, u32[]{:S(2)}) async-start(bf16[16,8,1024]{2,1,0:T(8,128)(2,1)} %get-tuple-element.79), calls=%async_computation.4 | async-start | bytes 524288 | tf_op jit(solution)/shard_map/all_to_all | solution.py:67
  118.0 7.6 %collective-permute-start.6 = (f32[8,1024]{1,0:T(8,128)S(1)}, f32[8,1024]{1,0:T(8,128)S(1)}, u32[]{:S(2)}, u32[]{:S(2)}) collective-permute-start(f32[8,1024]{1,0:T(8,128)S(1)} %get-tuple-element.80), channel_id=1, source_target_pairs={{0,0},{24,1},{32,2},{56,3},{64,4},{88,5},{96,6},{120,7},{128,8},{1... | collective-permute-start | bytes 98312 | tf_op jit(solution)/shard_map/ppermute | solution.py:59
  130.1 3.7 %collective-permute-start.7 = (bf16[8,8,1024]{2,1,0:T(8,128)(2,1)S(1)}, bf16[8,8,1024]{2,1,0:T(8,128)(2,1)S(1)}, u32[]{:S(2)}, u32[]{:S(2)}) collective-permute-start(bf16[8,8,1024]{2,1,0:T(8,128)(2,1)S(1)} %get-tuple-element.87), channel_id=1, source_target_pairs={{0,16},{16,0},{1,17},{17,1},{2,18},{18,2},{3,19},{19,3},{4,20},{20... | collective-permute-start | bytes 393224 | tf_op jit(solution)/shard_map/ppermute | solution.py:63
  149.8 25.2 %copy-start.2 = (bf16[2048,128]{1,0:T(8,128)(2,1)S(1)}, bf16[2048,128]{1,0:T(8,128)(2,1)}, u32[]{:S(2)}) copy-start(bf16[2048,128]{1,0:T(8,128)(2,1)} %copy-done.1) | copy-start | bytes 1572868
  153.6 11.8 %all-to-all-start.6 = ((bf16[16,8,128]{2,1,0:T(8,128)(2,1)}), bf16[16,8,128]{2,1,0:T(8,128)(2,1)S(1)}, u32[]{:S(2)}, u32[]{:S(2)}) async-start(bf16[16,8,128]{2,1,0:T(8,128)(2,1)} %coarse_product.1), calls=%async_computation.6 | async-start | bytes 65536 | tf_op jit(solution)/shard_map/all_to_all | solution.py:67
  185.6 10.3 %all-to-all-start.9 = ((bf16[16,8,128]{2,1,0:T(8,128)(2,1)}), bf16[16,8,128]{2,1,0:T(8,128)(2,1)S(1)}, u32[]{:S(2)}, u32[]{:S(2)}) async-start(bf16[16,8,128]{2,1,0:T(8,128)(2,1)} %coarse_coef_of.1), calls=%async_computation.9 | async-start | bytes 65536 | tf_op jit(solution)/shard_map/all_to_all | solution.py:67
  214.1 10.2 %collective-permute-start.8 = (bf16[32,8,1152]{2,1,0:T(8,128)(2,1)S(1)}, bf16[32,8,1152]{2,1,0:T(8,128)(2,1)S(1)}, u32[]{:S(2)}, u32[]{:S(2)}) collective-permute-start(bf16[32,8,1152]{2,1,0:T(8,128)(2,1)S(1)} %all_to_all.64.own_ref), channel_id=1, source_target_pairs={{0,16},{16,0},{1,17},{17,1},{2,18},{18,2},{3,19},{19,3},{4,20},{20... | collective-permute-start | bytes 1769480 | tf_op jit(solution)/shard_map/ppermute | solution.py:63
  233.6 9.2 %all-to-all-start.11 = ((bf16[4,128,256]{2,1,0:T(8,128)(2,1)}), bf16[4,128,256]{2,1,0:T(8,128)(2,1)S(1)}, u32[]{:S(2)}, u32[]{:S(2)}) async-start(bf16[4,128,256]{2,1,0:T(8,128)(2,1)} %product_quarter.1), calls=%async_computation.11 | async-start | bytes 524288 | tf_op jit(solution)/shard_map/all_to_all | solution.py:67
